TPU v7x, 128 devices: a whole 4x4x4 slice. The times are simulated.
128 devices in a mesh: dom: 32 (over y, x, core), rep: 4 (over z).
Axes of the slice: x: 4, y: 4, z: 4, core: 2. Of those that a mesh axis runs over, the one named last changes fastest.
Arguments:
- right_sides: float32 [4, 192, 16, 384], P(None, 'dom', 'rep'), may hold values from -6 to 6
- diag_inverse: bfloat16 [4, 192, 384, 384], P(None, 'dom'), may hold values from -0.3125 to 0.3125
- panel_mats: bfloat16 [3, 2048, 384, 384], P(None, ('dom', 'rep')), may hold values from -0.08984375 to 0.08984375
- panel_src: int32 [3, 2048], P(None, ('dom', 'rep')), may hold values from 0 to 17, as said below
- panel_dst: int32 [3, 2048], P(None, ('dom', 'rep')), may hold values from -1 to 191, as said below
Outputs:
- solution: float32 [4, 192, 16, 384], P(None, 'dom', 'rep')
Inputs may be any that keep to these rules, and one draw needn't show every extreme that they name: `panel_src`: an entry of row l is below (l + 1) * 6, so the source tile lies in a level at most l; most of the entries lie in level l itself. A live entry of a list owned by dom index o names a tile of dom index (o + j) mod 32 with -2 <= j <= 2 or j = 16. Among the 16 entries of one device's list for one row, at most 3 live entries have the same destination dom index (panel_dst // 6), and in every list some dom index has exactly 3; lists of low dom indices tend to hold more live entries than those of high ones.
All inputs are finite; a program needn't handle non-finite values.
Results may differ from a plain program's by a relative error of at most 0.012.
Values may be sent and summed in bfloat16 or wider, within the bound.
No kernel may reach another device: no remote copies, remote signals or barrier semaphores. Data moves between devices by JAX's collectives and lax.ppermute only.
A program may use at most 128 MiB of HBM per device.

v0:
```python
import jax
import jax.numpy as jnp
from jax import lax
from jax.sharding import PartitionSpec as P

HALF = 2
SLOTS = 3


def passed_along(value, axis, by):
    size = lax.axis_size(axis)
    return lax.ppermute(value, axis, [(i, (i + by) % size) for i in range(size)])


def from_everyone(value, axis):
    size = lax.axis_size(axis)
    return lax.all_to_all(
        jnp.broadcast_to(value[None], (size, *value.shape)), axis, 0, 0, tiled=True
    )


def in_order(blocks, dim):
    dims = list(blocks.shape[1:])
    dims[dim] *= blocks.shape[0]
    return jnp.moveaxis(blocks, 0, dim).reshape(dims)


def gather_directly(value, axis, dim):
    blocks = from_everyone(value, axis)
    return in_order(blocks, dim)


def panel_updates(solved_store, matrices, source_ids):
    sources = solved_store[source_ids]
    return jnp.einsum("pcx,pxy->pcy", sources, matrices, preferred_element_type=jnp.float32)


def deliver(contribution, destinations, tile_count, col_count):
    dom_size = lax.axis_size("dom")
    rep_size = lax.axis_size("rep")
    panel_count = contribution.shape[0]
    span_width = contribution.shape[2]
    split_cols = contribution.reshape(panel_count, rep_size, col_count, span_width)
    hood = 2 * HALF + 2
    far_offset = dom_size // 2
    owner = lax.axis_index("dom")
    is_live = destinations >= 0
    target = jnp.where(is_live, destinations // tile_count, -1)
    distance = (target - owner) % dom_size
    reach = jnp.where(distance == far_offset, hood - 1, (distance + HALF) % dom_size)
    dest_slot = destinations % tile_count
    positions = jnp.arange(panel_count, dtype=jnp.int32)
    earlier = (
        (target[:, None] == target[None, :])
        & is_live[None, :]
        & (positions[None, :] < positions[:, None])
    )
    ranking = jnp.sum(earlier.astype(jnp.int32), axis=1)
    placing = (
        is_live[:, None, None]
        & (reach[:, None, None] == jnp.arange(hood, dtype=jnp.int32)[None, :, None])
        & (ranking[:, None, None] == jnp.arange(SLOTS, dtype=jnp.int32)[None, None, :])
    )
    slot_vals = jnp.einsum("pjk,prcx->jkrcx", placing.astype(jnp.float32), split_cols)
    slot_ids = jnp.sum(jnp.where(placing, dest_slot[:, None, None] + 1, 0), axis=0) - 1
    slot_ids = jnp.broadcast_to(slot_ids[:, :, None], (hood, SLOTS, rep_size)).astype(jnp.float32)
    got_vals, got_ids = (
        lax.all_to_all(
            slot_vals.astype(jnp.bfloat16), "rep", split_axis=2, concat_axis=2, tiled=True
        ).astype(slot_vals.dtype),
        lax.all_to_all(
            slot_ids.astype(jnp.bfloat16), "rep", split_axis=2, concat_axis=2, tiled=True
        ).astype(slot_ids.dtype),
    )
    tile_range = jnp.arange(tile_count, dtype=jnp.float32)
    total = jnp.zeros((tile_count, col_count, span_width), jnp.float32)
    for reach_index in range(hood):
        offset = far_offset if reach_index == hood - 1 else reach_index - HALF
        piece_vals = got_vals[reach_index]
        piece_ids = got_ids[reach_index]
        if offset != 0:
            piece_vals, piece_ids = (
                passed_along(piece_vals.astype(jnp.bfloat16), "dom", offset).astype(
                    piece_vals.dtype
                ),
                passed_along(piece_ids.astype(jnp.bfloat16), "dom", offset).astype(piece_ids.dtype),
            )
        picker = (piece_ids[:, :, None] == tile_range[None, None, :]).astype(jnp.float32)
        total = total + jnp.einsum("kns,kncx->scx", picker, piece_vals)
    return total


def per_device(right_sides, diag_inverse, panel_mats, panel_src, panel_dst):
    level_count, tile_count, col_count, span_width = right_sides.shape
    rep_size = lax.axis_size("rep")
    solved_store = jnp.zeros(
        (level_count * tile_count, col_count * rep_size, span_width), jnp.bfloat16
    )
    results = []
    for level_index in range(level_count):
        residual = right_sides[level_index]
        if level_index > 0:
            contribution = panel_updates(
                solved_store, panel_mats[level_index - 1], panel_src[level_index - 1]
            )
            incoming = deliver(contribution, panel_dst[level_index - 1], tile_count, col_count)
            residual = residual - incoming
        solved = jnp.einsum(
            "scx,sxy->scy",
            residual.astype(jnp.bfloat16),
            diag_inverse[level_index],
            preferred_element_type=jnp.float32,
        )
        results.append(solved)
        if level_index + 1 < level_count:
            gathered = gather_directly(solved.astype(jnp.bfloat16), "rep", 1)
            solved_store = lax.dynamic_update_slice_in_dim(
                solved_store, gathered, level_index * tile_count, 0
            )
    return jnp.stack(results)


def solution(mesh):
    return jax.shard_map(
        per_device,
        mesh=mesh,
        in_specs=(
            P(None, "dom", "rep", None),
            P(None, "dom", None, None),
            P(None, ("dom", "rep"), None, None),
            P(None, ("dom", "rep")),
            P(None, ("dom", "rep")),
        ),
        out_specs=P(None, "dom", "rep", None),
        check_vma=False,
    )
```

profile of v0, /device:TPU:0, one launch (start us, length us, event | category | flops | bytes accessed | tf_op | source)
XLA Modules:
  0.0 152.1 jit_solution(1440767985097345752)
XLA Ops:
  0.0 1.9 %fusion.150 = (bf16[6,4,384]{2,1,0:T(4,128)(2,1)S(1)}, f32[6,4,384]{2,1,0:T(4,128)S(1)}) fusion(bf16[4,6,384,384]{3,2,1,0:T(8,128)(2,1)} %param.6, f32[4,6,4,384]{3,2,1,0:T(4,128)} %param.5), kind=kOutput, calls=%fused_computation.266 | convolution fusion | flops 7087104 | bytes 1843200 | tf_op jit(solution)/shard_map/scx,sxy->scy/dot_general | solution.py:108
  1.9 0.7 broadcast_in_dim.50
  2.5 5.4 %all-to-all-start.1 = ((bf16[4,6,4,384]{3,2,1,0:T(4,128)(2,1)}), bf16[4,6,4,384]{3,2,1,0:T(4,128)(2,1)S(1)}, u32[]{:S(2)}, u32[]{:S(2)}) async-start(bf16[4,6,4,384]{3,2,1,0:T(4,128)(2,1)} %broadcast_in_dim.50), calls=%async_computation.1 | async-start | bytes 147456 | tf_op jit(solution)/shard_map/all_to_all | solution.py:17
  7.9 0.8 fusion.146
  8.7 0.8 compare_bitcast_fusion
  9.5 0.8 compare_select_fusion.15
  10.4 0.8 fusion.127
  11.8 0.8 fusion.139
  13.0 0.6 all-to-all-done.1
  13.6 0.6 broadcast_in_dim.49
  14.2 4.2 %all-to-all-start = ((bf16[6,3,4]{0,1,2:T(4,128)(2,1)}), bf16[6,3,4]{0,1,2:T(4,128)(2,1)S(1)}, u32[]{:S(2)}, u32[]{:S(2)}) async-start(bf16[6,3,4]{0,1,2:T(4,128)(2,1)} %broadcast_in_dim.49), calls=%async_computation | async-start | bytes 8192 | tf_op jit(solution)/shard_map/all_to_all | solution.py:71
  18.5 0.6 gather_fusion
  19.1 3.1 %fusion.4 = bf16[16,16,384]{2,1,0:T(8,128)(2,1)S(1)} fusion(bf16[16,16,384]{2,1,0:T(8,128)(2,1)S(1)} %gather_fusion, bf16[3,16,384,384]{3,2,1,0:T(8,128)(2,1)} %param.7), kind=kOutput, calls=%fused_computation.7 | convolution fusion | flops 75497472 | bytes 5111808 | tf_op jit(solution)/shard_map/pcx,pxy->pcy/dot_general | solution.py:35
  22.5 0.8 copy.154
  23.2 0.4 all-to-all-done
  23.7 4.4 %all-to-all-start.2 = ((bf16[6,3,4,4,384]{4,3,1,0,2:T(4,128)(2,1)}), bf16[6,3,4,4,384]{4,3,1,0,2:T(4,128)(2,1)S(1)}, u32[]{:S(2)}, u32[]{:S(2)}) async-start(bf16[6,3,4,4,384]{4,3,1,0,2:T(4,128)(2,1)} %copy.154), calls=%async_computation.2 | async-start | bytes 442368 | tf_op jit(solution)/shard_map/all_to_all | solution.py:68
  28.2 1.5 collective-permute-start.6
  30.0 5.1 %collective-permute-start.2 = (bf16[3,4]{1,0:T(4,128)(2,1)S(1)}, bf16[3,4]{1,0:T(4,128)(2,1)S(1)}, u32[]{:S(2)}, u32[]{:S(2)}) collective-permute-start(bf16[3,4]{1,0:T(4,128)(2,1)S(1)} %bitcast.410), channel_id=1, source_target_pairs={{0,124},{4,0},{8,4},{12,8},{16,12},{20,16},{24,20},{28,24},{32,28}... | collective-permute-start | bytes 80 | tf_op jit(solution)/shard_map/ppermute | solution.py:12
  35.3 2.0 %collective-permute-start.8 = (bf16[3,4]{1,0:T(4,128)(2,1)S(1)}, bf16[3,4]{1,0:T(4,128)(2,1)S(1)}, u32[]{:S(2)}, u32[]{:S(2)}) collective-permute-start(bf16[3,4]{1,0:T(4,128)(2,1)S(1)} %bitcast.418), channel_id=1, source_target_pairs={{0,64},{4,68},{8,72},{12,76},{16,80},{20,84},{24,88},{28,92},{32,9... | collective-permute-start | bytes 80 | tf_op jit(solution)/shard_map/ppermute | solution.py:12
  37.4 1.1 collective-permute-start
  38.6 1.8 %collective-permute-done.8 = bf16[3,4]{1,0:T(4,128)(2,1)S(1)} collective-permute-done((bf16[3,4]{1,0:T(4,128)(2,1)S(1)}, bf16[3,4]{1,0:T(4,128)(2,1)S(1)}, u32[]{:S(2)}, u32[]{:S(2)}) %collective-permute-start.8) | collective-permute-done | bytes 56 | tf_op jit(solution)/shard_map/ppermute | solution.py:12
  40.4 0.6 collective-permute-done
  41.3 5.1 %collective-permute-start.3 = (bf16[3,4,4,384]{3,1,0,2:T(4,128)(2,1)S(1)}, bf16[3,4,4,384]{3,1,0,2:T(4,128)(2,1)S(1)}, u32[]{:S(2)}, u32[]{:S(2)}) collective-permute-start(bf16[3,4,4,384]{3,1,0,2:T(4,128)(2,1)S(1)} %copy.159), channel_id=1, source_target_pairs={{0,124},{4,0},{8,4},{12,8},{16,12},{20,16},{24,20},{28,24},{32,28}... | collective-permute-start | bytes 110600 | tf_op jit(solution)/shard_map/ppermute | solution.py:12
  46.9 2.7 %collective-permute-start.1 = (bf16[3,4,4,384]{3,1,0,2:T(4,128)(2,1)S(1)}, bf16[3,4,4,384]{3,1,0,2:T(4,128)(2,1)S(1)}, u32[]{:S(2)}, u32[]{:S(2)}) collective-permute-start(bf16[3,4,4,384]{3,1,0,2:T(4,128)(2,1)S(1)} %copy.156), channel_id=1, source_target_pairs={{0,120},{4,124},{8,0},{12,4},{16,8},{20,12},{24,16},{28,20},{32,24... | collective-permute-start | bytes 110600 | tf_op jit(solution)/shard_map/ppermute | solution.py:12
  50.6 1.3 collective-permute-done.9
  52.5 1.8 %fusion.151 = (bf16[6,4,384]{2,1,0:T(4,128)(2,1)S(1)}, f32[6,4,384]{2,1,0:T(4,128)S(1)}) fusion(bf16[4,6,384,384]{3,2,1,0:T(8,128)(2,1)} %param.6, bf16[6,4,384]{2,0,1:T(8,128)(2,1)S(1)} %fusion.44), kind=kOutput, calls=%fused_computation.267 | convolution fusion | flops 7087104 | bytes 1843200 | tf_op jit(solution)/shard_map/scx,sxy->scy/dot_general | solution.py:108
  54.4 0.7 broadcast_in_dim.53
  55.0 4.8 %all-to-all-start.4 = ((bf16[4,6,4,384]{3,2,1,0:T(4,128)(2,1)}), bf16[4,6,4,384]{3,2,1,0:T(4,128)(2,1)S(1)}, u32[]{:S(2)}, u32[]{:S(2)}) async-start(bf16[4,6,4,384]{3,2,1,0:T(4,128)(2,1)} %broadcast_in_dim.53), calls=%async_computation.4 | async-start | bytes 147456 | tf_op jit(solution)/shard_map/all_to_all | solution.py:17
  59.9 5.7 %all-to-all-done.4 = bf16[4,6,4,384]{3,2,1,0:T(4,128)(2,1)S(1)} async-done(((bf16[4,6,4,384]{3,2,1,0:T(4,128)(2,1)}), bf16[4,6,4,384]{3,2,1,0:T(4,128)(2,1)S(1)}, u32[]{:S(2)}, u32[]{:S(2)}) %all-to-all-start.4) | async-done | bytes 73760 | tf_op jit(solution)/shard_map/all_to_all | solution.py:17
  65.5 0.6 broadcast_in_dim.52
  66.1 3.2 %all-to-all-start.3 = ((bf16[6,3,4]{0,1,2:T(4,128)(2,1)}), bf16[6,3,4]{0,1,2:T(4,128)(2,1)S(1)}, u32[]{:S(2)}, u32[]{:S(2)}) async-start(bf16[6,3,4]{0,1,2:T(4,128)(2,1)} %broadcast_in_dim.52), calls=%async_computation.3 | async-start | bytes 8192 | tf_op jit(solution)/shard_map/all_to_all | solution.py:71
  69.4 0.6 gather_fusion.1
  70.0 3.1 %fusion.2 = bf16[16,16,384]{2,1,0:T(8,128)(2,1)S(1)} fusion(bf16[16,16,384]{2,1,0:T(8,128)(2,1)S(1)} %gather_fusion.1, bf16[3,16,384,384]{3,2,1,0:T(8,128)(2,1)} %param.7), kind=kOutput, calls=%fused_computation.5 | convolution fusion | flops 75497472 | bytes 5111808 | tf_op jit(solution)/shard_map/pcx,pxy->pcy/dot_general | solution.py:35
  73.5 0.8 copy.177
  74.6 4.4 %all-to-all-start.5 = ((bf16[6,3,4,4,384]{4,3,1,0,2:T(4,128)(2,1)}), bf16[6,3,4,4,384]{4,3,1,0,2:T(4,128)(2,1)S(1)}, u32[]{:S(2)}, u32[]{:S(2)}) async-start(bf16[6,3,4,4,384]{4,3,1,0,2:T(4,128)(2,1)} %copy.177), calls=%async_computation.5 | async-start | bytes 442368 | tf_op jit(solution)/shard_map/all_to_all | solution.py:68
  79.5 0.5 collective-permute-start.14
  80.2 1.8 %collective-permute-start.18 = (bf16[3,4]{1,0:T(4,128)(2,1)S(1)}, bf16[3,4]{1,0:T(4,128)(2,1)S(1)}, u32[]{:S(2)}, u32[]{:S(2)}) collective-permute-start(bf16[3,4]{1,0:T(4,128)(2,1)S(1)} %bitcast.419), channel_id=1, source_target_pairs={{0,64},{4,68},{8,72},{12,76},{16,80},{20,84},{24,88},{28,92},{32,9... | collective-permute-start | bytes 80 | tf_op jit(solution)/shard_map/ppermute | solution.py:12
  82.2 4.4 %collective-permute-start.10 = (bf16[3,4]{1,0:T(4,128)(2,1)S(1)}, bf16[3,4]{1,0:T(4,128)(2,1)S(1)}, u32[]{:S(2)}, u32[]{:S(2)}) collective-permute-start(bf16[3,4]{1,0:T(4,128)(2,1)S(1)} %bitcast.421), channel_id=1, source_target_pairs={{0,120},{4,124},{8,0},{12,4},{16,8},{20,12},{24,16},{28,20},{32,24... | collective-permute-start | bytes 80 | tf_op jit(solution)/shard_map/ppermute | solution.py:12
  86.7 1.2 collective-permute-done.10
  88.0 3.8 %collective-permute-start.13 = (bf16[3,4,4,384]{3,1,0,2:T(4,128)(2,1)S(1)}, bf16[3,4,4,384]{3,1,0,2:T(4,128)(2,1)S(1)}, u32[]{:S(2)}, u32[]{:S(2)}) collective-permute-start(bf16[3,4,4,384]{3,1,0,2:T(4,128)(2,1)S(1)} %copy.182), channel_id=1, source_target_pairs={{0,124},{4,0},{8,4},{12,8},{16,12},{20,16},{24,20},{28,24},{32,28}... | collective-permute-start | bytes 110600 | tf_op jit(solution)/shard_map/ppermute | solution.py:12
  92.1 0.6 collective-permute-start.19
  92.7 5.1 %collective-permute-start.11 = (bf16[3,4,4,384]{3,1,0,2:T(4,128)(2,1)S(1)}, bf16[3,4,4,384]{3,1,0,2:T(4,128)(2,1)S(1)}, u32[]{:S(2)}, u32[]{:S(2)}) collective-permute-start(bf16[3,4,4,384]{3,1,0,2:T(4,128)(2,1)S(1)} %copy.179), channel_id=1, source_target_pairs={{0,120},{4,124},{8,0},{12,4},{16,8},{20,12},{24,16},{28,20},{32,24... | collective-permute-start | bytes 110600 | tf_op jit(solution)/shard_map/ppermute | solution.py:12
  98.3 0.9 collective-permute-done.17
  100.4 1.8 %fusion.152 = (bf16[6,4,384]{2,1,0:T(4,128)(2,1)S(1)}, f32[6,4,384]{2,1,0:T(4,128)S(1)}) fusion(bf16[4,6,384,384]{3,2,1,0:T(8,128)(2,1)} %param.6, bf16[6,4,384]{2,0,1:T(8,128)(2,1)S(1)} %fusion.43), kind=kOutput, calls=%fused_computation.268 | convolution fusion | flops 7087104 | bytes 1843200 | tf_op jit(solution)/shard_map/scx,sxy->scy/dot_general | solution.py:108
  102.2 0.7 broadcast_in_dim.56
  102.9 4.8 %all-to-all-start.7 = ((bf16[4,6,4,384]{3,2,1,0:T(4,128)(2,1)}), bf16[4,6,4,384]{3,2,1,0:T(4,128)(2,1)S(1)}, u32[]{:S(2)}, u32[]{:S(2)}) async-start(bf16[4,6,4,384]{3,2,1,0:T(4,128)(2,1)} %broadcast_in_dim.56), calls=%async_computation.7 | async-start | bytes 147456 | tf_op jit(solution)/shard_map/all_to_all | solution.py:17
  107.7 5.7 %all-to-all-done.7 = bf16[4,6,4,384]{3,2,1,0:T(4,128)(2,1)S(1)} async-done(((bf16[4,6,4,384]{3,2,1,0:T(4,128)(2,1)}), bf16[4,6,4,384]{3,2,1,0:T(4,128)(2,1)S(1)}, u32[]{:S(2)}, u32[]{:S(2)}) %all-to-all-start.7) | async-done | bytes 73760 | tf_op jit(solution)/shard_map/all_to_all | solution.py:17
  113.3 0.6 broadcast_in_dim.55
  113.9 3.2 %all-to-all-start.6 = ((bf16[6,3,4]{0,1,2:T(4,128)(2,1)}), bf16[6,3,4]{0,1,2:T(4,128)(2,1)S(1)}, u32[]{:S(2)}, u32[]{:S(2)}) async-start(bf16[6,3,4]{0,1,2:T(4,128)(2,1)} %broadcast_in_dim.55), calls=%async_computation.6 | async-start | bytes 8192 | tf_op jit(solution)/shard_map/all_to_all | solution.py:71
  117.3 0.6 gather_fusion.2
  117.9 3.1 %fusion = bf16[16,16,384]{2,1,0:T(8,128)(2,1)S(1)} fusion(bf16[16,16,384]{2,1,0:T(8,128)(2,1)S(1)} %gather_fusion.2, bf16[3,16,384,384]{3,2,1,0:T(8,128)(2,1)} %param.7), kind=kOutput, calls=%fused_computation.3 | convolution fusion | flops 75497472 | bytes 5111808 | tf_op jit(solution)/shard_map/pcx,pxy->pcy/dot_general | solution.py:35
  121.3 0.8 copy.200
  122.4 4.4 %all-to-all-start.8 = ((bf16[6,3,4,4,384]{4,3,1,0,2:T(4,128)(2,1)}), bf16[6,3,4,4,384]{4,3,1,0,2:T(4,128)(2,1)S(1)}, u32[]{:S(2)}, u32[]{:S(2)}) async-start(bf16[6,3,4,4,384]{4,3,1,0,2:T(4,128)(2,1)} %copy.200), calls=%async_computation.8 | async-start | bytes 442368 | tf_op jit(solution)/shard_map/all_to_all | solution.py:68
  127.3 5.1 %collective-permute-start.22 = (bf16[3,4]{1,0:T(4,128)(2,1)S(1)}, bf16[3,4]{1,0:T(4,128)(2,1)S(1)}, u32[]{:S(2)}, u32[]{:S(2)}) collective-permute-start(bf16[3,4]{1,0:T(4,128)(2,1)S(1)} %bitcast.416), channel_id=1, source_target_pairs={{0,124},{4,0},{8,4},{12,8},{16,12},{20,16},{24,20},{28,24},{32,28}... | collective-permute-start | bytes 80 | tf_op jit(solution)/shard_map/ppermute | solution.py:12
  132.5 1.1 collective-permute-start.28
  133.8 2.9 %collective-permute-start.20 = (bf16[3,4]{1,0:T(4,128)(2,1)S(1)}, bf16[3,4]{1,0:T(4,128)(2,1)S(1)}, u32[]{:S(2)}, u32[]{:S(2)}) collective-permute-start(bf16[3,4]{1,0:T(4,128)(2,1)S(1)} %bitcast.422), channel_id=1, source_target_pairs={{0,120},{4,124},{8,0},{12,4},{16,8},{20,12},{24,16},{28,20},{32,24... | collective-permute-start | bytes 80 | tf_op jit(solution)/shard_map/ppermute | solution.py:12
  136.7 0.8 collective-permute-done.28
  137.5 0.5 collective-permute-done.20
  138.3 5.1 %collective-permute-start.23 = (bf16[3,4,4,384]{3,1,0,2:T(4,128)(2,1)S(1)}, bf16[3,4,4,384]{3,1,0,2:T(4,128)(2,1)S(1)}, u32[]{:S(2)}, u32[]{:S(2)}) collective-permute-start(bf16[3,4,4,384]{3,1,0,2:T(4,128)(2,1)S(1)} %copy.205), channel_id=1, source_target_pairs={{0,124},{4,0},{8,4},{12,8},{16,12},{20,16},{24,20},{28,24},{32,28}... | collective-permute-start | bytes 110600 | tf_op jit(solution)/shard_map/ppermute | solution.py:12
  143.5 0.7 collective-permute-start.29
  144.2 2.7 %collective-permute-start.21 = (bf16[3,4,4,384]{3,1,0,2:T(4,128)(2,1)S(1)}, bf16[3,4,4,384]{3,1,0,2:T(4,128)(2,1)S(1)}, u32[]{:S(2)}, u32[]{:S(2)}) collective-permute-start(bf16[3,4,4,384]{3,1,0,2:T(4,128)(2,1)S(1)} %copy.202), channel_id=1, source_target_pairs={{0,120},{4,124},{8,0},{12,4},{16,8},{20,12},{24,16},{28,20},{32,24... | collective-permute-start | bytes 110600 | tf_op jit(solution)/shard_map/ppermute | solution.py:12
  147.9 1.1 collective-permute-done.29
  149.6 1.8 %fusion.39 = f32[1,6,4,384]{3,2,1,0:T(4,128)S(1)} fusion(bf16[4,6,384,384]{3,2,1,0:T(8,128)(2,1)} %param.6, bf16[6,4,384]{2,0,1:T(8,128)(2,1)S(1)} %fusion.42), kind=kOutput, calls=%fused_computation.63 | convolution fusion | flops 7077888 | bytes 1824768 | tf_op jit(solution)/shard_map/scx,sxy->scy/dot_general | solution.py:108
  151.4 0.7 pad_maximum_fusion
  (145 shorter events, 11.6 us)
Async XLA Ops:
  2.5 11.1 %all-to-all-start.1 = ((bf16[4,6,4,384]{3,2,1,0:T(4,128)(2,1)}), bf16[4,6,4,384]{3,2,1,0:T(4,128)(2,1)S(1)}, u32[]{:S(2)}, u32[]{:S(2)}) async-start(bf16[4,6,4,384]{3,2,1,0:T(4,128)(2,1)} %broadcast_in_dim.50), calls=%async_computation.1 | async-start | bytes 147456 | tf_op jit(solution)/shard_map/all_to_all | solution.py:17
  14.2 9.5 %all-to-all-start = ((bf16[6,3,4]{0,1,2:T(4,128)(2,1)}), bf16[6,3,4]{0,1,2:T(4,128)(2,1)S(1)}, u32[]{:S(2)}, u32[]{:S(2)}) async-start(bf16[6,3,4]{0,1,2:T(4,128)(2,1)} %broadcast_in_dim.49), calls=%async_computation | async-start | bytes 8192 | tf_op jit(solution)/shard_map/all_to_all | solution.py:71
  23.7 17.3 %all-to-all-start.2 = ((bf16[6,3,4,4,384]{4,3,1,0,2:T(4,128)(2,1)}), bf16[6,3,4,4,384]{4,3,1,0,2:T(4,128)(2,1)S(1)}, u32[]{:S(2)}, u32[]{:S(2)}) async-start(bf16[6,3,4,4,384]{4,3,1,0,2:T(4,128)(2,1)} %copy.154), calls=%async_computation.2 | async-start | bytes 442368 | tf_op jit(solution)/shard_map/all_to_all | solution.py:68
  28.2 10.3 %collective-permute-start.6 = (bf16[3,4]{1,0:T(4,128)(2,1)S(1)}, bf16[3,4]{1,0:T(4,128)(2,1)S(1)}, u32[]{:S(2)}, u32[]{:S(2)}) collective-permute-start(bf16[3,4]{1,0:T(4,128)(2,1)S(1)} %bitcast.408), channel_id=1, source_target_pairs={{0,8},{4,12},{8,16},{12,20},{16,24},{20,28},{24,32},{28,36},{32,40... | collective-permute-start | bytes 80 | tf_op jit(solution)/shard_map/ppermute | solution.py:12
  29.9 8.7 %collective-permute-start.4 = (bf16[3,4]{1,0:T(4,128)(2,1)S(1)}, bf16[3,4]{1,0:T(4,128)(2,1)S(1)}, u32[]{:S(2)}, u32[]{:S(2)}) collective-permute-start(bf16[3,4]{1,0:T(4,128)(2,1)S(1)} %bitcast.409), channel_id=1, source_target_pairs={{0,4},{4,8},{8,12},{12,16},{16,20},{20,24},{24,28},{28,32},{32,36}... | collective-permute-start | bytes 80 | tf_op jit(solution)/shard_map/ppermute | solution.py:12
  30.0 8.6 %collective-permute-start.2 = (bf16[3,4]{1,0:T(4,128)(2,1)S(1)}, bf16[3,4]{1,0:T(4,128)(2,1)S(1)}, u32[]{:S(2)}, u32[]{:S(2)}) collective-permute-start(bf16[3,4]{1,0:T(4,128)(2,1)S(1)} %bitcast.410), channel_id=1, source_target_pairs={{0,124},{4,0},{8,4},{12,8},{16,12},{20,16},{24,20},{28,24},{32,28}... | collective-permute-start | bytes 80 | tf_op jit(solution)/shard_map/ppermute | solution.py:12
  35.3 5.1 %collective-permute-start.8 = (bf16[3,4]{1,0:T(4,128)(2,1)S(1)}, bf16[3,4]{1,0:T(4,128)(2,1)S(1)}, u32[]{:S(2)}, u32[]{:S(2)}) collective-permute-start(bf16[3,4]{1,0:T(4,128)(2,1)S(1)} %bitcast.418), channel_id=1, source_target_pairs={{0,64},{4,68},{8,72},{12,76},{16,80},{20,84},{24,88},{28,92},{32,9... | collective-permute-start | bytes 80 | tf_op jit(solution)/shard_map/ppermute | solution.py:12
  37.4 3.6 %collective-permute-start = (bf16[3,4]{1,0:T(4,128)(2,1)S(1)}, bf16[3,4]{1,0:T(4,128)(2,1)S(1)}, u32[]{:S(2)}, u32[]{:S(2)}) collective-permute-start(bf16[3,4]{1,0:T(4,128)(2,1)S(1)} %bitcast.420), channel_id=1, source_target_pairs={{0,120},{4,124},{8,0},{12,4},{16,8},{20,12},{24,16},{28,20},{32,24... | collective-permute-start | bytes 80 | tf_op jit(solution)/shard_map/ppermute | solution.py:12
  41.1 8.7 %collective-permute-start.7 = (bf16[3,4,4,384]{3,1,0,2:T(4,128)(2,1)S(1)}, bf16[3,4,4,384]{3,1,0,2:T(4,128)(2,1)S(1)}, u32[]{:S(2)}, u32[]{:S(2)}) collective-permute-start(bf16[3,4,4,384]{3,1,0,2:T(4,128)(2,1)S(1)} %copy.168), channel_id=1, source_target_pairs={{0,8},{4,12},{8,16},{12,20},{16,24},{20,28},{24,32},{28,36},{32,40... | collective-permute-start | bytes 110600 | tf_op jit(solution)/shard_map/ppermute | solution.py:12
  41.2 8.9 %collective-permute-start.5 = (bf16[3,4,4,384]{3,1,0,2:T(4,128)(2,1)S(1)}, bf16[3,4,4,384]{3,1,0,2:T(4,128)(2,1)S(1)}, u32[]{:S(2)}, u32[]{:S(2)}) collective-permute-start(bf16[3,4,4,384]{3,1,0,2:T(4,128)(2,1)S(1)} %copy.165), channel_id=1, source_target_pairs={{0,4},{4,8},{8,12},{12,16},{16,20},{20,24},{24,28},{28,32},{32,36}... | collective-permute-start | bytes 110600 | tf_op jit(solution)/shard_map/ppermute | solution.py:12
  41.3 9.1 %collective-permute-start.3 = (bf16[3,4,4,384]{3,1,0,2:T(4,128)(2,1)S(1)}, bf16[3,4,4,384]{3,1,0,2:T(4,128)(2,1)S(1)}, u32[]{:S(2)}, u32[]{:S(2)}) collective-permute-start(bf16[3,4,4,384]{3,1,0,2:T(4,128)(2,1)S(1)} %copy.159), channel_id=1, source_target_pairs={{0,124},{4,0},{8,4},{12,8},{16,12},{20,16},{24,20},{28,24},{32,28}... | collective-permute-start | bytes 110600 | tf_op jit(solution)/shard_map/ppermute | solution.py:12
  46.4 5.5 %collective-permute-start.9 = (bf16[3,4,4,384]{3,1,0,2:T(4,128)(2,1)S(1)}, bf16[3,4,4,384]{3,1,0,2:T(4,128)(2,1)S(1)}, u32[]{:S(2)}, u32[]{:S(2)}) collective-permute-start(bf16[3,4,4,384]{3,1,0,2:T(4,128)(2,1)S(1)} %copy.171), channel_id=1, source_target_pairs={{0,64},{4,68},{8,72},{12,76},{16,80},{20,84},{24,88},{28,92},{32,9... | collective-permute-start | bytes 110600 | tf_op jit(solution)/shard_map/ppermute | solution.py:12
  46.9 5.4 %collective-permute-start.1 = (bf16[3,4,4,384]{3,1,0,2:T(4,128)(2,1)S(1)}, bf16[3,4,4,384]{3,1,0,2:T(4,128)(2,1)S(1)}, u32[]{:S(2)}, u32[]{:S(2)}) collective-permute-start(bf16[3,4,4,384]{3,1,0,2:T(4,128)(2,1)S(1)} %copy.156), channel_id=1, source_target_pairs={{0,120},{4,124},{8,0},{12,4},{16,8},{20,12},{24,16},{28,20},{32,24... | collective-permute-start | bytes 110600 | tf_op jit(solution)/shard_map/ppermute | solution.py:12
  55.0 10.5 %all-to-all-start.4 = ((bf16[4,6,4,384]{3,2,1,0:T(4,128)(2,1)}), bf16[4,6,4,384]{3,2,1,0:T(4,128)(2,1)S(1)}, u32[]{:S(2)}, u32[]{:S(2)}) async-start(bf16[4,6,4,384]{3,2,1,0:T(4,128)(2,1)} %broadcast_in_dim.53), calls=%async_computation.4 | async-start | bytes 147456 | tf_op jit(solution)/shard_map/all_to_all | solution.py:17
  66.1 8.5 %all-to-all-start.3 = ((bf16[6,3,4]{0,1,2:T(4,128)(2,1)}), bf16[6,3,4]{0,1,2:T(4,128)(2,1)S(1)}, u32[]{:S(2)}, u32[]{:S(2)}) async-start(bf16[6,3,4]{0,1,2:T(4,128)(2,1)} %broadcast_in_dim.52), calls=%async_computation.3 | async-start | bytes 8192 | tf_op jit(solution)/shard_map/all_to_all | solution.py:71
  74.6 13.3 %all-to-all-start.5 = ((bf16[6,3,4,4,384]{4,3,1,0,2:T(4,128)(2,1)}), bf16[6,3,4,4,384]{4,3,1,0,2:T(4,128)(2,1)S(1)}, u32[]{:S(2)}, u32[]{:S(2)}) async-start(bf16[6,3,4,4,384]{4,3,1,0,2:T(4,128)(2,1)} %copy.177), calls=%async_computation.5 | async-start | bytes 442368 | tf_op jit(solution)/shard_map/all_to_all | solution.py:68
  79.2 7.4 %collective-permute-start.12 = (bf16[3,4]{1,0:T(4,128)(2,1)S(1)}, bf16[3,4]{1,0:T(4,128)(2,1)S(1)}, u32[]{:S(2)}, u32[]{:S(2)}) collective-permute-start(bf16[3,4]{1,0:T(4,128)(2,1)S(1)} %bitcast.411), channel_id=1, source_target_pairs={{0,124},{4,0},{8,4},{12,8},{16,12},{20,16},{24,20},{28,24},{32,28}... | collective-permute-start | bytes 80 | tf_op jit(solution)/shard_map/ppermute | solution.py:12
  79.3 7.3 %collective-permute-start.16 = (bf16[3,4]{1,0:T(4,128)(2,1)S(1)}, bf16[3,4]{1,0:T(4,128)(2,1)S(1)}, u32[]{:S(2)}, u32[]{:S(2)}) collective-permute-start(bf16[3,4]{1,0:T(4,128)(2,1)S(1)} %bitcast.412), channel_id=1, source_target_pairs={{0,8},{4,12},{8,16},{12,20},{16,24},{20,28},{24,32},{28,36},{32,40... | collective-permute-start | bytes 80 | tf_op jit(solution)/shard_map/ppermute | solution.py:12
  79.5 7.2 %collective-permute-start.14 = (bf16[3,4]{1,0:T(4,128)(2,1)S(1)}, bf16[3,4]{1,0:T(4,128)(2,1)S(1)}, u32[]{:S(2)}, u32[]{:S(2)}) collective-permute-start(bf16[3,4]{1,0:T(4,128)(2,1)S(1)} %bitcast.413), channel_id=1, source_target_pairs={{0,4},{4,8},{8,12},{12,16},{16,20},{20,24},{24,28},{28,32},{32,36}... | collective-permute-start | bytes 80 | tf_op jit(solution)/shard_map/ppermute | solution.py:12
  80.2 6.5 %collective-permute-start.18 = (bf16[3,4]{1,0:T(4,128)(2,1)S(1)}, bf16[3,4]{1,0:T(4,128)(2,1)S(1)}, u32[]{:S(2)}, u32[]{:S(2)}) collective-permute-start(bf16[3,4]{1,0:T(4,128)(2,1)S(1)} %bitcast.419), channel_id=1, source_target_pairs={{0,64},{4,68},{8,72},{12,76},{16,80},{20,84},{24,88},{28,92},{32,9... | collective-permute-start | bytes 80 | tf_op jit(solution)/shard_map/ppermute | solution.py:12
  82.2 5.7 %collective-permute-start.10 = (bf16[3,4]{1,0:T(4,128)(2,1)S(1)}, bf16[3,4]{1,0:T(4,128)(2,1)S(1)}, u32[]{:S(2)}, u32[]{:S(2)}) collective-permute-start(bf16[3,4]{1,0:T(4,128)(2,1)S(1)} %bitcast.421), channel_id=1, source_target_pairs={{0,120},{4,124},{8,0},{12,4},{16,8},{20,12},{24,16},{28,20},{32,24... | collective-permute-start | bytes 80 | tf_op jit(solution)/shard_map/ppermute | solution.py:12
  88.0 10.0 %collective-permute-start.13 = (bf16[3,4,4,384]{3,1,0,2:T(4,128)(2,1)S(1)}, bf16[3,4,4,384]{3,1,0,2:T(4,128)(2,1)S(1)}, u32[]{:S(2)}, u32[]{:S(2)}) collective-permute-start(bf16[3,4,4,384]{3,1,0,2:T(4,128)(2,1)S(1)} %copy.182), channel_id=1, source_target_pairs={{0,124},{4,0},{8,4},{12,8},{16,12},{20,16},{24,20},{28,24},{32,28}... | collective-permute-start | bytes 110600 | tf_op jit(solution)/shard_map/ppermute | solution.py:12
  91.9 7.3 %collective-permute-start.17 = (bf16[3,4,4,384]{3,1,0,2:T(4,128)(2,1)S(1)}, bf16[3,4,4,384]{3,1,0,2:T(4,128)(2,1)S(1)}, u32[]{:S(2)}, u32[]{:S(2)}) collective-permute-start(bf16[3,4,4,384]{3,1,0,2:T(4,128)(2,1)S(1)} %copy.191), channel_id=1, source_target_pairs={{0,8},{4,12},{8,16},{12,20},{16,24},{20,28},{24,32},{28,36},{32,40... | collective-permute-start | bytes 110600 | tf_op jit(solution)/shard_map/ppermute | solution.py:12
  92.0 7.5 %collective-permute-start.15 = (bf16[3,4,4,384]{3,1,0,2:T(4,128)(2,1)S(1)}, bf16[3,4,4,384]{3,1,0,2:T(4,128)(2,1)S(1)}, u32[]{:S(2)}, u32[]{:S(2)}) collective-permute-start(bf16[3,4,4,384]{3,1,0,2:T(4,128)(2,1)S(1)} %copy.188), channel_id=1, source_target_pairs={{0,4},{4,8},{8,12},{12,16},{16,20},{20,24},{24,28},{28,32},{32,36}... | collective-permute-start | bytes 110600 | tf_op jit(solution)/shard_map/ppermute | solution.py:12
  92.1 7.7 %collective-permute-start.19 = (bf16[3,4,4,384]{3,1,0,2:T(4,128)(2,1)S(1)}, bf16[3,4,4,384]{3,1,0,2:T(4,128)(2,1)S(1)}, u32[]{:S(2)}, u32[]{:S(2)}) collective-permute-start(bf16[3,4,4,384]{3,1,0,2:T(4,128)(2,1)S(1)} %copy.194), channel_id=1, source_target_pairs={{0,64},{4,68},{8,72},{12,76},{16,80},{20,84},{24,88},{28,92},{32,9... | collective-permute-start | bytes 110600 | tf_op jit(solution)/shard_map/ppermute | solution.py:12
  92.7 7.4 %collective-permute-start.11 = (bf16[3,4,4,384]{3,1,0,2:T(4,128)(2,1)S(1)}, bf16[3,4,4,384]{3,1,0,2:T(4,128)(2,1)S(1)}, u32[]{:S(2)}, u32[]{:S(2)}) collective-permute-start(bf16[3,4,4,384]{3,1,0,2:T(4,128)(2,1)S(1)} %copy.179), channel_id=1, source_target_pairs={{0,120},{4,124},{8,0},{12,4},{16,8},{20,12},{24,16},{28,20},{32,24... | collective-permute-start | bytes 110600 | tf_op jit(solution)/shard_map/ppermute | solution.py:12
  102.9 10.5 %all-to-all-start.7 = ((bf16[4,6,4,384]{3,2,1,0:T(4,128)(2,1)}), bf16[4,6,4,384]{3,2,1,0:T(4,128)(2,1)S(1)}, u32[]{:S(2)}, u32[]{:S(2)}) async-start(bf16[4,6,4,384]{3,2,1,0:T(4,128)(2,1)} %broadcast_in_dim.56), calls=%async_computation.7 | async-start | bytes 147456 | tf_op jit(solution)/shard_map/all_to_all | solution.py:17
  113.9 8.5 %all-to-all-start.6 = ((bf16[6,3,4]{0,1,2:T(4,128)(2,1)}), bf16[6,3,4]{0,1,2:T(4,128)(2,1)S(1)}, u32[]{:S(2)}, u32[]{:S(2)}) async-start(bf16[6,3,4]{0,1,2:T(4,128)(2,1)} %broadcast_in_dim.55), calls=%async_computation.6 | async-start | bytes 8192 | tf_op jit(solution)/shard_map/all_to_all | solution.py:71
  122.4 15.6 %all-to-all-start.8 = ((bf16[6,3,4,4,384]{4,3,1,0,2:T(4,128)(2,1)}), bf16[6,3,4,4,384]{4,3,1,0,2:T(4,128)(2,1)S(1)}, u32[]{:S(2)}, u32[]{:S(2)}) async-start(bf16[6,3,4,4,384]{4,3,1,0,2:T(4,128)(2,1)} %copy.200), calls=%async_computation.8 | async-start | bytes 442368 | tf_op jit(solution)/shard_map/all_to_all | solution.py:68
  127.0 9.7 %collective-permute-start.26 = (bf16[3,4]{1,0:T(4,128)(2,1)S(1)}, bf16[3,4]{1,0:T(4,128)(2,1)S(1)}, u32[]{:S(2)}, u32[]{:S(2)}) collective-permute-start(bf16[3,4]{1,0:T(4,128)(2,1)S(1)} %bitcast.414), channel_id=1, source_target_pairs={{0,8},{4,12},{8,16},{12,20},{16,24},{20,28},{24,32},{28,36},{32,40... | collective-permute-start | bytes 80 | tf_op jit(solution)/shard_map/ppermute | solution.py:12
  127.1 9.6 %collective-permute-start.24 = (bf16[3,4]{1,0:T(4,128)(2,1)S(1)}, bf16[3,4]{1,0:T(4,128)(2,1)S(1)}, u32[]{:S(2)}, u32[]{:S(2)}) collective-permute-start(bf16[3,4]{1,0:T(4,128)(2,1)S(1)} %bitcast.415), channel_id=1, source_target_pairs={{0,4},{4,8},{8,12},{12,16},{16,20},{20,24},{24,28},{28,32},{32,36}... | collective-permute-start | bytes 80 | tf_op jit(solution)/shard_map/ppermute | solution.py:12
  127.3 9.4 %collective-permute-start.22 = (bf16[3,4]{1,0:T(4,128)(2,1)S(1)}, bf16[3,4]{1,0:T(4,128)(2,1)S(1)}, u32[]{:S(2)}, u32[]{:S(2)}) collective-permute-start(bf16[3,4]{1,0:T(4,128)(2,1)S(1)} %bitcast.416), channel_id=1, source_target_pairs={{0,124},{4,0},{8,4},{12,8},{16,12},{20,16},{24,20},{28,24},{32,28}... | collective-permute-start | bytes 80 | tf_op jit(solution)/shard_map/ppermute | solution.py:12
  132.5 5.1 %collective-permute-start.28 = (bf16[3,4]{1,0:T(4,128)(2,1)S(1)}, bf16[3,4]{1,0:T(4,128)(2,1)S(1)}, u32[]{:S(2)}, u32[]{:S(2)}) collective-permute-start(bf16[3,4]{1,0:T(4,128)(2,1)S(1)} %bitcast.417), channel_id=1, source_target_pairs={{0,64},{4,68},{8,72},{12,76},{16,80},{20,84},{24,88},{28,92},{32,9... | collective-permute-start | bytes 80 | tf_op jit(solution)/shard_map/ppermute | solution.py:12
  133.8 4.2 %collective-permute-start.20 = (bf16[3,4]{1,0:T(4,128)(2,1)S(1)}, bf16[3,4]{1,0:T(4,128)(2,1)S(1)}, u32[]{:S(2)}, u32[]{:S(2)}) collective-permute-start(bf16[3,4]{1,0:T(4,128)(2,1)S(1)} %bitcast.422), channel_id=1, source_target_pairs={{0,120},{4,124},{8,0},{12,4},{16,8},{20,12},{24,16},{28,20},{32,24... | collective-permute-start | bytes 80 | tf_op jit(solution)/shard_map/ppermute | solution.py:12
  138.1 9.0 %collective-permute-start.27 = (bf16[3,4,4,384]{3,1,0,2:T(4,128)(2,1)S(1)}, bf16[3,4,4,384]{3,1,0,2:T(4,128)(2,1)S(1)}, u32[]{:S(2)}, u32[]{:S(2)}) collective-permute-start(bf16[3,4,4,384]{3,1,0,2:T(4,128)(2,1)S(1)} %copy.214), channel_id=1, source_target_pairs={{0,8},{4,12},{8,16},{12,20},{16,24},{20,28},{24,32},{28,36},{32,40... | collective-permute-start | bytes 110600 | tf_op jit(solution)/shard_map/ppermute | solution.py:12
  138.2 9.2 %collective-permute-start.25 = (bf16[3,4,4,384]{3,1,0,2:T(4,128)(2,1)S(1)}, bf16[3,4,4,384]{3,1,0,2:T(4,128)(2,1)S(1)}, u32[]{:S(2)}, u32[]{:S(2)}) collective-permute-start(bf16[3,4,4,384]{3,1,0,2:T(4,128)(2,1)S(1)} %copy.211), channel_id=1, source_target_pairs={{0,4},{4,8},{8,12},{12,16},{16,20},{20,24},{24,28},{28,32},{32,36}... | collective-permute-start | bytes 110600 | tf_op jit(solution)/shard_map/ppermute | solution.py:12
  138.3 9.3 %collective-permute-start.23 = (bf16[3,4,4,384]{3,1,0,2:T(4,128)(2,1)S(1)}, bf16[3,4,4,384]{3,1,0,2:T(4,128)(2,1)S(1)}, u32[]{:S(2)}, u32[]{:S(2)}) collective-permute-start(bf16[3,4,4,384]{3,1,0,2:T(4,128)(2,1)S(1)} %copy.205), channel_id=1, source_target_pairs={{0,124},{4,0},{8,4},{12,8},{16,12},{20,16},{24,20},{28,24},{32,28}... | collective-permute-start | bytes 110600 | tf_op jit(solution)/shard_map/ppermute | solution.py:12
  143.5 5.5 %collective-permute-start.29 = (bf16[3,4,4,384]{3,1,0,2:T(4,128)(2,1)S(1)}, bf16[3,4,4,384]{3,1,0,2:T(4,128)(2,1)S(1)}, u32[]{:S(2)}, u32[]{:S(2)}) collective-permute-start(bf16[3,4,4,384]{3,1,0,2:T(4,128)(2,1)S(1)} %copy.217), channel_id=1, source_target_pairs={{0,64},{4,68},{8,72},{12,76},{16,80},{20,84},{24,88},{28,92},{32,9... | collective-permute-start | bytes 110600 | tf_op jit(solution)/shard_map/ppermute | solution.py:12
  144.2 5.1 %collective-permute-start.21 = (bf16[3,4,4,384]{3,1,0,2:T(4,128)(2,1)S(1)}, bf16[3,4,4,384]{3,1,0,2:T(4,128)(2,1)S(1)}, u32[]{:S(2)}, u32[]{:S(2)}) collective-permute-start(bf16[3,4,4,384]{3,1,0,2:T(4,128)(2,1)S(1)} %copy.202), channel_id=1, source_target_pairs={{0,120},{4,124},{8,0},{12,4},{16,8},{20,12},{24,16},{28,20},{32,24... | collective-permute-start | bytes 110600 | tf_op jit(solution)/shard_map/ppermute | solution.py:12
where the time goes:
time: 153 us; the launch traced here: 152 us
  starting transfers between devices  91 us (59%)
  matrix products  22.3 us (15%)
  waiting for transfers between devices  21.4 us (14%)
  local copies, waits for them, and re-layouts  11.7 us (8%)
  other arithmetic  5.2 us (3%)
    ppermute x30, starting transfers between devices, passed_along(): lax.ppermute(value, axis, [(i, (i + by) % size) for i in range(size)])  52.2 us
    all_to_all x3, starting transfers between devices, from_everyone(): lax.all_to_all(jnp.broadcast_to(value[None], (size, *value.shape)), axis,...  15 us
    all_to_all x3, starting transfers between devices, deliver(): lax.all_to_all(slot_vals.astype(jnp.bfloat16), 'rep', split_axis=2, conca...  13.1 us
    all_to_all x3, waiting for transfers between devices, from_everyone(): lax.all_to_all(jnp.broadcast_to(value[None], (size, *value.shape)), axis,...  11.9 us
    all_to_all x3, starting transfers between devices, deliver(): lax.all_to_all(slot_ids.astype(jnp.bfloat16), 'rep', split_axis=2, concat...  10.7 us
    dot_general x3, matrix products, panel_updates(): jnp.einsum('pcx,pxy->pcy', sources, matrices, preferred_element_type=jnp....  9.37 us
    ppermute x30, waiting for transfers between devices, passed_along(): lax.ppermute(value, axis, [(i, (i + by) % size) for i in range(size)])  8.25 us
    dot_general x4, matrix products, per_device(): jnp.einsum('scx,sxy->scy', residual.astype(jnp.bfloat16), diag_inverse[le...  7.38 us
  transfers between devices with their start and end apart: 39, of which 14 were waited for; matrix products, arithmetic and copies ran while one was open for 17% of the time, Pallas kernels for 0%

commit v1 on v0

v1 whole, which is shorter than its diff:
```python
import functools

import jax
import jax.numpy as jnp
from jax import lax
from jax.experimental import pallas as pl
from jax.experimental.pallas import tpu as pltpu
from jax.sharding import PartitionSpec as P

HALF = 2
HOOD = 2 * HALF + 2


def passed_along(value, axis, by):
    size = lax.axis_size(axis)
    return lax.ppermute(value, axis, [(i, (i + by) % size) for i in range(size)])


def level_body(level, last, *refs):
    refs = list(refs)
    rep_ref = refs.pop(0)
    src_ref, slot_ref = (refs.pop(0), refs.pop(0)) if not last else (None, None)
    parts = [refs.pop(0) for _ in range(4)]
    diag_ref = refs.pop(0)
    mats_ref = refs.pop(0) if not last else None
    prev = [refs.pop(0) for _ in range(level)]
    out_ref = refs.pop(0)
    if last:
        (solved_scr,) = refs
    else:
        stored_ref = refs.pop(0)
        messages = [refs.pop(0) for _ in range(HOOD)]
        solved_scr, store_scr, acc_scr = refs
    tiles, cols, _ = parts[0].shape
    group = cols // 4
    for t in range(tiles):
        residual = sum(part[t].astype(jnp.float32) for part in parts).astype(jnp.bfloat16)
        solved = jnp.dot(residual, diag_ref[t], preferred_element_type=jnp.float32)
        solved_scr[t] = solved
        if not last:
            stored_ref[t] = solved.astype(jnp.bfloat16)
            store_scr[level * tiles + t] = solved.astype(jnp.bfloat16)
    own = solved_scr[:, :group, :]
    for other in range(1, cols // group):
        own = jnp.where(rep_ref[0] == other, solved_scr[:, other * group : (other + 1) * group, :], own)
    if last:
        for earlier in range(level):
            out_ref[earlier] = prev[earlier][...]
        out_ref[level] = own
        return
    out_ref[...] = own
    for earlier in range(level):
        for t in range(tiles):
            store_scr[earlier * tiles + t] = prev[earlier][t]
    acc_scr[...] = jnp.zeros_like(acc_scr)
    for p in range(mats_ref.shape[0]):
        update = jnp.dot(store_scr[src_ref[p]], mats_ref[p], preferred_element_type=jnp.float32)
        slot = slot_ref[p]
        acc_scr[slot] = acc_scr[slot] + update
    for j in range(HOOD):
        messages[j][...] = acc_scr[j * tiles : (j + 1) * tiles].astype(jnp.bfloat16)


def run_level(level, last, rep, ids, parts, diag, mats, prev, out_shape):
    tiles, cols, span = parts[0].shape
    group = cols // 4
    smem = pl.BlockSpec(memory_space=pltpu.SMEM)
    vmem = pl.BlockSpec(memory_space=pltpu.VMEM)
    args = [rep, *ids, *parts, diag]
    specs = [smem] * (1 + len(ids)) + [vmem] * 5
    if not last:
        args.append(mats)
        specs.append(vmem)
    args += prev
    specs += [vmem] * len(prev)
    scratch = [pltpu.VMEM((tiles, cols, span), jnp.float32)]
    if last:
        outs = jax.ShapeDtypeStruct(out_shape, jnp.float32)
        out_specs = vmem
    else:
        block = jax.ShapeDtypeStruct((tiles, cols, span), jnp.bfloat16)
        outs = [jax.ShapeDtypeStruct((tiles, group, span), jnp.float32), block] + [block] * HOOD
        out_specs = [vmem] * len(outs)
        scratch.append(pltpu.VMEM(((level + 1) * tiles, cols, span), jnp.bfloat16))
        scratch.append(pltpu.VMEM((HOOD * tiles + 1, cols, span), jnp.float32))
    return pl.pallas_call(
        functools.partial(level_body, level, last),
        out_shape=outs,
        in_specs=specs,
        out_specs=out_specs,
        scratch_shapes=scratch,
        compiler_params=pltpu.CompilerParams(vmem_limit_bytes=40 << 20),
    )(*args)


def per_device(right_sides, diag_inverse, panel_mats, panel_src, panel_dst):
    levels, tiles, group, span = right_sides.shape
    dom_size = lax.axis_size("dom")
    rep_size = lax.axis_size("rep")
    far = dom_size // 2
    rep = lax.axis_index("rep").astype(jnp.int32)
    owner = lax.axis_index("dom")
    cols = group * rep_size
    place = lax.broadcasted_iota(jnp.int32, (levels, tiles, cols, span), 2) // group == rep
    own_rhs = jnp.where(place, jnp.tile(right_sides, (1, 1, rep_size, 1)), 0.0)
    distance = (panel_dst // tiles - owner) % dom_size
    reach = jnp.where(distance == far, HOOD - 1, (distance + HALF) % dom_size)
    slots = jnp.where(panel_dst >= 0, reach * tiles + panel_dst % tiles, HOOD * tiles)
    partial = own_rhs[0].astype(jnp.bfloat16)
    store = []
    results = []
    for level in range(levels):
        parts = [partial] + [passed_along(partial, "rep", by) for by in range(1, rep_size)]
        if level + 1 == levels:
            return run_level(
                level, True, rep[None], [], parts, diag_inverse[level], None, results, right_sides.shape
            )
        solved, stored, *messages = run_level(
            level,
            False,
            rep[None],
            [panel_src[level], slots[level]],
            parts,
            diag_inverse[level],
            panel_mats[level],
            store,
            None,
        )
        results.append(solved)
        store.append(stored)
        incoming = jnp.zeros((tiles, cols, span), jnp.float32)
        for index in range(HOOD):
            offset = far if index == HOOD - 1 else index - HALF
            piece = messages[index]
            if offset != 0:
                piece = passed_along(piece, "dom", offset)
            incoming = incoming + piece.astype(jnp.float32)
        partial = (own_rhs[level + 1] - incoming).astype(jnp.bfloat16)


def solution(mesh):
    return jax.shard_map(
        per_device,
        mesh=mesh,
        in_specs=(
            P(None, "dom", "rep", None),
            P(None, "dom", None, None),
            P(None, ("dom", "rep"), None, None),
            P(None, ("dom", "rep")),
            P(None, ("dom", "rep")),
        ),
        out_specs=P(None, "dom", "rep", None),
        check_vma=False,
    )
```

time: 153 us -> 88 us (0.58)
  starting transfers between devices: 91 us -> 26.7 us
  matrix products: 22.3 us -> 0 us
  waiting for transfers between devices: 21.4 us -> 42.5 us
  Pallas kernels: 0 us -> 6.77 us
  other arithmetic: 5.2 us -> 0.39 us
    all_to_all x9 -> x0, starting transfers between devices: 38.8 us -> none  [the longest x3 15 us: from_everyone(): lax.all_to_all(jnp.broadcast_to(value[None], (size, *value.shape)), axis,...]
    ppermute x30 -> x27, waiting for transfers between devices: 8.25 us -> 42.5 us  [passed_along(): lax.ppermute(value, axis, [(i, (i + by) % size) for i in range(size)])]
    ppermute x30 -> x27, starting transfers between devices: 52.2 us -> 26.7 us  [passed_along(): lax.ppermute(value, axis, [(i, (i + by) % size) for i in range(size)])]
    dot_general x28 -> x0, matrix products: 22.3 us -> none  [the longest x3 9.37 us: panel_updates(): jnp.einsum('pcx,pxy->pcy', sources, matrices, preferred_element_type=jnp....]
    all_to_all x9 -> x0, waiting for transfers between devices: 13.2 us -> none  [the longest x3 11.9 us: from_everyone(): lax.all_to_all(jnp.broadcast_to(value[None], (size, *value.shape)), axis,...]
    squeeze x0 -> x3, local copies, waits for them, and re-layouts: none -> 10.1 us  [the longest x1 6.17 us: per_device(): panel_mats[level]]
    pallas_call x0 -> x4, Pallas kernels: none -> 6.77 us  [run_level(): pl.pallas_call(functools.partial(level_body, level, last), out_shape=outs...]
    broadcast_in_dim x6 -> x0, local copies, waits for them, and re-layouts: 3.78 us -> none  [the longest x3 1.99 us: from_everyone(): jnp.broadcast_to(value[None], (size, *value.shape))]
  transfers between devices with their start and end apart: 39 -> 27, of which waited for: 14 -> 20; matrix products, arithmetic and copies ran while one was open for 17% -> 12% of each run, Pallas kernels for 0% -> 0%
where the time goes in v1:
time: 88 us; the launch traced here: 87.9 us
  waiting for transfers between devices  42.5 us (48%)
  starting transfers between devices  26.7 us (30%)
  local copies, waits for them, and re-layouts  11.3 us (13%)
  Pallas kernels  6.77 us (8%)
    ppermute x27, waiting for transfers between devices, passed_along(): lax.ppermute(value, axis, [(i, (i + by) % size) for i in range(size)])  42.5 us
    ppermute x27, starting transfers between devices, passed_along(): lax.ppermute(value, axis, [(i, (i + by) % size) for i in range(size)])  26.7 us
    pallas_call x4, Pallas kernels, run_level(): pl.pallas_call(functools.partial(level_body, level, last), out_shape=outs...  6.77 us
    squeeze x1, local copies, waits for them, and re-layouts, per_device(): panel_mats[level]  6.17 us
    squeeze x1, local copies, waits for them, and re-layouts, per_device(): diag_inverse[level]  3.93 us
  transfers between devices with their start and end apart: 27, of which 20 were waited for; matrix products, arithmetic and copies ran while one was open for 12% of the time, Pallas kernels for 0%

profile of v1, /device:TPU:0, one launch (start us, length us, event | category | flops | bytes accessed | tf_op | source)
XLA Modules:
  0.0 87.9 jit_solution(11164231456046954805)
XLA Ops:
  0.0 1.0 %tile.4 = f32[4,6,4,4,384]{4,3,2,1,0:T(4,128)S(1)} broadcast(f32[4,6,4,384]{3,2,1,0:T(4,128)} %param.5), dimensions={0,1,3,4} | broadcast | bytes 737280 | tf_op jit(solution)/shard_map/tile | solution.py:105
  1.0 0.2 tile.10
  1.2 0.1 fusion
  1.4 4.2 %collective-permute-start.2 = (bf16[6,16,384]{2,1,0:T(8,128)(2,1)S(1)}, bf16[6,16,384]{2,1,0:T(8,128)(2,1)S(1)}, u32[]{:S(2)}, u32[]{:S(2)}) collective-permute-start(bf16[6,16,384]{2,1,0:T(8,128)(2,1)S(1)} %fusion.7.refs_3_), channel_id=1, source_target_pairs={{0,3},{1,0},{2,1},{3,2},{4,7},{5,4},{6,5},{7,6},{8,11},{9,8},{10,9... | collective-permute-start | bytes 221192 | tf_op jit(solution)/shard_map/ppermute | solution.py:16
  5.6 0.0 collective-permute-start.1
  5.6 1.3 %collective-permute-start = (bf16[6,16,384]{2,1,0:T(8,128)(2,1)S(1)}, bf16[6,16,384]{2,1,0:T(8,128)(2,1)S(1)}, u32[]{:S(2)}, u32[]{:S(2)}) collective-permute-start(bf16[6,16,384]{2,1,0:T(8,128)(2,1)S(1)} %fusion.7.refs_3_), channel_id=1, source_target_pairs={{0,1},{1,2},{2,3},{3,0},{4,5},{5,6},{6,7},{7,4},{8,9},{9,10},{10,1... | collective-permute-start | bytes 221192 | tf_op jit(solution)/shard_map/ppermute | solution.py:16
  6.8 3.9 %slice_bitcast_fusion.3 = (bf16[6,384,384]{2,1,0:T(8,128)(2,1)S(1)}, bf16[6,384,384]{2,1,0:T(8,128)(2,1)S(1)}, bf16[6,384,384]{2,1,0:T(8,128)(2,1)S(1)}, bf16[6,384,384]{2,1,0:T(8,128)(2,1)S(1)}) fusion(bf16[4,6,384,384]{3,2,1,0:T(8,128)(2,1)} %param.6), kind=kLoop, calls=%fused_computation.3 | loop fusion | bytes 14155776 | tf_op jit(solution)/shard_map/squeeze | solution.py:116
  10.8 0.0 copy-start
  10.8 0.0 copy-start.1
  10.8 6.2 %slice_bitcast_fusion = (bf16[16,384,384]{2,1,0:T(8,128)(2,1)S(1)}, bf16[16,384,384]{2,1,0:T(8,128)(2,1)S(1)}, bf16[16,384,384]{2,1,0:T(8,128)(2,1)S(1)}) fusion(bf16[3,16,384,384]{3,2,1,0:T(8,128)(2,1)} %param.7), kind=kLoop, calls=%fused_computation | loop fusion | bytes 28311552 | tf_op jit(solution)/shard_map/squeeze | solution.py:125
  17.0 0.0 collective-permute-done.2.refs_6_
  17.0 0.0 collective-permute-done.1.refs_5_
  17.1 0.0 collective-permute-done.refs_4_
  17.1 1.8 %shard_map.55 = (f32[6,4,384]{2,1,0:T(4,128)S(1)}, bf16[6,16,384]{2,1,0:T(8,128)(2,1)S(1)}, bf16[6,16,384]{2,1,0:T(8,128)(2,1)S(1)}, bf16[6,16,384]{2,1,0:T(8,12...) custom-call(s32[1]{0:T(128)} %bitcast.refs_0_, ...), custom_call_target="tpu_custom_call" | custom-call | tf_op jit(solution)/shard_map/pallas_call | solution.py:86
  18.9 5.3 %collective-permute-start.3 = (bf16[6,16,384]{2,1,0:T(8,128)(2,1)S(1)}, bf16[6,16,384]{2,1,0:T(8,128)(2,1)S(1)}, u32[]{:S(2)}, u32[]{:S(2)}) collective-permute-start(bf16[6,16,384]{2,1,0:T(8,128)(2,1)S(1)} %get-tuple-element.28), channel_id=1, source_target_pairs={{0,120},{4,124},{8,0},{12,4},{16,8},{20,12},{24,16},{28,20},{32,24... | collective-permute-start | bytes 221192 | tf_op jit(solution)/shard_map/ppermute | solution.py:16
  24.2 0.5 collective-permute-start.5
  24.7 0.0 collective-permute-start.6
  24.7 0.6 collective-permute-start.7
  25.3 0.8 collective-permute-done.3
  26.1 0.7 collective-permute-done.4
  26.8 4.4 %collective-permute-done.5 = bf16[6,16,384]{2,1,0:T(8,128)(2,1)S(1)} collective-permute-done((bf16[6,16,384]{2,1,0:T(8,128)(2,1)S(1)}, bf16[6,16,384]{2,1,0:T(8,128)(2,1)S(1)}, u32[]{:S(2)}, u32[]{:S(2)}) %collective-permute-start.5) | collective-permute-done | bytes 73760 | tf_op jit(solution)/shard_map/ppermute | solution.py:16
  31.3 2.4 %collective-permute-done.6 = bf16[6,16,384]{2,1,0:T(8,128)(2,1)S(1)} collective-permute-done((bf16[6,16,384]{2,1,0:T(8,128)(2,1)S(1)}, bf16[6,16,384]{2,1,0:T(8,128)(2,1)S(1)}, u32[]{:S(2)}, u32[]{:S(2)}) %collective-permute-start.6) | collective-permute-done | bytes 73760 | tf_op jit(solution)/shard_map/ppermute | solution.py:16
  33.6 0.0 collective-permute-done.7
  33.6 0.1 fusion.2.refs_3_
  33.7 2.3 %collective-permute-start.10 = (bf16[6,16,384]{2,1,0:T(8,128)(2,1)S(1)}, bf16[6,16,384]{2,1,0:T(8,128)(2,1)S(1)}, u32[]{:S(2)}, u32[]{:S(2)}) collective-permute-start(bf16[6,16,384]{2,1,0:T(8,128)(2,1)S(1)} %fusion.2.refs_3_), channel_id=1, source_target_pairs={{0,3},{1,0},{2,1},{3,2},{4,7},{5,4},{6,5},{7,6},{8,11},{9,8},{10,9... | collective-permute-start | bytes 221192 | tf_op jit(solution)/shard_map/ppermute | solution.py:16
  36.0 2.1 %collective-permute-start.9 = (bf16[6,16,384]{2,1,0:T(8,128)(2,1)S(1)}, bf16[6,16,384]{2,1,0:T(8,128)(2,1)S(1)}, u32[]{:S(2)}, u32[]{:S(2)}) collective-permute-start(bf16[6,16,384]{2,1,0:T(8,128)(2,1)S(1)} %fusion.2.refs_3_), channel_id=1, source_target_pairs={{0,2},{1,3},{2,0},{3,1},{4,6},{5,7},{6,4},{7,5},{8,10},{9,11},{10,... | collective-permute-start | bytes 221192 | tf_op jit(solution)/shard_map/ppermute | solution.py:16
  38.1 0.0 collective-permute-start.8
  38.1 0.6 collective-permute-done.10.refs_6_
  38.7 3.3 %collective-permute-done.9.refs_5_ = bf16[6,16,384]{2,1,0:T(8,128)(2,1)S(1)} collective-permute-done((bf16[6,16,384]{2,1,0:T(8,128)(2,1)S(1)}, bf16[6,16,384]{2,1,0:T(8,128)(2,1)S(1)}, u32[]{:S(2)}, u32[]{:S(2)}) %collective-permute-start.9) | collective-permute-done | bytes 73760 | tf_op jit(solution)/shard_map/ppermute | solution.py:16
  42.0 1.7 %collective-permute-done.8.refs_4_ = bf16[6,16,384]{2,1,0:T(8,128)(2,1)S(1)} collective-permute-done((bf16[6,16,384]{2,1,0:T(8,128)(2,1)S(1)}, bf16[6,16,384]{2,1,0:T(8,128)(2,1)S(1)}, u32[]{:S(2)}, u32[]{:S(2)}) %collective-permute-start.8) | collective-permute-done | bytes 73760 | tf_op jit(solution)/shard_map/ppermute | solution.py:16
  43.7 1.8 %shard_map.56 = (f32[6,4,384]{2,1,0:T(4,128)S(1)}, bf16[6,16,384]{2,1,0:T(8,128)(2,1)S(1)}, bf16[6,16,384]{2,1,0:T(8,128)(2,1)S(1)}, bf16[6,16,384]{2,1,0:T(8,12...) custom-call(s32[1]{0:T(128)} %bitcast.refs_0_, ...), custom_call_target="tpu_custom_call" | custom-call | tf_op jit(solution)/shard_map/pallas_call | solution.py:86
  45.5 2.3 %collective-permute-start.11 = (bf16[6,16,384]{2,1,0:T(8,128)(2,1)S(1)}, bf16[6,16,384]{2,1,0:T(8,128)(2,1)S(1)}, u32[]{:S(2)}, u32[]{:S(2)}) collective-permute-start(bf16[6,16,384]{2,1,0:T(8,128)(2,1)S(1)} %get-tuple-element.35), channel_id=1, source_target_pairs={{0,120},{4,124},{8,0},{12,4},{16,8},{20,12},{24,16},{28,20},{32,24... | collective-permute-start | bytes 221192 | tf_op jit(solution)/shard_map/ppermute | solution.py:16
  47.8 0.5 collective-permute-start.13
  48.3 0.0 collective-permute-start.15
  48.3 1.6 %collective-permute-done.11 = bf16[6,16,384]{2,1,0:T(8,128)(2,1)S(1)} collective-permute-done((bf16[6,16,384]{2,1,0:T(8,128)(2,1)S(1)}, bf16[6,16,384]{2,1,0:T(8,128)(2,1)S(1)}, u32[]{:S(2)}, u32[]{:S(2)}) %collective-permute-start.11) | collective-permute-done | bytes 73760 | tf_op jit(solution)/shard_map/ppermute | solution.py:16
  49.9 0.5 collective-permute-done.12
  50.4 5.0 %collective-permute-done.13 = bf16[6,16,384]{2,1,0:T(8,128)(2,1)S(1)} collective-permute-done((bf16[6,16,384]{2,1,0:T(8,128)(2,1)S(1)}, bf16[6,16,384]{2,1,0:T(8,128)(2,1)S(1)}, u32[]{:S(2)}, u32[]{:S(2)}) %collective-permute-start.13) | collective-permute-done | bytes 73760 | tf_op jit(solution)/shard_map/ppermute | solution.py:16
  55.4 2.5 %collective-permute-done.14 = bf16[6,16,384]{2,1,0:T(8,128)(2,1)S(1)} collective-permute-done((bf16[6,16,384]{2,1,0:T(8,128)(2,1)S(1)}, bf16[6,16,384]{2,1,0:T(8,128)(2,1)S(1)}, u32[]{:S(2)}, u32[]{:S(2)}) %collective-permute-start.14) | collective-permute-done | bytes 73760 | tf_op jit(solution)/shard_map/ppermute | solution.py:16
  57.9 0.0 collective-permute-done.15
  57.9 0.1 fusion.4.refs_3_
  58.0 0.1 collective-permute-start.18
  58.1 1.6 %collective-permute-start.17 = (bf16[6,16,384]{2,1,0:T(8,128)(2,1)S(1)}, bf16[6,16,384]{2,1,0:T(8,128)(2,1)S(1)}, u32[]{:S(2)}, u32[]{:S(2)}) collective-permute-start(bf16[6,16,384]{2,1,0:T(8,128)(2,1)S(1)} %fusion.4.refs_3_), channel_id=1, source_target_pairs={{0,2},{1,3},{2,0},{3,1},{4,6},{5,7},{6,4},{7,5},{8,10},{9,11},{10,... | collective-permute-start | bytes 221192 | tf_op jit(solution)/shard_map/ppermute | solution.py:16
  59.7 0.6 collective-permute-start.16
  60.3 2.2 %collective-permute-done.18.refs_6_ = bf16[6,16,384]{2,1,0:T(8,128)(2,1)S(1)} collective-permute-done((bf16[6,16,384]{2,1,0:T(8,128)(2,1)S(1)}, bf16[6,16,384]{2,1,0:T(8,128)(2,1)S(1)}, u32[]{:S(2)}, u32[]{:S(2)}) %collective-permute-start.18) | collective-permute-done | bytes 73760 | tf_op jit(solution)/shard_map/ppermute | solution.py:16
  62.5 1.9 %collective-permute-done.17.refs_5_ = bf16[6,16,384]{2,1,0:T(8,128)(2,1)S(1)} collective-permute-done((bf16[6,16,384]{2,1,0:T(8,128)(2,1)S(1)}, bf16[6,16,384]{2,1,0:T(8,128)(2,1)S(1)}, u32[]{:S(2)}, u32[]{:S(2)}) %collective-permute-start.17) | collective-permute-done | bytes 73760 | tf_op jit(solution)/shard_map/ppermute | solution.py:16
  64.4 0.9 collective-permute-done.16.refs_4_
  65.3 2.1 %shard_map.57 = (f32[6,4,384]{2,1,0:T(4,128)S(1)}, bf16[6,16,384]{2,1,0:T(8,128)(2,1)}, bf16[6,16,384]{2,1,0:T(8,128)(2,1)S(1)}, bf16[6,16,384]{2,1,0:T(8,128)(2...) custom-call(s32[1]{0:T(128)} %bitcast.refs_0_, ...), custom_call_target="tpu_custom_call" | custom-call | tf_op jit(solution)/shard_map/pallas_call | solution.py:86
  67.4 1.5 %collective-permute-start.19 = (bf16[6,16,384]{2,1,0:T(8,128)(2,1)S(1)}, bf16[6,16,384]{2,1,0:T(8,128)(2,1)S(1)}, u32[]{:S(2)}, u32[]{:S(2)}) collective-permute-start(bf16[6,16,384]{2,1,0:T(8,128)(2,1)S(1)} %get-tuple-element.42), channel_id=1, source_target_pairs={{0,120},{4,124},{8,0},{12,4},{16,8},{20,12},{24,16},{28,20},{32,24... | collective-permute-start | bytes 221192 | tf_op jit(solution)/shard_map/ppermute | solution.py:16
  68.9 0.0 collective-permute-start.20
  68.9 0.5 collective-permute-start.21
  69.4 0.5 collective-permute-start.22
  69.9 0.0 collective-permute-start.23
  69.9 1.8 %collective-permute-done.19 = bf16[6,16,384]{2,1,0:T(8,128)(2,1)S(1)} collective-permute-done((bf16[6,16,384]{2,1,0:T(8,128)(2,1)S(1)}, bf16[6,16,384]{2,1,0:T(8,128)(2,1)S(1)}, u32[]{:S(2)}, u32[]{:S(2)}) %collective-permute-start.19) | collective-permute-done | bytes 73760 | tf_op jit(solution)/shard_map/ppermute | solution.py:16
  71.7 4.8 %collective-permute-done.21 = bf16[6,16,384]{2,1,0:T(8,128)(2,1)S(1)} collective-permute-done((bf16[6,16,384]{2,1,0:T(8,128)(2,1)S(1)}, bf16[6,16,384]{2,1,0:T(8,128)(2,1)S(1)}, u32[]{:S(2)}, u32[]{:S(2)}) %collective-permute-start.21) | collective-permute-done | bytes 73760 | tf_op jit(solution)/shard_map/ppermute | solution.py:16
  76.6 1.6 %collective-permute-done.22 = bf16[6,16,384]{2,1,0:T(8,128)(2,1)S(1)} collective-permute-done((bf16[6,16,384]{2,1,0:T(8,128)(2,1)S(1)}, bf16[6,16,384]{2,1,0:T(8,128)(2,1)S(1)}, u32[]{:S(2)}, u32[]{:S(2)}) %collective-permute-start.22) | collective-permute-done | bytes 73760 | tf_op jit(solution)/shard_map/ppermute | solution.py:16
  78.1 0.0 collective-permute-done.23
  78.1 0.1 fusion.6.refs_1_
  78.2 1.9 %collective-permute-start.26 = (bf16[6,16,384]{2,1,0:T(8,128)(2,1)S(1)}, bf16[6,16,384]{2,1,0:T(8,128)(2,1)S(1)}, u32[]{:S(2)}, u32[]{:S(2)}) collective-permute-start(bf16[6,16,384]{2,1,0:T(8,128)(2,1)S(1)} %fusion.6.refs_1_), channel_id=1, source_target_pairs={{0,3},{1,0},{2,1},{3,2},{4,7},{5,4},{6,5},{7,6},{8,11},{9,8},{10,9... | collective-permute-start | bytes 221192 | tf_op jit(solution)/shard_map/ppermute | solution.py:16
  80.1 0.9 %collective-permute-start.25 = (bf16[6,16,384]{2,1,0:T(8,128)(2,1)S(1)}, bf16[6,16,384]{2,1,0:T(8,128)(2,1)S(1)}, u32[]{:S(2)}, u32[]{:S(2)}) collective-permute-start(bf16[6,16,384]{2,1,0:T(8,128)(2,1)S(1)} %fusion.6.refs_1_), channel_id=1, source_target_pairs={{0,2},{1,3},{2,0},{3,1},{4,6},{5,7},{6,4},{7,5},{8,10},{9,11},{10,... | collective-permute-start | bytes 221192 | tf_op jit(solution)/shard_map/ppermute | solution.py:16
  81.0 0.0 collective-permute-start.24
  81.1 1.9 %collective-permute-done.26.refs_4_ = bf16[6,16,384]{2,1,0:T(8,128)(2,1)S(1)} collective-permute-done((bf16[6,16,384]{2,1,0:T(8,128)(2,1)S(1)}, bf16[6,16,384]{2,1,0:T(8,128)(2,1)S(1)}, u32[]{:S(2)}, u32[]{:S(2)}) %collective-permute-start.26) | collective-permute-done | bytes 73760 | tf_op jit(solution)/shard_map/ppermute | solution.py:16
  83.0 3.1 %collective-permute-done.25.refs_3_ = bf16[6,16,384]{2,1,0:T(8,128)(2,1)S(1)} collective-permute-done((bf16[6,16,384]{2,1,0:T(8,128)(2,1)S(1)}, bf16[6,16,384]{2,1,0:T(8,128)(2,1)S(1)}, u32[]{:S(2)}, u32[]{:S(2)}) %collective-permute-start.25) | collective-permute-done | bytes 73760 | tf_op jit(solution)/shard_map/ppermute | solution.py:16
  86.0 0.8 collective-permute-done.24.refs_2_
  86.8 1.1 %shard_map.58 = f32[4,6,4,384]{3,2,1,0:T(4,128)} custom-call(s32[1]{0:T(128)} %bitcast.refs_0_, bf16[6,16,384]{2,1,0:T(8,128)(2,1)S(1)} %fusion.6.refs_1_, bf16[6,16,384]{2,1,0:T(8,128)(2,1)S(1)} %collective-permute-done.24.refs_2_, bf16[6,16,384]{2,1,0:T(8,128)(2,1)S(1)} %collective-permute-done.25.refs_3_, ...), custom_call_target="tpu_custom_call" | custom-call | tf_op jit(solution)/shard_map/pallas_call | solution.py:86
  (11 shorter events, 0.1 us)
Async XLA Ops:
  1.4 15.7 %collective-permute-start.2 = (bf16[6,16,384]{2,1,0:T(8,128)(2,1)S(1)}, bf16[6,16,384]{2,1,0:T(8,128)(2,1)S(1)}, u32[]{:S(2)}, u32[]{:S(2)}) collective-permute-start(bf16[6,16,384]{2,1,0:T(8,128)(2,1)S(1)} %fusion.7.refs_3_), channel_id=1, source_target_pairs={{0,3},{1,0},{2,1},{3,2},{4,7},{5,4},{6,5},{7,6},{8,11},{9,8},{10,9... | collective-permute-start | bytes 221192 | tf_op jit(solution)/shard_map/ppermute | solution.py:16
  5.6 11.5 %collective-permute-start.1 = (bf16[6,16,384]{2,1,0:T(8,128)(2,1)S(1)}, bf16[6,16,384]{2,1,0:T(8,128)(2,1)S(1)}, u32[]{:S(2)}, u32[]{:S(2)}) collective-permute-start(bf16[6,16,384]{2,1,0:T(8,128)(2,1)S(1)} %fusion.7.refs_3_), channel_id=1, source_target_pairs={{0,2},{1,3},{2,0},{3,1},{4,6},{5,7},{6,4},{7,5},{8,10},{9,11},{10,... | collective-permute-start | bytes 221192 | tf_op jit(solution)/shard_map/ppermute | solution.py:16
  5.6 11.5 %collective-permute-start = (bf16[6,16,384]{2,1,0:T(8,128)(2,1)S(1)}, bf16[6,16,384]{2,1,0:T(8,128)(2,1)S(1)}, u32[]{:S(2)}, u32[]{:S(2)}) collective-permute-start(bf16[6,16,384]{2,1,0:T(8,128)(2,1)S(1)} %fusion.7.refs_3_), channel_id=1, source_target_pairs={{0,1},{1,2},{2,3},{3,0},{4,5},{5,6},{6,7},{7,4},{8,9},{9,10},{10,1... | collective-permute-start | bytes 221192 | tf_op jit(solution)/shard_map/ppermute | solution.py:16
  10.8 6.2 %copy-start = (s32[3,16]{1,0:T(4,128)S(1)}, s32[3,16]{1,0:T(4,128)}, u32[]{:S(2)}) copy-start(s32[3,16]{1,0:T(4,128)} %param.9) | copy-start | bytes 580
  10.8 6.2 %copy-start.1 = (s32[3,16]{1,0:T(4,128)S(1)}, s32[3,16]{1,0:T(4,128)}, u32[]{:S(2)}) copy-start(s32[3,16]{1,0:T(4,128)} %param.8) | copy-start | bytes 580
  18.9 7.3 %collective-permute-start.3 = (bf16[6,16,384]{2,1,0:T(8,128)(2,1)S(1)}, bf16[6,16,384]{2,1,0:T(8,128)(2,1)S(1)}, u32[]{:S(2)}, u32[]{:S(2)}) collective-permute-start(bf16[6,16,384]{2,1,0:T(8,128)(2,1)S(1)} %get-tuple-element.28), channel_id=1, source_target_pairs={{0,120},{4,124},{8,0},{12,4},{16,8},{20,12},{24,16},{28,20},{32,24... | collective-permute-start | bytes 221192 | tf_op jit(solution)/shard_map/ppermute | solution.py:16
  24.2 2.7 %collective-permute-start.4 = (bf16[6,16,384]{2,1,0:T(8,128)(2,1)S(1)}, bf16[6,16,384]{2,1,0:T(8,128)(2,1)S(1)}, u32[]{:S(2)}, u32[]{:S(2)}) collective-permute-start(bf16[6,16,384]{2,1,0:T(8,128)(2,1)S(1)} %get-tuple-element.29), channel_id=1, source_target_pairs={{0,124},{4,0},{8,4},{12,8},{16,12},{20,16},{24,20},{28,24},{32,28}... | collective-permute-start | bytes 221192 | tf_op jit(solution)/shard_map/ppermute | solution.py:16
  24.2 7.1 %collective-permute-start.5 = (bf16[6,16,384]{2,1,0:T(8,128)(2,1)S(1)}, bf16[6,16,384]{2,1,0:T(8,128)(2,1)S(1)}, u32[]{:S(2)}, u32[]{:S(2)}) collective-permute-start(bf16[6,16,384]{2,1,0:T(8,128)(2,1)S(1)} %get-tuple-element.31), channel_id=1, source_target_pairs={{0,4},{4,8},{8,12},{12,16},{16,20},{20,24},{24,28},{28,32},{32,36}... | collective-permute-start | bytes 221192 | tf_op jit(solution)/shard_map/ppermute | solution.py:16
  24.7 9.0 %collective-permute-start.6 = (bf16[6,16,384]{2,1,0:T(8,128)(2,1)S(1)}, bf16[6,16,384]{2,1,0:T(8,128)(2,1)S(1)}, u32[]{:S(2)}, u32[]{:S(2)}) collective-permute-start(bf16[6,16,384]{2,1,0:T(8,128)(2,1)S(1)} %get-tuple-element.32), channel_id=1, source_target_pairs={{0,8},{4,12},{8,16},{12,20},{16,24},{20,28},{24,32},{28,36},{32,40... | collective-permute-start | bytes 221192 | tf_op jit(solution)/shard_map/ppermute | solution.py:16
  24.7 9.0 %collective-permute-start.7 = (bf16[6,16,384]{2,1,0:T(8,128)(2,1)S(1)}, bf16[6,16,384]{2,1,0:T(8,128)(2,1)S(1)}, u32[]{:S(2)}, u32[]{:S(2)}) collective-permute-start(bf16[6,16,384]{2,1,0:T(8,128)(2,1)S(1)} %get-tuple-element.33), channel_id=1, source_target_pairs={{0,64},{4,68},{8,72},{12,76},{16,80},{20,84},{24,88},{28,92},{32,9... | collective-permute-start | bytes 221192 | tf_op jit(solution)/shard_map/ppermute | solution.py:16
  33.7 5.0 %collective-permute-start.10 = (bf16[6,16,384]{2,1,0:T(8,128)(2,1)S(1)}, bf16[6,16,384]{2,1,0:T(8,128)(2,1)S(1)}, u32[]{:S(2)}, u32[]{:S(2)}) collective-permute-start(bf16[6,16,384]{2,1,0:T(8,128)(2,1)S(1)} %fusion.2.refs_3_), channel_id=1, source_target_pairs={{0,3},{1,0},{2,1},{3,2},{4,7},{5,4},{6,5},{7,6},{8,11},{9,8},{10,9... | collective-permute-start | bytes 221192 | tf_op jit(solution)/shard_map/ppermute | solution.py:16
  36.0 6.0 %collective-permute-start.9 = (bf16[6,16,384]{2,1,0:T(8,128)(2,1)S(1)}, bf16[6,16,384]{2,1,0:T(8,128)(2,1)S(1)}, u32[]{:S(2)}, u32[]{:S(2)}) collective-permute-start(bf16[6,16,384]{2,1,0:T(8,128)(2,1)S(1)} %fusion.2.refs_3_), channel_id=1, source_target_pairs={{0,2},{1,3},{2,0},{3,1},{4,6},{5,7},{6,4},{7,5},{8,10},{9,11},{10,... | collective-permute-start | bytes 221192 | tf_op jit(solution)/shard_map/ppermute | solution.py:16
  38.1 5.6 %collective-permute-start.8 = (bf16[6,16,384]{2,1,0:T(8,128)(2,1)S(1)}, bf16[6,16,384]{2,1,0:T(8,128)(2,1)S(1)}, u32[]{:S(2)}, u32[]{:S(2)}) collective-permute-start(bf16[6,16,384]{2,1,0:T(8,128)(2,1)S(1)} %fusion.2.refs_3_), channel_id=1, source_target_pairs={{0,1},{1,2},{2,3},{3,0},{4,5},{5,6},{6,7},{7,4},{8,9},{9,10},{10,1... | collective-permute-start | bytes 221192 | tf_op jit(solution)/shard_map/ppermute | solution.py:16
  45.5 4.4 %collective-permute-start.11 = (bf16[6,16,384]{2,1,0:T(8,128)(2,1)S(1)}, bf16[6,16,384]{2,1,0:T(8,128)(2,1)S(1)}, u32[]{:S(2)}, u32[]{:S(2)}) collective-permute-start(bf16[6,16,384]{2,1,0:T(8,128)(2,1)S(1)} %get-tuple-element.35), channel_id=1, source_target_pairs={{0,120},{4,124},{8,0},{12,4},{16,8},{20,12},{24,16},{28,20},{32,24... | collective-permute-start | bytes 221192 | tf_op jit(solution)/shard_map/ppermute | solution.py:16
  47.7 2.7 %collective-permute-start.12 = (bf16[6,16,384]{2,1,0:T(8,128)(2,1)S(1)}, bf16[6,16,384]{2,1,0:T(8,128)(2,1)S(1)}, u32[]{:S(2)}, u32[]{:S(2)}) collective-permute-start(bf16[6,16,384]{2,1,0:T(8,128)(2,1)S(1)} %get-tuple-element.36), channel_id=1, source_target_pairs={{0,124},{4,0},{8,4},{12,8},{16,12},{20,16},{24,20},{28,24},{32,28}... | collective-permute-start | bytes 221192 | tf_op jit(solution)/shard_map/ppermute | solution.py:16
  47.8 7.7 %collective-permute-start.13 = (bf16[6,16,384]{2,1,0:T(8,128)(2,1)S(1)}, bf16[6,16,384]{2,1,0:T(8,128)(2,1)S(1)}, u32[]{:S(2)}, u32[]{:S(2)}) collective-permute-start(bf16[6,16,384]{2,1,0:T(8,128)(2,1)S(1)} %get-tuple-element.38), channel_id=1, source_target_pairs={{0,4},{4,8},{8,12},{12,16},{16,20},{20,24},{24,28},{28,32},{32,36}... | collective-permute-start | bytes 221192 | tf_op jit(solution)/shard_map/ppermute | solution.py:16
  48.3 9.7 %collective-permute-start.14 = (bf16[6,16,384]{2,1,0:T(8,128)(2,1)S(1)}, bf16[6,16,384]{2,1,0:T(8,128)(2,1)S(1)}, u32[]{:S(2)}, u32[]{:S(2)}) collective-permute-start(bf16[6,16,384]{2,1,0:T(8,128)(2,1)S(1)} %get-tuple-element.39), channel_id=1, source_target_pairs={{0,8},{4,12},{8,16},{12,20},{16,24},{20,28},{24,32},{28,36},{32,40... | collective-permute-start | bytes 221192 | tf_op jit(solution)/shard_map/ppermute | solution.py:16
  48.3 9.7 %collective-permute-start.15 = (bf16[6,16,384]{2,1,0:T(8,128)(2,1)S(1)}, bf16[6,16,384]{2,1,0:T(8,128)(2,1)S(1)}, u32[]{:S(2)}, u32[]{:S(2)}) collective-permute-start(bf16[6,16,384]{2,1,0:T(8,128)(2,1)S(1)} %get-tuple-element.40), channel_id=1, source_target_pairs={{0,64},{4,68},{8,72},{12,76},{16,80},{20,84},{24,88},{28,92},{32,9... | collective-permute-start | bytes 221192 | tf_op jit(solution)/shard_map/ppermute | solution.py:16
  58.0 4.5 %collective-permute-start.18 = (bf16[6,16,384]{2,1,0:T(8,128)(2,1)S(1)}, bf16[6,16,384]{2,1,0:T(8,128)(2,1)S(1)}, u32[]{:S(2)}, u32[]{:S(2)}) collective-permute-start(bf16[6,16,384]{2,1,0:T(8,128)(2,1)S(1)} %fusion.4.refs_3_), channel_id=1, source_target_pairs={{0,3},{1,0},{2,1},{3,2},{4,7},{5,4},{6,5},{7,6},{8,11},{9,8},{10,9... | collective-permute-start | bytes 221192 | tf_op jit(solution)/shard_map/ppermute | solution.py:16
  58.1 6.3 %collective-permute-start.17 = (bf16[6,16,384]{2,1,0:T(8,128)(2,1)S(1)}, bf16[6,16,384]{2,1,0:T(8,128)(2,1)S(1)}, u32[]{:S(2)}, u32[]{:S(2)}) collective-permute-start(bf16[6,16,384]{2,1,0:T(8,128)(2,1)S(1)} %fusion.4.refs_3_), channel_id=1, source_target_pairs={{0,2},{1,3},{2,0},{3,1},{4,6},{5,7},{6,4},{7,5},{8,10},{9,11},{10,... | collective-permute-start | bytes 221192 | tf_op jit(solution)/shard_map/ppermute | solution.py:16
  59.7 5.6 %collective-permute-start.16 = (bf16[6,16,384]{2,1,0:T(8,128)(2,1)S(1)}, bf16[6,16,384]{2,1,0:T(8,128)(2,1)S(1)}, u32[]{:S(2)}, u32[]{:S(2)}) collective-permute-start(bf16[6,16,384]{2,1,0:T(8,128)(2,1)S(1)} %fusion.4.refs_3_), channel_id=1, source_target_pairs={{0,1},{1,2},{2,3},{3,0},{4,5},{5,6},{6,7},{7,4},{8,9},{9,10},{10,1... | collective-permute-start | bytes 221192 | tf_op jit(solution)/shard_map/ppermute | solution.py:16
  67.4 4.4 %collective-permute-start.19 = (bf16[6,16,384]{2,1,0:T(8,128)(2,1)S(1)}, bf16[6,16,384]{2,1,0:T(8,128)(2,1)S(1)}, u32[]{:S(2)}, u32[]{:S(2)}) collective-permute-start(bf16[6,16,384]{2,1,0:T(8,128)(2,1)S(1)} %get-tuple-element.42), channel_id=1, source_target_pairs={{0,120},{4,124},{8,0},{12,4},{16,8},{20,12},{24,16},{28,20},{32,24... | collective-permute-start | bytes 221192 | tf_op jit(solution)/shard_map/ppermute | solution.py:16
  68.9 2.8 %collective-permute-start.20 = (bf16[6,16,384]{2,1,0:T(8,128)(2,1)S(1)}, bf16[6,16,384]{2,1,0:T(8,128)(2,1)S(1)}, u32[]{:S(2)}, u32[]{:S(2)}) collective-permute-start(bf16[6,16,384]{2,1,0:T(8,128)(2,1)S(1)} %get-tuple-element.43), channel_id=1, source_target_pairs={{0,124},{4,0},{8,4},{12,8},{16,12},{20,16},{24,20},{28,24},{32,28}... | collective-permute-start | bytes 221192 | tf_op jit(solution)/shard_map/ppermute | solution.py:16
  68.9 7.6 %collective-permute-start.21 = (bf16[6,16,384]{2,1,0:T(8,128)(2,1)S(1)}, bf16[6,16,384]{2,1,0:T(8,128)(2,1)S(1)}, u32[]{:S(2)}, u32[]{:S(2)}) collective-permute-start(bf16[6,16,384]{2,1,0:T(8,128)(2,1)S(1)} %get-tuple-element.45), channel_id=1, source_target_pairs={{0,4},{4,8},{8,12},{12,16},{16,20},{20,24},{24,28},{28,32},{32,36}... | collective-permute-start | bytes 221192 | tf_op jit(solution)/shard_map/ppermute | solution.py:16
  69.4 8.7 %collective-permute-start.22 = (bf16[6,16,384]{2,1,0:T(8,128)(2,1)S(1)}, bf16[6,16,384]{2,1,0:T(8,128)(2,1)S(1)}, u32[]{:S(2)}, u32[]{:S(2)}) collective-permute-start(bf16[6,16,384]{2,1,0:T(8,128)(2,1)S(1)} %get-tuple-element.46), channel_id=1, source_target_pairs={{0,8},{4,12},{8,16},{12,20},{16,24},{20,28},{24,32},{28,36},{32,40... | collective-permute-start | bytes 221192 | tf_op jit(solution)/shard_map/ppermute | solution.py:16
  69.9 8.2 %collective-permute-start.23 = (bf16[6,16,384]{2,1,0:T(8,128)(2,1)S(1)}, bf16[6,16,384]{2,1,0:T(8,128)(2,1)S(1)}, u32[]{:S(2)}, u32[]{:S(2)}) collective-permute-start(bf16[6,16,384]{2,1,0:T(8,128)(2,1)S(1)} %get-tuple-element.47), channel_id=1, source_target_pairs={{0,64},{4,68},{8,72},{12,76},{16,80},{20,84},{24,88},{28,92},{32,9... | collective-permute-start | bytes 221192 | tf_op jit(solution)/shard_map/ppermute | solution.py:16
  78.2 4.7 %collective-permute-start.26 = (bf16[6,16,384]{2,1,0:T(8,128)(2,1)S(1)}, bf16[6,16,384]{2,1,0:T(8,128)(2,1)S(1)}, u32[]{:S(2)}, u32[]{:S(2)}) collective-permute-start(bf16[6,16,384]{2,1,0:T(8,128)(2,1)S(1)} %fusion.6.refs_1_), channel_id=1, source_target_pairs={{0,3},{1,0},{2,1},{3,2},{4,7},{5,4},{6,5},{7,6},{8,11},{9,8},{10,9... | collective-permute-start | bytes 221192 | tf_op jit(solution)/shard_map/ppermute | solution.py:16
  80.1 5.9 %collective-permute-start.25 = (bf16[6,16,384]{2,1,0:T(8,128)(2,1)S(1)}, bf16[6,16,384]{2,1,0:T(8,128)(2,1)S(1)}, u32[]{:S(2)}, u32[]{:S(2)}) collective-permute-start(bf16[6,16,384]{2,1,0:T(8,128)(2,1)S(1)} %fusion.6.refs_1_), channel_id=1, source_target_pairs={{0,2},{1,3},{2,0},{3,1},{4,6},{5,7},{6,4},{7,5},{8,10},{9,11},{10,... | collective-permute-start | bytes 221192 | tf_op jit(solution)/shard_map/ppermute | solution.py:16
  81.0 5.7 %collective-permute-start.24 = (bf16[6,16,384]{2,1,0:T(8,128)(2,1)S(1)}, bf16[6,16,384]{2,1,0:T(8,128)(2,1)S(1)}, u32[]{:S(2)}, u32[]{:S(2)}) collective-permute-start(bf16[6,16,384]{2,1,0:T(8,128)(2,1)S(1)} %fusion.6.refs_1_), channel_id=1, source_target_pairs={{0,1},{1,2},{2,3},{3,0},{4,5},{5,6},{6,7},{7,4},{8,9},{9,10},{10,1... | collective-permute-start | bytes 221192 | tf_op jit(solution)/shard_map/ppermute | solution.py:16

commit v2 on v1

v2 whole, which is shorter than its diff:
```python
import functools

import jax
import jax.numpy as jnp
from jax import lax
from jax.experimental import pallas as pl
from jax.experimental.pallas import tpu as pltpu
from jax.sharding import PartitionSpec as P

HALF = 2
OWN, FAR, SIBLING, HANDED, PASSED, DIRECT = range(6)
GROUPS = 6
BACK = (2, 1, 3)
CHUNKS = 4


def dom_permute(value, target):
    size = lax.axis_size("dom")
    return lax.ppermute(value, "dom", [(i, target(i) % size) for i in range(size)])


def to_sibling(value):
    return dom_permute(value, lambda i: i ^ 1)


def to_far(value):
    half = lax.axis_size("dom") // 2
    return dom_permute(value, lambda i: i + half)


def to_next_chip(value):
    return dom_permute(value, lambda i: i + 2 if i % 2 else i - 2)


def along_rep(value, by):
    size = lax.axis_size("rep")
    return lax.ppermute(value, "rep", [(i, (i + by) % size) for i in range(size)])


def place_columns(parts, rep, group):
    size = len(parts)
    blocks = [part[...].astype(jnp.float32) for part in parts]
    placed = []
    for index in range(size):
        chosen = blocks[0]
        for block, back in zip(blocks[1:], BACK):
            chosen = jnp.where((rep + size - back) % size == index, block, chosen)
        placed.append(chosen)
    return placed


def level_body(level, last, *refs):
    refs = list(refs)
    take = lambda count: [refs.pop(0) for _ in range(count)]
    (rep_ref,) = take(1)
    ids_ref, rhs_hbm = take(2) if not last else (None, None)
    parts = take(4)
    (diag_ref,) = take(1)
    (mats_ref,) = take(1) if not last else (None,)
    prev = take(level)
    (out_ref,) = take(1)
    if not last:
        stored_ref, own_ref, far_ref, sibling_ref, chip_ref = take(5)
    (solved_scr,) = take(1)
    if not last:
        store_scr, acc_scr, rhs_ref, rhs_sem = take(4)
    tiles, cols, _ = solved_scr.shape
    group = cols // 4
    copies = []
    if not last:
        rhs_copy = pltpu.make_async_copy(rhs_hbm.at[level + 1], rhs_ref, rhs_sem.at[0])
    if level == 0:
        diag_hbm, mats_hbm = diag_ref, mats_ref
        diag_ref, mats_ref, sems = take(3)
        copies = [pltpu.make_async_copy(diag_hbm.at[0], diag_ref, sems.at[0])]
        for chunk in range(CHUNKS):
            some = pl.ds(chunk * (mats_ref.shape[0] // CHUNKS), mats_ref.shape[0] // CHUNKS)
            copies.append(pltpu.make_async_copy(mats_hbm.at[0, some], mats_ref.at[some], sems.at[1 + chunk]))
        for copy in copies:
            copy.start()
        rhs_copy.start()
        for index, block in enumerate(place_columns(parts, rep_ref[0], group)):
            solved_scr[:, index * group : (index + 1) * group, :] = block
        residuals = [solved_scr[t].astype(jnp.bfloat16) for t in range(tiles)]
        copies[0].wait()
    else:
        if not last:
            rhs_copy.start()
        residuals = [
            sum(part[t].astype(jnp.float32) for part in parts).astype(jnp.bfloat16) for t in range(tiles)
        ]
    for t in range(tiles):
        solved = jnp.dot(residuals[t], diag_ref[t], preferred_element_type=jnp.float32)
        solved_scr[t] = solved
        if not last:
            stored_ref[t] = solved.astype(jnp.bfloat16)
            store_scr[level * tiles + t] = solved.astype(jnp.bfloat16)
    own = solved_scr[:, :group, :]
    for other in range(1, cols // group):
        own = jnp.where(rep_ref[0] == other, solved_scr[:, other * group : (other + 1) * group, :], own)
    if last:
        for earlier in range(level):
            out_ref[earlier] = prev[earlier][...]
        out_ref[level] = own
        return
    out_ref[...] = own
    for earlier in range(level):
        for t in range(tiles):
            store_scr[earlier * tiles + t] = prev[earlier][t]
    acc_scr[...] = jnp.zeros_like(acc_scr)
    count = mats_ref.shape[0]
    for p in range(count):
        if copies and p % (count // CHUNKS) == 0:
            copies[1 + p // (count // CHUNKS)].wait()
        update = jnp.dot(store_scr[ids_ref[0, level, p]], mats_ref[p], preferred_element_type=jnp.float32)
        slot = ids_ref[1, level, p]
        acc_scr[slot] = acc_scr[slot] + update

    def sums(index):
        return acc_scr[index * tiles : (index + 1) * tiles]

    far_ref[...] = sums(FAR).astype(jnp.bfloat16)
    sibling_ref[0] = sums(HANDED).astype(jnp.bfloat16)
    sibling_ref[1] = sums(SIBLING).astype(jnp.bfloat16)
    chip_ref[0] = sums(PASSED).astype(jnp.bfloat16)
    chip_ref[1] = sums(DIRECT).astype(jnp.bfloat16)
    rhs_copy.wait()
    rhs = rhs_ref[...]
    for index in range(cols // group):
        rows = slice(index * group, (index + 1) * group)
        own_ref[:, rows, :] = jnp.where(rep_ref[0] == index, rhs, 0.0) - acc_scr[OWN * tiles : (OWN + 1) * tiles, rows, :]


def run_level(level, last, rep, ids, parts, diag, mats, prev, right_sides):
    levels, tiles, group, span = right_sides.shape
    cols = 4 * group
    smem = pl.BlockSpec(memory_space=pltpu.SMEM)
    vmem = pl.BlockSpec(memory_space=pltpu.VMEM)
    hbm = pl.BlockSpec(memory_space=pltpu.HBM)
    weights = hbm if level == 0 else vmem
    args = [rep]
    specs = [smem]
    if not last:
        args += [ids, right_sides]
        specs += [smem, hbm]
    args += [*parts, diag]
    specs += [vmem] * len(parts) + [weights]
    if not last:
        args.append(mats)
        specs.append(weights)
    args += prev
    specs += [vmem] * len(prev)
    scratch = [pltpu.VMEM((tiles, cols, span), jnp.float32)]
    if last:
        outs = jax.ShapeDtypeStruct(right_sides.shape, jnp.float32)
        out_specs = vmem
    else:
        block = jax.ShapeDtypeStruct((tiles, cols, span), jnp.bfloat16)
        pair = jax.ShapeDtypeStruct((2, tiles, cols, span), jnp.bfloat16)
        outs = [
            jax.ShapeDtypeStruct((tiles, group, span), jnp.float32),
            block,
            jax.ShapeDtypeStruct((tiles, cols, span), jnp.float32),
            block,
            pair,
            pair,
        ]
        out_specs = [vmem] * len(outs)
        scratch.append(pltpu.VMEM(((level + 1) * tiles, cols, span), jnp.bfloat16))
        scratch.append(pltpu.VMEM((GROUPS * tiles + 1, cols, span), jnp.float32))
        scratch.append(pltpu.VMEM((tiles, group, span), jnp.float32))
        scratch.append(pltpu.SemaphoreType.DMA((1,)))
    if level == 0:
        scratch.append(pltpu.VMEM(diag.shape[1:], diag.dtype))
        scratch.append(pltpu.VMEM(mats.shape[1:], mats.dtype))
        scratch.append(pltpu.SemaphoreType.DMA((1 + CHUNKS,)))
    return pl.pallas_call(
        functools.partial(level_body, level, last),
        out_shape=outs,
        in_specs=specs,
        out_specs=out_specs,
        scratch_shapes=scratch,
        compiler_params=pltpu.CompilerParams(vmem_limit_bytes=12 << 20),
    )(*args)


def fetch_body(level, with_mats, *refs):
    count = 1 + with_mats
    sems = refs[-1]
    copies = [
        pltpu.make_async_copy(refs[1 + i].at[level], refs[1 + count + i], sems.at[i]) for i in range(count)
    ]
    for copy in copies:
        copy.start()
    for copy in copies:
        copy.wait()


def fetch(level, after, *weights):
    vmem = pl.BlockSpec(memory_space=pltpu.VMEM)
    return pl.pallas_call(
        functools.partial(fetch_body, level, len(weights) - 1),
        out_shape=[pltpu.VMEM(w.shape[1:], w.dtype) for w in weights],
        in_specs=[vmem] + [pl.BlockSpec(memory_space=pltpu.HBM)] * len(weights),
        out_specs=[vmem] * len(weights),
        scratch_shapes=[pltpu.SemaphoreType.DMA((len(weights),))],
        compiler_params=pltpu.CompilerParams(vmem_limit_bytes=1 << 20),
    )(after, *weights)


def slots_of(panel_dst, tiles):
    dom_size = lax.axis_size("dom")
    owner = lax.axis_index("dom")
    distance = (panel_dst // tiles - owner) % dom_size
    near = (distance + HALF) % dom_size - HALF
    onward = jnp.where(owner % 2 == 1, near, -near)
    group = jnp.where(
        distance == dom_size // 2,
        FAR,
        jnp.where(
            onward == 0,
            OWN,
            jnp.where(
                onward == 1, PASSED, jnp.where(onward == 2, DIRECT, jnp.where(onward == -1, SIBLING, HANDED))
            ),
        ),
    )
    return jnp.where(panel_dst >= 0, group * tiles + panel_dst % tiles, GROUPS * tiles)


def per_device(right_sides, diag_inverse, panel_mats, panel_src, panel_dst):
    levels, tiles, group, span = right_sides.shape
    rep = lax.axis_index("rep").astype(jnp.int32)
    cols = group * lax.axis_size("rep")
    first = lax.broadcasted_iota(jnp.int32, (2, tiles, cols, span), 0) == 0
    ids = jnp.stack([panel_src, slots_of(panel_dst, tiles)])
    partial = right_sides[0].astype(jnp.bfloat16)
    diag_inverse, panel_mats, rhs = (
        pltpu.with_memory_space_constraint(x, pltpu.HBM) for x in (diag_inverse, panel_mats, right_sides)
    )
    diag, mats = diag_inverse, panel_mats
    store = []
    results = []
    for level in range(levels):
        last = level + 1 == levels
        parts = [partial] + [along_rep(partial, by) for by in BACK]
        if last:
            return run_level(level, last, rep[None], None, parts, diag, None, results, rhs)
        solved, stored, own, far, sibling, chip = run_level(
            level, last, rep[None], ids, parts, diag, mats, store, rhs
        )
        results.append(solved)
        store.append(stored)
        from_sibling = to_sibling(sibling)
        from_far = to_far(far)
        handed = jnp.where(first, from_sibling.astype(jnp.float32), 0.0)
        chip = (chip.astype(jnp.float32) + handed).astype(jnp.bfloat16)
        from_chip = to_next_chip(chip)
        if level + 2 == levels:
            (diag,) = fetch(level + 1, chip, diag_inverse)
        else:
            diag, mats = fetch(level + 1, chip, diag_inverse, panel_mats)
        across = to_sibling(from_chip[0])
        incoming = sum(
            piece.astype(jnp.float32) for piece in (from_sibling[1], from_far, from_chip[1], across)
        )
        partial = (own - incoming).astype(jnp.bfloat16)


def solution(mesh):
    return jax.shard_map(
        per_device,
        mesh=mesh,
        in_specs=(
            P(None, "dom", "rep", None),
            P(None, "dom", None, None),
            P(None, ("dom", "rep"), None, None),
            P(None, ("dom", "rep")),
            P(None, ("dom", "rep")),
        ),
        out_specs=P(None, "dom", "rep", None),
        check_vma=False,
    )
```

time: 88 us -> 85.3 us (0.969)
  waiting for transfers between devices: 42.5 us -> 29.5 us
  Pallas kernels: 6.77 us -> 17.5 us
  local copies, waits for them, and re-layouts: 11.3 us -> 0.8 us
  starting transfers between devices: 26.7 us -> 35 us
  other arithmetic: 0.39 us -> 1.96 us
    ppermute x27 -> x24, waiting for transfers between devices: 42.5 us -> 29.5 us  [the longest x12 20.4 us: dom_permute(): lax.ppermute(value, 'dom', [(i, target(i) % size) for i in range(size)])]
    squeeze x3, local copies, waits for them, and re-layouts: 10.1 us -> 0.03 us  [per_device(): across = to_sibling(from_chip[0])]
    ppermute x27 -> x24, starting transfers between devices: 26.7 us -> 35 us  [the longest x12 18.6 us: along_rep(): lax.ppermute(value, 'rep', [(i, (i + by) % size) for i in range(size)])]
    pallas_call x0 -> x3, Pallas kernels: none -> 7.27 us  [fetch(): pl.pallas_call(functools.partial(fetch_body, level, len(weights) - 1), ou...]
    pallas_call x4, Pallas kernels: 6.77 us -> 10.2 us  [run_level(): pl.pallas_call(functools.partial(level_body, level, last), out_shape=outs...]
    another operation x0 -> x2, other arithmetic: none -> 1.41 us  [per_device(): ids = jnp.stack([panel_src, slots_of(panel_dst, tiles)])]
    another operation x2 -> x0, local copies, waits for them, and re-layouts: 1.19 us -> none  [per_device(): own_rhs = jnp.where(place, jnp.tile(right_sides, (1, 1, rep_size, 1)), 0.0)]
  transfers between devices with their start and end apart: 27 -> 24, of which waited for: 20 -> 14; matrix products, arithmetic and copies ran while one was open for 12% -> 2% of each run, Pallas kernels for 0% -> 9%
where the time goes in v2:
time: 85.3 us; the launch traced here: 84.9 us
  starting transfers between devices  35 us (41%)
  waiting for transfers between devices  29.5 us (35%)
  Pallas kernels  17.5 us (21%)
  other arithmetic  1.96 us (2%)
    ppermute x12, waiting for transfers between devices, dom_permute(): lax.ppermute(value, 'dom', [(i, target(i) % size) for i in range(size)])  20.4 us
    ppermute x12, starting transfers between devices, along_rep(): lax.ppermute(value, 'rep', [(i, (i + by) % size) for i in range(size)])  18.6 us
    ppermute x12, starting transfers between devices, dom_permute(): lax.ppermute(value, 'dom', [(i, target(i) % size) for i in range(size)])  16.5 us
    pallas_call x4, Pallas kernels, run_level(): pl.pallas_call(functools.partial(level_body, level, last), out_shape=outs...  10.2 us
    ppermute x12, waiting for transfers between devices, along_rep(): lax.ppermute(value, 'rep', [(i, (i + by) % size) for i in range(size)])  9.11 us
    pallas_call x3, Pallas kernels, fetch(): pl.pallas_call(functools.partial(fetch_body, level, len(weights) - 1), ou...  7.27 us
  transfers between devices with their start and end apart: 24, of which 14 were waited for; matrix products, arithmetic and copies ran while one was open for 2% of the time, Pallas kernels for 9%

profile of v2, /device:TPU:0, one launch (start us, length us, event | category | flops | bytes accessed | tf_op | source)
XLA Modules:
  0.0 84.9 jit_solution(4834839045606383468)
XLA Ops:
  0.0 0.8 fusion.9.refs_3_
  0.8 4.1 %collective-permute-start.2 = (bf16[6,4,384]{2,1,0:T(4,128)(2,1)S(1)}, bf16[6,4,384]{2,1,0:T(4,128)(2,1)S(1)}, u32[]{:S(2)}, u32[]{:S(2)}) collective-permute-start(bf16[6,4,384]{2,1,0:T(4,128)(2,1)S(1)} %fusion.9.refs_3_), channel_id=1, source_target_pairs={{0,3},{1,0},{2,1},{3,2},{4,7},{5,4},{6,5},{7,6},{8,11},{9,8},{10,9... | collective-permute-start | bytes 55304 | tf_op jit(solution)/shard_map/ppermute | solution.py:37
  4.9 0.0 collective-permute-start.1
  4.9 1.9 %collective-permute-start = (bf16[6,4,384]{2,1,0:T(4,128)(2,1)S(1)}, bf16[6,4,384]{2,1,0:T(4,128)(2,1)S(1)}, u32[]{:S(2)}, u32[]{:S(2)}) collective-permute-start(bf16[6,4,384]{2,1,0:T(4,128)(2,1)S(1)} %fusion.9.refs_3_), channel_id=1, source_target_pairs={{0,2},{1,3},{2,0},{3,1},{4,6},{5,7},{6,4},{7,5},{8,10},{9,11},{10,... | collective-permute-start | bytes 55304 | tf_op jit(solution)/shard_map/ppermute | solution.py:37
  6.8 0.7 fusion.15
  7.5 0.7 pad_add_fusion.refs_1_
  8.2 0.0 collective-permute-done.2.refs_6_
  8.2 1.7 %collective-permute-done.1.refs_5_ = bf16[6,4,384]{2,1,0:T(4,128)(2,1)S(1)} collective-permute-done((bf16[6,4,384]{2,1,0:T(4,128)(2,1)S(1)}, bf16[6,4,384]{2,1,0:T(4,128)(2,1)S(1)}, u32[]{:S(2)}, u32[]{:S(2)}) %collective-permute-start.1) | collective-permute-done | bytes 18464 | tf_op jit(solution)/shard_map/ppermute | solution.py:37
  9.9 0.3 collective-permute-done.refs_4_
  10.2 3.9 %shard_map.55 = (f32[6,4,384]{2,1,0:T(4,128)S(1)}, bf16[6,16,384]{2,1,0:T(8,128)(2,1)S(1)}, f32[6,16,384]{2,1,0:T(8,128)S(1)}, bf16[6,16,384]{2,1,0:T(8,128)(2,1...) custom-call(s32[1]{0:T(128)} %bitcast.refs_0_, s32[2,3,16]{2,1,0:T(4,128)S(1)} %pad_add_fusion.refs_1_, ...), custom_call_target="tpu_custom_call" | custom-call | tf_op jit(solution)/shard_map/pallas_call | solution.py:177
  14.0 0.1 collective-permute-start.3
  14.2 1.3 %collective-permute-done.3 = bf16[2,6,16,384]{3,2,1,0:T(8,128)(2,1)S(1)} collective-permute-done((bf16[2,6,16,384]{3,2,1,0:T(8,128)(2,1)S(1)}, bf16[2,6,16,384]{3,2,1,0:T(8,128)(2,1)S(1)}, u32[]{:S(2)}, u32[]{:S(2)}) %collective-permute-start.3) | collective-permute-done | bytes 147488 | tf_op jit(solution)/shard_map/ppermute | solution.py:19
  15.5 0.1 add_convert_fusion.2.refs_0_
  15.6 5.3 %collective-permute-start.5 = (bf16[2,6,16,384]{3,2,1,0:T(8,128)(2,1)S(1)}, bf16[2,6,16,384]{3,2,1,0:T(8,128)(2,1)S(1)}, u32[]{:S(2)}, u32[]{:S(2)}) collective-permute-start(bf16[2,6,16,384]{3,2,1,0:T(8,128)(2,1)S(1)} %add_convert_fusion.2.refs_0_), channel_id=1, source_target_pairs={{0,120},{4,12},{8,0},{12,20},{16,8},{20,28},{24,16},{28,36},{32,24... | collective-permute-start | bytes 442376 | tf_op jit(solution)/shard_map/ppermute | solution.py:19
  20.9 0.6 collective-permute-start.4
  21.5 2.0 %collective-permute-done.5 = bf16[2,6,16,384]{3,2,1,0:T(8,128)(2,1)S(1)} collective-permute-done((bf16[2,6,16,384]{3,2,1,0:T(8,128)(2,1)S(1)}, bf16[2,6,16,384]{3,2,1,0:T(8,128)(2,1)S(1)}, u32[]{:S(2)}, u32[]{:S(2)}) %collective-permute-start.5) | collective-permute-done | bytes 147488 | tf_op jit(solution)/shard_map/ppermute | solution.py:19
  23.6 0.1 collective-permute-start.6
  23.7 3.1 %collective-permute-done.4 = bf16[6,16,384]{2,1,0:T(8,128)(2,1)S(1)} collective-permute-done((bf16[6,16,384]{2,1,0:T(8,128)(2,1)S(1)}, bf16[6,16,384]{2,1,0:T(8,128)(2,1)S(1)}, u32[]{:S(2)}, u32[]{:S(2)}) %collective-permute-start.4) | collective-permute-done | bytes 73760 | tf_op jit(solution)/shard_map/ppermute | solution.py:19
  26.8 0.0 collective-permute-done.6
  26.8 0.1 fusion.8.refs_3_
  26.8 3.3 %collective-permute-start.9 = (bf16[6,16,384]{2,1,0:T(8,128)(2,1)S(1)}, bf16[6,16,384]{2,1,0:T(8,128)(2,1)S(1)}, u32[]{:S(2)}, u32[]{:S(2)}) collective-permute-start(bf16[6,16,384]{2,1,0:T(8,128)(2,1)S(1)} %fusion.8.refs_3_), channel_id=1, source_target_pairs={{0,3},{1,0},{2,1},{3,2},{4,7},{5,4},{6,5},{7,6},{8,11},{9,8},{10,9... | collective-permute-start | bytes 221192 | tf_op jit(solution)/shard_map/ppermute | solution.py:37
  30.1 0.0 collective-permute-start.8
  30.1 1.5 %collective-permute-start.7 = (bf16[6,16,384]{2,1,0:T(8,128)(2,1)S(1)}, bf16[6,16,384]{2,1,0:T(8,128)(2,1)S(1)}, u32[]{:S(2)}, u32[]{:S(2)}) collective-permute-start(bf16[6,16,384]{2,1,0:T(8,128)(2,1)S(1)} %fusion.8.refs_3_), channel_id=1, source_target_pairs={{0,2},{1,3},{2,0},{3,1},{4,6},{5,7},{6,4},{7,5},{8,10},{9,11},{10,... | collective-permute-start | bytes 221192 | tf_op jit(solution)/shard_map/ppermute | solution.py:37
  31.7 2.9 %shard_map.56 = (bf16[6,384,384]{2,1,0:T(8,128)(2,1)S(1)}, bf16[16,384,384]{2,1,0:T(8,128)(2,1)S(1)}) custom-call(bf16[2,6,16,384]{3,2,1,0:T(8,128)(2,1)S(1)} %add_convert_fusion.2.refs_0_, bf16[4,6,384,384]{3,2,1,0:T(8,128)(2,1)} %refs_1_.5, bf16[3,16,384,384]{3,2,1,0:T(8,128)(2,1)} %refs_2_.8), custom_call_target="tpu_custom_call" | custom-call | tf_op jit(solution)/shard_map/pallas_call | solution.py:201
  34.6 0.0 collective-permute-done.9.refs_6_
  34.6 1.9 %collective-permute-done.8.refs_5_ = bf16[6,16,384]{2,1,0:T(8,128)(2,1)S(1)} collective-permute-done((bf16[6,16,384]{2,1,0:T(8,128)(2,1)S(1)}, bf16[6,16,384]{2,1,0:T(8,128)(2,1)S(1)}, u32[]{:S(2)}, u32[]{:S(2)}) %collective-permute-start.8) | collective-permute-done | bytes 73760 | tf_op jit(solution)/shard_map/ppermute | solution.py:37
  36.5 0.0 collective-permute-done.7.refs_4_
  36.5 2.3 %shard_map.57 = (f32[6,4,384]{2,1,0:T(4,128)S(1)}, bf16[6,16,384]{2,1,0:T(8,128)(2,1)S(1)}, f32[6,16,384]{2,1,0:T(8,128)S(1)}, bf16[6,16,384]{2,1,0:T(8,128)(2,1...) custom-call(s32[1]{0:T(128)} %bitcast.refs_0_, s32[2,3,16]{2,1,0:T(4,128)S(1)} %pad_add_fusion.refs_1_, ...), custom_call_target="tpu_custom_call" | custom-call | tf_op jit(solution)/shard_map/pallas_call | solution.py:177
  38.8 0.1 collective-permute-start.10
  38.9 1.4 %collective-permute-done.10 = bf16[2,6,16,384]{3,2,1,0:T(8,128)(2,1)S(1)} collective-permute-done((bf16[2,6,16,384]{3,2,1,0:T(8,128)(2,1)S(1)}, bf16[2,6,16,384]{3,2,1,0:T(8,128)(2,1)S(1)}, u32[]{:S(2)}, u32[]{:S(2)}) %collective-permute-start.10) | collective-permute-done | bytes 147488 | tf_op jit(solution)/shard_map/ppermute | solution.py:19
  40.3 0.1 add_convert_fusion.1.refs_0_
  40.4 5.2 %collective-permute-start.12 = (bf16[2,6,16,384]{3,2,1,0:T(8,128)(2,1)S(1)}, bf16[2,6,16,384]{3,2,1,0:T(8,128)(2,1)S(1)}, u32[]{:S(2)}, u32[]{:S(2)}) collective-permute-start(bf16[2,6,16,384]{3,2,1,0:T(8,128)(2,1)S(1)} %add_convert_fusion.1.refs_0_), channel_id=1, source_target_pairs={{0,120},{4,12},{8,0},{12,20},{16,8},{20,28},{24,16},{28,36},{32,24... | collective-permute-start | bytes 442376 | tf_op jit(solution)/shard_map/ppermute | solution.py:19
  45.6 0.0 collective-permute-start.11
  45.6 2.7 %collective-permute-done.12 = bf16[2,6,16,384]{3,2,1,0:T(8,128)(2,1)S(1)} collective-permute-done((bf16[2,6,16,384]{3,2,1,0:T(8,128)(2,1)S(1)}, bf16[2,6,16,384]{3,2,1,0:T(8,128)(2,1)S(1)}, u32[]{:S(2)}, u32[]{:S(2)}) %collective-permute-start.12) | collective-permute-done | bytes 147488 | tf_op jit(solution)/shard_map/ppermute | solution.py:19
  48.3 0.1 collective-permute-start.13
  48.4 3.1 %collective-permute-done.11 = bf16[6,16,384]{2,1,0:T(8,128)(2,1)S(1)} collective-permute-done((bf16[6,16,384]{2,1,0:T(8,128)(2,1)S(1)}, bf16[6,16,384]{2,1,0:T(8,128)(2,1)S(1)}, u32[]{:S(2)}, u32[]{:S(2)}) %collective-permute-start.11) | collective-permute-done | bytes 73760 | tf_op jit(solution)/shard_map/ppermute | solution.py:19
  51.5 0.0 collective-permute-done.13
  51.5 0.1 fusion.5.refs_3_
  51.5 2.3 %collective-permute-start.16 = (bf16[6,16,384]{2,1,0:T(8,128)(2,1)S(1)}, bf16[6,16,384]{2,1,0:T(8,128)(2,1)S(1)}, u32[]{:S(2)}, u32[]{:S(2)}) collective-permute-start(bf16[6,16,384]{2,1,0:T(8,128)(2,1)S(1)} %fusion.5.refs_3_), channel_id=1, source_target_pairs={{0,3},{1,0},{2,1},{3,2},{4,7},{5,4},{6,5},{7,6},{8,11},{9,8},{10,9... | collective-permute-start | bytes 221192 | tf_op jit(solution)/shard_map/ppermute | solution.py:37
  53.9 0.0 collective-permute-start.15
  53.9 1.5 %collective-permute-start.14 = (bf16[6,16,384]{2,1,0:T(8,128)(2,1)S(1)}, bf16[6,16,384]{2,1,0:T(8,128)(2,1)S(1)}, u32[]{:S(2)}, u32[]{:S(2)}) collective-permute-start(bf16[6,16,384]{2,1,0:T(8,128)(2,1)S(1)} %fusion.5.refs_3_), channel_id=1, source_target_pairs={{0,2},{1,3},{2,0},{3,1},{4,6},{5,7},{6,4},{7,5},{8,10},{9,11},{10,... | collective-permute-start | bytes 221192 | tf_op jit(solution)/shard_map/ppermute | solution.py:37
  55.4 2.9 %shard_map.58 = (bf16[6,384,384]{2,1,0:T(8,128)(2,1)S(1)}, bf16[16,384,384]{2,1,0:T(8,128)(2,1)S(1)}) custom-call(bf16[2,6,16,384]{3,2,1,0:T(8,128)(2,1)S(1)} %add_convert_fusion.1.refs_0_, bf16[4,6,384,384]{3,2,1,0:T(8,128)(2,1)} %refs_1_.5, bf16[3,16,384,384]{3,2,1,0:T(8,128)(2,1)} %refs_2_.8), custom_call_target="tpu_custom_call" | custom-call | tf_op jit(solution)/shard_map/pallas_call | solution.py:201
  58.3 0.0 collective-permute-done.16.refs_6_
  58.3 1.9 %collective-permute-done.15.refs_5_ = bf16[6,16,384]{2,1,0:T(8,128)(2,1)S(1)} collective-permute-done((bf16[6,16,384]{2,1,0:T(8,128)(2,1)S(1)}, bf16[6,16,384]{2,1,0:T(8,128)(2,1)S(1)}, u32[]{:S(2)}, u32[]{:S(2)}) %collective-permute-start.15) | collective-permute-done | bytes 73760 | tf_op jit(solution)/shard_map/ppermute | solution.py:37
  60.2 0.0 collective-permute-done.14.refs_4_
  60.2 2.9 %shard_map.59 = (f32[6,4,384]{2,1,0:T(4,128)S(1)}, bf16[6,16,384]{2,1,0:T(8,128)(2,1)}, f32[6,16,384]{2,1,0:T(8,128)S(1)}, bf16[6,16,384]{2,1,0:T(8,128)(2,1)S(1...) custom-call(s32[1]{0:T(128)} %bitcast.refs_0_, s32[2,3,16]{2,1,0:T(4,128)S(1)} %pad_add_fusion.refs_1_, ...), custom_call_target="tpu_custom_call" | custom-call | tf_op jit(solution)/shard_map/pallas_call | solution.py:177
  63.2 0.1 collective-permute-start.17
  63.3 1.4 %collective-permute-done.17 = bf16[2,6,16,384]{3,2,1,0:T(8,128)(2,1)S(1)} collective-permute-done((bf16[2,6,16,384]{3,2,1,0:T(8,128)(2,1)S(1)}, bf16[2,6,16,384]{3,2,1,0:T(8,128)(2,1)S(1)}, u32[]{:S(2)}, u32[]{:S(2)}) %collective-permute-start.17) | collective-permute-done | bytes 147488 | tf_op jit(solution)/shard_map/ppermute | solution.py:19
  64.6 0.1 add_convert_fusion.refs_0_
  64.7 4.5 %collective-permute-start.19 = (bf16[2,6,16,384]{3,2,1,0:T(8,128)(2,1)S(1)}, bf16[2,6,16,384]{3,2,1,0:T(8,128)(2,1)S(1)}, u32[]{:S(2)}, u32[]{:S(2)}) collective-permute-start(bf16[2,6,16,384]{3,2,1,0:T(8,128)(2,1)S(1)} %add_convert_fusion.refs_0_), channel_id=1, source_target_pairs={{0,120},{4,12},{8,0},{12,20},{16,8},{20,28},{24,16},{28,36},{32,24... | collective-permute-start | bytes 442376 | tf_op jit(solution)/shard_map/ppermute | solution.py:19
  69.3 0.0 collective-permute-start.18
  69.3 2.7 %collective-permute-done.19 = bf16[2,6,16,384]{3,2,1,0:T(8,128)(2,1)S(1)} collective-permute-done((bf16[2,6,16,384]{3,2,1,0:T(8,128)(2,1)S(1)}, bf16[2,6,16,384]{3,2,1,0:T(8,128)(2,1)S(1)}, u32[]{:S(2)}, u32[]{:S(2)}) %collective-permute-start.19) | collective-permute-done | bytes 147488 | tf_op jit(solution)/shard_map/ppermute | solution.py:19
  71.9 0.4 collective-permute-start.20
  72.4 2.8 %collective-permute-done.18 = bf16[6,16,384]{2,1,0:T(8,128)(2,1)S(1)} collective-permute-done((bf16[6,16,384]{2,1,0:T(8,128)(2,1)S(1)}, bf16[6,16,384]{2,1,0:T(8,128)(2,1)S(1)}, u32[]{:S(2)}, u32[]{:S(2)}) %collective-permute-start.18) | collective-permute-done | bytes 73760 | tf_op jit(solution)/shard_map/ppermute | solution.py:19
  75.1 0.0 collective-permute-done.20
  75.1 0.1 fusion.2.refs_1_
  75.2 2.3 %collective-permute-start.23 = (bf16[6,16,384]{2,1,0:T(8,128)(2,1)S(1)}, bf16[6,16,384]{2,1,0:T(8,128)(2,1)S(1)}, u32[]{:S(2)}, u32[]{:S(2)}) collective-permute-start(bf16[6,16,384]{2,1,0:T(8,128)(2,1)S(1)} %fusion.2.refs_1_), channel_id=1, source_target_pairs={{0,3},{1,0},{2,1},{3,2},{4,7},{5,4},{6,5},{7,6},{8,11},{9,8},{10,9... | collective-permute-start | bytes 221192 | tf_op jit(solution)/shard_map/ppermute | solution.py:37
  77.5 0.0 collective-permute-start.22
  77.5 1.5 %collective-permute-start.21 = (bf16[6,16,384]{2,1,0:T(8,128)(2,1)S(1)}, bf16[6,16,384]{2,1,0:T(8,128)(2,1)S(1)}, u32[]{:S(2)}, u32[]{:S(2)}) collective-permute-start(bf16[6,16,384]{2,1,0:T(8,128)(2,1)S(1)} %fusion.2.refs_1_), channel_id=1, source_target_pairs={{0,2},{1,3},{2,0},{3,1},{4,6},{5,7},{6,4},{7,5},{8,10},{9,11},{10,... | collective-permute-start | bytes 221192 | tf_op jit(solution)/shard_map/ppermute | solution.py:37
  79.0 1.5 %shard_map.60.refs_5_ = bf16[6,384,384]{2,1,0:T(8,128)(2,1)S(1)} custom-call(bf16[2,6,16,384]{3,2,1,0:T(8,128)(2,1)S(1)} %add_convert_fusion.refs_0_, bf16[4,6,384,384]{3,2,1,0:T(8,128)(2,1)} %refs_1_.5), custom_call_target="tpu_custom_call" | custom-call | tf_op jit(solution)/shard_map/pallas_call | solution.py:201
  80.5 0.0 collective-permute-done.23.refs_4_
  80.5 3.3 %collective-permute-done.22.refs_3_ = bf16[6,16,384]{2,1,0:T(8,128)(2,1)S(1)} collective-permute-done((bf16[6,16,384]{2,1,0:T(8,128)(2,1)S(1)}, bf16[6,16,384]{2,1,0:T(8,128)(2,1)S(1)}, u32[]{:S(2)}, u32[]{:S(2)}) %collective-permute-start.22) | collective-permute-done | bytes 73760 | tf_op jit(solution)/shard_map/ppermute | solution.py:37
  83.8 0.0 collective-permute-done.21.refs_2_
  83.9 1.1 %shard_map.61 = f32[4,6,4,384]{3,2,1,0:T(4,128)} custom-call(s32[1]{0:T(128)} %bitcast.refs_0_, bf16[6,16,384]{2,1,0:T(8,128)(2,1)S(1)} %fusion.2.refs_1_, bf16[6,16,384]{2,1,0:T(8,128)(2,1)S(1)} %collective-permute-done.21.refs_2_, bf16[6,16,384]{2,1,0:T(8,128)(2,1)S(1)} %collective-permute-done.22.refs_3_, ...), custom_call_target="tpu_custom_call" | custom-call | tf_op jit(solution)/shard_map/pallas_call | solution.py:177
  (4 shorter events, 0.0 us)
Async XLA Ops:
  0.8 7.4 %collective-permute-start.2 = (bf16[6,4,384]{2,1,0:T(4,128)(2,1)S(1)}, bf16[6,4,384]{2,1,0:T(4,128)(2,1)S(1)}, u32[]{:S(2)}, u32[]{:S(2)}) collective-permute-start(bf16[6,4,384]{2,1,0:T(4,128)(2,1)S(1)} %fusion.9.refs_3_), channel_id=1, source_target_pairs={{0,3},{1,0},{2,1},{3,2},{4,7},{5,4},{6,5},{7,6},{8,11},{9,8},{10,9... | collective-permute-start | bytes 55304 | tf_op jit(solution)/shard_map/ppermute | solution.py:37
  4.9 5.0 %collective-permute-start.1 = (bf16[6,4,384]{2,1,0:T(4,128)(2,1)S(1)}, bf16[6,4,384]{2,1,0:T(4,128)(2,1)S(1)}, u32[]{:S(2)}, u32[]{:S(2)}) collective-permute-start(bf16[6,4,384]{2,1,0:T(4,128)(2,1)S(1)} %fusion.9.refs_3_), channel_id=1, source_target_pairs={{0,1},{1,2},{2,3},{3,0},{4,5},{5,6},{6,7},{7,4},{8,9},{9,10},{10,1... | collective-permute-start | bytes 55304 | tf_op jit(solution)/shard_map/ppermute | solution.py:37
  4.9 5.3 %collective-permute-start = (bf16[6,4,384]{2,1,0:T(4,128)(2,1)S(1)}, bf16[6,4,384]{2,1,0:T(4,128)(2,1)S(1)}, u32[]{:S(2)}, u32[]{:S(2)}) collective-permute-start(bf16[6,4,384]{2,1,0:T(4,128)(2,1)S(1)} %fusion.9.refs_3_), channel_id=1, source_target_pairs={{0,2},{1,3},{2,0},{3,1},{4,6},{5,7},{6,4},{7,5},{8,10},{9,11},{10,... | collective-permute-start | bytes 55304 | tf_op jit(solution)/shard_map/ppermute | solution.py:37
  14.0 1.5 %collective-permute-start.3 = (bf16[2,6,16,384]{3,2,1,0:T(8,128)(2,1)S(1)}, bf16[2,6,16,384]{3,2,1,0:T(8,128)(2,1)S(1)}, u32[]{:S(2)}, u32[]{:S(2)}) collective-permute-start(bf16[2,6,16,384]{3,2,1,0:T(8,128)(2,1)S(1)} %get-tuple-element.27), channel_id=1, source_target_pairs={{0,4},{4,0},{8,12},{12,8},{16,20},{20,16},{24,28},{28,24},{32,36},... | collective-permute-start | bytes 442376 | tf_op jit(solution)/shard_map/ppermute | solution.py:19
  15.6 8.0 %collective-permute-start.5 = (bf16[2,6,16,384]{3,2,1,0:T(8,128)(2,1)S(1)}, bf16[2,6,16,384]{3,2,1,0:T(8,128)(2,1)S(1)}, u32[]{:S(2)}, u32[]{:S(2)}) collective-permute-start(bf16[2,6,16,384]{3,2,1,0:T(8,128)(2,1)S(1)} %add_convert_fusion.2.refs_0_), channel_id=1, source_target_pairs={{0,120},{4,12},{8,0},{12,20},{16,8},{20,28},{24,16},{28,36},{32,24... | collective-permute-start | bytes 442376 | tf_op jit(solution)/shard_map/ppermute | solution.py:19
  20.9 5.9 %collective-permute-start.4 = (bf16[6,16,384]{2,1,0:T(8,128)(2,1)S(1)}, bf16[6,16,384]{2,1,0:T(8,128)(2,1)S(1)}, u32[]{:S(2)}, u32[]{:S(2)}) collective-permute-start(bf16[6,16,384]{2,1,0:T(8,128)(2,1)S(1)} %get-tuple-element.28), channel_id=1, source_target_pairs={{0,64},{4,68},{8,72},{12,76},{16,80},{20,84},{24,88},{28,92},{32,9... | collective-permute-start | bytes 221192 | tf_op jit(solution)/shard_map/ppermute | solution.py:19
  23.6 3.2 %collective-permute-start.6 = (bf16[6,16,384]{2,1,0:T(8,128)(2,1)S(1)}, bf16[6,16,384]{2,1,0:T(8,128)(2,1)S(1)}, u32[]{:S(2)}, u32[]{:S(2)}) collective-permute-start(bf16[6,16,384]{2,1,0:T(8,128)(2,1)S(1)} %slice_bitcast_fusion.6), channel_id=1, source_target_pairs={{0,4},{4,0},{8,12},{12,8},{16,20},{20,16},{24,28},{28,24},{32,36},... | collective-permute-start | bytes 221192 | tf_op jit(solution)/shard_map/ppermute | solution.py:19
  26.8 7.8 %collective-permute-start.9 = (bf16[6,16,384]{2,1,0:T(8,128)(2,1)S(1)}, bf16[6,16,384]{2,1,0:T(8,128)(2,1)S(1)}, u32[]{:S(2)}, u32[]{:S(2)}) collective-permute-start(bf16[6,16,384]{2,1,0:T(8,128)(2,1)S(1)} %fusion.8.refs_3_), channel_id=1, source_target_pairs={{0,3},{1,0},{2,1},{3,2},{4,7},{5,4},{6,5},{7,6},{8,11},{9,8},{10,9... | collective-permute-start | bytes 221192 | tf_op jit(solution)/shard_map/ppermute | solution.py:37
  30.1 6.4 %collective-permute-start.8 = (bf16[6,16,384]{2,1,0:T(8,128)(2,1)S(1)}, bf16[6,16,384]{2,1,0:T(8,128)(2,1)S(1)}, u32[]{:S(2)}, u32[]{:S(2)}) collective-permute-start(bf16[6,16,384]{2,1,0:T(8,128)(2,1)S(1)} %fusion.8.refs_3_), channel_id=1, source_target_pairs={{0,1},{1,2},{2,3},{3,0},{4,5},{5,6},{6,7},{7,4},{8,9},{9,10},{10,1... | collective-permute-start | bytes 221192 | tf_op jit(solution)/shard_map/ppermute | solution.py:37
  30.1 6.4 %collective-permute-start.7 = (bf16[6,16,384]{2,1,0:T(8,128)(2,1)S(1)}, bf16[6,16,384]{2,1,0:T(8,128)(2,1)S(1)}, u32[]{:S(2)}, u32[]{:S(2)}) collective-permute-start(bf16[6,16,384]{2,1,0:T(8,128)(2,1)S(1)} %fusion.8.refs_3_), channel_id=1, source_target_pairs={{0,2},{1,3},{2,0},{3,1},{4,6},{5,7},{6,4},{7,5},{8,10},{9,11},{10,... | collective-permute-start | bytes 221192 | tf_op jit(solution)/shard_map/ppermute | solution.py:37
  38.8 1.5 %collective-permute-start.10 = (bf16[2,6,16,384]{3,2,1,0:T(8,128)(2,1)S(1)}, bf16[2,6,16,384]{3,2,1,0:T(8,128)(2,1)S(1)}, u32[]{:S(2)}, u32[]{:S(2)}) collective-permute-start(bf16[2,6,16,384]{3,2,1,0:T(8,128)(2,1)S(1)} %get-tuple-element.34), channel_id=1, source_target_pairs={{0,4},{4,0},{8,12},{12,8},{16,20},{20,16},{24,28},{28,24},{32,36},... | collective-permute-start | bytes 442376 | tf_op jit(solution)/shard_map/ppermute | solution.py:19
  40.4 7.9 %collective-permute-start.12 = (bf16[2,6,16,384]{3,2,1,0:T(8,128)(2,1)S(1)}, bf16[2,6,16,384]{3,2,1,0:T(8,128)(2,1)S(1)}, u32[]{:S(2)}, u32[]{:S(2)}) collective-permute-start(bf16[2,6,16,384]{3,2,1,0:T(8,128)(2,1)S(1)} %add_convert_fusion.1.refs_0_), channel_id=1, source_target_pairs={{0,120},{4,12},{8,0},{12,20},{16,8},{20,28},{24,16},{28,36},{32,24... | collective-permute-start | bytes 442376 | tf_op jit(solution)/shard_map/ppermute | solution.py:19
  45.6 5.9 %collective-permute-start.11 = (bf16[6,16,384]{2,1,0:T(8,128)(2,1)S(1)}, bf16[6,16,384]{2,1,0:T(8,128)(2,1)S(1)}, u32[]{:S(2)}, u32[]{:S(2)}) collective-permute-start(bf16[6,16,384]{2,1,0:T(8,128)(2,1)S(1)} %get-tuple-element.35), channel_id=1, source_target_pairs={{0,64},{4,68},{8,72},{12,76},{16,80},{20,84},{24,88},{28,92},{32,9... | collective-permute-start | bytes 221192 | tf_op jit(solution)/shard_map/ppermute | solution.py:19
  48.3 3.2 %collective-permute-start.13 = (bf16[6,16,384]{2,1,0:T(8,128)(2,1)S(1)}, bf16[6,16,384]{2,1,0:T(8,128)(2,1)S(1)}, u32[]{:S(2)}, u32[]{:S(2)}) collective-permute-start(bf16[6,16,384]{2,1,0:T(8,128)(2,1)S(1)} %slice_bitcast_fusion.3), channel_id=1, source_target_pairs={{0,4},{4,0},{8,12},{12,8},{16,20},{20,16},{24,28},{28,24},{32,36},... | collective-permute-start | bytes 221192 | tf_op jit(solution)/shard_map/ppermute | solution.py:19
  51.5 6.8 %collective-permute-start.16 = (bf16[6,16,384]{2,1,0:T(8,128)(2,1)S(1)}, bf16[6,16,384]{2,1,0:T(8,128)(2,1)S(1)}, u32[]{:S(2)}, u32[]{:S(2)}) collective-permute-start(bf16[6,16,384]{2,1,0:T(8,128)(2,1)S(1)} %fusion.5.refs_3_), channel_id=1, source_target_pairs={{0,3},{1,0},{2,1},{3,2},{4,7},{5,4},{6,5},{7,6},{8,11},{9,8},{10,9... | collective-permute-start | bytes 221192 | tf_op jit(solution)/shard_map/ppermute | solution.py:37
  53.9 6.4 %collective-permute-start.15 = (bf16[6,16,384]{2,1,0:T(8,128)(2,1)S(1)}, bf16[6,16,384]{2,1,0:T(8,128)(2,1)S(1)}, u32[]{:S(2)}, u32[]{:S(2)}) collective-permute-start(bf16[6,16,384]{2,1,0:T(8,128)(2,1)S(1)} %fusion.5.refs_3_), channel_id=1, source_target_pairs={{0,1},{1,2},{2,3},{3,0},{4,5},{5,6},{6,7},{7,4},{8,9},{9,10},{10,1... | collective-permute-start | bytes 221192 | tf_op jit(solution)/shard_map/ppermute | solution.py:37
  53.9 6.4 %collective-permute-start.14 = (bf16[6,16,384]{2,1,0:T(8,128)(2,1)S(1)}, bf16[6,16,384]{2,1,0:T(8,128)(2,1)S(1)}, u32[]{:S(2)}, u32[]{:S(2)}) collective-permute-start(bf16[6,16,384]{2,1,0:T(8,128)(2,1)S(1)} %fusion.5.refs_3_), channel_id=1, source_target_pairs={{0,2},{1,3},{2,0},{3,1},{4,6},{5,7},{6,4},{7,5},{8,10},{9,11},{10,... | collective-permute-start | bytes 221192 | tf_op jit(solution)/shard_map/ppermute | solution.py:37
  63.2 1.5 %collective-permute-start.17 = (bf16[2,6,16,384]{3,2,1,0:T(8,128)(2,1)S(1)}, bf16[2,6,16,384]{3,2,1,0:T(8,128)(2,1)S(1)}, u32[]{:S(2)}, u32[]{:S(2)}) collective-permute-start(bf16[2,6,16,384]{3,2,1,0:T(8,128)(2,1)S(1)} %get-tuple-element.41), channel_id=1, source_target_pairs={{0,4},{4,0},{8,12},{12,8},{16,20},{20,16},{24,28},{28,24},{32,36},... | collective-permute-start | bytes 442376 | tf_op jit(solution)/shard_map/ppermute | solution.py:19
  64.7 7.2 %collective-permute-start.19 = (bf16[2,6,16,384]{3,2,1,0:T(8,128)(2,1)S(1)}, bf16[2,6,16,384]{3,2,1,0:T(8,128)(2,1)S(1)}, u32[]{:S(2)}, u32[]{:S(2)}) collective-permute-start(bf16[2,6,16,384]{3,2,1,0:T(8,128)(2,1)S(1)} %add_convert_fusion.refs_0_), channel_id=1, source_target_pairs={{0,120},{4,12},{8,0},{12,20},{16,8},{20,28},{24,16},{28,36},{32,24... | collective-permute-start | bytes 442376 | tf_op jit(solution)/shard_map/ppermute | solution.py:19
  69.3 5.9 %collective-permute-start.18 = (bf16[6,16,384]{2,1,0:T(8,128)(2,1)S(1)}, bf16[6,16,384]{2,1,0:T(8,128)(2,1)S(1)}, u32[]{:S(2)}, u32[]{:S(2)}) collective-permute-start(bf16[6,16,384]{2,1,0:T(8,128)(2,1)S(1)} %get-tuple-element.42), channel_id=1, source_target_pairs={{0,64},{4,68},{8,72},{12,76},{16,80},{20,84},{24,88},{28,92},{32,9... | collective-permute-start | bytes 221192 | tf_op jit(solution)/shard_map/ppermute | solution.py:19
  71.9 3.2 %collective-permute-start.20 = (bf16[6,16,384]{2,1,0:T(8,128)(2,1)S(1)}, bf16[6,16,384]{2,1,0:T(8,128)(2,1)S(1)}, u32[]{:S(2)}, u32[]{:S(2)}) collective-permute-start(bf16[6,16,384]{2,1,0:T(8,128)(2,1)S(1)} %slice_bitcast_fusion), channel_id=1, source_target_pairs={{0,4},{4,0},{8,12},{12,8},{16,20},{20,16},{24,28},{28,24},{32,36},... | collective-permute-start | bytes 221192 | tf_op jit(solution)/shard_map/ppermute | solution.py:19
  75.2 5.4 %collective-permute-start.23 = (bf16[6,16,384]{2,1,0:T(8,128)(2,1)S(1)}, bf16[6,16,384]{2,1,0:T(8,128)(2,1)S(1)}, u32[]{:S(2)}, u32[]{:S(2)}) collective-permute-start(bf16[6,16,384]{2,1,0:T(8,128)(2,1)S(1)} %fusion.2.refs_1_), channel_id=1, source_target_pairs={{0,3},{1,0},{2,1},{3,2},{4,7},{5,4},{6,5},{7,6},{8,11},{9,8},{10,9... | collective-permute-start | bytes 221192 | tf_op jit(solution)/shard_map/ppermute | solution.py:37
  77.5 6.4 %collective-permute-start.22 = (bf16[6,16,384]{2,1,0:T(8,128)(2,1)S(1)}, bf16[6,16,384]{2,1,0:T(8,128)(2,1)S(1)}, u32[]{:S(2)}, u32[]{:S(2)}) collective-permute-start(bf16[6,16,384]{2,1,0:T(8,128)(2,1)S(1)} %fusion.2.refs_1_), channel_id=1, source_target_pairs={{0,1},{1,2},{2,3},{3,0},{4,5},{5,6},{6,7},{7,4},{8,9},{9,10},{10,1... | collective-permute-start | bytes 221192 | tf_op jit(solution)/shard_map/ppermute | solution.py:37
  77.5 6.4 %collective-permute-start.21 = (bf16[6,16,384]{2,1,0:T(8,128)(2,1)S(1)}, bf16[6,16,384]{2,1,0:T(8,128)(2,1)S(1)}, u32[]{:S(2)}, u32[]{:S(2)}) collective-permute-start(bf16[6,16,384]{2,1,0:T(8,128)(2,1)S(1)} %fusion.2.refs_1_), channel_id=1, source_target_pairs={{0,2},{1,3},{2,0},{3,1},{4,6},{5,7},{6,4},{7,5},{8,10},{9,11},{10,... | collective-permute-start | bytes 221192 | tf_op jit(solution)/shard_map/ppermute | solution.py:37

commit v3 on v2

v3 whole, which is shorter than its diff:
```python
import functools

import jax
import jax.numpy as jnp
from jax import lax
from jax.experimental import pallas as pl
from jax.experimental.pallas import tpu as pltpu
from jax.sharding import PartitionSpec as P

HALF = 2
OWN, FAR, SIBLING, HANDED, PASSED, DIRECT = range(6)
GROUPS = 6
BACK = (2, 1, 3)
CHUNKS = 4


def dom_permute(value, target, sends=lambda i: True):
    size = lax.axis_size("dom")
    return lax.ppermute(value, "dom", [(i, target(i) % size) for i in range(size) if sends(i)])


def to_sibling(value):
    return dom_permute(value, lambda i: i ^ 1)


def to_far(value):
    half = lax.axis_size("dom") // 2
    return dom_permute(value, lambda i: i + half, lambda i: i % 2 == (i // 2 % 4 < 2))


def to_next_chip(value):
    return dom_permute(value, lambda i: i + 2 if i % 2 else i - 2)


def along_rep(value, by):
    size = lax.axis_size("rep")
    return lax.ppermute(value, "rep", [(i, (i + by) % size) for i in range(size)])


def place_columns(parts, rep):
    size = len(parts)
    blocks = [part[...].astype(jnp.float32) for part in parts]
    placed = []
    for index in range(size):
        chosen = blocks[0]
        for block, back in zip(blocks[1:], BACK):
            chosen = jnp.where((rep + size - back) % size == index, block, chosen)
        placed.append(chosen)
    return placed


def weight_copies(level, sources, targets, sems):
    copies = []
    for source, target in zip(sources, targets):
        step = target.shape[0] // 2 if target.shape[0] < 8 else target.shape[0] // CHUNKS
        for start in range(0, target.shape[0], step):
            some = pl.ds(start, step)
            copies.append(
                pltpu.make_async_copy(source.at[level, some], target.at[some], sems.at[len(copies)])
            )
    return copies


def level_body(level, last, ahead, *refs):
    refs = list(refs)
    take = lambda count: [refs.pop(0) for _ in range(count)]
    (rep_ref,) = take(1)
    (ids_ref,) = take(1) if not last else (None,)
    parts = take(4)
    (diag_ref,) = take(1)
    (mats_ref,) = take(1) if not last else (None,)
    prev = take(level)
    sources = take(ahead)
    (out_ref,) = take(1)
    if not last:
        stored_ref, own_ref, sibling_ref, far_ref, chip_ref = take(5)
    targets = take(ahead)
    (solved_scr,) = take(1)
    if not last:
        store_scr, acc_scr = take(2)
    copies = weight_copies(level + 1, sources, targets, take(1)[0]) if ahead else []
    for copy in copies:
        copy.start()
    tiles, cols, _ = solved_scr.shape
    group = cols // 4
    if level == 0:
        for index, block in enumerate(place_columns(parts, rep_ref[0])):
            solved_scr[:, index * group : (index + 1) * group, :] = block
        residuals = [solved_scr[t].astype(jnp.bfloat16) for t in range(tiles)]
    else:
        residuals = [
            sum(part[t].astype(jnp.float32) for part in parts).astype(jnp.bfloat16) for t in range(tiles)
        ]
    for t in range(tiles):
        solved = jnp.dot(residuals[t], diag_ref[t], preferred_element_type=jnp.float32)
        solved_scr[t] = solved
        if not last:
            stored_ref[t] = solved.astype(jnp.bfloat16)
            store_scr[level * tiles + t] = solved.astype(jnp.bfloat16)
    own = solved_scr[:, :group, :]
    for other in range(1, cols // group):
        own = jnp.where(rep_ref[0] == other, solved_scr[:, other * group : (other + 1) * group, :], own)
    if last:
        for earlier in range(level):
            out_ref[earlier] = prev[earlier][...]
        out_ref[level] = own
        return
    out_ref[...] = own
    for earlier in range(level):
        for t in range(tiles):
            store_scr[earlier * tiles + t] = prev[earlier][t]
    acc_scr[...] = jnp.zeros_like(acc_scr)
    for p in range(mats_ref.shape[0]):
        update = jnp.dot(
            store_scr[ids_ref[0, level, p]], mats_ref[p], preferred_element_type=jnp.float32
        )
        slot = ids_ref[1, level, p]
        acc_scr[slot] = acc_scr[slot] + update

    def sums(index):
        return acc_scr[index * tiles : (index + 1) * tiles].astype(jnp.bfloat16)

    own_ref[...] = sums(OWN)
    far_ref[0] = sums(FAR)
    far_ref[1] = sums(FAR)
    sibling_ref[0] = sums(HANDED)
    sibling_ref[1] = sums(SIBLING)
    sibling_ref[2] = sums(FAR)
    chip_ref[0] = sums(PASSED)
    chip_ref[1] = sums(DIRECT)
    for copy in copies:
        copy.wait()


def run_level(level, last, rep, ids, parts, weights, prev, ahead, shape):
    levels, tiles, group, span = shape
    cols = 4 * group
    smem = pl.BlockSpec(memory_space=pltpu.SMEM)
    vmem = pl.BlockSpec(memory_space=pltpu.VMEM)
    hbm = pl.BlockSpec(memory_space=pltpu.HBM)
    args = [rep]
    specs = [smem]
    if not last:
        args.append(ids)
        specs.append(smem)
    inner = [*parts, *weights, *prev]
    args += inner + ahead
    specs += [vmem] * len(inner) + [hbm] * len(ahead)
    scratch = [pltpu.VMEM((tiles, cols, span), jnp.float32)]
    if last:
        outs = jax.ShapeDtypeStruct(shape, jnp.float32)
        out_specs = vmem
    else:
        outs = [jax.ShapeDtypeStruct((tiles, group, span), jnp.float32)] + [
            jax.ShapeDtypeStruct((*lead, tiles, cols, span), jnp.bfloat16) for lead in ((), (), (3,), (2,), (2,))
        ]
        outs += [pltpu.VMEM(w.shape[1:], w.dtype) for w in ahead]
        out_specs = [vmem] * len(outs)
        scratch.append(pltpu.VMEM(((level + 1) * tiles, cols, span), jnp.bfloat16))
        scratch.append(pltpu.VMEM((GROUPS * tiles + 1, cols, span), jnp.float32))
        scratch.append(pltpu.SemaphoreType.DMA((2 + CHUNKS,)))
    return pl.pallas_call(
        functools.partial(level_body, level, last, len(ahead)),
        out_shape=outs,
        in_specs=specs,
        out_specs=out_specs,
        scratch_shapes=scratch,
        compiler_params=pltpu.CompilerParams(vmem_limit_bytes=6 << 20),
    )(*args)


def fetch_body(*refs):
    _, diag_hbm, mats_hbm, diag_ref, mats_ref, sems = refs
    copies = weight_copies(0, [diag_hbm, mats_hbm], [diag_ref, mats_ref], sems)
    for copy in copies:
        copy.start()
    for copy in copies:
        copy.wait()


def fetch(after, diag, mats):
    vmem = pl.BlockSpec(memory_space=pltpu.VMEM)
    hbm = pl.BlockSpec(memory_space=pltpu.HBM)
    return pl.pallas_call(
        fetch_body,
        out_shape=[pltpu.VMEM(w.shape[1:], w.dtype) for w in (diag, mats)],
        in_specs=[vmem, hbm, hbm],
        out_specs=[vmem, vmem],
        scratch_shapes=[pltpu.SemaphoreType.DMA((2 + CHUNKS,))],
        compiler_params=pltpu.CompilerParams(vmem_limit_bytes=1 << 20),
    )(after, diag, mats)


def slots_of(panel_dst, tiles):
    dom_size = lax.axis_size("dom")
    owner = lax.axis_index("dom")
    distance = (panel_dst // tiles - owner) % dom_size
    near = (distance + HALF) % dom_size - HALF
    onward = jnp.where(owner % 2 == 1, near, -near)
    group = jnp.where(
        distance == dom_size // 2,
        FAR,
        jnp.where(
            onward == 0,
            OWN,
            jnp.where(
                onward == 1, PASSED, jnp.where(onward == 2, DIRECT, jnp.where(onward == -1, SIBLING, HANDED))
            ),
        ),
    )
    return jnp.where(panel_dst >= 0, group * tiles + panel_dst % tiles, GROUPS * tiles)


def per_device(right_sides, diag_inverse, panel_mats, panel_src, panel_dst):
    levels, tiles, group, span = right_sides.shape
    rep_size = lax.axis_size("rep")
    rep = lax.axis_index("rep").astype(jnp.int32)
    cols = group * rep_size
    first = lax.broadcasted_iota(jnp.int32, (2, tiles, cols, span), 0) == 0
    ids = jnp.stack([panel_src, slots_of(panel_dst, tiles)])
    partial = right_sides[0].astype(jnp.bfloat16)
    place = lax.broadcasted_iota(jnp.int32, (levels, tiles, cols, span), 2) // group == rep
    own_rhs = jnp.where(place, jnp.concatenate([right_sides] * rep_size, 2), 0.0)
    diag_inverse, panel_mats = (
        pltpu.with_memory_space_constraint(x, pltpu.HBM) for x in (diag_inverse, panel_mats)
    )
    weights = fetch(partial, diag_inverse, panel_mats)
    store = []
    results = []
    for level in range(levels):
        last = level + 1 == levels
        parts = [partial] + [along_rep(partial, by) for by in BACK]
        ahead = [] if last else [diag_inverse] if level + 2 == levels else [diag_inverse, panel_mats]
        if last:
            return run_level(
                level, last, rep[None], None, parts, weights, results, ahead, right_sides.shape
            )
        solved, stored, own, sibling, far, chip, *weights = run_level(
            level, last, rep[None], ids, parts, weights, store, ahead, right_sides.shape
        )
        results.append(solved)
        store.append(stored)
        from_sibling = to_sibling(sibling)
        handed = jnp.where(first, from_sibling[:2].astype(jnp.float32), 0.0)
        from_far = to_far(jnp.where(first, far, from_sibling[1:]))
        from_chip = to_next_chip((chip.astype(jnp.float32) + handed).astype(jnp.bfloat16))
        across = to_sibling(
            (from_chip[0].astype(jnp.float32) + from_far[1].astype(jnp.float32)).astype(jnp.bfloat16)
        )
        incoming = sum(
            piece.astype(jnp.float32) for piece in (own, from_sibling[1], from_chip[1], from_far[0], across)
        )
        partial = (own_rhs[level + 1] - incoming).astype(jnp.bfloat16)


def solution(mesh):
    return jax.shard_map(
        per_device,
        mesh=mesh,
        in_specs=(
            P(None, "dom", "rep", None),
            P(None, "dom", None, None),
            P(None, ("dom", "rep"), None, None),
            P(None, ("dom", "rep")),
            P(None, ("dom", "rep")),
        ),
        out_specs=P(None, "dom", "rep", None),
        check_vma=False,
    )
```

time: 85.3 us -> 92.4 us (1.083)
  starting transfers between devices: 35 us -> 42.2 us
    ppermute x12, waiting for transfers between devices: 20.4 us -> 12.7 us  [dom_permute(): lax.ppermute(value, 'dom', [(i, target(i) % size) for i in range(size) if...]
    ppermute x12, starting transfers between devices: 16.5 us -> 24.2 us  [dom_permute(): lax.ppermute(value, 'dom', [(i, target(i) % size) for i in range(size) if...]
    ppermute x12, waiting for transfers between devices: 9.11 us -> 16 us  [along_rep(): lax.ppermute(value, 'rep', [(i, (i + by) % size) for i in range(size)])]
    pallas_call x7 -> x5, Pallas kernels: 17.5 us -> 16.8 us  [the longest x4 13.8 us: run_level(): pl.pallas_call(functools.partial(level_body, level, last, len(ahead)), ou...]
  transfers between devices with their start and end apart: 24 -> 24, of which waited for: 14 -> 15; matrix products, arithmetic and copies ran while one was open for 2% -> 2% of each run, Pallas kernels for 9% -> 3%
where the time goes in v3:
time: 92.4 us; the launch traced here: 91.1 us
  starting transfers between devices  42.2 us (46%)
  waiting for transfers between devices  28.6 us (31%)
  Pallas kernels  16.8 us (18%)
  other arithmetic  2.5 us (3%)
    ppermute x12, starting transfers between devices, dom_permute(): lax.ppermute(value, 'dom', [(i, target(i) % size) for i in range(size) if...  24.2 us
    ppermute x12, starting transfers between devices, along_rep(): lax.ppermute(value, 'rep', [(i, (i + by) % size) for i in range(size)])  18.1 us
    ppermute x12, waiting for transfers between devices, along_rep(): lax.ppermute(value, 'rep', [(i, (i + by) % size) for i in range(size)])  16 us
    pallas_call x4, Pallas kernels, run_level(): pl.pallas_call(functools.partial(level_body, level, last, len(ahead)), ou...  13.8 us
    ppermute x12, waiting for transfers between devices, dom_permute(): lax.ppermute(value, 'dom', [(i, target(i) % size) for i in range(size) if...  12.7 us
    pallas_call x1, Pallas kernels, fetch(): pl.pallas_call(fetch_body, out_shape=[pltpu.VMEM(w.shape[1:], w.dtype) fo...  2.92 us
  transfers between devices with their start and end apart: 24, of which 15 were waited for; matrix products, arithmetic and copies ran while one was open for 2% of the time, Pallas kernels for 3%

profile of v3, /device:TPU:0, one launch (start us, length us, event | category | flops | bytes accessed | tf_op | source)
XLA Modules:
  0.0 91.1 jit_solution(137083168515550797)
XLA Ops:
  0.0 0.8 fusion.12.refs_0_.refs_2_
  0.8 4.1 %collective-permute-start.2 = (bf16[6,4,384]{2,1,0:T(4,128)(2,1)S(1)}, bf16[6,4,384]{2,1,0:T(4,128)(2,1)S(1)}, u32[]{:S(2)}, u32[]{:S(2)}) collective-permute-start(bf16[6,4,384]{2,1,0:T(4,128)(2,1)S(1)} %fusion.12.refs_0_.refs_2_), channel_id=1, source_target_pairs={{0,3},{1,0},{2,1},{3,2},{4,7},{5,4},{6,5},{7,6},{8,11},{9,8},{10,9... | collective-permute-start | bytes 55304 | tf_op jit(solution)/shard_map/ppermute | solution.py:37
  4.9 0.0 collective-permute-start.1
  4.9 1.9 %collective-permute-start = (bf16[6,4,384]{2,1,0:T(4,128)(2,1)S(1)}, bf16[6,4,384]{2,1,0:T(4,128)(2,1)S(1)}, u32[]{:S(2)}, u32[]{:S(2)}) collective-permute-start(bf16[6,4,384]{2,1,0:T(4,128)(2,1)S(1)} %fusion.12.refs_0_.refs_2_), channel_id=1, source_target_pairs={{0,2},{1,3},{2,0},{3,1},{4,6},{5,7},{6,4},{7,5},{8,10},{9,11},{10,... | collective-permute-start | bytes 55304 | tf_op jit(solution)/shard_map/ppermute | solution.py:37
  6.8 0.7 fusion.18
  7.5 0.7 pad_add_fusion.refs_1_
  8.2 2.9 %shard_map.55 = (bf16[6,384,384]{2,1,0:T(8,128)(2,1)S(1)}, bf16[16,384,384]{2,1,0:T(8,128)(2,1)S(1)}) custom-call(bf16[6,4,384]{2,1,0:T(4,128)(2,1)S(1)} %fusion.12.refs_0_.refs_2_, bf16[4,6,384,384]{3,2,1,0:T(8,128)(2,1)} %refs_10_.3, bf16[3,16,384,384]{3,2,1,0:T(8,128)(2,1)} %refs_10_.2), custom_call_target="tpu_custom_call" | custom-call | tf_op jit(solution)/shard_map/pallas_call | solution.py:184
  11.1 0.0 collective-permute-done.2.refs_5_
  11.1 0.0 collective-permute-done.1.refs_4_
  11.1 0.0 collective-permute-done.refs_3_
  11.1 0.0 copy-start
  11.1 4.6 %shard_map.56 = (f32[6,4,384]{2,1,0:T(4,128)S(1)}, bf16[6,16,384]{2,1,0:T(8,128)(2,1)S(1)}, bf16[6,16,384]{2,1,0:T(8,128)(2,1)S(1)}, bf16[3,6,16,384]{3,2,1,0:T(...) custom-call(s32[1]{0:T(128)} %bitcast.refs_0_, ...), custom_call_target="tpu_custom_call" | custom-call | tf_op jit(solution)/shard_map/pallas_call | solution.py:162
  15.8 0.1 collective-permute-start.3
  15.9 1.5 %collective-permute-done.3 = bf16[3,6,16,384]{3,2,1,0:T(8,128)(2,1)S(1)} collective-permute-done((bf16[3,6,16,384]{3,2,1,0:T(8,128)(2,1)S(1)}, bf16[3,6,16,384]{3,2,1,0:T(8,128)(2,1)S(1)}, u32[]{:S(2)}, u32[]{:S(2)}) %collective-permute-start.3) | collective-permute-done | bytes 221216 | tf_op jit(solution)/shard_map/ppermute | solution.py:19
  17.3 0.1 add_convert_fusion.2
  17.5 5.3 %collective-permute-start.4 = (bf16[2,6,16,384]{3,2,1,0:T(8,128)(2,1)S(1)}, bf16[2,6,16,384]{3,2,1,0:T(8,128)(2,1)S(1)}, u32[]{:S(2)}, u32[]{:S(2)}) collective-permute-start(bf16[2,6,16,384]{3,2,1,0:T(8,128)(2,1)S(1)} %add_convert_fusion.2), channel_id=1, source_target_pairs={{0,120},{4,12},{8,0},{12,20},{16,8},{20,28},{24,16},{28,36},{32,24... | collective-permute-start | bytes 442376 | tf_op jit(solution)/shard_map/ppermute | solution.py:19
  22.7 0.1 slice_select_fusion.2
  22.8 0.7 collective-permute-start.5
  23.5 1.9 %collective-permute-done.4 = bf16[2,6,16,384]{3,2,1,0:T(8,128)(2,1)S(1)} collective-permute-done((bf16[2,6,16,384]{3,2,1,0:T(8,128)(2,1)S(1)}, bf16[2,6,16,384]{3,2,1,0:T(8,128)(2,1)S(1)}, u32[]{:S(2)}, u32[]{:S(2)}) %collective-permute-start.4) | collective-permute-done | bytes 147488 | tf_op jit(solution)/shard_map/ppermute | solution.py:19
  25.4 2.5 %collective-permute-start.6 = (bf16[6,16,384]{2,1,0:T(8,128)(2,1)S(1)}, bf16[6,16,384]{2,1,0:T(8,128)(2,1)S(1)}, u32[]{:S(2)}, u32[]{:S(2)}) collective-permute-start(bf16[6,16,384]{2,1,0:T(8,128)(2,1)S(1)} %fusion.9), channel_id=1, source_target_pairs={{0,4},{4,0},{8,12},{12,8},{16,20},{20,16},{24,28},{28,24},{32,36},... | collective-permute-start | bytes 221192 | tf_op jit(solution)/shard_map/ppermute | solution.py:19
  27.9 0.1 maximum_select_fusion
  28.1 0.8 collective-permute-done.6
  28.8 0.1 fusion.1.refs_2_
  28.9 2.3 %collective-permute-start.9 = (bf16[6,16,384]{2,1,0:T(8,128)(2,1)S(1)}, bf16[6,16,384]{2,1,0:T(8,128)(2,1)S(1)}, u32[]{:S(2)}, u32[]{:S(2)}) collective-permute-start(bf16[6,16,384]{2,1,0:T(8,128)(2,1)S(1)} %fusion.1.refs_2_), channel_id=1, source_target_pairs={{0,3},{1,0},{2,1},{3,2},{4,7},{5,4},{6,5},{7,6},{8,11},{9,8},{10,9... | collective-permute-start | bytes 221192 | tf_op jit(solution)/shard_map/ppermute | solution.py:37
  31.2 0.1 collective-permute-start.8
  31.3 2.0 %collective-permute-start.7 = (bf16[6,16,384]{2,1,0:T(8,128)(2,1)S(1)}, bf16[6,16,384]{2,1,0:T(8,128)(2,1)S(1)}, u32[]{:S(2)}, u32[]{:S(2)}) collective-permute-start(bf16[6,16,384]{2,1,0:T(8,128)(2,1)S(1)} %fusion.1.refs_2_), channel_id=1, source_target_pairs={{0,2},{1,3},{2,0},{3,1},{4,6},{5,7},{6,4},{7,5},{8,10},{9,11},{10,... | collective-permute-start | bytes 221192 | tf_op jit(solution)/shard_map/ppermute | solution.py:37
  33.3 0.7 collective-permute-done.9.refs_5_
  34.0 4.3 %collective-permute-done.8.refs_4_ = bf16[6,16,384]{2,1,0:T(8,128)(2,1)S(1)} collective-permute-done((bf16[6,16,384]{2,1,0:T(8,128)(2,1)S(1)}, bf16[6,16,384]{2,1,0:T(8,128)(2,1)S(1)}, u32[]{:S(2)}, u32[]{:S(2)}) %collective-permute-start.8) | collective-permute-done | bytes 73760 | tf_op jit(solution)/shard_map/ppermute | solution.py:37
  38.2 4.6 %shard_map.57 = (f32[6,4,384]{2,1,0:T(4,128)S(1)}, bf16[6,16,384]{2,1,0:T(8,128)(2,1)S(1)}, bf16[6,16,384]{2,1,0:T(8,128)(2,1)S(1)}, bf16[3,6,16,384]{3,2,1,0:T(...) custom-call(s32[1]{0:T(128)} %bitcast.refs_0_, ...), custom_call_target="tpu_custom_call" | custom-call | tf_op jit(solution)/shard_map/pallas_call | solution.py:162
  42.8 0.1 collective-permute-start.10
  42.9 1.5 %collective-permute-done.10 = bf16[3,6,16,384]{3,2,1,0:T(8,128)(2,1)S(1)} collective-permute-done((bf16[3,6,16,384]{3,2,1,0:T(8,128)(2,1)S(1)}, bf16[3,6,16,384]{3,2,1,0:T(8,128)(2,1)S(1)}, u32[]{:S(2)}, u32[]{:S(2)}) %collective-permute-start.10) | collective-permute-done | bytes 221216 | tf_op jit(solution)/shard_map/ppermute | solution.py:19
  44.4 0.1 add_convert_fusion.1
  44.5 5.2 %collective-permute-start.11 = (bf16[2,6,16,384]{3,2,1,0:T(8,128)(2,1)S(1)}, bf16[2,6,16,384]{3,2,1,0:T(8,128)(2,1)S(1)}, u32[]{:S(2)}, u32[]{:S(2)}) collective-permute-start(bf16[2,6,16,384]{3,2,1,0:T(8,128)(2,1)S(1)} %add_convert_fusion.1), channel_id=1, source_target_pairs={{0,120},{4,12},{8,0},{12,20},{16,8},{20,28},{24,16},{28,36},{32,24... | collective-permute-start | bytes 442376 | tf_op jit(solution)/shard_map/ppermute | solution.py:19
  49.7 0.1 slice_select_fusion.1
  49.8 0.7 collective-permute-start.12
  50.5 1.9 %collective-permute-done.11 = bf16[2,6,16,384]{3,2,1,0:T(8,128)(2,1)S(1)} collective-permute-done((bf16[2,6,16,384]{3,2,1,0:T(8,128)(2,1)S(1)}, bf16[2,6,16,384]{3,2,1,0:T(8,128)(2,1)S(1)}, u32[]{:S(2)}, u32[]{:S(2)}) %collective-permute-start.11) | collective-permute-done | bytes 147488 | tf_op jit(solution)/shard_map/ppermute | solution.py:19
  52.4 0.0 collective-permute-done.12
  52.4 1.4 %collective-permute-start.13 = (bf16[6,16,384]{2,1,0:T(8,128)(2,1)S(1)}, bf16[6,16,384]{2,1,0:T(8,128)(2,1)S(1)}, u32[]{:S(2)}, u32[]{:S(2)}) collective-permute-start(bf16[6,16,384]{2,1,0:T(8,128)(2,1)S(1)} %fusion.10), channel_id=1, source_target_pairs={{0,4},{4,0},{8,12},{12,8},{16,20},{20,16},{24,28},{28,24},{32,36},... | collective-permute-start | bytes 221192 | tf_op jit(solution)/shard_map/ppermute | solution.py:19
  53.8 0.9 %collective-permute-done.13 = bf16[6,16,384]{2,1,0:T(8,128)(2,1)S(1)} collective-permute-done((bf16[6,16,384]{2,1,0:T(8,128)(2,1)S(1)}, bf16[6,16,384]{2,1,0:T(8,128)(2,1)S(1)}, u32[]{:S(2)}, u32[]{:S(2)}) %collective-permute-start.13) | collective-permute-done | bytes 73760 | tf_op jit(solution)/shard_map/ppermute | solution.py:19
  54.7 0.1 fusion.3.refs_2_
  54.8 2.3 %collective-permute-start.16 = (bf16[6,16,384]{2,1,0:T(8,128)(2,1)S(1)}, bf16[6,16,384]{2,1,0:T(8,128)(2,1)S(1)}, u32[]{:S(2)}, u32[]{:S(2)}) collective-permute-start(bf16[6,16,384]{2,1,0:T(8,128)(2,1)S(1)} %fusion.3.refs_2_), channel_id=1, source_target_pairs={{0,3},{1,0},{2,1},{3,2},{4,7},{5,4},{6,5},{7,6},{8,11},{9,8},{10,9... | collective-permute-start | bytes 221192 | tf_op jit(solution)/shard_map/ppermute | solution.py:37
  57.1 1.5 %collective-permute-start.14 = (bf16[6,16,384]{2,1,0:T(8,128)(2,1)S(1)}, bf16[6,16,384]{2,1,0:T(8,128)(2,1)S(1)}, u32[]{:S(2)}, u32[]{:S(2)}) collective-permute-start(bf16[6,16,384]{2,1,0:T(8,128)(2,1)S(1)} %fusion.3.refs_2_), channel_id=1, source_target_pairs={{0,2},{1,3},{2,0},{3,1},{4,6},{5,7},{6,4},{7,5},{8,10},{9,11},{10,... | collective-permute-start | bytes 221192 | tf_op jit(solution)/shard_map/ppermute | solution.py:37
  58.6 0.7 collective-permute-done.16.refs_5_
  59.4 4.8 %collective-permute-done.15.refs_4_ = bf16[6,16,384]{2,1,0:T(8,128)(2,1)S(1)} collective-permute-done((bf16[6,16,384]{2,1,0:T(8,128)(2,1)S(1)}, bf16[6,16,384]{2,1,0:T(8,128)(2,1)S(1)}, u32[]{:S(2)}, u32[]{:S(2)}) %collective-permute-start.15) | collective-permute-done | bytes 73760 | tf_op jit(solution)/shard_map/ppermute | solution.py:37
  64.1 0.0 collective-permute-done.14.refs_3_
  64.1 3.6 %shard_map.58 = (f32[6,4,384]{2,1,0:T(4,128)S(1)}, bf16[6,16,384]{2,1,0:T(8,128)(2,1)}, bf16[6,16,384]{2,1,0:T(8,128)(2,1)S(1)}, bf16[3,6,16,384]{3,2,1,0:T(8,12...) custom-call(s32[1]{0:T(128)} %bitcast.refs_0_, ...), custom_call_target="tpu_custom_call" | custom-call | tf_op jit(solution)/shard_map/pallas_call | solution.py:162
  67.7 0.1 collective-permute-start.17
  67.8 1.5 %collective-permute-done.17 = bf16[3,6,16,384]{3,2,1,0:T(8,128)(2,1)S(1)} collective-permute-done((bf16[3,6,16,384]{3,2,1,0:T(8,128)(2,1)S(1)}, bf16[3,6,16,384]{3,2,1,0:T(8,128)(2,1)S(1)}, u32[]{:S(2)}, u32[]{:S(2)}) %collective-permute-start.17) | collective-permute-done | bytes 221216 | tf_op jit(solution)/shard_map/ppermute | solution.py:19
  69.3 0.1 add_convert_fusion
  69.4 6.3 %collective-permute-start.18 = (bf16[2,6,16,384]{3,2,1,0:T(8,128)(2,1)S(1)}, bf16[2,6,16,384]{3,2,1,0:T(8,128)(2,1)S(1)}, u32[]{:S(2)}, u32[]{:S(2)}) collective-permute-start(bf16[2,6,16,384]{3,2,1,0:T(8,128)(2,1)S(1)} %add_convert_fusion), channel_id=1, source_target_pairs={{0,120},{4,12},{8,0},{12,20},{16,8},{20,28},{24,16},{28,36},{32,24... | collective-permute-start | bytes 442376 | tf_op jit(solution)/shard_map/ppermute | solution.py:19
  75.7 0.1 slice_select_fusion
  75.8 0.7 collective-permute-start.19
  76.5 1.9 %collective-permute-done.18 = bf16[2,6,16,384]{3,2,1,0:T(8,128)(2,1)S(1)} collective-permute-done((bf16[2,6,16,384]{3,2,1,0:T(8,128)(2,1)S(1)}, bf16[2,6,16,384]{3,2,1,0:T(8,128)(2,1)S(1)}, u32[]{:S(2)}, u32[]{:S(2)}) %collective-permute-start.18) | collective-permute-done | bytes 147488 | tf_op jit(solution)/shard_map/ppermute | solution.py:19
  78.4 0.0 collective-permute-done.19
  78.4 1.3 %collective-permute-start.20 = (bf16[6,16,384]{2,1,0:T(8,128)(2,1)S(1)}, bf16[6,16,384]{2,1,0:T(8,128)(2,1)S(1)}, u32[]{:S(2)}, u32[]{:S(2)}) collective-permute-start(bf16[6,16,384]{2,1,0:T(8,128)(2,1)S(1)} %fusion.11), channel_id=1, source_target_pairs={{0,4},{4,0},{8,12},{12,8},{16,20},{20,16},{24,28},{28,24},{32,36},... | collective-permute-start | bytes 221192 | tf_op jit(solution)/shard_map/ppermute | solution.py:19
  79.7 0.9 %collective-permute-done.20 = bf16[6,16,384]{2,1,0:T(8,128)(2,1)S(1)} collective-permute-done((bf16[6,16,384]{2,1,0:T(8,128)(2,1)S(1)}, bf16[6,16,384]{2,1,0:T(8,128)(2,1)S(1)}, u32[]{:S(2)}, u32[]{:S(2)}) %collective-permute-start.20) | collective-permute-done | bytes 73760 | tf_op jit(solution)/shard_map/ppermute | solution.py:19
  80.6 0.1 fusion.5.refs_1_
  80.7 2.3 %collective-permute-start.23 = (bf16[6,16,384]{2,1,0:T(8,128)(2,1)S(1)}, bf16[6,16,384]{2,1,0:T(8,128)(2,1)S(1)}, u32[]{:S(2)}, u32[]{:S(2)}) collective-permute-start(bf16[6,16,384]{2,1,0:T(8,128)(2,1)S(1)} %fusion.5.refs_1_), channel_id=1, source_target_pairs={{0,3},{1,0},{2,1},{3,2},{4,7},{5,4},{6,5},{7,6},{8,11},{9,8},{10,9... | collective-permute-start | bytes 221192 | tf_op jit(solution)/shard_map/ppermute | solution.py:37
  83.0 0.0 collective-permute-start.22
  83.0 1.5 %collective-permute-start.21 = (bf16[6,16,384]{2,1,0:T(8,128)(2,1)S(1)}, bf16[6,16,384]{2,1,0:T(8,128)(2,1)S(1)}, u32[]{:S(2)}, u32[]{:S(2)}) collective-permute-start(bf16[6,16,384]{2,1,0:T(8,128)(2,1)S(1)} %fusion.5.refs_1_), channel_id=1, source_target_pairs={{0,2},{1,3},{2,0},{3,1},{4,6},{5,7},{6,4},{7,5},{8,10},{9,11},{10,... | collective-permute-start | bytes 221192 | tf_op jit(solution)/shard_map/ppermute | solution.py:37
  84.5 0.7 collective-permute-done.23.refs_4_
  85.3 4.8 %collective-permute-done.22.refs_3_ = bf16[6,16,384]{2,1,0:T(8,128)(2,1)S(1)} collective-permute-done((bf16[6,16,384]{2,1,0:T(8,128)(2,1)S(1)}, bf16[6,16,384]{2,1,0:T(8,128)(2,1)S(1)}, u32[]{:S(2)}, u32[]{:S(2)}) %collective-permute-start.22) | collective-permute-done | bytes 73760 | tf_op jit(solution)/shard_map/ppermute | solution.py:37
  90.0 0.0 collective-permute-done.21.refs_2_
  90.0 1.1 %shard_map.59 = f32[4,6,4,384]{3,2,1,0:T(4,128)} custom-call(s32[1]{0:T(128)} %bitcast.refs_0_, bf16[6,16,384]{2,1,0:T(8,128)(2,1)S(1)} %fusion.5.refs_1_, bf16[6,16,384]{2,1,0:T(8,128)(2,1)S(1)} %collective-permute-done.21.refs_2_, bf16[6,16,384]{2,1,0:T(8,128)(2,1)S(1)} %collective-permute-done.22.refs_3_, ...), custom_call_target="tpu_custom_call" | custom-call | tf_op jit(solution)/shard_map/pallas_call | solution.py:162
  (10 shorter events, 0.1 us)
Async XLA Ops:
  0.8 10.3 %collective-permute-start.2 = (bf16[6,4,384]{2,1,0:T(4,128)(2,1)S(1)}, bf16[6,4,384]{2,1,0:T(4,128)(2,1)S(1)}, u32[]{:S(2)}, u32[]{:S(2)}) collective-permute-start(bf16[6,4,384]{2,1,0:T(4,128)(2,1)S(1)} %fusion.12.refs_0_.refs_2_), channel_id=1, source_target_pairs={{0,3},{1,0},{2,1},{3,2},{4,7},{5,4},{6,5},{7,6},{8,11},{9,8},{10,9... | collective-permute-start | bytes 55304 | tf_op jit(solution)/shard_map/ppermute | solution.py:37
  4.9 6.2 %collective-permute-start.1 = (bf16[6,4,384]{2,1,0:T(4,128)(2,1)S(1)}, bf16[6,4,384]{2,1,0:T(4,128)(2,1)S(1)}, u32[]{:S(2)}, u32[]{:S(2)}) collective-permute-start(bf16[6,4,384]{2,1,0:T(4,128)(2,1)S(1)} %fusion.12.refs_0_.refs_2_), channel_id=1, source_target_pairs={{0,1},{1,2},{2,3},{3,0},{4,5},{5,6},{6,7},{7,4},{8,9},{9,10},{10,1... | collective-permute-start | bytes 55304 | tf_op jit(solution)/shard_map/ppermute | solution.py:37
  4.9 6.2 %collective-permute-start = (bf16[6,4,384]{2,1,0:T(4,128)(2,1)S(1)}, bf16[6,4,384]{2,1,0:T(4,128)(2,1)S(1)}, u32[]{:S(2)}, u32[]{:S(2)}) collective-permute-start(bf16[6,4,384]{2,1,0:T(4,128)(2,1)S(1)} %fusion.12.refs_0_.refs_2_), channel_id=1, source_target_pairs={{0,2},{1,3},{2,0},{3,1},{4,6},{5,7},{6,4},{7,5},{8,10},{9,11},{10,... | collective-permute-start | bytes 55304 | tf_op jit(solution)/shard_map/ppermute | solution.py:37
  11.1 16.8 %copy-start = (f32[4,6,4,384]{3,2,1,0:T(4,128)S(1)}, f32[4,6,4,384]{3,2,1,0:T(4,128)}, u32[]{:S(2)}) copy-start(f32[4,6,4,384]{3,2,1,0:T(4,128)} %param.5) | copy-start | bytes 442372
  15.8 1.6 %collective-permute-start.3 = (bf16[3,6,16,384]{3,2,1,0:T(8,128)(2,1)S(1)}, bf16[3,6,16,384]{3,2,1,0:T(8,128)(2,1)S(1)}, u32[]{:S(2)}, u32[]{:S(2)}) collective-permute-start(bf16[3,6,16,384]{3,2,1,0:T(8,128)(2,1)S(1)} %get-tuple-element.32), channel_id=1, source_target_pairs={{0,4},{4,0},{8,12},{12,8},{16,20},{20,16},{24,28},{28,24},{32,36},... | collective-permute-start | bytes 663560 | tf_op jit(solution)/shard_map/ppermute | solution.py:19
  17.5 8.0 %collective-permute-start.4 = (bf16[2,6,16,384]{3,2,1,0:T(8,128)(2,1)S(1)}, bf16[2,6,16,384]{3,2,1,0:T(8,128)(2,1)S(1)}, u32[]{:S(2)}, u32[]{:S(2)}) collective-permute-start(bf16[2,6,16,384]{3,2,1,0:T(8,128)(2,1)S(1)} %add_convert_fusion.2), channel_id=1, source_target_pairs={{0,120},{4,12},{8,0},{12,20},{16,8},{20,28},{24,16},{28,36},{32,24... | collective-permute-start | bytes 442376 | tf_op jit(solution)/shard_map/ppermute | solution.py:19
  22.8 2.6 %collective-permute-start.5 = (bf16[2,6,16,384]{3,2,1,0:T(8,128)(2,1)S(1)}, bf16[2,6,16,384]{3,2,1,0:T(8,128)(2,1)S(1)}, u32[]{:S(2)}, u32[]{:S(2)}) collective-permute-start(bf16[2,6,16,384]{3,2,1,0:T(8,128)(2,1)S(1)} %slice_select_fusion.2), channel_id=1, source_target_pairs={{4,68},{12,76},{16,80},{24,88},{36,100},{44,108},{48,112},{56,120}... | collective-permute-start | bytes 442376 | tf_op jit(solution)/shard_map/ppermute | solution.py:19
  25.4 3.4 %collective-permute-start.6 = (bf16[6,16,384]{2,1,0:T(8,128)(2,1)S(1)}, bf16[6,16,384]{2,1,0:T(8,128)(2,1)S(1)}, u32[]{:S(2)}, u32[]{:S(2)}) collective-permute-start(bf16[6,16,384]{2,1,0:T(8,128)(2,1)S(1)} %fusion.9), channel_id=1, source_target_pairs={{0,4},{4,0},{8,12},{12,8},{16,20},{20,16},{24,28},{28,24},{32,36},... | collective-permute-start | bytes 221192 | tf_op jit(solution)/shard_map/ppermute | solution.py:19
  28.9 5.1 %collective-permute-start.9 = (bf16[6,16,384]{2,1,0:T(8,128)(2,1)S(1)}, bf16[6,16,384]{2,1,0:T(8,128)(2,1)S(1)}, u32[]{:S(2)}, u32[]{:S(2)}) collective-permute-start(bf16[6,16,384]{2,1,0:T(8,128)(2,1)S(1)} %fusion.1.refs_2_), channel_id=1, source_target_pairs={{0,3},{1,0},{2,1},{3,2},{4,7},{5,4},{6,5},{7,6},{8,11},{9,8},{10,9... | collective-permute-start | bytes 221192 | tf_op jit(solution)/shard_map/ppermute | solution.py:37
  31.2 7.0 %collective-permute-start.8 = (bf16[6,16,384]{2,1,0:T(8,128)(2,1)S(1)}, bf16[6,16,384]{2,1,0:T(8,128)(2,1)S(1)}, u32[]{:S(2)}, u32[]{:S(2)}) collective-permute-start(bf16[6,16,384]{2,1,0:T(8,128)(2,1)S(1)} %fusion.1.refs_2_), channel_id=1, source_target_pairs={{0,1},{1,2},{2,3},{3,0},{4,5},{5,6},{6,7},{7,4},{8,9},{9,10},{10,1... | collective-permute-start | bytes 221192 | tf_op jit(solution)/shard_map/ppermute | solution.py:37
  31.3 7.0 %collective-permute-start.7 = (bf16[6,16,384]{2,1,0:T(8,128)(2,1)S(1)}, bf16[6,16,384]{2,1,0:T(8,128)(2,1)S(1)}, u32[]{:S(2)}, u32[]{:S(2)}) collective-permute-start(bf16[6,16,384]{2,1,0:T(8,128)(2,1)S(1)} %fusion.1.refs_2_), channel_id=1, source_target_pairs={{0,2},{1,3},{2,0},{3,1},{4,6},{5,7},{6,4},{7,5},{8,10},{9,11},{10,... | collective-permute-start | bytes 221192 | tf_op jit(solution)/shard_map/ppermute | solution.py:37
  42.8 1.6 %collective-permute-start.10 = (bf16[3,6,16,384]{3,2,1,0:T(8,128)(2,1)S(1)}, bf16[3,6,16,384]{3,2,1,0:T(8,128)(2,1)S(1)}, u32[]{:S(2)}, u32[]{:S(2)}) collective-permute-start(bf16[3,6,16,384]{3,2,1,0:T(8,128)(2,1)S(1)} %get-tuple-element.39), channel_id=1, source_target_pairs={{0,4},{4,0},{8,12},{12,8},{16,20},{20,16},{24,28},{28,24},{32,36},... | collective-permute-start | bytes 663560 | tf_op jit(solution)/shard_map/ppermute | solution.py:19
  44.5 7.9 %collective-permute-start.11 = (bf16[2,6,16,384]{3,2,1,0:T(8,128)(2,1)S(1)}, bf16[2,6,16,384]{3,2,1,0:T(8,128)(2,1)S(1)}, u32[]{:S(2)}, u32[]{:S(2)}) collective-permute-start(bf16[2,6,16,384]{3,2,1,0:T(8,128)(2,1)S(1)} %add_convert_fusion.1), channel_id=1, source_target_pairs={{0,120},{4,12},{8,0},{12,20},{16,8},{20,28},{24,16},{28,36},{32,24... | collective-permute-start | bytes 442376 | tf_op jit(solution)/shard_map/ppermute | solution.py:19
  49.8 2.6 %collective-permute-start.12 = (bf16[2,6,16,384]{3,2,1,0:T(8,128)(2,1)S(1)}, bf16[2,6,16,384]{3,2,1,0:T(8,128)(2,1)S(1)}, u32[]{:S(2)}, u32[]{:S(2)}) collective-permute-start(bf16[2,6,16,384]{3,2,1,0:T(8,128)(2,1)S(1)} %slice_select_fusion.1), channel_id=1, source_target_pairs={{4,68},{12,76},{16,80},{24,88},{36,100},{44,108},{48,112},{56,120}... | collective-permute-start | bytes 442376 | tf_op jit(solution)/shard_map/ppermute | solution.py:19
  52.4 2.3 %collective-permute-start.13 = (bf16[6,16,384]{2,1,0:T(8,128)(2,1)S(1)}, bf16[6,16,384]{2,1,0:T(8,128)(2,1)S(1)}, u32[]{:S(2)}, u32[]{:S(2)}) collective-permute-start(bf16[6,16,384]{2,1,0:T(8,128)(2,1)S(1)} %fusion.10), channel_id=1, source_target_pairs={{0,4},{4,0},{8,12},{12,8},{16,20},{20,16},{24,28},{28,24},{32,36},... | collective-permute-start | bytes 221192 | tf_op jit(solution)/shard_map/ppermute | solution.py:19
  54.8 4.6 %collective-permute-start.16 = (bf16[6,16,384]{2,1,0:T(8,128)(2,1)S(1)}, bf16[6,16,384]{2,1,0:T(8,128)(2,1)S(1)}, u32[]{:S(2)}, u32[]{:S(2)}) collective-permute-start(bf16[6,16,384]{2,1,0:T(8,128)(2,1)S(1)} %fusion.3.refs_2_), channel_id=1, source_target_pairs={{0,3},{1,0},{2,1},{3,2},{4,7},{5,4},{6,5},{7,6},{8,11},{9,8},{10,9... | collective-permute-start | bytes 221192 | tf_op jit(solution)/shard_map/ppermute | solution.py:37
  57.1 7.0 %collective-permute-start.15 = (bf16[6,16,384]{2,1,0:T(8,128)(2,1)S(1)}, bf16[6,16,384]{2,1,0:T(8,128)(2,1)S(1)}, u32[]{:S(2)}, u32[]{:S(2)}) collective-permute-start(bf16[6,16,384]{2,1,0:T(8,128)(2,1)S(1)} %fusion.3.refs_2_), channel_id=1, source_target_pairs={{0,1},{1,2},{2,3},{3,0},{4,5},{5,6},{6,7},{7,4},{8,9},{9,10},{10,1... | collective-permute-start | bytes 221192 | tf_op jit(solution)/shard_map/ppermute | solution.py:37
  57.1 7.0 %collective-permute-start.14 = (bf16[6,16,384]{2,1,0:T(8,128)(2,1)S(1)}, bf16[6,16,384]{2,1,0:T(8,128)(2,1)S(1)}, u32[]{:S(2)}, u32[]{:S(2)}) collective-permute-start(bf16[6,16,384]{2,1,0:T(8,128)(2,1)S(1)} %fusion.3.refs_2_), channel_id=1, source_target_pairs={{0,2},{1,3},{2,0},{3,1},{4,6},{5,7},{6,4},{7,5},{8,10},{9,11},{10,... | collective-permute-start | bytes 221192 | tf_op jit(solution)/shard_map/ppermute | solution.py:37
  67.7 1.6 %collective-permute-start.17 = (bf16[3,6,16,384]{3,2,1,0:T(8,128)(2,1)S(1)}, bf16[3,6,16,384]{3,2,1,0:T(8,128)(2,1)S(1)}, u32[]{:S(2)}, u32[]{:S(2)}) collective-permute-start(bf16[3,6,16,384]{3,2,1,0:T(8,128)(2,1)S(1)} %get-tuple-element.46), channel_id=1, source_target_pairs={{0,4},{4,0},{8,12},{12,8},{16,20},{20,16},{24,28},{28,24},{32,36},... | collective-permute-start | bytes 663560 | tf_op jit(solution)/shard_map/ppermute | solution.py:19
  69.4 9.0 %collective-permute-start.18 = (bf16[2,6,16,384]{3,2,1,0:T(8,128)(2,1)S(1)}, bf16[2,6,16,384]{3,2,1,0:T(8,128)(2,1)S(1)}, u32[]{:S(2)}, u32[]{:S(2)}) collective-permute-start(bf16[2,6,16,384]{3,2,1,0:T(8,128)(2,1)S(1)} %add_convert_fusion), channel_id=1, source_target_pairs={{0,120},{4,12},{8,0},{12,20},{16,8},{20,28},{24,16},{28,36},{32,24... | collective-permute-start | bytes 442376 | tf_op jit(solution)/shard_map/ppermute | solution.py:19
  75.8 2.6 %collective-permute-start.19 = (bf16[2,6,16,384]{3,2,1,0:T(8,128)(2,1)S(1)}, bf16[2,6,16,384]{3,2,1,0:T(8,128)(2,1)S(1)}, u32[]{:S(2)}, u32[]{:S(2)}) collective-permute-start(bf16[2,6,16,384]{3,2,1,0:T(8,128)(2,1)S(1)} %slice_select_fusion), channel_id=1, source_target_pairs={{4,68},{12,76},{16,80},{24,88},{36,100},{44,108},{48,112},{56,120}... | collective-permute-start | bytes 442376 | tf_op jit(solution)/shard_map/ppermute | solution.py:19
  78.4 2.2 %collective-permute-start.20 = (bf16[6,16,384]{2,1,0:T(8,128)(2,1)S(1)}, bf16[6,16,384]{2,1,0:T(8,128)(2,1)S(1)}, u32[]{:S(2)}, u32[]{:S(2)}) collective-permute-start(bf16[6,16,384]{2,1,0:T(8,128)(2,1)S(1)} %fusion.11), channel_id=1, source_target_pairs={{0,4},{4,0},{8,12},{12,8},{16,20},{20,16},{24,28},{28,24},{32,36},... | collective-permute-start | bytes 221192 | tf_op jit(solution)/shard_map/ppermute | solution.py:19
  80.7 4.6 %collective-permute-start.23 = (bf16[6,16,384]{2,1,0:T(8,128)(2,1)S(1)}, bf16[6,16,384]{2,1,0:T(8,128)(2,1)S(1)}, u32[]{:S(2)}, u32[]{:S(2)}) collective-permute-start(bf16[6,16,384]{2,1,0:T(8,128)(2,1)S(1)} %fusion.5.refs_1_), channel_id=1, source_target_pairs={{0,3},{1,0},{2,1},{3,2},{4,7},{5,4},{6,5},{7,6},{8,11},{9,8},{10,9... | collective-permute-start | bytes 221192 | tf_op jit(solution)/shard_map/ppermute | solution.py:37
  83.0 7.0 %collective-permute-start.22 = (bf16[6,16,384]{2,1,0:T(8,128)(2,1)S(1)}, bf16[6,16,384]{2,1,0:T(8,128)(2,1)S(1)}, u32[]{:S(2)}, u32[]{:S(2)}) collective-permute-start(bf16[6,16,384]{2,1,0:T(8,128)(2,1)S(1)} %fusion.5.refs_1_), channel_id=1, source_target_pairs={{0,1},{1,2},{2,3},{3,0},{4,5},{5,6},{6,7},{7,4},{8,9},{9,10},{10,1... | collective-permute-start | bytes 221192 | tf_op jit(solution)/shard_map/ppermute | solution.py:37
  83.0 7.0 %collective-permute-start.21 = (bf16[6,16,384]{2,1,0:T(8,128)(2,1)S(1)}, bf16[6,16,384]{2,1,0:T(8,128)(2,1)S(1)}, u32[]{:S(2)}, u32[]{:S(2)}) collective-permute-start(bf16[6,16,384]{2,1,0:T(8,128)(2,1)S(1)} %fusion.5.refs_1_), channel_id=1, source_target_pairs={{0,2},{1,3},{2,0},{3,1},{4,6},{5,7},{6,4},{7,5},{8,10},{9,11},{10,... | collective-permute-start | bytes 221192 | tf_op jit(solution)/shard_map/ppermute | solution.py:37

commit v4 on v3

v4 whole, which is shorter than its diff:
```python
import functools

import jax
import jax.numpy as jnp
from jax import lax
from jax.experimental import pallas as pl
from jax.experimental.pallas import tpu as pltpu
from jax.sharding import PartitionSpec as P

HALF = 2
OWN, FAR, SIBLING, HANDED, PASSED, DIRECT = range(6)
GROUPS = 6
APART = (3, 2, 1)
CHUNKS = 4


def dom_permute(value, target):
    size = lax.axis_size("dom")
    return lax.ppermute(value, "dom", [(i, target(i) % size) for i in range(size)])


def to_sibling(value):
    return dom_permute(value, lambda i: i ^ 1)


def to_far(value):
    half = lax.axis_size("dom") // 2
    return dom_permute(value, lambda i: i + half)


def to_next_chip(value):
    return dom_permute(value, lambda i: i + 2 if i % 2 else i - 2)


def along_rep(value, apart):
    return lax.ppermute(value, "rep", [(i, i ^ apart) for i in range(lax.axis_size("rep"))])


def place_columns(parts, rep):
    size = len(parts)
    blocks = [part[...].astype(jnp.float32) for part in parts]
    placed = []
    for index in range(size):
        chosen = blocks[0]
        for block, apart in zip(blocks[1:], APART):
            chosen = jnp.where(rep == index ^ apart, block, chosen)
        placed.append(chosen)
    return placed


def level_body(level, last, *refs):
    refs = list(refs)
    take = lambda count: [refs.pop(0) for _ in range(count)]
    (rep_ref,) = take(1)
    (ids_ref,) = take(1) if not last else (None,)
    parts = take(4)
    (diag_ref,) = take(1)
    (mats_ref,) = take(1) if not last else (None,)
    prev = take(level)
    (out_ref,) = take(1)
    if not last:
        stored_ref, own_ref, sibling_ref, handed_ref, far_ref, chip_ref = take(6)
    (solved_scr,) = take(1)
    if not last:
        store_scr, acc_scr = take(2)
    tiles, cols, _ = solved_scr.shape
    group = cols // 4
    if level == 0:
        for index, block in enumerate(place_columns(parts, rep_ref[0])):
            solved_scr[:, index * group : (index + 1) * group, :] = block
        residuals = [solved_scr[t].astype(jnp.bfloat16) for t in range(tiles)]
    else:
        residuals = [
            sum(part[t].astype(jnp.float32) for part in parts).astype(jnp.bfloat16) for t in range(tiles)
        ]
    for t in range(tiles):
        solved = jnp.dot(residuals[t], diag_ref[level, t], preferred_element_type=jnp.float32)
        solved_scr[t] = solved
        if not last:
            stored_ref[t] = solved.astype(jnp.bfloat16)
            store_scr[level * tiles + t] = solved.astype(jnp.bfloat16)
    own = solved_scr[:, :group, :]
    for other in range(1, cols // group):
        own = jnp.where(rep_ref[0] == other, solved_scr[:, other * group : (other + 1) * group, :], own)
    if last:
        for earlier in range(level):
            out_ref[earlier] = prev[earlier][...]
        out_ref[level] = own
        return
    out_ref[...] = own
    for earlier in range(level):
        for t in range(tiles):
            store_scr[earlier * tiles + t] = prev[earlier][t]
    acc_scr[...] = jnp.zeros_like(acc_scr)
    for p in range(mats_ref.shape[1]):
        update = jnp.dot(
            store_scr[ids_ref[0, level, p]], mats_ref[level, p], preferred_element_type=jnp.float32
        )
        slot = ids_ref[1, level, p]
        acc_scr[slot] = acc_scr[slot] + update

    def sums(index):
        return acc_scr[index * tiles : (index + 1) * tiles].astype(jnp.bfloat16)

    own_ref[...] = sums(OWN)
    sibling_ref[...] = sums(SIBLING)
    handed_ref[...] = sums(HANDED)
    far_ref[...] = sums(FAR)
    chip_ref[0] = sums(PASSED)
    chip_ref[1] = sums(DIRECT)


def run_level(level, last, rep, ids, parts, weights, prev, shape):
    levels, tiles, group, span = shape
    cols = 4 * group
    smem = pl.BlockSpec(memory_space=pltpu.SMEM)
    vmem = pl.BlockSpec(memory_space=pltpu.VMEM)
    args = [rep]
    specs = [smem]
    if not last:
        args.append(ids)
        specs.append(smem)
    inner = [*parts, *weights, *prev]
    args += inner
    specs += [vmem] * len(inner)
    scratch = [pltpu.VMEM((tiles, cols, span), jnp.float32)]
    if last:
        outs = jax.ShapeDtypeStruct(shape, jnp.float32)
        out_specs = vmem
    else:
        outs = [jax.ShapeDtypeStruct((tiles, group, span), jnp.float32)] + [
            jax.ShapeDtypeStruct((*lead, tiles, cols, span), jnp.bfloat16) for lead in ((), (), (), (), (), (2,))
        ]
        out_specs = [vmem] * len(outs)
        scratch.append(pltpu.VMEM(((level + 1) * tiles, cols, span), jnp.bfloat16))
        scratch.append(pltpu.VMEM((GROUPS * tiles + 1, cols, span), jnp.float32))
    return pl.pallas_call(
        functools.partial(level_body, level, last),
        out_shape=outs,
        in_specs=specs,
        out_specs=out_specs,
        scratch_shapes=scratch,
        compiler_params=pltpu.CompilerParams(vmem_limit_bytes=6 << 20),
    )(*args)


def slots_of(panel_dst, owner, dom_size, tiles):
    target = jnp.zeros_like(panel_dst)
    for other in range(1, dom_size):
        target = target + (panel_dst >= other * tiles).astype(jnp.int32)
    distance = target - owner
    distance = jnp.where(distance < 0, distance + dom_size, distance)
    near = jnp.where(distance > dom_size // 2, distance - dom_size, distance)
    onward = jnp.where(owner % 2 == 1, near, -near)
    group = jnp.where(
        distance == dom_size // 2,
        FAR,
        jnp.where(
            onward == 0,
            OWN,
            jnp.where(
                onward == 1, PASSED, jnp.where(onward == 2, DIRECT, jnp.where(onward == -1, SIBLING, HANDED))
            ),
        ),
    )
    return jnp.where(panel_dst >= 0, group * tiles + panel_dst - target * tiles, GROUPS * tiles)


def fetch_body(dom_size, *refs):
    owner_ref, _, src_ref, dst_ref, diag_hbm, mats_hbm, ids_ref, diag_ref, mats_ref, sems = refs
    copies = [pltpu.make_async_copy(diag_hbm.at[pl.ds(0, 1)], diag_ref.at[pl.ds(0, 1)], sems.at[0])]
    step = mats_ref.shape[1] // CHUNKS
    for chunk in range(CHUNKS):
        some = pl.ds(chunk * step, step)
        copies.append(
            pltpu.make_async_copy(mats_hbm.at[pl.ds(0, 1), some], mats_ref.at[:, some], sems.at[1 + chunk])
        )
    copies.append(
        pltpu.make_async_copy(diag_hbm.at[pl.ds(1, 1)], diag_ref.at[pl.ds(1, 1)], sems.at[1 + CHUNKS])
    )
    for copy in copies:
        copy.start()
    ids_ref[0] = src_ref[...]
    ids_ref[1] = slots_of(dst_ref[...], owner_ref[0], dom_size, diag_ref.shape[1])
    for copy in copies:
        copy.wait()


def fetch(after, src, dst, diag, mats):
    vmem = pl.BlockSpec(memory_space=pltpu.VMEM)
    hbm = pl.BlockSpec(memory_space=pltpu.HBM)
    owner = lax.axis_index("dom").astype(jnp.int32)
    return pl.pallas_call(
        functools.partial(fetch_body, lax.axis_size("dom")),
        out_shape=[
            jax.ShapeDtypeStruct((2, *src.shape), jnp.int32),
            pltpu.VMEM((2, *diag.shape[1:]), diag.dtype),
            pltpu.VMEM((1, *mats.shape[1:]), mats.dtype),
        ],
        in_specs=[pl.BlockSpec(memory_space=pltpu.SMEM), vmem, vmem, vmem, hbm, hbm],
        out_specs=[vmem, vmem, vmem],
        scratch_shapes=[pltpu.SemaphoreType.DMA((2 + CHUNKS,))],
        compiler_params=pltpu.CompilerParams(vmem_limit_bytes=1 << 20),
    )(owner[None], after, src, dst, diag, mats)


def per_device(right_sides, diag_inverse, panel_mats, panel_src, panel_dst):
    levels, tiles, group, span = right_sides.shape
    rep_size = lax.axis_size("rep")
    rep = lax.axis_index("rep").astype(jnp.int32)
    cols = group * rep_size
    top = lax.broadcasted_iota(jnp.int32, (2, tiles, cols, span), 0) == 0
    partial = right_sides[0].astype(jnp.bfloat16)
    place = lax.broadcasted_iota(jnp.int32, (levels, tiles, cols, span), 2) // group == rep
    own_rhs = jnp.where(place, jnp.concatenate([right_sides] * rep_size, 2), 0.0)
    ids, early_diag, early_mats = fetch(
        partial,
        panel_src,
        panel_dst,
        *(pltpu.with_memory_space_constraint(x, pltpu.HBM) for x in (diag_inverse, panel_mats)),
    )
    late_diag, late_mats = (
        pltpu.with_memory_space_constraint(x, pltpu.VMEM) for x in (diag_inverse, panel_mats)
    )
    store = []
    results = []
    for level in range(levels):
        last = level + 1 == levels
        parts = [partial] + [along_rep(partial, apart) for apart in APART]
        weights = [early_diag if level < 2 else late_diag, early_mats if level < 1 else late_mats]
        if last:
            return run_level(
                level, last, rep[None], None, parts, weights[:1], results, right_sides.shape
            )
        solved, stored, own, sibling, handed, far, chip = run_level(
            level, last, rep[None], ids, parts, weights, store, right_sides.shape
        )
        results.append(solved)
        store.append(stored)
        handed = jnp.where(top, to_sibling(handed), jnp.zeros_like(handed))
        from_chip = to_next_chip(
            (chip.astype(jnp.float32) + handed.astype(jnp.float32)).astype(jnp.bfloat16)
        )
        from_far = to_far(far)
        across = to_sibling(
            (from_chip[0].astype(jnp.float32) + sibling.astype(jnp.float32)).astype(jnp.bfloat16)
        )
        incoming = sum(piece.astype(jnp.float32) for piece in (own, from_chip[1], from_far, across))
        partial = (own_rhs[level + 1] - incoming).astype(jnp.bfloat16)


def solution(mesh):
    return jax.shard_map(
        per_device,
        mesh=mesh,
        in_specs=(
            P(None, "dom", "rep", None),
            P(None, "dom", None, None),
            P(None, ("dom", "rep"), None, None),
            P(None, ("dom", "rep")),
            P(None, ("dom", "rep")),
        ),
        out_specs=P(None, "dom", "rep", None),
        check_vma=False,
    )
```

time: 92.4 us -> 79.5 us (0.86); the launches traced: 91.1 us -> 79.3 us
  starting transfers between devices: 42.2 us -> 34 us
  Pallas kernels: 16.8 us -> 10.6 us
  waiting for transfers between devices: 28.6 us -> 31.5 us
  other arithmetic: 2.5 us -> 0.79 us
  local copies, waits for them, and re-layouts: 0.78 us -> 2.17 us
    ppermute x24, starting transfers between devices: 42.2 us -> 34 us  [the longest x12 17.6 us: along_rep(): lax.ppermute(value, 'rep', [(i, i ^ apart) for i in range(lax.axis_size('...]
    pallas_call x5, Pallas kernels: 16.8 us -> 10.6 us  [the longest x4 6.99 us: run_level(): pl.pallas_call(functools.partial(level_body, level, last), out_shape=outs...]
    ppermute x24, waiting for transfers between devices: 28.6 us -> 31.5 us  [the longest x12 19.9 us: dom_permute(): lax.ppermute(value, 'dom', [(i, target(i) % size) for i in range(size)])]
    another operation x2 -> x0, other arithmetic: 1.41 us -> none  [per_device(): ids = jnp.stack([panel_src, slots_of(panel_dst, tiles)])]
    unnamed x2 -> x18, local copies, waits for them, and re-layouts: 0.01 us -> 1.4 us
  transfers between devices with their start and end apart: 24 -> 24, of which waited for: 15 -> 15; matrix products, arithmetic and copies ran while one was open for 2% -> 0% of each run, Pallas kernels for 3% -> 5%
where the time goes in v4:
time: 79.5 us; the launch traced here: 79.3 us
  starting transfers between devices  34 us (43%)
  waiting for transfers between devices  31.5 us (40%)
  Pallas kernels  10.6 us (13%)
  local copies, waits for them, and re-layouts  2.17 us (3%)
    ppermute x12, waiting for transfers between devices, dom_permute(): lax.ppermute(value, 'dom', [(i, target(i) % size) for i in range(size)])  19.9 us
    ppermute x12, starting transfers between devices, along_rep(): lax.ppermute(value, 'rep', [(i, i ^ apart) for i in range(lax.axis_size('...  17.6 us
    ppermute x12, starting transfers between devices, dom_permute(): lax.ppermute(value, 'dom', [(i, target(i) % size) for i in range(size)])  16.4 us
    ppermute x12, waiting for transfers between devices, along_rep(): lax.ppermute(value, 'rep', [(i, i ^ apart) for i in range(lax.axis_size('...  11.7 us
    pallas_call x4, Pallas kernels, run_level(): pl.pallas_call(functools.partial(level_body, level, last), out_shape=outs...  6.99 us
    pallas_call x1, Pallas kernels, fetch(): pl.pallas_call(functools.partial(fetch_body, lax.axis_size('dom')), out_s...  3.61 us
  transfers between devices with their start and end apart: 24, of which 15 were waited for; matrix products, arithmetic and copies ran while one was open for 0% of the time, Pallas kernels for 5%

profile of v4, /device:TPU:0, one launch (start us, length us, event | category | flops | bytes accessed | tf_op | source)
XLA Modules:
  0.0 79.3 jit_solution(429098694630291726)
XLA Ops:
  0.0 0.8 fusion.15.refs_1_.refs_2_
  0.8 4.1 %collective-permute-start = (bf16[6,4,384]{2,1,0:T(4,128)(2,1)S(1)}, bf16[6,4,384]{2,1,0:T(4,128)(2,1)S(1)}, u32[]{:S(2)}, u32[]{:S(2)}) collective-permute-start(bf16[6,4,384]{2,1,0:T(4,128)(2,1)S(1)} %fusion.15.refs_1_.refs_2_), channel_id=1, source_target_pairs={{0,3},{1,2},{2,1},{3,0},{4,7},{5,6},{6,5},{7,4},{8,11},{9,10},{10,... | collective-permute-start | bytes 55304 | tf_op jit(solution)/shard_map/ppermute | solution.py:36
  4.9 0.0 collective-permute-start.1
  4.9 0.9 %collective-permute-start.2 = (bf16[6,4,384]{2,1,0:T(4,128)(2,1)S(1)}, bf16[6,4,384]{2,1,0:T(4,128)(2,1)S(1)}, u32[]{:S(2)}, u32[]{:S(2)}) collective-permute-start(bf16[6,4,384]{2,1,0:T(4,128)(2,1)S(1)} %fusion.15.refs_1_.refs_2_), channel_id=1, source_target_pairs={{0,1},{1,0},{2,3},{3,2},{4,5},{5,4},{6,7},{7,6},{8,9},{9,8},{10,11... | collective-permute-start | bytes 55304 | tf_op jit(solution)/shard_map/ppermute | solution.py:36
  5.8 0.7 copy-done
  6.5 0.7 copy-done.1
  7.2 3.6 %shard_map.55 = (s32[2,3,16]{2,1,0:T(4,128)S(1)}, bf16[2,6,384,384]{3,2,1,0:T(8,128)(2,1)S(1)}, bf16[1,16,384,384]{3,2,1,0:T(8,128)(2,1)S(1)}) custom-call(s32[1]{0:T(128)} %bitcast.2.refs_0_, bf16[6,4,384]{2,1,0:T(4,128)(2,1)S(1)} %fusion.15.refs_1_.refs_2_, s32[3,16]{1,0:T(4,128)S(1)} %copy-done, s32[3,16]{1,0:T(4,128)S(1)} %copy-done.1, ...), custom_call_target="tpu_custom_call" | custom-call | tf_op jit(solution)/shard_map/pallas_call | solution.py:193
  10.8 0.0 copy-start.2
  10.8 0.0 collective-permute-done.refs_3_
  10.9 0.0 collective-permute-done.1.refs_4_
  10.9 0.0 collective-permute-done.2.refs_5_
  10.9 0.0 slice-start.3
  10.9 1.9 %shard_map.56 = (f32[6,4,384]{2,1,0:T(4,128)S(1)}, bf16[6,16,384]{2,1,0:T(8,128)(2,1)S(1)}, bf16[6,16,384]{2,1,0:T(8,128)(2,1)S(1)}, bf16[6,16,384]{2,1,0:T(8,12...) custom-call(s32[1]{0:T(128)} %bitcast.refs_0_, ...), custom_call_target="tpu_custom_call" | custom-call | tf_op jit(solution)/shard_map/pallas_call | solution.py:137
  12.8 0.1 collective-permute-start.3
  12.9 1.2 %collective-permute-done.3 = bf16[6,16,384]{2,1,0:T(8,128)(2,1)S(1)} collective-permute-done((bf16[6,16,384]{2,1,0:T(8,128)(2,1)S(1)}, bf16[6,16,384]{2,1,0:T(8,128)(2,1)S(1)}, u32[]{:S(2)}, u32[]{:S(2)}) %collective-permute-start.3) | collective-permute-done | bytes 73760 | tf_op jit(solution)/shard_map/ppermute | solution.py:19
  14.1 0.1 add_convert_fusion.2
  14.3 5.3 %collective-permute-start.4 = (bf16[2,6,16,384]{3,2,1,0:T(8,128)(2,1)S(1)}, bf16[2,6,16,384]{3,2,1,0:T(8,128)(2,1)S(1)}, u32[]{:S(2)}, u32[]{:S(2)}) collective-permute-start(bf16[2,6,16,384]{3,2,1,0:T(8,128)(2,1)S(1)} %add_convert_fusion.2), channel_id=1, source_target_pairs={{0,120},{4,12},{8,0},{12,20},{16,8},{20,28},{24,16},{28,36},{32,24... | collective-permute-start | bytes 442376 | tf_op jit(solution)/shard_map/ppermute | solution.py:19
  19.6 0.7 collective-permute-start.5
  20.3 2.0 %collective-permute-done.4 = bf16[2,6,16,384]{3,2,1,0:T(8,128)(2,1)S(1)} collective-permute-done((bf16[2,6,16,384]{3,2,1,0:T(8,128)(2,1)S(1)}, bf16[2,6,16,384]{3,2,1,0:T(8,128)(2,1)S(1)}, u32[]{:S(2)}, u32[]{:S(2)}) %collective-permute-start.4) | collective-permute-done | bytes 147488 | tf_op jit(solution)/shard_map/ppermute | solution.py:19
  22.2 0.1 collective-permute-start.6
  22.3 0.1 maximum_select_fusion
  22.5 3.0 %collective-permute-done.5 = bf16[6,16,384]{2,1,0:T(8,128)(2,1)S(1)} collective-permute-done((bf16[6,16,384]{2,1,0:T(8,128)(2,1)S(1)}, bf16[6,16,384]{2,1,0:T(8,128)(2,1)S(1)}, u32[]{:S(2)}, u32[]{:S(2)}) %collective-permute-start.5) | collective-permute-done | bytes 73760 | tf_op jit(solution)/shard_map/ppermute | solution.py:19
  25.5 0.0 collective-permute-done.6
  25.5 0.1 fusion.1.refs_2_
  25.6 3.2 %collective-permute-start.7 = (bf16[6,16,384]{2,1,0:T(8,128)(2,1)S(1)}, bf16[6,16,384]{2,1,0:T(8,128)(2,1)S(1)}, u32[]{:S(2)}, u32[]{:S(2)}) collective-permute-start(bf16[6,16,384]{2,1,0:T(8,128)(2,1)S(1)} %fusion.1.refs_2_), channel_id=1, source_target_pairs={{0,3},{1,2},{2,1},{3,0},{4,7},{5,6},{6,5},{7,4},{8,11},{9,10},{10,... | collective-permute-start | bytes 221192 | tf_op jit(solution)/shard_map/ppermute | solution.py:36
  28.8 0.0 collective-permute-start.8
  28.8 0.9 %collective-permute-start.9 = (bf16[6,16,384]{2,1,0:T(8,128)(2,1)S(1)}, bf16[6,16,384]{2,1,0:T(8,128)(2,1)S(1)}, u32[]{:S(2)}, u32[]{:S(2)}) collective-permute-start(bf16[6,16,384]{2,1,0:T(8,128)(2,1)S(1)} %fusion.1.refs_2_), channel_id=1, source_target_pairs={{0,1},{1,0},{2,3},{3,2},{4,5},{5,4},{6,7},{7,6},{8,9},{9,8},{10,11... | collective-permute-start | bytes 221192 | tf_op jit(solution)/shard_map/ppermute | solution.py:36
  29.7 2.3 %collective-permute-done.7.refs_3_ = bf16[6,16,384]{2,1,0:T(8,128)(2,1)S(1)} collective-permute-done((bf16[6,16,384]{2,1,0:T(8,128)(2,1)S(1)}, bf16[6,16,384]{2,1,0:T(8,128)(2,1)S(1)}, u32[]{:S(2)}, u32[]{:S(2)}) %collective-permute-start.7) | collective-permute-done | bytes 73760 | tf_op jit(solution)/shard_map/ppermute | solution.py:36
  32.0 2.7 %collective-permute-done.8.refs_4_ = bf16[6,16,384]{2,1,0:T(8,128)(2,1)S(1)} collective-permute-done((bf16[6,16,384]{2,1,0:T(8,128)(2,1)S(1)}, bf16[6,16,384]{2,1,0:T(8,128)(2,1)S(1)}, u32[]{:S(2)}, u32[]{:S(2)}) %collective-permute-start.8) | collective-permute-done | bytes 73760 | tf_op jit(solution)/shard_map/ppermute | solution.py:36
  34.6 0.0 collective-permute-done.9.refs_5_
  34.7 0.0 slice-start.5
  34.7 1.9 %shard_map.57 = (f32[6,4,384]{2,1,0:T(4,128)S(1)}, bf16[6,16,384]{2,1,0:T(8,128)(2,1)S(1)}, bf16[6,16,384]{2,1,0:T(8,128)(2,1)S(1)}, bf16[6,16,384]{2,1,0:T(8,12...) custom-call(s32[1]{0:T(128)} %bitcast.refs_0_, ...), custom_call_target="tpu_custom_call" | custom-call | tf_op jit(solution)/shard_map/pallas_call | solution.py:137
  36.6 0.1 collective-permute-start.10
  36.7 1.3 %collective-permute-done.10 = bf16[6,16,384]{2,1,0:T(8,128)(2,1)S(1)} collective-permute-done((bf16[6,16,384]{2,1,0:T(8,128)(2,1)S(1)}, bf16[6,16,384]{2,1,0:T(8,128)(2,1)S(1)}, u32[]{:S(2)}, u32[]{:S(2)}) %collective-permute-start.10) | collective-permute-done | bytes 73760 | tf_op jit(solution)/shard_map/ppermute | solution.py:19
  37.9 0.1 add_convert_fusion.1
  38.0 5.1 %collective-permute-start.11 = (bf16[2,6,16,384]{3,2,1,0:T(8,128)(2,1)S(1)}, bf16[2,6,16,384]{3,2,1,0:T(8,128)(2,1)S(1)}, u32[]{:S(2)}, u32[]{:S(2)}) collective-permute-start(bf16[2,6,16,384]{3,2,1,0:T(8,128)(2,1)S(1)} %add_convert_fusion.1), channel_id=1, source_target_pairs={{0,120},{4,12},{8,0},{12,20},{16,8},{20,28},{24,16},{28,36},{32,24... | collective-permute-start | bytes 442376 | tf_op jit(solution)/shard_map/ppermute | solution.py:19
  43.2 0.0 collective-permute-start.12
  43.2 2.7 %collective-permute-done.11 = bf16[2,6,16,384]{3,2,1,0:T(8,128)(2,1)S(1)} collective-permute-done((bf16[2,6,16,384]{3,2,1,0:T(8,128)(2,1)S(1)}, bf16[2,6,16,384]{3,2,1,0:T(8,128)(2,1)S(1)}, u32[]{:S(2)}, u32[]{:S(2)}) %collective-permute-start.11) | collective-permute-done | bytes 147488 | tf_op jit(solution)/shard_map/ppermute | solution.py:19
  45.9 0.1 collective-permute-start.13
  46.0 3.1 %collective-permute-done.12 = bf16[6,16,384]{2,1,0:T(8,128)(2,1)S(1)} collective-permute-done((bf16[6,16,384]{2,1,0:T(8,128)(2,1)S(1)}, bf16[6,16,384]{2,1,0:T(8,128)(2,1)S(1)}, u32[]{:S(2)}, u32[]{:S(2)}) %collective-permute-start.12) | collective-permute-done | bytes 73760 | tf_op jit(solution)/shard_map/ppermute | solution.py:19
  49.0 0.1 fusion.3.refs_2_
  49.1 1.4 %collective-permute-start.14 = (bf16[6,16,384]{2,1,0:T(8,128)(2,1)S(1)}, bf16[6,16,384]{2,1,0:T(8,128)(2,1)S(1)}, u32[]{:S(2)}, u32[]{:S(2)}) collective-permute-start(bf16[6,16,384]{2,1,0:T(8,128)(2,1)S(1)} %fusion.3.refs_2_), channel_id=1, source_target_pairs={{0,3},{1,2},{2,1},{3,0},{4,7},{5,6},{6,5},{7,4},{8,11},{9,10},{10,... | collective-permute-start | bytes 221192 | tf_op jit(solution)/shard_map/ppermute | solution.py:36
  50.5 0.6 collective-permute-start.15
  51.1 2.2 %collective-permute-start.16 = (bf16[6,16,384]{2,1,0:T(8,128)(2,1)S(1)}, bf16[6,16,384]{2,1,0:T(8,128)(2,1)S(1)}, u32[]{:S(2)}, u32[]{:S(2)}) collective-permute-start(bf16[6,16,384]{2,1,0:T(8,128)(2,1)S(1)} %fusion.3.refs_2_), channel_id=1, source_target_pairs={{0,1},{1,0},{2,3},{3,2},{4,5},{5,4},{6,7},{7,6},{8,9},{9,8},{10,11... | collective-permute-start | bytes 221192 | tf_op jit(solution)/shard_map/ppermute | solution.py:36
  53.3 1.5 %collective-permute-done.14.refs_3_ = bf16[6,16,384]{2,1,0:T(8,128)(2,1)S(1)} collective-permute-done((bf16[6,16,384]{2,1,0:T(8,128)(2,1)S(1)}, bf16[6,16,384]{2,1,0:T(8,128)(2,1)S(1)}, u32[]{:S(2)}, u32[]{:S(2)}) %collective-permute-start.14) | collective-permute-done | bytes 73760 | tf_op jit(solution)/shard_map/ppermute | solution.py:36
  54.7 1.6 %collective-permute-done.15.refs_4_ = bf16[6,16,384]{2,1,0:T(8,128)(2,1)S(1)} collective-permute-done((bf16[6,16,384]{2,1,0:T(8,128)(2,1)S(1)}, bf16[6,16,384]{2,1,0:T(8,128)(2,1)S(1)}, u32[]{:S(2)}, u32[]{:S(2)}) %collective-permute-start.15) | collective-permute-done | bytes 73760 | tf_op jit(solution)/shard_map/ppermute | solution.py:36
  56.4 0.0 collective-permute-done.16.refs_5_
  56.4 2.2 %shard_map.58 = (f32[6,4,384]{2,1,0:T(4,128)S(1)}, bf16[6,16,384]{2,1,0:T(8,128)(2,1)}, bf16[6,16,384]{2,1,0:T(8,128)(2,1)S(1)}, bf16[6,16,384]{2,1,0:T(8,128)(2...) custom-call(s32[1]{0:T(128)} %bitcast.refs_0_, ...), custom_call_target="tpu_custom_call" | custom-call | tf_op jit(solution)/shard_map/pallas_call | solution.py:137
  58.6 1.3 %collective-permute-done.17 = bf16[6,16,384]{2,1,0:T(8,128)(2,1)S(1)} collective-permute-done((bf16[6,16,384]{2,1,0:T(8,128)(2,1)S(1)}, bf16[6,16,384]{2,1,0:T(8,128)(2,1)S(1)}, u32[]{:S(2)}, u32[]{:S(2)}) %collective-permute-start.17) | collective-permute-done | bytes 73760 | tf_op jit(solution)/shard_map/ppermute | solution.py:19
  59.8 0.1 add_convert_fusion
  60.0 4.5 %collective-permute-start.18 = (bf16[2,6,16,384]{3,2,1,0:T(8,128)(2,1)S(1)}, bf16[2,6,16,384]{3,2,1,0:T(8,128)(2,1)S(1)}, u32[]{:S(2)}, u32[]{:S(2)}) collective-permute-start(bf16[2,6,16,384]{3,2,1,0:T(8,128)(2,1)S(1)} %add_convert_fusion), channel_id=1, source_target_pairs={{0,120},{4,12},{8,0},{12,20},{16,8},{20,28},{24,16},{28,36},{32,24... | collective-permute-start | bytes 442376 | tf_op jit(solution)/shard_map/ppermute | solution.py:19
  64.5 0.0 collective-permute-start.19
  64.5 2.7 %collective-permute-done.18 = bf16[2,6,16,384]{3,2,1,0:T(8,128)(2,1)S(1)} collective-permute-done((bf16[2,6,16,384]{3,2,1,0:T(8,128)(2,1)S(1)}, bf16[2,6,16,384]{3,2,1,0:T(8,128)(2,1)S(1)}, u32[]{:S(2)}, u32[]{:S(2)}) %collective-permute-start.18) | collective-permute-done | bytes 147488 | tf_op jit(solution)/shard_map/ppermute | solution.py:19
  67.2 0.4 collective-permute-start.20
  67.6 2.7 %collective-permute-done.19 = bf16[6,16,384]{2,1,0:T(8,128)(2,1)S(1)} collective-permute-done((bf16[6,16,384]{2,1,0:T(8,128)(2,1)S(1)}, bf16[6,16,384]{2,1,0:T(8,128)(2,1)S(1)}, u32[]{:S(2)}, u32[]{:S(2)}) %collective-permute-start.19) | collective-permute-done | bytes 73760 | tf_op jit(solution)/shard_map/ppermute | solution.py:19
  70.4 0.0 collective-permute-done.20
  70.4 0.1 fusion.5.refs_1_
  70.4 2.0 %collective-permute-start.21 = (bf16[6,16,384]{2,1,0:T(8,128)(2,1)S(1)}, bf16[6,16,384]{2,1,0:T(8,128)(2,1)S(1)}, u32[]{:S(2)}, u32[]{:S(2)}) collective-permute-start(bf16[6,16,384]{2,1,0:T(8,128)(2,1)S(1)} %fusion.5.refs_1_), channel_id=1, source_target_pairs={{0,3},{1,2},{2,1},{3,0},{4,7},{5,6},{6,5},{7,4},{8,11},{9,10},{10,... | collective-permute-start | bytes 221192 | tf_op jit(solution)/shard_map/ppermute | solution.py:36
  72.4 0.9 %collective-permute-start.22 = (bf16[6,16,384]{2,1,0:T(8,128)(2,1)S(1)}, bf16[6,16,384]{2,1,0:T(8,128)(2,1)S(1)}, u32[]{:S(2)}, u32[]{:S(2)}) collective-permute-start(bf16[6,16,384]{2,1,0:T(8,128)(2,1)S(1)} %fusion.5.refs_1_), channel_id=1, source_target_pairs={{0,2},{1,3},{2,0},{3,1},{4,6},{5,7},{6,4},{7,5},{8,10},{9,11},{10,... | collective-permute-start | bytes 221192 | tf_op jit(solution)/shard_map/ppermute | solution.py:36
  73.3 1.3 %collective-permute-start.23 = (bf16[6,16,384]{2,1,0:T(8,128)(2,1)S(1)}, bf16[6,16,384]{2,1,0:T(8,128)(2,1)S(1)}, u32[]{:S(2)}, u32[]{:S(2)}) collective-permute-start(bf16[6,16,384]{2,1,0:T(8,128)(2,1)S(1)} %fusion.5.refs_1_), channel_id=1, source_target_pairs={{0,1},{1,0},{2,3},{3,2},{4,5},{5,4},{6,7},{7,6},{8,9},{9,8},{10,11... | collective-permute-start | bytes 221192 | tf_op jit(solution)/shard_map/ppermute | solution.py:36
  74.6 1.7 %collective-permute-done.21.refs_2_ = bf16[6,16,384]{2,1,0:T(8,128)(2,1)S(1)} collective-permute-done((bf16[6,16,384]{2,1,0:T(8,128)(2,1)S(1)}, bf16[6,16,384]{2,1,0:T(8,128)(2,1)S(1)}, u32[]{:S(2)}, u32[]{:S(2)}) %collective-permute-start.21) | collective-permute-done | bytes 73760 | tf_op jit(solution)/shard_map/ppermute | solution.py:36
  76.3 1.9 %collective-permute-done.22.refs_3_ = bf16[6,16,384]{2,1,0:T(8,128)(2,1)S(1)} collective-permute-done((bf16[6,16,384]{2,1,0:T(8,128)(2,1)S(1)}, bf16[6,16,384]{2,1,0:T(8,128)(2,1)S(1)}, u32[]{:S(2)}, u32[]{:S(2)}) %collective-permute-start.22) | collective-permute-done | bytes 73760 | tf_op jit(solution)/shard_map/ppermute | solution.py:36
  78.2 0.0 collective-permute-done.23.refs_4_
  78.2 1.1 %shard_map.59 = f32[4,6,4,384]{3,2,1,0:T(4,128)} custom-call(s32[1]{0:T(128)} %bitcast.refs_0_, bf16[6,16,384]{2,1,0:T(8,128)(2,1)S(1)} %fusion.5.refs_1_, bf16[6,16,384]{2,1,0:T(8,128)(2,1)S(1)} %collective-permute-done.21.refs_2_, bf16[6,16,384]{2,1,0:T(8,128)(2,1)S(1)} %collective-permute-done.22.refs_3_, ...), custom_call_target="tpu_custom_call" | custom-call | tf_op jit(solution)/shard_map/pallas_call | solution.py:137
  (23 shorter events, 0.1 us)
Async XLA Ops:
  0.8 10.1 %collective-permute-start = (bf16[6,4,384]{2,1,0:T(4,128)(2,1)S(1)}, bf16[6,4,384]{2,1,0:T(4,128)(2,1)S(1)}, u32[]{:S(2)}, u32[]{:S(2)}) collective-permute-start(bf16[6,4,384]{2,1,0:T(4,128)(2,1)S(1)} %fusion.15.refs_1_.refs_2_), channel_id=1, source_target_pairs={{0,3},{1,2},{2,1},{3,0},{4,7},{5,6},{6,5},{7,4},{8,11},{9,10},{10,... | collective-permute-start | bytes 55304 | tf_op jit(solution)/shard_map/ppermute | solution.py:36
  4.9 6.0 %collective-permute-start.1 = (bf16[6,4,384]{2,1,0:T(4,128)(2,1)S(1)}, bf16[6,4,384]{2,1,0:T(4,128)(2,1)S(1)}, u32[]{:S(2)}, u32[]{:S(2)}) collective-permute-start(bf16[6,4,384]{2,1,0:T(4,128)(2,1)S(1)} %fusion.15.refs_1_.refs_2_), channel_id=1, source_target_pairs={{0,2},{1,3},{2,0},{3,1},{4,6},{5,7},{6,4},{7,5},{8,10},{9,11},{10,... | collective-permute-start | bytes 55304 | tf_op jit(solution)/shard_map/ppermute | solution.py:36
  4.9 6.0 %collective-permute-start.2 = (bf16[6,4,384]{2,1,0:T(4,128)(2,1)S(1)}, bf16[6,4,384]{2,1,0:T(4,128)(2,1)S(1)}, u32[]{:S(2)}, u32[]{:S(2)}) collective-permute-start(bf16[6,4,384]{2,1,0:T(4,128)(2,1)S(1)} %fusion.15.refs_1_.refs_2_), channel_id=1, source_target_pairs={{0,1},{1,0},{2,3},{3,2},{4,5},{5,4},{6,7},{7,6},{8,9},{9,8},{10,11... | collective-permute-start | bytes 55304 | tf_op jit(solution)/shard_map/ppermute | solution.py:36
  5.8 0.7 copy-start
  6.5 0.7 copy-start.1
  7.2 27.4 %slice-start = ((s8[14155776]{0:T(1024)(128)(4,1)}), s8[4194304]{0:T(1024)(128)(4,1)S(1)}, s32[]{:S(2)}) async-start(s8[14155776]{0:T(1024)(128)(4,1)} %bitcast.52), calls=%async_computation | async-start | bytes 8388608
  7.2 27.4 %slice-start.1 = ((s8[14155776]{0:T(1024)(128)(4,1)}), s8[4194304]{0:T(1024)(128)(4,1)S(1)}, s32[]{:S(2)}) async-start(s8[14155776]{0:T(1024)(128)(4,1)} %bitcast.52), calls=%async_computation.1 | async-start | bytes 8388608
  7.2 27.4 %slice-start.2 = ((s8[14155776]{0:T(1024)(128)(4,1)}), s8[4194304]{0:T(1024)(128)(4,1)S(1)}, s32[]{:S(2)}) async-start(s8[14155776]{0:T(1024)(128)(4,1)} %bitcast.52), calls=%async_computation.2 | async-start | bytes 8388608
  10.8 11.5 %copy-start.2 = (f32[4,6,4,384]{3,2,1,0:T(4,128)S(1)}, f32[4,6,4,384]{3,2,1,0:T(4,128)}, u32[]{:S(2)}) copy-start(f32[4,6,4,384]{3,2,1,0:T(4,128)} %param.5) | copy-start | bytes 442372
  10.9 23.8 %slice-start.3 = ((s8[14155776]{0:T(1024)(128)(4,1)}), s8[1572864]{0:T(1024)(128)(4,1)S(1)}, s32[]{:S(2)}) async-start(s8[14155776]{0:T(1024)(128)(4,1)} %bitcast.52), calls=%async_computation.3 | async-start | bytes 3145728
  12.8 1.3 %collective-permute-start.3 = (bf16[6,16,384]{2,1,0:T(8,128)(2,1)S(1)}, bf16[6,16,384]{2,1,0:T(8,128)(2,1)S(1)}, u32[]{:S(2)}, u32[]{:S(2)}) collective-permute-start(bf16[6,16,384]{2,1,0:T(8,128)(2,1)S(1)} %get-tuple-element.33), channel_id=1, source_target_pairs={{0,4},{4,0},{8,12},{12,8},{16,20},{20,16},{24,28},{28,24},{32,36},... | collective-permute-start | bytes 221192 | tf_op jit(solution)/shard_map/ppermute | solution.py:19
  14.3 7.9 %collective-permute-start.4 = (bf16[2,6,16,384]{3,2,1,0:T(8,128)(2,1)S(1)}, bf16[2,6,16,384]{3,2,1,0:T(8,128)(2,1)S(1)}, u32[]{:S(2)}, u32[]{:S(2)}) collective-permute-start(bf16[2,6,16,384]{3,2,1,0:T(8,128)(2,1)S(1)} %add_convert_fusion.2), channel_id=1, source_target_pairs={{0,120},{4,12},{8,0},{12,20},{16,8},{20,28},{24,16},{28,36},{32,24... | collective-permute-start | bytes 442376 | tf_op jit(solution)/shard_map/ppermute | solution.py:19
  19.6 5.9 %collective-permute-start.5 = (bf16[6,16,384]{2,1,0:T(8,128)(2,1)S(1)}, bf16[6,16,384]{2,1,0:T(8,128)(2,1)S(1)}, u32[]{:S(2)}, u32[]{:S(2)}) collective-permute-start(bf16[6,16,384]{2,1,0:T(8,128)(2,1)S(1)} %get-tuple-element.34), channel_id=1, source_target_pairs={{0,64},{4,68},{8,72},{12,76},{16,80},{20,84},{24,88},{28,92},{32,9... | collective-permute-start | bytes 221192 | tf_op jit(solution)/shard_map/ppermute | solution.py:19
  22.2 3.3 %collective-permute-start.6 = (bf16[6,16,384]{2,1,0:T(8,128)(2,1)S(1)}, bf16[6,16,384]{2,1,0:T(8,128)(2,1)S(1)}, u32[]{:S(2)}, u32[]{:S(2)}) collective-permute-start(bf16[6,16,384]{2,1,0:T(8,128)(2,1)S(1)} %fusion.12), channel_id=1, source_target_pairs={{0,4},{4,0},{8,12},{12,8},{16,20},{20,16},{24,28},{28,24},{32,36},... | collective-permute-start | bytes 221192 | tf_op jit(solution)/shard_map/ppermute | solution.py:19
  25.5 30.9 %slice-start.4 = ((s8[7077888]{0:T(1024)(128)(4,1)}), s8[4194304]{0:T(1024)(128)(4,1)S(1)}, s32[]{:S(2)}) async-start(s8[7077888]{0:T(1024)(128)(4,1)} %bitcast.54), calls=%async_computation.4 | async-start | bytes 8388608
  25.6 6.4 %collective-permute-start.7 = (bf16[6,16,384]{2,1,0:T(8,128)(2,1)S(1)}, bf16[6,16,384]{2,1,0:T(8,128)(2,1)S(1)}, u32[]{:S(2)}, u32[]{:S(2)}) collective-permute-start(bf16[6,16,384]{2,1,0:T(8,128)(2,1)S(1)} %fusion.1.refs_2_), channel_id=1, source_target_pairs={{0,3},{1,2},{2,1},{3,0},{4,7},{5,6},{6,5},{7,4},{8,11},{9,10},{10,... | collective-permute-start | bytes 221192 | tf_op jit(solution)/shard_map/ppermute | solution.py:36
  28.8 5.9 %collective-permute-start.8 = (bf16[6,16,384]{2,1,0:T(8,128)(2,1)S(1)}, bf16[6,16,384]{2,1,0:T(8,128)(2,1)S(1)}, u32[]{:S(2)}, u32[]{:S(2)}) collective-permute-start(bf16[6,16,384]{2,1,0:T(8,128)(2,1)S(1)} %fusion.1.refs_2_), channel_id=1, source_target_pairs={{0,2},{1,3},{2,0},{3,1},{4,6},{5,7},{6,4},{7,5},{8,10},{9,11},{10,... | collective-permute-start | bytes 221192 | tf_op jit(solution)/shard_map/ppermute | solution.py:36
  28.8 5.9 %collective-permute-start.9 = (bf16[6,16,384]{2,1,0:T(8,128)(2,1)S(1)}, bf16[6,16,384]{2,1,0:T(8,128)(2,1)S(1)}, u32[]{:S(2)}, u32[]{:S(2)}) collective-permute-start(bf16[6,16,384]{2,1,0:T(8,128)(2,1)S(1)} %fusion.1.refs_2_), channel_id=1, source_target_pairs={{0,1},{1,0},{2,3},{3,2},{4,5},{5,4},{6,7},{7,6},{8,9},{9,8},{10,11... | collective-permute-start | bytes 221192 | tf_op jit(solution)/shard_map/ppermute | solution.py:36
  34.7 21.7 %slice-start.5 = ((s8[7077888]{0:T(1024)(128)(4,1)}), s8[2883584]{0:T(1024)(128)(4,1)S(1)}, s32[]{:S(2)}) async-start(s8[7077888]{0:T(1024)(128)(4,1)} %bitcast.54), calls=%async_computation.5 | async-start | bytes 5767168
  36.6 1.3 %collective-permute-start.10 = (bf16[6,16,384]{2,1,0:T(8,128)(2,1)S(1)}, bf16[6,16,384]{2,1,0:T(8,128)(2,1)S(1)}, u32[]{:S(2)}, u32[]{:S(2)}) collective-permute-start(bf16[6,16,384]{2,1,0:T(8,128)(2,1)S(1)} %get-tuple-element.39), channel_id=1, source_target_pairs={{0,4},{4,0},{8,12},{12,8},{16,20},{20,16},{24,28},{28,24},{32,36},... | collective-permute-start | bytes 221192 | tf_op jit(solution)/shard_map/ppermute | solution.py:19
  38.0 7.8 %collective-permute-start.11 = (bf16[2,6,16,384]{3,2,1,0:T(8,128)(2,1)S(1)}, bf16[2,6,16,384]{3,2,1,0:T(8,128)(2,1)S(1)}, u32[]{:S(2)}, u32[]{:S(2)}) collective-permute-start(bf16[2,6,16,384]{3,2,1,0:T(8,128)(2,1)S(1)} %add_convert_fusion.1), channel_id=1, source_target_pairs={{0,120},{4,12},{8,0},{12,20},{16,8},{20,28},{24,16},{28,36},{32,24... | collective-permute-start | bytes 442376 | tf_op jit(solution)/shard_map/ppermute | solution.py:19
  43.2 5.9 %collective-permute-start.12 = (bf16[6,16,384]{2,1,0:T(8,128)(2,1)S(1)}, bf16[6,16,384]{2,1,0:T(8,128)(2,1)S(1)}, u32[]{:S(2)}, u32[]{:S(2)}) collective-permute-start(bf16[6,16,384]{2,1,0:T(8,128)(2,1)S(1)} %get-tuple-element.40), channel_id=1, source_target_pairs={{0,64},{4,68},{8,72},{12,76},{16,80},{20,84},{24,88},{28,92},{32,9... | collective-permute-start | bytes 221192 | tf_op jit(solution)/shard_map/ppermute | solution.py:19
  45.9 3.2 %collective-permute-start.13 = (bf16[6,16,384]{2,1,0:T(8,128)(2,1)S(1)}, bf16[6,16,384]{2,1,0:T(8,128)(2,1)S(1)}, u32[]{:S(2)}, u32[]{:S(2)}) collective-permute-start(bf16[6,16,384]{2,1,0:T(8,128)(2,1)S(1)} %fusion.9), channel_id=1, source_target_pairs={{0,4},{4,0},{8,12},{12,8},{16,20},{20,16},{24,28},{28,24},{32,36},... | collective-permute-start | bytes 221192 | tf_op jit(solution)/shard_map/ppermute | solution.py:19
  49.1 5.6 %collective-permute-start.14 = (bf16[6,16,384]{2,1,0:T(8,128)(2,1)S(1)}, bf16[6,16,384]{2,1,0:T(8,128)(2,1)S(1)}, u32[]{:S(2)}, u32[]{:S(2)}) collective-permute-start(bf16[6,16,384]{2,1,0:T(8,128)(2,1)S(1)} %fusion.3.refs_2_), channel_id=1, source_target_pairs={{0,3},{1,2},{2,1},{3,0},{4,7},{5,6},{6,5},{7,4},{8,11},{9,10},{10,... | collective-permute-start | bytes 221192 | tf_op jit(solution)/shard_map/ppermute | solution.py:36
  50.5 5.9 %collective-permute-start.15 = (bf16[6,16,384]{2,1,0:T(8,128)(2,1)S(1)}, bf16[6,16,384]{2,1,0:T(8,128)(2,1)S(1)}, u32[]{:S(2)}, u32[]{:S(2)}) collective-permute-start(bf16[6,16,384]{2,1,0:T(8,128)(2,1)S(1)} %fusion.3.refs_2_), channel_id=1, source_target_pairs={{0,2},{1,3},{2,0},{3,1},{4,6},{5,7},{6,4},{7,5},{8,10},{9,11},{10,... | collective-permute-start | bytes 221192 | tf_op jit(solution)/shard_map/ppermute | solution.py:36
  51.1 5.3 %collective-permute-start.16 = (bf16[6,16,384]{2,1,0:T(8,128)(2,1)S(1)}, bf16[6,16,384]{2,1,0:T(8,128)(2,1)S(1)}, u32[]{:S(2)}, u32[]{:S(2)}) collective-permute-start(bf16[6,16,384]{2,1,0:T(8,128)(2,1)S(1)} %fusion.3.refs_2_), channel_id=1, source_target_pairs={{0,1},{1,0},{2,3},{3,2},{4,5},{5,4},{6,7},{7,6},{8,9},{9,8},{10,11... | collective-permute-start | bytes 221192 | tf_op jit(solution)/shard_map/ppermute | solution.py:36
  58.6 1.3 %collective-permute-start.17 = (bf16[6,16,384]{2,1,0:T(8,128)(2,1)S(1)}, bf16[6,16,384]{2,1,0:T(8,128)(2,1)S(1)}, u32[]{:S(2)}, u32[]{:S(2)}) collective-permute-start(bf16[6,16,384]{2,1,0:T(8,128)(2,1)S(1)} %get-tuple-element.45), channel_id=1, source_target_pairs={{0,4},{4,0},{8,12},{12,8},{16,20},{20,16},{24,28},{28,24},{32,36},... | collective-permute-start | bytes 221192 | tf_op jit(solution)/shard_map/ppermute | solution.py:19
  60.0 7.2 %collective-permute-start.18 = (bf16[2,6,16,384]{3,2,1,0:T(8,128)(2,1)S(1)}, bf16[2,6,16,384]{3,2,1,0:T(8,128)(2,1)S(1)}, u32[]{:S(2)}, u32[]{:S(2)}) collective-permute-start(bf16[2,6,16,384]{3,2,1,0:T(8,128)(2,1)S(1)} %add_convert_fusion), channel_id=1, source_target_pairs={{0,120},{4,12},{8,0},{12,20},{16,8},{20,28},{24,16},{28,36},{32,24... | collective-permute-start | bytes 442376 | tf_op jit(solution)/shard_map/ppermute | solution.py:19
  64.5 5.9 %collective-permute-start.19 = (bf16[6,16,384]{2,1,0:T(8,128)(2,1)S(1)}, bf16[6,16,384]{2,1,0:T(8,128)(2,1)S(1)}, u32[]{:S(2)}, u32[]{:S(2)}) collective-permute-start(bf16[6,16,384]{2,1,0:T(8,128)(2,1)S(1)} %get-tuple-element.46), channel_id=1, source_target_pairs={{0,64},{4,68},{8,72},{12,76},{16,80},{20,84},{24,88},{28,92},{32,9... | collective-permute-start | bytes 221192 | tf_op jit(solution)/shard_map/ppermute | solution.py:19
  67.2 3.2 %collective-permute-start.20 = (bf16[6,16,384]{2,1,0:T(8,128)(2,1)S(1)}, bf16[6,16,384]{2,1,0:T(8,128)(2,1)S(1)}, u32[]{:S(2)}, u32[]{:S(2)}) collective-permute-start(bf16[6,16,384]{2,1,0:T(8,128)(2,1)S(1)} %fusion.6), channel_id=1, source_target_pairs={{0,4},{4,0},{8,12},{12,8},{16,20},{20,16},{24,28},{28,24},{32,36},... | collective-permute-start | bytes 221192 | tf_op jit(solution)/shard_map/ppermute | solution.py:19
  70.4 5.9 %collective-permute-start.21 = (bf16[6,16,384]{2,1,0:T(8,128)(2,1)S(1)}, bf16[6,16,384]{2,1,0:T(8,128)(2,1)S(1)}, u32[]{:S(2)}, u32[]{:S(2)}) collective-permute-start(bf16[6,16,384]{2,1,0:T(8,128)(2,1)S(1)} %fusion.5.refs_1_), channel_id=1, source_target_pairs={{0,3},{1,2},{2,1},{3,0},{4,7},{5,6},{6,5},{7,4},{8,11},{9,10},{10,... | collective-permute-start | bytes 221192 | tf_op jit(solution)/shard_map/ppermute | solution.py:36
  72.4 5.9 %collective-permute-start.22 = (bf16[6,16,384]{2,1,0:T(8,128)(2,1)S(1)}, bf16[6,16,384]{2,1,0:T(8,128)(2,1)S(1)}, u32[]{:S(2)}, u32[]{:S(2)}) collective-permute-start(bf16[6,16,384]{2,1,0:T(8,128)(2,1)S(1)} %fusion.5.refs_1_), channel_id=1, source_target_pairs={{0,2},{1,3},{2,0},{3,1},{4,6},{5,7},{6,4},{7,5},{8,10},{9,11},{10,... | collective-permute-start | bytes 221192 | tf_op jit(solution)/shard_map/ppermute | solution.py:36
  73.3 4.9 %collective-permute-start.23 = (bf16[6,16,384]{2,1,0:T(8,128)(2,1)S(1)}, bf16[6,16,384]{2,1,0:T(8,128)(2,1)S(1)}, u32[]{:S(2)}, u32[]{:S(2)}) collective-permute-start(bf16[6,16,384]{2,1,0:T(8,128)(2,1)S(1)} %fusion.5.refs_1_), channel_id=1, source_target_pairs={{0,1},{1,0},{2,3},{3,2},{4,5},{5,4},{6,7},{7,6},{8,9},{9,8},{10,11... | collective-permute-start | bytes 221192 | tf_op jit(solution)/shard_map/ppermute | solution.py:36

commit v5 on v4

--- a/solution.py
+++ b/solution.py
@@ -10,8 +10,9 @@
 HALF = 2
 OWN, FAR, SIBLING, HANDED, PASSED, DIRECT = range(6)
 GROUPS = 6
-APART = (3, 2, 1)
+APART = (2, 3, 1)
 CHUNKS = 4
+SLOTS = 3
 
 
 def dom_permute(value, target):
@@ -48,7 +49,7 @@
     return placed
 
 
-def level_body(level, last, *refs):
+def solve_body(level, last, *refs):
     refs = list(refs)
     take = lambda count: [refs.pop(0) for _ in range(count)]
     (rep_ref,) = take(1)
@@ -59,10 +60,10 @@
     prev = take(level)
     (out_ref,) = take(1)
     if not last:
-        stored_ref, own_ref, sibling_ref, handed_ref, far_ref, chip_ref = take(6)
+        stored_ref, handed_ref = take(2)
     (solved_scr,) = take(1)
     if not last:
-        store_scr, acc_scr = take(2)
+        store_scr, acc_scr, chosen_ref = take(3)
     tiles, cols, _ = solved_scr.shape
     group = cols // 4
     if level == 0:
@@ -91,6 +92,35 @@
     for earlier in range(level):
         for t in range(tiles):
             store_scr[earlier * tiles + t] = prev[earlier][t]
+    for r in range(SLOTS):
+        chosen_ref[r] = 0
+    count = jnp.int32(0)
+    for p in range(mats_ref.shape[1]):
+        row = ids_ref[1, level, p] - HANDED * tiles
+        live = jnp.logical_and(row >= 0, row < tiles)
+        chosen_ref[jnp.minimum(count, SLOTS)] = jnp.int32(p)
+        count = count + live.astype(jnp.int32)
+    acc_scr[...] = jnp.zeros_like(acc_scr)
+    for r in range(SLOTS):
+        p = chosen_ref[r]
+        update = jnp.dot(
+            store_scr[ids_ref[0, level, p]], mats_ref[level, p], preferred_element_type=jnp.float32
+        )
+        row = jnp.where(r < count, ids_ref[1, level, p] - HANDED * tiles, tiles)
+        acc_scr[row] = acc_scr[row] + update
+    handed_ref[...] = acc_scr[:tiles].astype(jnp.bfloat16)
+
+
+def panels_body(level, *refs):
+    refs = list(refs)
+    take = lambda count: [refs.pop(0) for _ in range(count)]
+    ids_ref, mats_ref = take(2)
+    stores = take(level + 1)
+    own_ref, sibling_ref, far_ref, chip_ref, store_scr, acc_scr = refs
+    tiles = own_ref.shape[0]
+    for earlier in range(level + 1):
+        for t in range(tiles):
+            store_scr[earlier * tiles + t] = stores[earlier][t]
     acc_scr[...] = jnp.zeros_like(acc_scr)
     for p in range(mats_ref.shape[1]):
         update = jnp.dot(
@@ -104,44 +134,56 @@
 
     own_ref[...] = sums(OWN)
     sibling_ref[...] = sums(SIBLING)
-    handed_ref[...] = sums(HANDED)
     far_ref[...] = sums(FAR)
     chip_ref[0] = sums(PASSED)
     chip_ref[1] = sums(DIRECT)
 
 
-def run_level(level, last, rep, ids, parts, weights, prev, shape):
+def run_solve(level, last, rep, ids, parts, weights, prev, shape):
     levels, tiles, group, span = shape
     cols = 4 * group
     smem = pl.BlockSpec(memory_space=pltpu.SMEM)
     vmem = pl.BlockSpec(memory_space=pltpu.VMEM)
-    args = [rep]
-    specs = [smem]
-    if not last:
-        args.append(ids)
-        specs.append(smem)
+    scalars = [rep] if last else [rep, ids]
     inner = [*parts, *weights, *prev]
-    args += inner
-    specs += [vmem] * len(inner)
     scratch = [pltpu.VMEM((tiles, cols, span), jnp.float32)]
     if last:
         outs = jax.ShapeDtypeStruct(shape, jnp.float32)
         out_specs = vmem
     else:
-        outs = [jax.ShapeDtypeStruct((tiles, group, span), jnp.float32)] + [
-            jax.ShapeDtypeStruct((*lead, tiles, cols, span), jnp.bfloat16) for lead in ((), (), (), (), (), (2,))
-        ]
+        block = jax.ShapeDtypeStruct((tiles, cols, span), jnp.bfloat16)
+        outs = [jax.ShapeDtypeStruct((tiles, group, span), jnp.float32), block, block]
         out_specs = [vmem] * len(outs)
         scratch.append(pltpu.VMEM(((level + 1) * tiles, cols, span), jnp.bfloat16))
-        scratch.append(pltpu.VMEM((GROUPS * tiles + 1, cols, span), jnp.float32))
+        scratch.append(pltpu.VMEM((tiles + 1, cols, span), jnp.float32))
+        scratch.append(pltpu.SMEM((SLOTS + 1,), jnp.int32))
     return pl.pallas_call(
-        functools.partial(level_body, level, last),
+        functools.partial(solve_body, level, last),
         out_shape=outs,
-        in_specs=specs,
+        in_specs=[smem] * len(scalars) + [vmem] * len(inner),
         out_specs=out_specs,
         scratch_shapes=scratch,
         compiler_params=pltpu.CompilerParams(vmem_limit_bytes=6 << 20),
-    )(*args)
+    )(*scalars, *inner)
+
+
+def run_panels(level, ids, mats, stores):
+    smem = pl.BlockSpec(memory_space=pltpu.SMEM)
+    vmem = pl.BlockSpec(memory_space=pltpu.VMEM)
+    tiles, cols, span = stores[0].shape
+    return pl.pallas_call(
+        functools.partial(panels_body, level),
+        out_shape=[
+            jax.ShapeDtypeStruct((*lead, tiles, cols, span), jnp.bfloat16) for lead in ((), (), (), (2,))
+        ],
+        in_specs=[smem] + [vmem] * (1 + len(stores)),
+        out_specs=[vmem] * 4,
+        scratch_shapes=[
+            pltpu.VMEM(((level + 1) * tiles, cols, span), jnp.bfloat16),
+            pltpu.VMEM((GROUPS * tiles + 1, cols, span), jnp.float32),
+        ],
+        compiler_params=pltpu.CompilerParams(vmem_limit_bytes=6 << 20),
+    )(ids, mats, *stores)
 
 
 def slots_of(panel_dst, owner, dom_size, tiles):
@@ -167,7 +209,13 @@
 
 
 def fetch_body(dom_size, *refs):
-    owner_ref, _, src_ref, dst_ref, diag_hbm, mats_hbm, ids_ref, diag_ref, mats_ref, sems = refs
+    owner_ref, _, src_hbm, dst_hbm, diag_hbm, mats_hbm, ids_ref, diag_ref, mats_ref, dst_ref, sems = refs
+    lists = [
+        pltpu.make_async_copy(src_hbm, ids_ref.at[0], sems.at[2 + CHUNKS]),
+        pltpu.make_async_copy(dst_hbm, dst_ref, sems.at[3 + CHUNKS]),
+    ]
+    for copy in lists:
+        copy.start()
     copies = [pltpu.make_async_copy(diag_hbm.at[pl.ds(0, 1)], diag_ref.at[pl.ds(0, 1)], sems.at[0])]
     step = mats_ref.shape[1] // CHUNKS
     for chunk in range(CHUNKS):
@@ -180,7 +228,8 @@
     )
     for copy in copies:
         copy.start()
-    ids_ref[0] = src_ref[...]
+    for copy in lists:
+        copy.wait()
     ids_ref[1] = slots_of(dst_ref[...], owner_ref[0], dom_size, diag_ref.shape[1])
     for copy in copies:
         copy.wait()
@@ -197,9 +246,9 @@
             pltpu.VMEM((2, *diag.shape[1:]), diag.dtype),
             pltpu.VMEM((1, *mats.shape[1:]), mats.dtype),
         ],
-        in_specs=[pl.BlockSpec(memory_space=pltpu.SMEM), vmem, vmem, vmem, hbm, hbm],
+        in_specs=[pl.BlockSpec(memory_space=pltpu.SMEM), vmem, hbm, hbm, hbm, hbm],
         out_specs=[vmem, vmem, vmem],
-        scratch_shapes=[pltpu.SemaphoreType.DMA((2 + CHUNKS,))],
+        scratch_shapes=[pltpu.VMEM(dst.shape, dst.dtype), pltpu.SemaphoreType.DMA((4 + CHUNKS,))],
         compiler_params=pltpu.CompilerParams(vmem_limit_bytes=1 << 20),
     )(owner[None], after, src, dst, diag, mats)
 
@@ -215,9 +264,10 @@
     own_rhs = jnp.where(place, jnp.concatenate([right_sides] * rep_size, 2), 0.0)
     ids, early_diag, early_mats = fetch(
         partial,
-        panel_src,
-        panel_dst,
-        *(pltpu.with_memory_space_constraint(x, pltpu.HBM) for x in (diag_inverse, panel_mats)),
+        *(
+            pltpu.with_memory_space_constraint(x, pltpu.HBM)
+            for x in (panel_src, panel_dst, diag_inverse, panel_mats)
+        ),
     )
     late_diag, late_mats = (
         pltpu.with_memory_space_constraint(x, pltpu.VMEM) for x in (diag_inverse, panel_mats)
@@ -229,14 +279,15 @@
         parts = [partial] + [along_rep(partial, apart) for apart in APART]
         weights = [early_diag if level < 2 else late_diag, early_mats if level < 1 else late_mats]
         if last:
-            return run_level(
+            return run_solve(
                 level, last, rep[None], None, parts, weights[:1], results, right_sides.shape
             )
-        solved, stored, own, sibling, handed, far, chip = run_level(
+        solved, stored, handed = run_solve(
             level, last, rep[None], ids, parts, weights, store, right_sides.shape
         )
         results.append(solved)
         store.append(stored)
+        own, sibling, far, chip = run_panels(level, ids, weights[1], store)
         handed = jnp.where(top, to_sibling(handed), jnp.zeros_like(handed))
         from_chip = to_next_chip(
             (chip.astype(jnp.float32) + handed.astype(jnp.float32)).astype(jnp.bfloat16)

time: 79.5 us -> 76.1 us (0.957)
  waiting for transfers between devices: 31.5 us -> 27.7 us
  Pallas kernels: 10.6 us -> 12.9 us
  local copies, waits for them, and re-layouts: 2.17 us -> 0.81 us
    ppermute x12, waiting for transfers between devices: 19.9 us -> 14.8 us  [dom_permute(): lax.ppermute(value, 'dom', [(i, target(i) % size) for i in range(size)])]
    pallas_call x4 -> x7, Pallas kernels: 6.99 us -> 9.25 us  [the longest x4 4.75 us: run_solve(): pl.pallas_call(functools.partial(solve_body, level, last), out_shape=outs...]
    unnamed x18 -> x14, local copies, waits for them, and re-layouts: 1.4 us -> 0.03 us
    ppermute x12, starting transfers between devices: 17.6 us -> 16.4 us  [along_rep(): lax.ppermute(value, 'rep', [(i, i ^ apart) for i in range(lax.axis_size('...]
    ppermute x12, waiting for transfers between devices: 11.7 us -> 12.9 us  [along_rep(): lax.ppermute(value, 'rep', [(i, i ^ apart) for i in range(lax.axis_size('...]
  transfers between devices with their start and end apart: 24 -> 24, of which waited for: 15 -> 14; matrix products, arithmetic and copies ran while one was open for 0% -> 0% of each run, Pallas kernels for 5% -> 11%
where the time goes in v5:
time: 76.1 us; the launch traced here: 75.9 us
  starting transfers between devices  33.4 us (44%)
  waiting for transfers between devices  27.7 us (36%)
  Pallas kernels  12.9 us (17%)
  local copies, waits for them, and re-layouts  0.81 us (1%)
  other arithmetic  0.78 us (1%)
    ppermute x12, starting transfers between devices, dom_permute(): lax.ppermute(value, 'dom', [(i, target(i) % size) for i in range(size)])  17.1 us
    ppermute x12, starting transfers between devices, along_rep(): lax.ppermute(value, 'rep', [(i, i ^ apart) for i in range(lax.axis_size('...  16.4 us
    ppermute x12, waiting for transfers between devices, dom_permute(): lax.ppermute(value, 'dom', [(i, target(i) % size) for i in range(size)])  14.8 us
    ppermute x12, waiting for transfers between devices, along_rep(): lax.ppermute(value, 'rep', [(i, i ^ apart) for i in range(lax.axis_size('...  12.9 us
    pallas_call x4, Pallas kernels, run_solve(): pl.pallas_call(functools.partial(solve_body, level, last), out_shape=outs...  4.75 us
    pallas_call x3, Pallas kernels, run_panels(): pl.pallas_call(functools.partial(panels_body, level), out_shape=[jax.Shap...  4.5 us
    pallas_call x1, Pallas kernels, fetch(): pl.pallas_call(functools.partial(fetch_body, lax.axis_size('dom')), out_s...  3.66 us
  transfers between devices with their start and end apart: 24, of which 14 were waited for; matrix products, arithmetic and copies ran while one was open for 0% of the time, Pallas kernels for 11%

profile of v5, /device:TPU:0, one launch (start us, length us, event | category | flops | bytes accessed | tf_op | source)
XLA Modules:
  0.0 75.9 jit_solution(18102353896604040100)
XLA Ops:
  0.0 0.8 %fusion.15.refs_1_.refs_2_ = bf16[6,4,384]{2,1,0:T(4,128)(2,1)S(1)} fusion(f32[4,6,4,384]{3,2,1,0:T(4,128)} %param.5), kind=kLoop, calls=%fused_computation.36 | loop fusion | bytes 36864 | tf_op jit(solution)/shard_map/convert_element_type | solution.py:262
  0.8 4.0 %collective-permute-start = (bf16[6,4,384]{2,1,0:T(4,128)(2,1)S(1)}, bf16[6,4,384]{2,1,0:T(4,128)(2,1)S(1)}, u32[]{:S(2)}, u32[]{:S(2)}) collective-permute-start(bf16[6,4,384]{2,1,0:T(4,128)(2,1)S(1)} %fusion.15.refs_1_.refs_2_), channel_id=1, source_target_pairs={{0,2},{1,3},{2,0},{3,1},{4,6},{5,7},{6,4},{7,5},{8,10},{9,11},{10,... | collective-permute-start | bytes 55304 | tf_op jit(solution)/shard_map/ppermute | solution.py:37
  4.7 0.7 collective-permute-start.1
  5.5 0.3 collective-permute-start.2
  5.8 3.7 %shard_map.55 = (s32[2,3,16]{2,1,0:T(4,128)S(1)}, bf16[2,6,384,384]{3,2,1,0:T(8,128)(2,1)S(1)}, bf16[1,16,384,384]{3,2,1,0:T(8,128)(2,1)S(1)}) custom-call(s32[1]{0:T(128)} %bitcast.2.refs_0_, bf16[6,4,384]{2,1,0:T(4,128)(2,1)S(1)} %fusion.15.refs_1_.refs_2_, s32[3,16]{1,0:T(4,128)} %refs_2_.1, s32[3,16]{1,0:T(4,128)} %refs_3_.1, ...), custom_call_target="tpu_custom_call" | custom-call | tf_op jit(solution)/shard_map/pallas_call | solution.py:242
  9.4 0.0 copy-start
  9.4 0.0 collective-permute-done.refs_3_
  9.5 0.3 collective-permute-done.1.refs_4_
  9.7 0.0 collective-permute-done.2.refs_5_
  9.7 1.2 %shard_map.56 = (f32[6,4,384]{2,1,0:T(4,128)S(1)}, bf16[6,16,384]{2,1,0:T(8,128)(2,1)S(1)}, bf16[6,16,384]{2,1,0:T(8,128)(2,1)S(1)}) custom-call(s32[1]{0:T(128)} %bitcast.refs_0_, s32[2,3,16]{2,1,0:T(4,128)S(1)} %get-tuple-element.29.refs_1_.refs_0_, bf16[6,4,384]{2,1,0:T(4,128)(2,1)S(1)} %fusion.15.refs_1_.refs_2_, ...), custom_call_target="tpu_custom_call" | custom-call | tf_op jit(solution)/shard_map/pallas_call | solution.py:160
  11.0 0.1 collective-permute-start.3
  11.1 1.5 %shard_map.57 = (bf16[6,16,384]{2,1,0:T(8,128)(2,1)S(1)}, bf16[6,16,384]{2,1,0:T(8,128)(2,1)S(1)}, bf16[6,16,384]{2,1,0:T(8,128)(2,1)S(1)}, bf16[2,6,16,384]{3,2,1,0:T(8,128)(2,1)S(1)}) custom-call(s32[2,3,16]{2,1,0:T(4,128)S(1)} %get-tuple-element.29.refs_1_.refs_0_, bf16[1,16,384,384]{3,2,1,0:T(8,128)(2,1)S(1)} %get-tuple-element.31.refs_7_.refs_1_, ...), custom_call_target="tpu_custom_call" | custom-call | tf_op jit(solution)/shard_map/pallas_call | solution.py:174
  12.6 0.0 collective-permute-done.3
  12.6 0.1 add_convert_fusion.2
  12.7 5.3 %collective-permute-start.4 = (bf16[2,6,16,384]{3,2,1,0:T(8,128)(2,1)S(1)}, bf16[2,6,16,384]{3,2,1,0:T(8,128)(2,1)S(1)}, u32[]{:S(2)}, u32[]{:S(2)}) collective-permute-start(bf16[2,6,16,384]{3,2,1,0:T(8,128)(2,1)S(1)} %add_convert_fusion.2), channel_id=1, source_target_pairs={{0,120},{4,12},{8,0},{12,20},{16,8},{20,28},{24,16},{28,36},{32,24... | collective-permute-start | bytes 442376 | tf_op jit(solution)/shard_map/ppermute | solution.py:20
  18.0 0.7 collective-permute-start.5
  18.7 2.0 %collective-permute-done.4 = bf16[2,6,16,384]{3,2,1,0:T(8,128)(2,1)S(1)} collective-permute-done((bf16[2,6,16,384]{3,2,1,0:T(8,128)(2,1)S(1)}, bf16[2,6,16,384]{3,2,1,0:T(8,128)(2,1)S(1)}, u32[]{:S(2)}, u32[]{:S(2)}) %collective-permute-start.4) | collective-permute-done | bytes 147488 | tf_op jit(solution)/shard_map/ppermute | solution.py:20
  20.7 0.3 collective-permute-start.6
  21.0 0.1 maximum_select_fusion
  21.1 2.8 %collective-permute-done.5 = bf16[6,16,384]{2,1,0:T(8,128)(2,1)S(1)} collective-permute-done((bf16[6,16,384]{2,1,0:T(8,128)(2,1)S(1)}, bf16[6,16,384]{2,1,0:T(8,128)(2,1)S(1)}, u32[]{:S(2)}, u32[]{:S(2)}) %collective-permute-start.5) | collective-permute-done | bytes 73760 | tf_op jit(solution)/shard_map/ppermute | solution.py:20
  23.9 0.0 collective-permute-done.6
  23.9 0.1 fusion.3.refs_2_
  24.0 0.0 slice-start.5
  24.0 3.5 %collective-permute-start.7 = (bf16[6,16,384]{2,1,0:T(8,128)(2,1)S(1)}, bf16[6,16,384]{2,1,0:T(8,128)(2,1)S(1)}, u32[]{:S(2)}, u32[]{:S(2)}) collective-permute-start(bf16[6,16,384]{2,1,0:T(8,128)(2,1)S(1)} %fusion.3.refs_2_), channel_id=1, source_target_pairs={{0,2},{1,3},{2,0},{3,1},{4,6},{5,7},{6,4},{7,5},{8,10},{9,11},{10,... | collective-permute-start | bytes 221192 | tf_op jit(solution)/shard_map/ppermute | solution.py:37
  27.5 0.7 collective-permute-start.8
  28.3 0.0 collective-permute-start.9
  28.3 1.8 %collective-permute-done.7.refs_3_ = bf16[6,16,384]{2,1,0:T(8,128)(2,1)S(1)} collective-permute-done((bf16[6,16,384]{2,1,0:T(8,128)(2,1)S(1)}, bf16[6,16,384]{2,1,0:T(8,128)(2,1)S(1)}, u32[]{:S(2)}, u32[]{:S(2)}) %collective-permute-start.7) | collective-permute-done | bytes 73760 | tf_op jit(solution)/shard_map/ppermute | solution.py:37
  30.0 3.1 %collective-permute-done.8.refs_4_ = bf16[6,16,384]{2,1,0:T(8,128)(2,1)S(1)} collective-permute-done((bf16[6,16,384]{2,1,0:T(8,128)(2,1)S(1)}, bf16[6,16,384]{2,1,0:T(8,128)(2,1)S(1)}, u32[]{:S(2)}, u32[]{:S(2)}) %collective-permute-start.8) | collective-permute-done | bytes 73760 | tf_op jit(solution)/shard_map/ppermute | solution.py:37
  33.1 0.0 collective-permute-done.9.refs_5_
  33.1 1.2 %shard_map.58 = (f32[6,4,384]{2,1,0:T(4,128)S(1)}, bf16[6,16,384]{2,1,0:T(8,128)(2,1)S(1)}, bf16[6,16,384]{2,1,0:T(8,128)(2,1)S(1)}) custom-call(s32[1]{0:T(128)} %bitcast.refs_0_, s32[2,3,16]{2,1,0:T(4,128)S(1)} %get-tuple-element.29.refs_1_.refs_0_, bf16[6,16,384]{2,1,0:T(8,128)(2,1)S(1)} %fusion.3.refs_2_, ...), custom_call_target="tpu_custom_call" | custom-call | tf_op jit(solution)/shard_map/pallas_call | solution.py:160
  34.4 0.1 collective-permute-start.10
  34.5 1.5 %shard_map.59 = (bf16[6,16,384]{2,1,0:T(8,128)(2,1)S(1)}, bf16[6,16,384]{2,1,0:T(8,128)(2,1)S(1)}, bf16[6,16,384]{2,1,0:T(8,128)(2,1)S(1)}, bf16[2,6,16,384]{3,2,1,0:T(8,128)(2,1)S(1)}) custom-call(s32[2,3,16]{2,1,0:T(4,128)S(1)} %get-tuple-element.29.refs_1_.refs_0_, bf16[3,16,384,384]{3,2,1,0:T(8,128)(2,1)S(1)} %bitcast.53, ...), custom_call_target="tpu_custom_call" | custom-call | tf_op jit(solution)/shard_map/pallas_call | solution.py:174
  36.0 0.0 collective-permute-done.10
  36.0 0.1 add_convert_fusion.1
  36.1 4.8 %collective-permute-start.11 = (bf16[2,6,16,384]{3,2,1,0:T(8,128)(2,1)S(1)}, bf16[2,6,16,384]{3,2,1,0:T(8,128)(2,1)S(1)}, u32[]{:S(2)}, u32[]{:S(2)}) collective-permute-start(bf16[2,6,16,384]{3,2,1,0:T(8,128)(2,1)S(1)} %add_convert_fusion.1), channel_id=1, source_target_pairs={{0,120},{4,12},{8,0},{12,20},{16,8},{20,28},{24,16},{28,36},{32,24... | collective-permute-start | bytes 442376 | tf_op jit(solution)/shard_map/ppermute | solution.py:20
  40.9 0.0 collective-permute-start.12
  40.9 2.7 %collective-permute-done.11 = bf16[2,6,16,384]{3,2,1,0:T(8,128)(2,1)S(1)} collective-permute-done((bf16[2,6,16,384]{3,2,1,0:T(8,128)(2,1)S(1)}, bf16[2,6,16,384]{3,2,1,0:T(8,128)(2,1)S(1)}, u32[]{:S(2)}, u32[]{:S(2)}) %collective-permute-start.11) | collective-permute-done | bytes 147488 | tf_op jit(solution)/shard_map/ppermute | solution.py:20
  43.6 0.5 collective-permute-start.13
  44.1 2.7 %collective-permute-done.12 = bf16[6,16,384]{2,1,0:T(8,128)(2,1)S(1)} collective-permute-done((bf16[6,16,384]{2,1,0:T(8,128)(2,1)S(1)}, bf16[6,16,384]{2,1,0:T(8,128)(2,1)S(1)}, u32[]{:S(2)}, u32[]{:S(2)}) %collective-permute-start.12) | collective-permute-done | bytes 73760 | tf_op jit(solution)/shard_map/ppermute | solution.py:20
  46.8 0.0 collective-permute-done.13
  46.8 0.1 fusion.1.refs_2_
  46.8 1.5 %collective-permute-start.14 = (bf16[6,16,384]{2,1,0:T(8,128)(2,1)S(1)}, bf16[6,16,384]{2,1,0:T(8,128)(2,1)S(1)}, u32[]{:S(2)}, u32[]{:S(2)}) collective-permute-start(bf16[6,16,384]{2,1,0:T(8,128)(2,1)S(1)} %fusion.1.refs_2_), channel_id=1, source_target_pairs={{0,2},{1,3},{2,0},{3,1},{4,6},{5,7},{6,4},{7,5},{8,10},{9,11},{10,... | collective-permute-start | bytes 221192 | tf_op jit(solution)/shard_map/ppermute | solution.py:37
  48.4 1.6 %collective-permute-start.15 = (bf16[6,16,384]{2,1,0:T(8,128)(2,1)S(1)}, bf16[6,16,384]{2,1,0:T(8,128)(2,1)S(1)}, u32[]{:S(2)}, u32[]{:S(2)}) collective-permute-start(bf16[6,16,384]{2,1,0:T(8,128)(2,1)S(1)} %fusion.1.refs_2_), channel_id=1, source_target_pairs={{0,3},{1,2},{2,1},{3,0},{4,7},{5,6},{6,5},{7,4},{8,11},{9,10},{10,... | collective-permute-start | bytes 221192 | tf_op jit(solution)/shard_map/ppermute | solution.py:37
  49.9 0.5 collective-permute-start.16
  50.4 2.8 %collective-permute-done.14.refs_3_ = bf16[6,16,384]{2,1,0:T(8,128)(2,1)S(1)} collective-permute-done((bf16[6,16,384]{2,1,0:T(8,128)(2,1)S(1)}, bf16[6,16,384]{2,1,0:T(8,128)(2,1)S(1)}, u32[]{:S(2)}, u32[]{:S(2)}) %collective-permute-start.14) | collective-permute-done | bytes 73760 | tf_op jit(solution)/shard_map/ppermute | solution.py:37
  53.3 0.8 %collective-permute-done.15.refs_4_ = bf16[6,16,384]{2,1,0:T(8,128)(2,1)S(1)} collective-permute-done((bf16[6,16,384]{2,1,0:T(8,128)(2,1)S(1)}, bf16[6,16,384]{2,1,0:T(8,128)(2,1)S(1)}, u32[]{:S(2)}, u32[]{:S(2)}) %collective-permute-start.15) | collective-permute-done | bytes 73760 | tf_op jit(solution)/shard_map/ppermute | solution.py:37
  54.0 0.2 collective-permute-done.16.refs_5_
  54.3 1.2 %shard_map.60 = (f32[6,4,384]{2,1,0:T(4,128)S(1)}, bf16[6,16,384]{2,1,0:T(8,128)(2,1)S(1)}, bf16[6,16,384]{2,1,0:T(8,128)(2,1)S(1)}) custom-call(s32[1]{0:T(128)} %bitcast.refs_0_, s32[2,3,16]{2,1,0:T(4,128)S(1)} %get-tuple-element.29.refs_1_.refs_0_, bf16[6,16,384]{2,1,0:T(8,128)(2,1)S(1)} %fusion.1.refs_2_, ...), custom_call_target="tpu_custom_call" | custom-call | tf_op jit(solution)/shard_map/pallas_call | solution.py:160
  55.5 0.1 collective-permute-start.17
  55.6 1.5 %shard_map.61 = (bf16[6,16,384]{2,1,0:T(8,128)(2,1)S(1)}, bf16[6,16,384]{2,1,0:T(8,128)(2,1)S(1)}, bf16[6,16,384]{2,1,0:T(8,128)(2,1)S(1)}, bf16[2,6,16,384]{3,2,1,0:T(8,128)(2,1)S(1)}) custom-call(s32[2,3,16]{2,1,0:T(4,128)S(1)} %get-tuple-element.29.refs_1_.refs_0_, bf16[3,16,384,384]{3,2,1,0:T(8,128)(2,1)S(1)} %bitcast.53, ...), custom_call_target="tpu_custom_call" | custom-call | tf_op jit(solution)/shard_map/pallas_call | solution.py:174
  57.1 0.1 add_convert_fusion
  57.3 4.1 %collective-permute-start.18 = (bf16[2,6,16,384]{3,2,1,0:T(8,128)(2,1)S(1)}, bf16[2,6,16,384]{3,2,1,0:T(8,128)(2,1)S(1)}, u32[]{:S(2)}, u32[]{:S(2)}) collective-permute-start(bf16[2,6,16,384]{3,2,1,0:T(8,128)(2,1)S(1)} %add_convert_fusion), channel_id=1, source_target_pairs={{0,120},{4,12},{8,0},{12,20},{16,8},{20,28},{24,16},{28,36},{32,24... | collective-permute-start | bytes 442376 | tf_op jit(solution)/shard_map/ppermute | solution.py:20
  61.4 2.7 %collective-permute-done.18 = bf16[2,6,16,384]{3,2,1,0:T(8,128)(2,1)S(1)} collective-permute-done((bf16[2,6,16,384]{3,2,1,0:T(8,128)(2,1)S(1)}, bf16[2,6,16,384]{3,2,1,0:T(8,128)(2,1)S(1)}, u32[]{:S(2)}, u32[]{:S(2)}) %collective-permute-start.18) | collective-permute-done | bytes 147488 | tf_op jit(solution)/shard_map/ppermute | solution.py:20
  64.1 1.1 %collective-permute-start.20 = (bf16[6,16,384]{2,1,0:T(8,128)(2,1)S(1)}, bf16[6,16,384]{2,1,0:T(8,128)(2,1)S(1)}, u32[]{:S(2)}, u32[]{:S(2)}) collective-permute-start(bf16[6,16,384]{2,1,0:T(8,128)(2,1)S(1)} %fusion.6), channel_id=1, source_target_pairs={{0,4},{4,0},{8,12},{12,8},{16,20},{20,16},{24,28},{28,24},{32,36},... | collective-permute-start | bytes 221192 | tf_op jit(solution)/shard_map/ppermute | solution.py:20
  65.2 2.0 %collective-permute-done.19 = bf16[6,16,384]{2,1,0:T(8,128)(2,1)S(1)} collective-permute-done((bf16[6,16,384]{2,1,0:T(8,128)(2,1)S(1)}, bf16[6,16,384]{2,1,0:T(8,128)(2,1)S(1)}, u32[]{:S(2)}, u32[]{:S(2)}) %collective-permute-start.19) | collective-permute-done | bytes 73760 | tf_op jit(solution)/shard_map/ppermute | solution.py:20
  67.3 0.0 collective-permute-done.20
  67.3 0.1 fusion.5.refs_1_
  67.3 1.9 %collective-permute-start.21 = (bf16[6,16,384]{2,1,0:T(8,128)(2,1)S(1)}, bf16[6,16,384]{2,1,0:T(8,128)(2,1)S(1)}, u32[]{:S(2)}, u32[]{:S(2)}) collective-permute-start(bf16[6,16,384]{2,1,0:T(8,128)(2,1)S(1)} %fusion.5.refs_1_), channel_id=1, source_target_pairs={{0,2},{1,3},{2,0},{3,1},{4,6},{5,7},{6,4},{7,5},{8,10},{9,11},{10,... | collective-permute-start | bytes 221192 | tf_op jit(solution)/shard_map/ppermute | solution.py:37
  69.2 1.2 %collective-permute-start.22 = (bf16[6,16,384]{2,1,0:T(8,128)(2,1)S(1)}, bf16[6,16,384]{2,1,0:T(8,128)(2,1)S(1)}, u32[]{:S(2)}, u32[]{:S(2)}) collective-permute-start(bf16[6,16,384]{2,1,0:T(8,128)(2,1)S(1)} %fusion.5.refs_1_), channel_id=1, source_target_pairs={{0,3},{1,2},{2,1},{3,0},{4,7},{5,6},{6,5},{7,4},{8,11},{9,10},{10,... | collective-permute-start | bytes 221192 | tf_op jit(solution)/shard_map/ppermute | solution.py:37
  70.5 0.4 collective-permute-start.23
  70.9 2.5 %collective-permute-done.21.refs_2_ = bf16[6,16,384]{2,1,0:T(8,128)(2,1)S(1)} collective-permute-done((bf16[6,16,384]{2,1,0:T(8,128)(2,1)S(1)}, bf16[6,16,384]{2,1,0:T(8,128)(2,1)S(1)}, u32[]{:S(2)}, u32[]{:S(2)}) %collective-permute-start.21) | collective-permute-done | bytes 73760 | tf_op jit(solution)/shard_map/ppermute | solution.py:37
  73.4 1.4 %collective-permute-done.22.refs_3_ = bf16[6,16,384]{2,1,0:T(8,128)(2,1)S(1)} collective-permute-done((bf16[6,16,384]{2,1,0:T(8,128)(2,1)S(1)}, bf16[6,16,384]{2,1,0:T(8,128)(2,1)S(1)}, u32[]{:S(2)}, u32[]{:S(2)}) %collective-permute-start.22) | collective-permute-done | bytes 73760 | tf_op jit(solution)/shard_map/ppermute | solution.py:37
  74.8 0.0 collective-permute-done.23.refs_4_
  74.8 1.1 %shard_map.62 = f32[4,6,4,384]{3,2,1,0:T(4,128)} custom-call(s32[1]{0:T(128)} %bitcast.refs_0_, bf16[6,16,384]{2,1,0:T(8,128)(2,1)S(1)} %fusion.5.refs_1_, bf16[6,16,384]{2,1,0:T(8,128)(2,1)S(1)} %collective-permute-done.21.refs_2_, bf16[6,16,384]{2,1,0:T(8,128)(2,1)S(1)} %collective-permute-done.22.refs_3_, ...), custom_call_target="tpu_custom_call" | custom-call | tf_op jit(solution)/shard_map/pallas_call | solution.py:160
  (22 shorter events, 0.1 us)
Async XLA Ops:
  0.8 8.7 %collective-permute-start = (bf16[6,4,384]{2,1,0:T(4,128)(2,1)S(1)}, bf16[6,4,384]{2,1,0:T(4,128)(2,1)S(1)}, u32[]{:S(2)}, u32[]{:S(2)}) collective-permute-start(bf16[6,4,384]{2,1,0:T(4,128)(2,1)S(1)} %fusion.15.refs_1_.refs_2_), channel_id=1, source_target_pairs={{0,2},{1,3},{2,0},{3,1},{4,6},{5,7},{6,4},{7,5},{8,10},{9,11},{10,... | collective-permute-start | bytes 55304 | tf_op jit(solution)/shard_map/ppermute | solution.py:37
  4.7 5.0 %collective-permute-start.1 = (bf16[6,4,384]{2,1,0:T(4,128)(2,1)S(1)}, bf16[6,4,384]{2,1,0:T(4,128)(2,1)S(1)}, u32[]{:S(2)}, u32[]{:S(2)}) collective-permute-start(bf16[6,4,384]{2,1,0:T(4,128)(2,1)S(1)} %fusion.15.refs_1_.refs_2_), channel_id=1, source_target_pairs={{0,3},{1,2},{2,1},{3,0},{4,7},{5,6},{6,5},{7,4},{8,11},{9,10},{10,... | collective-permute-start | bytes 55304 | tf_op jit(solution)/shard_map/ppermute | solution.py:37
  5.5 4.3 %collective-permute-start.2 = (bf16[6,4,384]{2,1,0:T(4,128)(2,1)S(1)}, bf16[6,4,384]{2,1,0:T(4,128)(2,1)S(1)}, u32[]{:S(2)}, u32[]{:S(2)}) collective-permute-start(bf16[6,4,384]{2,1,0:T(4,128)(2,1)S(1)} %fusion.15.refs_1_.refs_2_), channel_id=1, source_target_pairs={{0,1},{1,0},{2,3},{3,2},{4,5},{5,4},{6,7},{7,6},{8,9},{9,8},{10,11... | collective-permute-start | bytes 55304 | tf_op jit(solution)/shard_map/ppermute | solution.py:37
  5.8 27.4 %slice-start = ((s8[14155776]{0:T(1024)(128)(4,1)}), s8[4194304]{0:T(1024)(128)(4,1)S(1)}, s32[]{:S(2)}) async-start(s8[14155776]{0:T(1024)(128)(4,1)} %bitcast.52), calls=%async_computation | async-start | bytes 8388608
  5.8 27.4 %slice-start.1 = ((s8[14155776]{0:T(1024)(128)(4,1)}), s8[4194304]{0:T(1024)(128)(4,1)S(1)}, s32[]{:S(2)}) async-start(s8[14155776]{0:T(1024)(128)(4,1)} %bitcast.52), calls=%async_computation.1 | async-start | bytes 8388608
  5.8 27.4 %slice-start.2 = ((s8[14155776]{0:T(1024)(128)(4,1)}), s8[4194304]{0:T(1024)(128)(4,1)S(1)}, s32[]{:S(2)}) async-start(s8[14155776]{0:T(1024)(128)(4,1)} %bitcast.52), calls=%async_computation.2 | async-start | bytes 8388608
  9.4 11.5 %copy-start = (f32[4,6,4,384]{3,2,1,0:T(4,128)S(1)}, f32[4,6,4,384]{3,2,1,0:T(4,128)}, u32[]{:S(2)}) copy-start(f32[4,6,4,384]{3,2,1,0:T(4,128)} %param.5) | copy-start | bytes 442372
  9.7 23.4 %slice-start.3 = ((s8[14155776]{0:T(1024)(128)(4,1)}), s8[1572864]{0:T(1024)(128)(4,1)S(1)}, s32[]{:S(2)}) async-start(s8[14155776]{0:T(1024)(128)(4,1)} %bitcast.52), calls=%async_computation.3 | async-start | bytes 3145728
  11.0 1.6 %collective-permute-start.3 = (bf16[6,16,384]{2,1,0:T(8,128)(2,1)S(1)}, bf16[6,16,384]{2,1,0:T(8,128)(2,1)S(1)}, u32[]{:S(2)}, u32[]{:S(2)}) collective-permute-start(bf16[6,16,384]{2,1,0:T(8,128)(2,1)S(1)} %get-tuple-element.35), channel_id=1, source_target_pairs={{0,4},{4,0},{8,12},{12,8},{16,20},{20,16},{24,28},{28,24},{32,36},... | collective-permute-start | bytes 221192 | tf_op jit(solution)/shard_map/ppermute | solution.py:20
  12.7 8.0 %collective-permute-start.4 = (bf16[2,6,16,384]{3,2,1,0:T(8,128)(2,1)S(1)}, bf16[2,6,16,384]{3,2,1,0:T(8,128)(2,1)S(1)}, u32[]{:S(2)}, u32[]{:S(2)}) collective-permute-start(bf16[2,6,16,384]{3,2,1,0:T(8,128)(2,1)S(1)} %add_convert_fusion.2), channel_id=1, source_target_pairs={{0,120},{4,12},{8,0},{12,20},{16,8},{20,28},{24,16},{28,36},{32,24... | collective-permute-start | bytes 442376 | tf_op jit(solution)/shard_map/ppermute | solution.py:20
  18.0 5.9 %collective-permute-start.5 = (bf16[6,16,384]{2,1,0:T(8,128)(2,1)S(1)}, bf16[6,16,384]{2,1,0:T(8,128)(2,1)S(1)}, u32[]{:S(2)}, u32[]{:S(2)}) collective-permute-start(bf16[6,16,384]{2,1,0:T(8,128)(2,1)S(1)} %get-tuple-element.36), channel_id=1, source_target_pairs={{0,64},{4,68},{8,72},{12,76},{16,80},{20,84},{24,88},{28,92},{32,9... | collective-permute-start | bytes 221192 | tf_op jit(solution)/shard_map/ppermute | solution.py:20
  20.7 3.3 %collective-permute-start.6 = (bf16[6,16,384]{2,1,0:T(8,128)(2,1)S(1)}, bf16[6,16,384]{2,1,0:T(8,128)(2,1)S(1)}, u32[]{:S(2)}, u32[]{:S(2)}) collective-permute-start(bf16[6,16,384]{2,1,0:T(8,128)(2,1)S(1)} %fusion.12), channel_id=1, source_target_pairs={{0,4},{4,0},{8,12},{12,8},{16,20},{20,16},{24,28},{28,24},{32,36},... | collective-permute-start | bytes 221192 | tf_op jit(solution)/shard_map/ppermute | solution.py:20
  21.0 33.3 %slice-start.4 = ((s8[7077888]{0:T(1024)(128)(4,1)}), s8[4194304]{0:T(1024)(128)(4,1)S(1)}, s32[]{:S(2)}) async-start(s8[7077888]{0:T(1024)(128)(4,1)} %bitcast.54), calls=%async_computation.4 | async-start | bytes 8388608
  24.0 30.3 %slice-start.5 = ((s8[7077888]{0:T(1024)(128)(4,1)}), s8[2883584]{0:T(1024)(128)(4,1)S(1)}, s32[]{:S(2)}) async-start(s8[7077888]{0:T(1024)(128)(4,1)} %bitcast.54), calls=%async_computation.5 | async-start | bytes 5767168
  24.0 6.0 %collective-permute-start.7 = (bf16[6,16,384]{2,1,0:T(8,128)(2,1)S(1)}, bf16[6,16,384]{2,1,0:T(8,128)(2,1)S(1)}, u32[]{:S(2)}, u32[]{:S(2)}) collective-permute-start(bf16[6,16,384]{2,1,0:T(8,128)(2,1)S(1)} %fusion.3.refs_2_), channel_id=1, source_target_pairs={{0,2},{1,3},{2,0},{3,1},{4,6},{5,7},{6,4},{7,5},{8,10},{9,11},{10,... | collective-permute-start | bytes 221192 | tf_op jit(solution)/shard_map/ppermute | solution.py:37
  27.5 5.6 %collective-permute-start.8 = (bf16[6,16,384]{2,1,0:T(8,128)(2,1)S(1)}, bf16[6,16,384]{2,1,0:T(8,128)(2,1)S(1)}, u32[]{:S(2)}, u32[]{:S(2)}) collective-permute-start(bf16[6,16,384]{2,1,0:T(8,128)(2,1)S(1)} %fusion.3.refs_2_), channel_id=1, source_target_pairs={{0,3},{1,2},{2,1},{3,0},{4,7},{5,6},{6,5},{7,4},{8,11},{9,10},{10,... | collective-permute-start | bytes 221192 | tf_op jit(solution)/shard_map/ppermute | solution.py:37
  28.3 4.9 %collective-permute-start.9 = (bf16[6,16,384]{2,1,0:T(8,128)(2,1)S(1)}, bf16[6,16,384]{2,1,0:T(8,128)(2,1)S(1)}, u32[]{:S(2)}, u32[]{:S(2)}) collective-permute-start(bf16[6,16,384]{2,1,0:T(8,128)(2,1)S(1)} %fusion.3.refs_2_), channel_id=1, source_target_pairs={{0,1},{1,0},{2,3},{3,2},{4,5},{5,4},{6,7},{7,6},{8,9},{9,8},{10,11... | collective-permute-start | bytes 221192 | tf_op jit(solution)/shard_map/ppermute | solution.py:37
  34.4 1.6 %collective-permute-start.10 = (bf16[6,16,384]{2,1,0:T(8,128)(2,1)S(1)}, bf16[6,16,384]{2,1,0:T(8,128)(2,1)S(1)}, u32[]{:S(2)}, u32[]{:S(2)}) collective-permute-start(bf16[6,16,384]{2,1,0:T(8,128)(2,1)S(1)} %get-tuple-element.41), channel_id=1, source_target_pairs={{0,4},{4,0},{8,12},{12,8},{16,20},{20,16},{24,28},{28,24},{32,36},... | collective-permute-start | bytes 221192 | tf_op jit(solution)/shard_map/ppermute | solution.py:20
  36.1 7.5 %collective-permute-start.11 = (bf16[2,6,16,384]{3,2,1,0:T(8,128)(2,1)S(1)}, bf16[2,6,16,384]{3,2,1,0:T(8,128)(2,1)S(1)}, u32[]{:S(2)}, u32[]{:S(2)}) collective-permute-start(bf16[2,6,16,384]{3,2,1,0:T(8,128)(2,1)S(1)} %add_convert_fusion.1), channel_id=1, source_target_pairs={{0,120},{4,12},{8,0},{12,20},{16,8},{20,28},{24,16},{28,36},{32,24... | collective-permute-start | bytes 442376 | tf_op jit(solution)/shard_map/ppermute | solution.py:20
  40.9 5.9 %collective-permute-start.12 = (bf16[6,16,384]{2,1,0:T(8,128)(2,1)S(1)}, bf16[6,16,384]{2,1,0:T(8,128)(2,1)S(1)}, u32[]{:S(2)}, u32[]{:S(2)}) collective-permute-start(bf16[6,16,384]{2,1,0:T(8,128)(2,1)S(1)} %get-tuple-element.42), channel_id=1, source_target_pairs={{0,64},{4,68},{8,72},{12,76},{16,80},{20,84},{24,88},{28,92},{32,9... | collective-permute-start | bytes 221192 | tf_op jit(solution)/shard_map/ppermute | solution.py:20
  43.6 3.2 %collective-permute-start.13 = (bf16[6,16,384]{2,1,0:T(8,128)(2,1)S(1)}, bf16[6,16,384]{2,1,0:T(8,128)(2,1)S(1)}, u32[]{:S(2)}, u32[]{:S(2)}) collective-permute-start(bf16[6,16,384]{2,1,0:T(8,128)(2,1)S(1)} %fusion.9), channel_id=1, source_target_pairs={{0,4},{4,0},{8,12},{12,8},{16,20},{20,16},{24,28},{28,24},{32,36},... | collective-permute-start | bytes 221192 | tf_op jit(solution)/shard_map/ppermute | solution.py:20
  46.8 6.4 %collective-permute-start.14 = (bf16[6,16,384]{2,1,0:T(8,128)(2,1)S(1)}, bf16[6,16,384]{2,1,0:T(8,128)(2,1)S(1)}, u32[]{:S(2)}, u32[]{:S(2)}) collective-permute-start(bf16[6,16,384]{2,1,0:T(8,128)(2,1)S(1)} %fusion.1.refs_2_), channel_id=1, source_target_pairs={{0,2},{1,3},{2,0},{3,1},{4,6},{5,7},{6,4},{7,5},{8,10},{9,11},{10,... | collective-permute-start | bytes 221192 | tf_op jit(solution)/shard_map/ppermute | solution.py:37
  48.4 5.7 %collective-permute-start.15 = (bf16[6,16,384]{2,1,0:T(8,128)(2,1)S(1)}, bf16[6,16,384]{2,1,0:T(8,128)(2,1)S(1)}, u32[]{:S(2)}, u32[]{:S(2)}) collective-permute-start(bf16[6,16,384]{2,1,0:T(8,128)(2,1)S(1)} %fusion.1.refs_2_), channel_id=1, source_target_pairs={{0,3},{1,2},{2,1},{3,0},{4,7},{5,6},{6,5},{7,4},{8,11},{9,10},{10,... | collective-permute-start | bytes 221192 | tf_op jit(solution)/shard_map/ppermute | solution.py:37
  49.9 4.4 %collective-permute-start.16 = (bf16[6,16,384]{2,1,0:T(8,128)(2,1)S(1)}, bf16[6,16,384]{2,1,0:T(8,128)(2,1)S(1)}, u32[]{:S(2)}, u32[]{:S(2)}) collective-permute-start(bf16[6,16,384]{2,1,0:T(8,128)(2,1)S(1)} %fusion.1.refs_2_), channel_id=1, source_target_pairs={{0,1},{1,0},{2,3},{3,2},{4,5},{5,4},{6,7},{7,6},{8,9},{9,8},{10,11... | collective-permute-start | bytes 221192 | tf_op jit(solution)/shard_map/ppermute | solution.py:37
  55.5 1.6 %collective-permute-start.17 = (bf16[6,16,384]{2,1,0:T(8,128)(2,1)S(1)}, bf16[6,16,384]{2,1,0:T(8,128)(2,1)S(1)}, u32[]{:S(2)}, u32[]{:S(2)}) collective-permute-start(bf16[6,16,384]{2,1,0:T(8,128)(2,1)S(1)} %get-tuple-element.47), channel_id=1, source_target_pairs={{0,4},{4,0},{8,12},{12,8},{16,20},{20,16},{24,28},{28,24},{32,36},... | collective-permute-start | bytes 221192 | tf_op jit(solution)/shard_map/ppermute | solution.py:20
  57.3 6.8 %collective-permute-start.18 = (bf16[2,6,16,384]{3,2,1,0:T(8,128)(2,1)S(1)}, bf16[2,6,16,384]{3,2,1,0:T(8,128)(2,1)S(1)}, u32[]{:S(2)}, u32[]{:S(2)}) collective-permute-start(bf16[2,6,16,384]{3,2,1,0:T(8,128)(2,1)S(1)} %add_convert_fusion), channel_id=1, source_target_pairs={{0,120},{4,12},{8,0},{12,20},{16,8},{20,28},{24,16},{28,36},{32,24... | collective-permute-start | bytes 442376 | tf_op jit(solution)/shard_map/ppermute | solution.py:20
  61.4 5.9 %collective-permute-start.19 = (bf16[6,16,384]{2,1,0:T(8,128)(2,1)S(1)}, bf16[6,16,384]{2,1,0:T(8,128)(2,1)S(1)}, u32[]{:S(2)}, u32[]{:S(2)}) collective-permute-start(bf16[6,16,384]{2,1,0:T(8,128)(2,1)S(1)} %get-tuple-element.48), channel_id=1, source_target_pairs={{0,64},{4,68},{8,72},{12,76},{16,80},{20,84},{24,88},{28,92},{32,9... | collective-permute-start | bytes 221192 | tf_op jit(solution)/shard_map/ppermute | solution.py:20
  64.1 3.2 %collective-permute-start.20 = (bf16[6,16,384]{2,1,0:T(8,128)(2,1)S(1)}, bf16[6,16,384]{2,1,0:T(8,128)(2,1)S(1)}, u32[]{:S(2)}, u32[]{:S(2)}) collective-permute-start(bf16[6,16,384]{2,1,0:T(8,128)(2,1)S(1)} %fusion.6), channel_id=1, source_target_pairs={{0,4},{4,0},{8,12},{12,8},{16,20},{20,16},{24,28},{28,24},{32,36},... | collective-permute-start | bytes 221192 | tf_op jit(solution)/shard_map/ppermute | solution.py:20
  67.3 6.0 %collective-permute-start.21 = (bf16[6,16,384]{2,1,0:T(8,128)(2,1)S(1)}, bf16[6,16,384]{2,1,0:T(8,128)(2,1)S(1)}, u32[]{:S(2)}, u32[]{:S(2)}) collective-permute-start(bf16[6,16,384]{2,1,0:T(8,128)(2,1)S(1)} %fusion.5.refs_1_), channel_id=1, source_target_pairs={{0,2},{1,3},{2,0},{3,1},{4,6},{5,7},{6,4},{7,5},{8,10},{9,11},{10,... | collective-permute-start | bytes 221192 | tf_op jit(solution)/shard_map/ppermute | solution.py:37
  69.2 5.6 %collective-permute-start.22 = (bf16[6,16,384]{2,1,0:T(8,128)(2,1)S(1)}, bf16[6,16,384]{2,1,0:T(8,128)(2,1)S(1)}, u32[]{:S(2)}, u32[]{:S(2)}) collective-permute-start(bf16[6,16,384]{2,1,0:T(8,128)(2,1)S(1)} %fusion.5.refs_1_), channel_id=1, source_target_pairs={{0,3},{1,2},{2,1},{3,0},{4,7},{5,6},{6,5},{7,4},{8,11},{9,10},{10,... | collective-permute-start | bytes 221192 | tf_op jit(solution)/shard_map/ppermute | solution.py:37
  70.5 4.4 %collective-permute-start.23 = (bf16[6,16,384]{2,1,0:T(8,128)(2,1)S(1)}, bf16[6,16,384]{2,1,0:T(8,128)(2,1)S(1)}, u32[]{:S(2)}, u32[]{:S(2)}) collective-permute-start(bf16[6,16,384]{2,1,0:T(8,128)(2,1)S(1)} %fusion.5.refs_1_), channel_id=1, source_target_pairs={{0,1},{1,0},{2,3},{3,2},{4,5},{5,4},{6,7},{7,6},{8,9},{9,8},{10,11... | collective-permute-start | bytes 221192 | tf_op jit(solution)/shard_map/ppermute | solution.py:37

commit v6 on v5

--- a/solution.py
+++ b/solution.py
@@ -75,7 +75,7 @@
             sum(part[t].astype(jnp.float32) for part in parts).astype(jnp.bfloat16) for t in range(tiles)
         ]
     for t in range(tiles):
-        solved = jnp.dot(residuals[t], diag_ref[level, t], preferred_element_type=jnp.float32)
+        solved = jnp.dot(residuals[t], diag_ref[0, t], preferred_element_type=jnp.float32)
         solved_scr[t] = solved
         if not last:
             stored_ref[t] = solved.astype(jnp.bfloat16)
@@ -211,21 +211,18 @@
 def fetch_body(dom_size, *refs):
     owner_ref, _, src_hbm, dst_hbm, diag_hbm, mats_hbm, ids_ref, diag_ref, mats_ref, dst_ref, sems = refs
     lists = [
-        pltpu.make_async_copy(src_hbm, ids_ref.at[0], sems.at[2 + CHUNKS]),
-        pltpu.make_async_copy(dst_hbm, dst_ref, sems.at[3 + CHUNKS]),
+        pltpu.make_async_copy(src_hbm, ids_ref.at[0], sems.at[1 + CHUNKS]),
+        pltpu.make_async_copy(dst_hbm, dst_ref, sems.at[2 + CHUNKS]),
     ]
     for copy in lists:
         copy.start()
-    copies = [pltpu.make_async_copy(diag_hbm.at[pl.ds(0, 1)], diag_ref.at[pl.ds(0, 1)], sems.at[0])]
+    copies = [pltpu.make_async_copy(diag_hbm.at[pl.ds(0, 1)], diag_ref, sems.at[0])]
     step = mats_ref.shape[1] // CHUNKS
     for chunk in range(CHUNKS):
         some = pl.ds(chunk * step, step)
         copies.append(
             pltpu.make_async_copy(mats_hbm.at[pl.ds(0, 1), some], mats_ref.at[:, some], sems.at[1 + chunk])
         )
-    copies.append(
-        pltpu.make_async_copy(diag_hbm.at[pl.ds(1, 1)], diag_ref.at[pl.ds(1, 1)], sems.at[1 + CHUNKS])
-    )
     for copy in copies:
         copy.start()
     for copy in lists:
@@ -243,14 +240,43 @@
         functools.partial(fetch_body, lax.axis_size("dom")),
         out_shape=[
             jax.ShapeDtypeStruct((2, *src.shape), jnp.int32),
-            pltpu.VMEM((2, *diag.shape[1:]), diag.dtype),
+            pltpu.VMEM((1, *diag.shape[1:]), diag.dtype),
             pltpu.VMEM((1, *mats.shape[1:]), mats.dtype),
         ],
         in_specs=[pl.BlockSpec(memory_space=pltpu.SMEM), vmem, hbm, hbm, hbm, hbm],
         out_specs=[vmem, vmem, vmem],
-        scratch_shapes=[pltpu.VMEM(dst.shape, dst.dtype), pltpu.SemaphoreType.DMA((4 + CHUNKS,))],
+        scratch_shapes=[pltpu.VMEM(dst.shape, dst.dtype), pltpu.SemaphoreType.DMA((3 + CHUNKS,))],
         compiler_params=pltpu.CompilerParams(vmem_limit_bytes=1 << 20),
     )(owner[None], after, src, dst, diag, mats)
+
+
+def next_diag_body(level, *refs):
+    _, sibling_ref, diag_hbm, passed_ref, diag_ref, sems = refs
+    tiles = diag_ref.shape[1]
+    copies = [
+        pltpu.make_async_copy(diag_hbm.at[pl.ds(level, 1), some], diag_ref.at[:, some], sems.at[half])
+        for half, some in enumerate((pl.ds(0, tiles // 2), pl.ds(tiles // 2, tiles // 2)))
+    ]
+    for copy in copies:
+        copy.start()
+    passed_ref[...] = sibling_ref[...]
+    for copy in copies:
+        copy.wait()
+
+
+def next_diag(level, after, sibling, diag):
+    vmem = pl.BlockSpec(memory_space=pltpu.VMEM)
+    return pl.pallas_call(
+        functools.partial(next_diag_body, level),
+        out_shape=[
+            jax.ShapeDtypeStruct(sibling.shape, sibling.dtype),
+            pltpu.VMEM((1, *diag.shape[1:]), diag.dtype),
+        ],
+        in_specs=[vmem, vmem, pl.BlockSpec(memory_space=pltpu.HBM)],
+        out_specs=[vmem, vmem],
+        scratch_shapes=[pltpu.SemaphoreType.DMA((2,))],
+        compiler_params=pltpu.CompilerParams(vmem_limit_bytes=1 << 20),
+    )(after, sibling, diag)
 
 
 def per_device(right_sides, diag_inverse, panel_mats, panel_src, panel_dst):
@@ -262,22 +288,18 @@
     partial = right_sides[0].astype(jnp.bfloat16)
     place = lax.broadcasted_iota(jnp.int32, (levels, tiles, cols, span), 2) // group == rep
     own_rhs = jnp.where(place, jnp.concatenate([right_sides] * rep_size, 2), 0.0)
-    ids, early_diag, early_mats = fetch(
-        partial,
-        *(
-            pltpu.with_memory_space_constraint(x, pltpu.HBM)
-            for x in (panel_src, panel_dst, diag_inverse, panel_mats)
-        ),
+    src, dst, diag_hbm, mats_hbm = (
+        pltpu.with_memory_space_constraint(x, pltpu.HBM)
+        for x in (panel_src, panel_dst, diag_inverse, panel_mats)
     )
-    late_diag, late_mats = (
-        pltpu.with_memory_space_constraint(x, pltpu.VMEM) for x in (diag_inverse, panel_mats)
-    )
+    ids, diag, early_mats = fetch(partial, src, dst, diag_hbm, mats_hbm)
+    late_mats = pltpu.with_memory_space_constraint(panel_mats, pltpu.VMEM)
     store = []
     results = []
     for level in range(levels):
         last = level + 1 == levels
         parts = [partial] + [along_rep(partial, apart) for apart in APART]
-        weights = [early_diag if level < 2 else late_diag, early_mats if level < 1 else late_mats]
+        weights = [diag, late_mats if level else early_mats]
         if last:
             return run_solve(
                 level, last, rep[None], None, parts, weights[:1], results, right_sides.shape
@@ -289,9 +311,9 @@
         store.append(stored)
         own, sibling, far, chip = run_panels(level, ids, weights[1], store)
         handed = jnp.where(top, to_sibling(handed), jnp.zeros_like(handed))
-        from_chip = to_next_chip(
-            (chip.astype(jnp.float32) + handed.astype(jnp.float32)).astype(jnp.bfloat16)
-        )
+        chip = (chip.astype(jnp.float32) + handed.astype(jnp.float32)).astype(jnp.bfloat16)
+        from_chip = to_next_chip(chip)
+        sibling, diag = next_diag(level + 1, chip, sibling, diag_hbm)
         from_far = to_far(far)
         across = to_sibling(
             (from_chip[0].astype(jnp.float32) + sibling.astype(jnp.float32)).astype(jnp.bfloat16)

time: 76.1 us -> 75.5 us (level)
  waiting for transfers between devices: 27.7 us -> 23.9 us
  Pallas kernels: 12.9 us -> 16.7 us
    ppermute x12, waiting for transfers between devices: 14.8 us -> 10.4 us  [dom_permute(): lax.ppermute(value, 'dom', [(i, target(i) % size) for i in range(size)])]
    pallas_call x0 -> x3, Pallas kernels: none -> 4.39 us  [next_diag(): pl.pallas_call(functools.partial(next_diag_body, level), out_shape=[jax.S...]
  transfers between devices with their start and end apart: 24 -> 24, of which waited for: 14 -> 14; matrix products, arithmetic and copies ran while one was open for 0% -> 0% of each run, Pallas kernels for 11% -> 16%
where the time goes in v6:
time: 75.5 us; the launch traced here: 75.3 us
  starting transfers between devices  32.9 us (44%)
  waiting for transfers between devices  23.9 us (32%)
  Pallas kernels  16.7 us (22%)
  local copies, waits for them, and re-layouts  0.8 us (1%)
  other arithmetic  0.79 us (1%)
    ppermute x12, starting transfers between devices, dom_permute(): lax.ppermute(value, 'dom', [(i, target(i) % size) for i in range(size)])  17.1 us
    ppermute x12, starting transfers between devices, along_rep(): lax.ppermute(value, 'rep', [(i, i ^ apart) for i in range(lax.axis_size('...  15.8 us
    ppermute x12, waiting for transfers between devices, along_rep(): lax.ppermute(value, 'rep', [(i, i ^ apart) for i in range(lax.axis_size('...  13.5 us
    ppermute x12, waiting for transfers between devices, dom_permute(): lax.ppermute(value, 'dom', [(i, target(i) % size) for i in range(size)])  10.4 us
    pallas_call x4, Pallas kernels, run_solve(): pl.pallas_call(functools.partial(solve_body, level, last), out_shape=outs...  4.73 us
    pallas_call x3, Pallas kernels, run_panels(): pl.pallas_call(functools.partial(panels_body, level), out_shape=[jax.Shap...  4.5 us
    pallas_call x3, Pallas kernels, next_diag(): pl.pallas_call(functools.partial(next_diag_body, level), out_shape=[jax.S...  4.39 us
    pallas_call x1, Pallas kernels, fetch(): pl.pallas_call(functools.partial(fetch_body, lax.axis_size('dom')), out_s...  3.1 us
  transfers between devices with their start and end apart: 24, of which 14 were waited for; matrix products, arithmetic and copies ran while one was open for 0% of the time, Pallas kernels for 16%

profile of v6, /device:TPU:0, one launch (start us, length us, event | category | flops | bytes accessed | tf_op | source)
XLA Modules:
  0.0 75.3 jit_solution(10676934758549621238)
XLA Ops:
  0.0 0.8 %fusion.15.refs_1_.refs_2_ = bf16[6,4,384]{2,1,0:T(4,128)(2,1)S(1)} fusion(f32[4,6,4,384]{3,2,1,0:T(4,128)} %param.5), kind=kLoop, calls=%fused_computation.36 | loop fusion | bytes 36864 | tf_op jit(solution)/shard_map/convert_element_type | solution.py:288
  0.8 4.0 %collective-permute-start = (bf16[6,4,384]{2,1,0:T(4,128)(2,1)S(1)}, bf16[6,4,384]{2,1,0:T(4,128)(2,1)S(1)}, u32[]{:S(2)}, u32[]{:S(2)}) collective-permute-start(bf16[6,4,384]{2,1,0:T(4,128)(2,1)S(1)} %fusion.15.refs_1_.refs_2_), channel_id=1, source_target_pairs={{0,2},{1,3},{2,0},{3,1},{4,6},{5,7},{6,4},{7,5},{8,10},{9,11},{10,... | collective-permute-start | bytes 55304 | tf_op jit(solution)/shard_map/ppermute | solution.py:37
  4.7 0.7 collective-permute-start.1
  5.5 0.3 collective-permute-start.2
  5.8 3.1 %shard_map.55 = (s32[2,3,16]{2,1,0:T(4,128)S(1)}, bf16[1,6,384,384]{3,2,1,0:T(8,128)(2,1)S(1)}, bf16[1,16,384,384]{3,2,1,0:T(8,128)(2,1)S(1)}) custom-call(s32[1]{0:T(128)} %bitcast.2.refs_0_, bf16[6,4,384]{2,1,0:T(4,128)(2,1)S(1)} %fusion.15.refs_1_.refs_2_, s32[3,16]{1,0:T(4,128)} %refs_2_.4, s32[3,16]{1,0:T(4,128)} %refs_3_.1, ...), custom_call_target="tpu_custom_call" | custom-call | tf_op jit(solution)/shard_map/pallas_call | solution.py:239
  8.9 0.0 collective-permute-done.refs_3_
  8.9 0.8 %collective-permute-done.1.refs_4_ = bf16[6,4,384]{2,1,0:T(4,128)(2,1)S(1)} collective-permute-done((bf16[6,4,384]{2,1,0:T(4,128)(2,1)S(1)}, bf16[6,4,384]{2,1,0:T(4,128)(2,1)S(1)}, u32[]{:S(2)}, u32[]{:S(2)}) %collective-permute-start.1) | collective-permute-done | bytes 18464 | tf_op jit(solution)/shard_map/ppermute | solution.py:37
  9.7 0.0 collective-permute-done.2.refs_5_
  9.7 1.2 %shard_map.56 = (f32[6,4,384]{2,1,0:T(4,128)S(1)}, bf16[6,16,384]{2,1,0:T(8,128)(2,1)S(1)}, bf16[6,16,384]{2,1,0:T(8,128)(2,1)S(1)}) custom-call(s32[1]{0:T(128)} %bitcast.refs_0_, s32[2,3,16]{2,1,0:T(4,128)S(1)} %get-tuple-element.35.refs_1_.refs_0_, bf16[6,4,384]{2,1,0:T(4,128)(2,1)S(1)} %fusion.15.refs_1_.refs_2_, ...), custom_call_target="tpu_custom_call" | custom-call | tf_op jit(solution)/shard_map/pallas_call | solution.py:160
  11.0 0.1 collective-permute-start.3
  11.1 0.0 slice-start.3
  11.1 1.5 %shard_map.57 = (bf16[6,16,384]{2,1,0:T(8,128)(2,1)S(1)}, bf16[6,16,384]{2,1,0:T(8,128)(2,1)S(1)}, bf16[6,16,384]{2,1,0:T(8,128)(2,1)S(1)}, bf16[2,6,16,384]{3,2,1,0:T(8,128)(2,1)S(1)}) custom-call(s32[2,3,16]{2,1,0:T(4,128)S(1)} %get-tuple-element.35.refs_1_.refs_0_, bf16[1,16,384,384]{3,2,1,0:T(8,128)(2,1)S(1)} %get-tuple-element.37.refs_7_.refs_1_, ...), custom_call_target="tpu_custom_call" | custom-call | tf_op jit(solution)/shard_map/pallas_call | solution.py:174
  12.6 0.0 collective-permute-done.3
  12.6 0.1 add_convert_fusion.2.refs_0_
  12.7 5.3 %collective-permute-start.4 = (bf16[2,6,16,384]{3,2,1,0:T(8,128)(2,1)S(1)}, bf16[2,6,16,384]{3,2,1,0:T(8,128)(2,1)S(1)}, u32[]{:S(2)}, u32[]{:S(2)}) collective-permute-start(bf16[2,6,16,384]{3,2,1,0:T(8,128)(2,1)S(1)} %add_convert_fusion.2.refs_0_), channel_id=1, source_target_pairs={{0,120},{4,12},{8,0},{12,20},{16,8},{20,28},{24,16},{28,36},{32,24... | collective-permute-start | bytes 442376 | tf_op jit(solution)/shard_map/ppermute | solution.py:20
  18.0 0.7 collective-permute-start.5
  18.7 1.5 %shard_map.58 = (bf16[6,16,384]{2,1,0:T(8,128)(2,1)S(1)}, bf16[1,6,384,384]{3,2,1,0:T(8,128)(2,1)S(1)}) custom-call(bf16[2,6,16,384]{3,2,1,0:T(8,128)(2,1)S(1)} %add_convert_fusion.2.refs_0_, bf16[6,16,384]{2,1,0:T(8,128)(2,1)S(1)} %get-tuple-element.43.refs_1_, bf16[4,6,384,384]{3,2,1,0:T(8,128)(2,1)} %refs_2_.7), custom_call_target="tpu_custom_call" | custom-call | tf_op jit(solution)/shard_map/pallas_call | solution.py:269
  20.2 0.5 collective-permute-done.4
  20.7 0.3 collective-permute-start.6
  21.0 0.1 maximum_select_fusion
  21.1 2.8 %collective-permute-done.5 = bf16[6,16,384]{2,1,0:T(8,128)(2,1)S(1)} collective-permute-done((bf16[6,16,384]{2,1,0:T(8,128)(2,1)S(1)}, bf16[6,16,384]{2,1,0:T(8,128)(2,1)S(1)}, u32[]{:S(2)}, u32[]{:S(2)}) %collective-permute-start.5) | collective-permute-done | bytes 73760 | tf_op jit(solution)/shard_map/ppermute | solution.py:20
  23.9 0.1 fusion.3.refs_2_
  24.0 3.0 %collective-permute-start.7 = (bf16[6,16,384]{2,1,0:T(8,128)(2,1)S(1)}, bf16[6,16,384]{2,1,0:T(8,128)(2,1)S(1)}, u32[]{:S(2)}, u32[]{:S(2)}) collective-permute-start(bf16[6,16,384]{2,1,0:T(8,128)(2,1)S(1)} %fusion.3.refs_2_), channel_id=1, source_target_pairs={{0,2},{1,3},{2,0},{3,1},{4,6},{5,7},{6,4},{7,5},{8,10},{9,11},{10,... | collective-permute-start | bytes 221192 | tf_op jit(solution)/shard_map/ppermute | solution.py:37
  27.0 0.7 collective-permute-start.8
  27.7 0.0 collective-permute-start.9
  27.7 2.4 %collective-permute-done.7.refs_3_ = bf16[6,16,384]{2,1,0:T(8,128)(2,1)S(1)} collective-permute-done((bf16[6,16,384]{2,1,0:T(8,128)(2,1)S(1)}, bf16[6,16,384]{2,1,0:T(8,128)(2,1)S(1)}, u32[]{:S(2)}, u32[]{:S(2)}) %collective-permute-start.7) | collective-permute-done | bytes 73760 | tf_op jit(solution)/shard_map/ppermute | solution.py:37
  30.1 2.5 %collective-permute-done.8.refs_4_ = bf16[6,16,384]{2,1,0:T(8,128)(2,1)S(1)} collective-permute-done((bf16[6,16,384]{2,1,0:T(8,128)(2,1)S(1)}, bf16[6,16,384]{2,1,0:T(8,128)(2,1)S(1)}, u32[]{:S(2)}, u32[]{:S(2)}) %collective-permute-start.8) | collective-permute-done | bytes 73760 | tf_op jit(solution)/shard_map/ppermute | solution.py:37
  32.5 0.0 collective-permute-done.9.refs_5_
  32.6 1.2 %shard_map.59 = (f32[6,4,384]{2,1,0:T(4,128)S(1)}, bf16[6,16,384]{2,1,0:T(8,128)(2,1)S(1)}, bf16[6,16,384]{2,1,0:T(8,128)(2,1)S(1)}) custom-call(s32[1]{0:T(128)} %bitcast.refs_0_, s32[2,3,16]{2,1,0:T(4,128)S(1)} %get-tuple-element.35.refs_1_.refs_0_, bf16[6,16,384]{2,1,0:T(8,128)(2,1)S(1)} %fusion.3.refs_2_, ...), custom_call_target="tpu_custom_call" | custom-call | tf_op jit(solution)/shard_map/pallas_call | solution.py:160
  33.8 0.1 collective-permute-start.10
  33.9 1.5 %shard_map.60 = (bf16[6,16,384]{2,1,0:T(8,128)(2,1)S(1)}, bf16[6,16,384]{2,1,0:T(8,128)(2,1)S(1)}, bf16[6,16,384]{2,1,0:T(8,128)(2,1)S(1)}, bf16[2,6,16,384]{3,2,1,0:T(8,128)(2,1)S(1)}) custom-call(s32[2,3,16]{2,1,0:T(4,128)S(1)} %get-tuple-element.35.refs_1_.refs_0_, bf16[3,16,384,384]{3,2,1,0:T(8,128)(2,1)S(1)} %bitcast.53, ...), custom_call_target="tpu_custom_call" | custom-call | tf_op jit(solution)/shard_map/pallas_call | solution.py:174
  35.4 0.1 add_convert_fusion.1.refs_0_
  35.5 4.8 %collective-permute-start.11 = (bf16[2,6,16,384]{3,2,1,0:T(8,128)(2,1)S(1)}, bf16[2,6,16,384]{3,2,1,0:T(8,128)(2,1)S(1)}, u32[]{:S(2)}, u32[]{:S(2)}) collective-permute-start(bf16[2,6,16,384]{3,2,1,0:T(8,128)(2,1)S(1)} %add_convert_fusion.1.refs_0_), channel_id=1, source_target_pairs={{0,120},{4,12},{8,0},{12,20},{16,8},{20,28},{24,16},{28,36},{32,24... | collective-permute-start | bytes 442376 | tf_op jit(solution)/shard_map/ppermute | solution.py:20
  40.3 0.0 collective-permute-start.12
  40.3 1.5 %shard_map.61 = (bf16[6,16,384]{2,1,0:T(8,128)(2,1)S(1)}, bf16[1,6,384,384]{3,2,1,0:T(8,128)(2,1)S(1)}) custom-call(bf16[2,6,16,384]{3,2,1,0:T(8,128)(2,1)S(1)} %add_convert_fusion.1.refs_0_, bf16[6,16,384]{2,1,0:T(8,128)(2,1)S(1)} %get-tuple-element.51.refs_1_, bf16[4,6,384,384]{3,2,1,0:T(8,128)(2,1)} %refs_2_.7), custom_call_target="tpu_custom_call" | custom-call | tf_op jit(solution)/shard_map/pallas_call | solution.py:269
  41.8 1.2 %collective-permute-done.11 = bf16[2,6,16,384]{3,2,1,0:T(8,128)(2,1)S(1)} collective-permute-done((bf16[2,6,16,384]{3,2,1,0:T(8,128)(2,1)S(1)}, bf16[2,6,16,384]{3,2,1,0:T(8,128)(2,1)S(1)}, u32[]{:S(2)}, u32[]{:S(2)}) %collective-permute-start.11) | collective-permute-done | bytes 147488 | tf_op jit(solution)/shard_map/ppermute | solution.py:20
  43.0 0.5 collective-permute-start.13
  43.5 2.7 %collective-permute-done.12 = bf16[6,16,384]{2,1,0:T(8,128)(2,1)S(1)} collective-permute-done((bf16[6,16,384]{2,1,0:T(8,128)(2,1)S(1)}, bf16[6,16,384]{2,1,0:T(8,128)(2,1)S(1)}, u32[]{:S(2)}, u32[]{:S(2)}) %collective-permute-start.12) | collective-permute-done | bytes 73760 | tf_op jit(solution)/shard_map/ppermute | solution.py:20
  46.2 0.0 collective-permute-done.13
  46.2 0.1 fusion.1.refs_2_
  46.3 1.5 %collective-permute-start.14 = (bf16[6,16,384]{2,1,0:T(8,128)(2,1)S(1)}, bf16[6,16,384]{2,1,0:T(8,128)(2,1)S(1)}, u32[]{:S(2)}, u32[]{:S(2)}) collective-permute-start(bf16[6,16,384]{2,1,0:T(8,128)(2,1)S(1)} %fusion.1.refs_2_), channel_id=1, source_target_pairs={{0,2},{1,3},{2,0},{3,1},{4,6},{5,7},{6,4},{7,5},{8,10},{9,11},{10,... | collective-permute-start | bytes 221192 | tf_op jit(solution)/shard_map/ppermute | solution.py:37
  47.8 1.6 %collective-permute-start.15 = (bf16[6,16,384]{2,1,0:T(8,128)(2,1)S(1)}, bf16[6,16,384]{2,1,0:T(8,128)(2,1)S(1)}, u32[]{:S(2)}, u32[]{:S(2)}) collective-permute-start(bf16[6,16,384]{2,1,0:T(8,128)(2,1)S(1)} %fusion.1.refs_2_), channel_id=1, source_target_pairs={{0,3},{1,2},{2,1},{3,0},{4,7},{5,6},{6,5},{7,4},{8,11},{9,10},{10,... | collective-permute-start | bytes 221192 | tf_op jit(solution)/shard_map/ppermute | solution.py:37
  49.3 0.5 collective-permute-start.16
  49.8 2.9 %collective-permute-done.14.refs_3_ = bf16[6,16,384]{2,1,0:T(8,128)(2,1)S(1)} collective-permute-done((bf16[6,16,384]{2,1,0:T(8,128)(2,1)S(1)}, bf16[6,16,384]{2,1,0:T(8,128)(2,1)S(1)}, u32[]{:S(2)}, u32[]{:S(2)}) %collective-permute-start.14) | collective-permute-done | bytes 73760 | tf_op jit(solution)/shard_map/ppermute | solution.py:37
  52.7 0.8 %collective-permute-done.15.refs_4_ = bf16[6,16,384]{2,1,0:T(8,128)(2,1)S(1)} collective-permute-done((bf16[6,16,384]{2,1,0:T(8,128)(2,1)S(1)}, bf16[6,16,384]{2,1,0:T(8,128)(2,1)S(1)}, u32[]{:S(2)}, u32[]{:S(2)}) %collective-permute-start.15) | collective-permute-done | bytes 73760 | tf_op jit(solution)/shard_map/ppermute | solution.py:37
  53.5 0.2 collective-permute-done.16.refs_5_
  53.7 1.2 %shard_map.62 = (f32[6,4,384]{2,1,0:T(4,128)S(1)}, bf16[6,16,384]{2,1,0:T(8,128)(2,1)S(1)}, bf16[6,16,384]{2,1,0:T(8,128)(2,1)S(1)}) custom-call(s32[1]{0:T(128)} %bitcast.refs_0_, s32[2,3,16]{2,1,0:T(4,128)S(1)} %get-tuple-element.35.refs_1_.refs_0_, bf16[6,16,384]{2,1,0:T(8,128)(2,1)S(1)} %fusion.1.refs_2_, ...), custom_call_target="tpu_custom_call" | custom-call | tf_op jit(solution)/shard_map/pallas_call | solution.py:160
  54.9 0.1 collective-permute-start.17
  55.0 1.5 %shard_map.63 = (bf16[6,16,384]{2,1,0:T(8,128)(2,1)S(1)}, bf16[6,16,384]{2,1,0:T(8,128)(2,1)S(1)}, bf16[6,16,384]{2,1,0:T(8,128)(2,1)S(1)}, bf16[2,6,16,384]{3,2,1,0:T(8,128)(2,1)S(1)}) custom-call(s32[2,3,16]{2,1,0:T(4,128)S(1)} %get-tuple-element.35.refs_1_.refs_0_, bf16[3,16,384,384]{3,2,1,0:T(8,128)(2,1)S(1)} %bitcast.53, ...), custom_call_target="tpu_custom_call" | custom-call | tf_op jit(solution)/shard_map/pallas_call | solution.py:174
  56.5 0.1 add_convert_fusion.refs_0_
  56.7 4.1 %collective-permute-start.18 = (bf16[2,6,16,384]{3,2,1,0:T(8,128)(2,1)S(1)}, bf16[2,6,16,384]{3,2,1,0:T(8,128)(2,1)S(1)}, u32[]{:S(2)}, u32[]{:S(2)}) collective-permute-start(bf16[2,6,16,384]{3,2,1,0:T(8,128)(2,1)S(1)} %add_convert_fusion.refs_0_), channel_id=1, source_target_pairs={{0,120},{4,12},{8,0},{12,20},{16,8},{20,28},{24,16},{28,36},{32,24... | collective-permute-start | bytes 442376 | tf_op jit(solution)/shard_map/ppermute | solution.py:20
  60.8 0.0 collective-permute-start.19
  60.8 1.5 %shard_map.64 = (bf16[6,16,384]{2,1,0:T(8,128)(2,1)S(1)}, bf16[1,6,384,384]{3,2,1,0:T(8,128)(2,1)S(1)}) custom-call(bf16[2,6,16,384]{3,2,1,0:T(8,128)(2,1)S(1)} %add_convert_fusion.refs_0_, bf16[6,16,384]{2,1,0:T(8,128)(2,1)S(1)} %get-tuple-element.59.refs_1_, bf16[4,6,384,384]{3,2,1,0:T(8,128)(2,1)} %refs_2_.7), custom_call_target="tpu_custom_call" | custom-call | tf_op jit(solution)/shard_map/pallas_call | solution.py:269
  62.2 1.2 %collective-permute-done.18 = bf16[2,6,16,384]{3,2,1,0:T(8,128)(2,1)S(1)} collective-permute-done((bf16[2,6,16,384]{3,2,1,0:T(8,128)(2,1)S(1)}, bf16[2,6,16,384]{3,2,1,0:T(8,128)(2,1)S(1)}, u32[]{:S(2)}, u32[]{:S(2)}) %collective-permute-start.18) | collective-permute-done | bytes 147488 | tf_op jit(solution)/shard_map/ppermute | solution.py:20
  63.5 1.2 %collective-permute-start.20 = (bf16[6,16,384]{2,1,0:T(8,128)(2,1)S(1)}, bf16[6,16,384]{2,1,0:T(8,128)(2,1)S(1)}, u32[]{:S(2)}, u32[]{:S(2)}) collective-permute-start(bf16[6,16,384]{2,1,0:T(8,128)(2,1)S(1)} %fusion.6), channel_id=1, source_target_pairs={{0,4},{4,0},{8,12},{12,8},{16,20},{20,16},{24,28},{28,24},{32,36},... | collective-permute-start | bytes 221192 | tf_op jit(solution)/shard_map/ppermute | solution.py:20
  64.6 2.0 %collective-permute-done.19 = bf16[6,16,384]{2,1,0:T(8,128)(2,1)S(1)} collective-permute-done((bf16[6,16,384]{2,1,0:T(8,128)(2,1)S(1)}, bf16[6,16,384]{2,1,0:T(8,128)(2,1)S(1)}, u32[]{:S(2)}, u32[]{:S(2)}) %collective-permute-start.19) | collective-permute-done | bytes 73760 | tf_op jit(solution)/shard_map/ppermute | solution.py:20
  66.6 0.1 fusion.5.refs_1_
  66.7 1.9 %collective-permute-start.21 = (bf16[6,16,384]{2,1,0:T(8,128)(2,1)S(1)}, bf16[6,16,384]{2,1,0:T(8,128)(2,1)S(1)}, u32[]{:S(2)}, u32[]{:S(2)}) collective-permute-start(bf16[6,16,384]{2,1,0:T(8,128)(2,1)S(1)} %fusion.5.refs_1_), channel_id=1, source_target_pairs={{0,2},{1,3},{2,0},{3,1},{4,6},{5,7},{6,4},{7,5},{8,10},{9,11},{10,... | collective-permute-start | bytes 221192 | tf_op jit(solution)/shard_map/ppermute | solution.py:37
  68.6 1.2 %collective-permute-start.22 = (bf16[6,16,384]{2,1,0:T(8,128)(2,1)S(1)}, bf16[6,16,384]{2,1,0:T(8,128)(2,1)S(1)}, u32[]{:S(2)}, u32[]{:S(2)}) collective-permute-start(bf16[6,16,384]{2,1,0:T(8,128)(2,1)S(1)} %fusion.5.refs_1_), channel_id=1, source_target_pairs={{0,3},{1,2},{2,1},{3,0},{4,7},{5,6},{6,5},{7,4},{8,11},{9,10},{10,... | collective-permute-start | bytes 221192 | tf_op jit(solution)/shard_map/ppermute | solution.py:37
  69.9 0.4 collective-permute-start.23
  70.3 2.5 %collective-permute-done.21.refs_2_ = bf16[6,16,384]{2,1,0:T(8,128)(2,1)S(1)} collective-permute-done((bf16[6,16,384]{2,1,0:T(8,128)(2,1)S(1)}, bf16[6,16,384]{2,1,0:T(8,128)(2,1)S(1)}, u32[]{:S(2)}, u32[]{:S(2)}) %collective-permute-start.21) | collective-permute-done | bytes 73760 | tf_op jit(solution)/shard_map/ppermute | solution.py:37
  72.7 1.5 %collective-permute-done.22.refs_3_ = bf16[6,16,384]{2,1,0:T(8,128)(2,1)S(1)} collective-permute-done((bf16[6,16,384]{2,1,0:T(8,128)(2,1)S(1)}, bf16[6,16,384]{2,1,0:T(8,128)(2,1)S(1)}, u32[]{:S(2)}, u32[]{:S(2)}) %collective-permute-start.22) | collective-permute-done | bytes 73760 | tf_op jit(solution)/shard_map/ppermute | solution.py:37
  74.2 0.0 collective-permute-done.23.refs_4_
  74.2 1.1 %shard_map.65 = f32[4,6,4,384]{3,2,1,0:T(4,128)} custom-call(s32[1]{0:T(128)} %bitcast.refs_0_, bf16[6,16,384]{2,1,0:T(8,128)(2,1)S(1)} %fusion.5.refs_1_, bf16[6,16,384]{2,1,0:T(8,128)(2,1)S(1)} %collective-permute-done.21.refs_2_, bf16[6,16,384]{2,1,0:T(8,128)(2,1)S(1)} %collective-permute-done.22.refs_3_, ...), custom_call_target="tpu_custom_call" | custom-call | tf_op jit(solution)/shard_map/pallas_call | solution.py:160
  (20 shorter events, 0.1 us)
Async XLA Ops:
  0.8 8.1 %collective-permute-start = (bf16[6,4,384]{2,1,0:T(4,128)(2,1)S(1)}, bf16[6,4,384]{2,1,0:T(4,128)(2,1)S(1)}, u32[]{:S(2)}, u32[]{:S(2)}) collective-permute-start(bf16[6,4,384]{2,1,0:T(4,128)(2,1)S(1)} %fusion.15.refs_1_.refs_2_), channel_id=1, source_target_pairs={{0,2},{1,3},{2,0},{3,1},{4,6},{5,7},{6,4},{7,5},{8,10},{9,11},{10,... | collective-permute-start | bytes 55304 | tf_op jit(solution)/shard_map/ppermute | solution.py:37
  4.7 5.0 %collective-permute-start.1 = (bf16[6,4,384]{2,1,0:T(4,128)(2,1)S(1)}, bf16[6,4,384]{2,1,0:T(4,128)(2,1)S(1)}, u32[]{:S(2)}, u32[]{:S(2)}) collective-permute-start(bf16[6,4,384]{2,1,0:T(4,128)(2,1)S(1)} %fusion.15.refs_1_.refs_2_), channel_id=1, source_target_pairs={{0,3},{1,2},{2,1},{3,0},{4,7},{5,6},{6,5},{7,4},{8,11},{9,10},{10,... | collective-permute-start | bytes 55304 | tf_op jit(solution)/shard_map/ppermute | solution.py:37
  5.5 4.3 %collective-permute-start.2 = (bf16[6,4,384]{2,1,0:T(4,128)(2,1)S(1)}, bf16[6,4,384]{2,1,0:T(4,128)(2,1)S(1)}, u32[]{:S(2)}, u32[]{:S(2)}) collective-permute-start(bf16[6,4,384]{2,1,0:T(4,128)(2,1)S(1)} %fusion.15.refs_1_.refs_2_), channel_id=1, source_target_pairs={{0,1},{1,0},{2,3},{3,2},{4,5},{5,4},{6,7},{7,6},{8,9},{9,8},{10,11... | collective-permute-start | bytes 55304 | tf_op jit(solution)/shard_map/ppermute | solution.py:37
  5.8 26.8 %slice-start = ((s8[14155776]{0:T(1024)(128)(4,1)}), s8[4194304]{0:T(1024)(128)(4,1)S(1)}, s32[]{:S(2)}) async-start(s8[14155776]{0:T(1024)(128)(4,1)} %bitcast.52), calls=%async_computation | async-start | bytes 8388608
  5.8 26.8 %slice-start.1 = ((s8[14155776]{0:T(1024)(128)(4,1)}), s8[4194304]{0:T(1024)(128)(4,1)S(1)}, s32[]{:S(2)}) async-start(s8[14155776]{0:T(1024)(128)(4,1)} %bitcast.52), calls=%async_computation.1 | async-start | bytes 8388608
  5.8 26.8 %slice-start.2 = ((s8[14155776]{0:T(1024)(128)(4,1)}), s8[4194304]{0:T(1024)(128)(4,1)S(1)}, s32[]{:S(2)}) async-start(s8[14155776]{0:T(1024)(128)(4,1)} %bitcast.52), calls=%async_computation.2 | async-start | bytes 8388608
  11.0 1.6 %collective-permute-start.3 = (bf16[6,16,384]{2,1,0:T(8,128)(2,1)S(1)}, bf16[6,16,384]{2,1,0:T(8,128)(2,1)S(1)}, u32[]{:S(2)}, u32[]{:S(2)}) collective-permute-start(bf16[6,16,384]{2,1,0:T(8,128)(2,1)S(1)} %get-tuple-element.41), channel_id=1, source_target_pairs={{0,4},{4,0},{8,12},{12,8},{16,20},{20,16},{24,28},{28,24},{32,36},... | collective-permute-start | bytes 221192 | tf_op jit(solution)/shard_map/ppermute | solution.py:20
  11.1 21.5 %slice-start.3 = ((s8[14155776]{0:T(1024)(128)(4,1)}), s8[1572864]{0:T(1024)(128)(4,1)S(1)}, s32[]{:S(2)}) async-start(s8[14155776]{0:T(1024)(128)(4,1)} %bitcast.52), calls=%async_computation.3 | async-start | bytes 3145728
  12.7 8.0 %collective-permute-start.4 = (bf16[2,6,16,384]{3,2,1,0:T(8,128)(2,1)S(1)}, bf16[2,6,16,384]{3,2,1,0:T(8,128)(2,1)S(1)}, u32[]{:S(2)}, u32[]{:S(2)}) collective-permute-start(bf16[2,6,16,384]{3,2,1,0:T(8,128)(2,1)S(1)} %add_convert_fusion.2.refs_0_), channel_id=1, source_target_pairs={{0,120},{4,12},{8,0},{12,20},{16,8},{20,28},{24,16},{28,36},{32,24... | collective-permute-start | bytes 442376 | tf_op jit(solution)/shard_map/ppermute | solution.py:20
  18.0 5.9 %collective-permute-start.5 = (bf16[6,16,384]{2,1,0:T(8,128)(2,1)S(1)}, bf16[6,16,384]{2,1,0:T(8,128)(2,1)S(1)}, u32[]{:S(2)}, u32[]{:S(2)}) collective-permute-start(bf16[6,16,384]{2,1,0:T(8,128)(2,1)S(1)} %get-tuple-element.42), channel_id=1, source_target_pairs={{0,64},{4,68},{8,72},{12,76},{16,80},{20,84},{24,88},{28,92},{32,9... | collective-permute-start | bytes 221192 | tf_op jit(solution)/shard_map/ppermute | solution.py:20
  18.7 2.2 %copy-start = (f32[4,6,4,384]{3,2,1,0:T(4,128)S(1)}, f32[4,6,4,384]{3,2,1,0:T(4,128)}, u32[]{:S(2)}) copy-start(f32[4,6,4,384]{3,2,1,0:T(4,128)} %param.5) | copy-start | bytes 442372
  20.7 3.3 %collective-permute-start.6 = (bf16[6,16,384]{2,1,0:T(8,128)(2,1)S(1)}, bf16[6,16,384]{2,1,0:T(8,128)(2,1)S(1)}, u32[]{:S(2)}, u32[]{:S(2)}) collective-permute-start(bf16[6,16,384]{2,1,0:T(8,128)(2,1)S(1)} %fusion.12), channel_id=1, source_target_pairs={{0,4},{4,0},{8,12},{12,8},{16,20},{20,16},{24,28},{28,24},{32,36},... | collective-permute-start | bytes 221192 | tf_op jit(solution)/shard_map/ppermute | solution.py:20
  24.0 6.0 %collective-permute-start.7 = (bf16[6,16,384]{2,1,0:T(8,128)(2,1)S(1)}, bf16[6,16,384]{2,1,0:T(8,128)(2,1)S(1)}, u32[]{:S(2)}, u32[]{:S(2)}) collective-permute-start(bf16[6,16,384]{2,1,0:T(8,128)(2,1)S(1)} %fusion.3.refs_2_), channel_id=1, source_target_pairs={{0,2},{1,3},{2,0},{3,1},{4,6},{5,7},{6,4},{7,5},{8,10},{9,11},{10,... | collective-permute-start | bytes 221192 | tf_op jit(solution)/shard_map/ppermute | solution.py:37
  27.0 5.6 %collective-permute-start.8 = (bf16[6,16,384]{2,1,0:T(8,128)(2,1)S(1)}, bf16[6,16,384]{2,1,0:T(8,128)(2,1)S(1)}, u32[]{:S(2)}, u32[]{:S(2)}) collective-permute-start(bf16[6,16,384]{2,1,0:T(8,128)(2,1)S(1)} %fusion.3.refs_2_), channel_id=1, source_target_pairs={{0,3},{1,2},{2,1},{3,0},{4,7},{5,6},{6,5},{7,4},{8,11},{9,10},{10,... | collective-permute-start | bytes 221192 | tf_op jit(solution)/shard_map/ppermute | solution.py:37
  27.7 4.9 %collective-permute-start.9 = (bf16[6,16,384]{2,1,0:T(8,128)(2,1)S(1)}, bf16[6,16,384]{2,1,0:T(8,128)(2,1)S(1)}, u32[]{:S(2)}, u32[]{:S(2)}) collective-permute-start(bf16[6,16,384]{2,1,0:T(8,128)(2,1)S(1)} %fusion.3.refs_2_), channel_id=1, source_target_pairs={{0,1},{1,0},{2,3},{3,2},{4,5},{5,4},{6,7},{7,6},{8,9},{9,8},{10,11... | collective-permute-start | bytes 221192 | tf_op jit(solution)/shard_map/ppermute | solution.py:37
  33.8 1.6 %collective-permute-start.10 = (bf16[6,16,384]{2,1,0:T(8,128)(2,1)S(1)}, bf16[6,16,384]{2,1,0:T(8,128)(2,1)S(1)}, u32[]{:S(2)}, u32[]{:S(2)}) collective-permute-start(bf16[6,16,384]{2,1,0:T(8,128)(2,1)S(1)} %get-tuple-element.49), channel_id=1, source_target_pairs={{0,4},{4,0},{8,12},{12,8},{16,20},{20,16},{24,28},{28,24},{32,36},... | collective-permute-start | bytes 221192 | tf_op jit(solution)/shard_map/ppermute | solution.py:20
  35.5 7.5 %collective-permute-start.11 = (bf16[2,6,16,384]{3,2,1,0:T(8,128)(2,1)S(1)}, bf16[2,6,16,384]{3,2,1,0:T(8,128)(2,1)S(1)}, u32[]{:S(2)}, u32[]{:S(2)}) collective-permute-start(bf16[2,6,16,384]{3,2,1,0:T(8,128)(2,1)S(1)} %add_convert_fusion.1.refs_0_), channel_id=1, source_target_pairs={{0,120},{4,12},{8,0},{12,20},{16,8},{20,28},{24,16},{28,36},{32,24... | collective-permute-start | bytes 442376 | tf_op jit(solution)/shard_map/ppermute | solution.py:20
  40.3 5.9 %collective-permute-start.12 = (bf16[6,16,384]{2,1,0:T(8,128)(2,1)S(1)}, bf16[6,16,384]{2,1,0:T(8,128)(2,1)S(1)}, u32[]{:S(2)}, u32[]{:S(2)}) collective-permute-start(bf16[6,16,384]{2,1,0:T(8,128)(2,1)S(1)} %get-tuple-element.50), channel_id=1, source_target_pairs={{0,64},{4,68},{8,72},{12,76},{16,80},{20,84},{24,88},{28,92},{32,9... | collective-permute-start | bytes 221192 | tf_op jit(solution)/shard_map/ppermute | solution.py:20
  43.0 3.2 %collective-permute-start.13 = (bf16[6,16,384]{2,1,0:T(8,128)(2,1)S(1)}, bf16[6,16,384]{2,1,0:T(8,128)(2,1)S(1)}, u32[]{:S(2)}, u32[]{:S(2)}) collective-permute-start(bf16[6,16,384]{2,1,0:T(8,128)(2,1)S(1)} %fusion.9), channel_id=1, source_target_pairs={{0,4},{4,0},{8,12},{12,8},{16,20},{20,16},{24,28},{28,24},{32,36},... | collective-permute-start | bytes 221192 | tf_op jit(solution)/shard_map/ppermute | solution.py:20
  46.3 6.4 %collective-permute-start.14 = (bf16[6,16,384]{2,1,0:T(8,128)(2,1)S(1)}, bf16[6,16,384]{2,1,0:T(8,128)(2,1)S(1)}, u32[]{:S(2)}, u32[]{:S(2)}) collective-permute-start(bf16[6,16,384]{2,1,0:T(8,128)(2,1)S(1)} %fusion.1.refs_2_), channel_id=1, source_target_pairs={{0,2},{1,3},{2,0},{3,1},{4,6},{5,7},{6,4},{7,5},{8,10},{9,11},{10,... | collective-permute-start | bytes 221192 | tf_op jit(solution)/shard_map/ppermute | solution.py:37
  47.8 5.7 %collective-permute-start.15 = (bf16[6,16,384]{2,1,0:T(8,128)(2,1)S(1)}, bf16[6,16,384]{2,1,0:T(8,128)(2,1)S(1)}, u32[]{:S(2)}, u32[]{:S(2)}) collective-permute-start(bf16[6,16,384]{2,1,0:T(8,128)(2,1)S(1)} %fusion.1.refs_2_), channel_id=1, source_target_pairs={{0,3},{1,2},{2,1},{3,0},{4,7},{5,6},{6,5},{7,4},{8,11},{9,10},{10,... | collective-permute-start | bytes 221192 | tf_op jit(solution)/shard_map/ppermute | solution.py:37
  49.3 4.4 %collective-permute-start.16 = (bf16[6,16,384]{2,1,0:T(8,128)(2,1)S(1)}, bf16[6,16,384]{2,1,0:T(8,128)(2,1)S(1)}, u32[]{:S(2)}, u32[]{:S(2)}) collective-permute-start(bf16[6,16,384]{2,1,0:T(8,128)(2,1)S(1)} %fusion.1.refs_2_), channel_id=1, source_target_pairs={{0,1},{1,0},{2,3},{3,2},{4,5},{5,4},{6,7},{7,6},{8,9},{9,8},{10,11... | collective-permute-start | bytes 221192 | tf_op jit(solution)/shard_map/ppermute | solution.py:37
  54.9 1.6 %collective-permute-start.17 = (bf16[6,16,384]{2,1,0:T(8,128)(2,1)S(1)}, bf16[6,16,384]{2,1,0:T(8,128)(2,1)S(1)}, u32[]{:S(2)}, u32[]{:S(2)}) collective-permute-start(bf16[6,16,384]{2,1,0:T(8,128)(2,1)S(1)} %get-tuple-element.57), channel_id=1, source_target_pairs={{0,4},{4,0},{8,12},{12,8},{16,20},{20,16},{24,28},{28,24},{32,36},... | collective-permute-start | bytes 221192 | tf_op jit(solution)/shard_map/ppermute | solution.py:20
  56.7 6.8 %collective-permute-start.18 = (bf16[2,6,16,384]{3,2,1,0:T(8,128)(2,1)S(1)}, bf16[2,6,16,384]{3,2,1,0:T(8,128)(2,1)S(1)}, u32[]{:S(2)}, u32[]{:S(2)}) collective-permute-start(bf16[2,6,16,384]{3,2,1,0:T(8,128)(2,1)S(1)} %add_convert_fusion.refs_0_), channel_id=1, source_target_pairs={{0,120},{4,12},{8,0},{12,20},{16,8},{20,28},{24,16},{28,36},{32,24... | collective-permute-start | bytes 442376 | tf_op jit(solution)/shard_map/ppermute | solution.py:20
  60.8 5.9 %collective-permute-start.19 = (bf16[6,16,384]{2,1,0:T(8,128)(2,1)S(1)}, bf16[6,16,384]{2,1,0:T(8,128)(2,1)S(1)}, u32[]{:S(2)}, u32[]{:S(2)}) collective-permute-start(bf16[6,16,384]{2,1,0:T(8,128)(2,1)S(1)} %get-tuple-element.58), channel_id=1, source_target_pairs={{0,64},{4,68},{8,72},{12,76},{16,80},{20,84},{24,88},{28,92},{32,9... | collective-permute-start | bytes 221192 | tf_op jit(solution)/shard_map/ppermute | solution.py:20
  63.5 3.2 %collective-permute-start.20 = (bf16[6,16,384]{2,1,0:T(8,128)(2,1)S(1)}, bf16[6,16,384]{2,1,0:T(8,128)(2,1)S(1)}, u32[]{:S(2)}, u32[]{:S(2)}) collective-permute-start(bf16[6,16,384]{2,1,0:T(8,128)(2,1)S(1)} %fusion.6), channel_id=1, source_target_pairs={{0,4},{4,0},{8,12},{12,8},{16,20},{20,16},{24,28},{28,24},{32,36},... | collective-permute-start | bytes 221192 | tf_op jit(solution)/shard_map/ppermute | solution.py:20
  66.7 6.0 %collective-permute-start.21 = (bf16[6,16,384]{2,1,0:T(8,128)(2,1)S(1)}, bf16[6,16,384]{2,1,0:T(8,128)(2,1)S(1)}, u32[]{:S(2)}, u32[]{:S(2)}) collective-permute-start(bf16[6,16,384]{2,1,0:T(8,128)(2,1)S(1)} %fusion.5.refs_1_), channel_id=1, source_target_pairs={{0,2},{1,3},{2,0},{3,1},{4,6},{5,7},{6,4},{7,5},{8,10},{9,11},{10,... | collective-permute-start | bytes 221192 | tf_op jit(solution)/shard_map/ppermute | solution.py:37
  68.6 5.6 %collective-permute-start.22 = (bf16[6,16,384]{2,1,0:T(8,128)(2,1)S(1)}, bf16[6,16,384]{2,1,0:T(8,128)(2,1)S(1)}, u32[]{:S(2)}, u32[]{:S(2)}) collective-permute-start(bf16[6,16,384]{2,1,0:T(8,128)(2,1)S(1)} %fusion.5.refs_1_), channel_id=1, source_target_pairs={{0,3},{1,2},{2,1},{3,0},{4,7},{5,6},{6,5},{7,4},{8,11},{9,10},{10,... | collective-permute-start | bytes 221192 | tf_op jit(solution)/shard_map/ppermute | solution.py:37
  69.9 4.4 %collective-permute-start.23 = (bf16[6,16,384]{2,1,0:T(8,128)(2,1)S(1)}, bf16[6,16,384]{2,1,0:T(8,128)(2,1)S(1)}, u32[]{:S(2)}, u32[]{:S(2)}) collective-permute-start(bf16[6,16,384]{2,1,0:T(8,128)(2,1)S(1)} %fusion.5.refs_1_), channel_id=1, source_target_pairs={{0,1},{1,0},{2,3},{3,2},{4,5},{5,4},{6,7},{7,6},{8,9},{9,8},{10,11... | collective-permute-start | bytes 221192 | tf_op jit(solution)/shard_map/ppermute | solution.py:37

commit v7 on v6

--- a/solution.py
+++ b/solution.py
@@ -11,8 +11,10 @@
 OWN, FAR, SIBLING, HANDED, PASSED, DIRECT = range(6)
 GROUPS = 6
 APART = (2, 3, 1)
+APART_FIRST = (3, 2, 1)
 CHUNKS = 4
 SLOTS = 3
+WIDE = 256
 
 
 def dom_permute(value, target):
@@ -30,7 +32,7 @@
 
 
 def to_next_chip(value):
-    return dom_permute(value, lambda i: i + 2 if i % 2 else i - 2)
+    return dom_permute(value, lambda i: i + 1 if i % 2 else i - 1)
 
 
 def along_rep(value, apart):
@@ -43,10 +45,25 @@
     placed = []
     for index in range(size):
         chosen = blocks[0]
-        for block, apart in zip(blocks[1:], APART):
+        for block, apart in zip(blocks[1:], APART_FIRST):
             chosen = jnp.where(rep == index ^ apart, block, chosen)
         placed.append(chosen)
     return placed
+
+
+def two_products(left, right, left_matrix, right_matrix):
+    rows, span = left.shape
+    main = span // WIDE * WIDE
+    rest = span - main
+    dot = functools.partial(jnp.dot, preferred_element_type=jnp.float32)
+    tail = dot(
+        jnp.concatenate([left, right], 0),
+        jnp.concatenate([left_matrix[:, main:], right_matrix[:, main:]], 1),
+    )
+    return (
+        jnp.concatenate([dot(left, left_matrix[:, :main]), tail[:rows, :rest]], 1),
+        jnp.concatenate([dot(right, right_matrix[:, :main]), tail[rows:, rest:]], 1),
+    )
 
 
 def solve_body(level, last, *refs):
@@ -74,8 +91,10 @@
         residuals = [
             sum(part[t].astype(jnp.float32) for part in parts).astype(jnp.bfloat16) for t in range(tiles)
         ]
-    for t in range(tiles):
-        solved = jnp.dot(residuals[t], diag_ref[0, t], preferred_element_type=jnp.float32)
+    products = []
+    for t in range(0, tiles, 2):
+        products += two_products(residuals[t], residuals[t + 1], diag_ref[0, t], diag_ref[0, t + 1])
+    for t, solved in enumerate(products):
         solved_scr[t] = solved
         if not last:
             stored_ref[t] = solved.astype(jnp.bfloat16)
@@ -116,18 +135,22 @@
     take = lambda count: [refs.pop(0) for _ in range(count)]
     ids_ref, mats_ref = take(2)
     stores = take(level + 1)
-    own_ref, sibling_ref, far_ref, chip_ref, store_scr, acc_scr = refs
+    own_ref, sibling_ref, far_ref, chip_ref, store_scr, updates_scr, acc_scr = refs
     tiles = own_ref.shape[0]
     for earlier in range(level + 1):
         for t in range(tiles):
             store_scr[earlier * tiles + t] = stores[earlier][t]
+    for p in range(0, mats_ref.shape[1], 2):
+        updates_scr[p], updates_scr[p + 1] = two_products(
+            store_scr[ids_ref[0, level, p]],
+            store_scr[ids_ref[0, level, p + 1]],
+            mats_ref[level, p],
+            mats_ref[level, p + 1],
+        )
     acc_scr[...] = jnp.zeros_like(acc_scr)
     for p in range(mats_ref.shape[1]):
-        update = jnp.dot(
-            store_scr[ids_ref[0, level, p]], mats_ref[level, p], preferred_element_type=jnp.float32
-        )
         slot = ids_ref[1, level, p]
-        acc_scr[slot] = acc_scr[slot] + update
+        acc_scr[slot] = acc_scr[slot] + updates_scr[p]
 
     def sums(index):
         return acc_scr[index * tiles : (index + 1) * tiles].astype(jnp.bfloat16)
@@ -180,6 +203,7 @@
         out_specs=[vmem] * 4,
         scratch_shapes=[
             pltpu.VMEM(((level + 1) * tiles, cols, span), jnp.bfloat16),
+            pltpu.VMEM((mats.shape[1], cols, span), jnp.float32),
             pltpu.VMEM((GROUPS * tiles + 1, cols, span), jnp.float32),
         ],
         compiler_params=pltpu.CompilerParams(vmem_limit_bytes=6 << 20),
@@ -298,7 +322,9 @@
     results = []
     for level in range(levels):
         last = level + 1 == levels
-        parts = [partial] + [along_rep(partial, apart) for apart in APART]
+        parts = [partial] + [
+            along_rep(partial, apart) for apart in (APART if level else APART_FIRST)
+        ]
         weights = [diag, late_mats if level else early_mats]
         if last:
             return run_solve(
@@ -316,9 +342,9 @@
         sibling, diag = next_diag(level + 1, chip, sibling, diag_hbm)
         from_far = to_far(far)
         across = to_sibling(
-            (from_chip[0].astype(jnp.float32) + sibling.astype(jnp.float32)).astype(jnp.bfloat16)
-        )
-        incoming = sum(piece.astype(jnp.float32) for piece in (own, from_chip[1], from_far, across))
+            (from_chip[1].astype(jnp.float32) + sibling.astype(jnp.float32)).astype(jnp.bfloat16)
+        )
+        incoming = sum(piece.astype(jnp.float32) for piece in (own, from_chip[0], from_far, across))
         partial = (own_rhs[level + 1] - incoming).astype(jnp.bfloat16)
 
 

time: 75.5 us -> 74.5 us (0.987)
  starting transfers between devices: 32.9 us -> 30.3 us
  waiting for transfers between devices: 23.9 us -> 25.5 us
    ppermute x12, starting transfers between devices: 17.1 us -> 14.5 us  [dom_permute(): lax.ppermute(value, 'dom', [(i, target(i) % size) for i in range(size)])]
    ppermute x12, waiting for transfers between devices: 10.4 us -> 12 us  [dom_permute(): lax.ppermute(value, 'dom', [(i, target(i) % size) for i in range(size)])]
  transfers between devices with their start and end apart: 24 -> 24, of which waited for: 14 -> 15; matrix products, arithmetic and copies ran while one was open for 0% -> 0% of each run, Pallas kernels for 16% -> 16%
where the time goes in v7:
time: 74.5 us; the launch traced here: 74.1 us
  starting transfers between devices  30.3 us (41%)
  waiting for transfers between devices  25.5 us (34%)
  Pallas kernels  16.4 us (22%)
  local copies, waits for them, and re-layouts  0.8 us (1%)
  other arithmetic  0.78 us (1%)
    ppermute x12, starting transfers between devices, along_rep(): lax.ppermute(value, 'rep', [(i, i ^ apart) for i in range(lax.axis_size('...  15.8 us
    ppermute x12, starting transfers between devices, dom_permute(): lax.ppermute(value, 'dom', [(i, target(i) % size) for i in range(size)])  14.5 us
    ppermute x12, waiting for transfers between devices, along_rep(): lax.ppermute(value, 'rep', [(i, i ^ apart) for i in range(lax.axis_size('...  13.5 us
    ppermute x12, waiting for transfers between devices, dom_permute(): lax.ppermute(value, 'dom', [(i, target(i) % size) for i in range(size)])  12 us
    pallas_call x4, Pallas kernels, run_solve(): pl.pallas_call(functools.partial(solve_body, level, last), out_shape=outs...  4.76 us
    pallas_call x3, Pallas kernels, next_diag(): pl.pallas_call(functools.partial(next_diag_body, level), out_shape=[jax.S...  4.39 us
    pallas_call x3, Pallas kernels, run_panels(): pl.pallas_call(functools.partial(panels_body, level), out_shape=[jax.Shap...  4.15 us
    pallas_call x1, Pallas kernels, fetch(): pl.pallas_call(functools.partial(fetch_body, lax.axis_size('dom')), out_s...  3.1 us
  transfers between devices with their start and end apart: 24, of which 15 were waited for; matrix products, arithmetic and copies ran while one was open for 0% of the time, Pallas kernels for 16%

profile of v7, /device:TPU:0, one launch (start us, length us, event | category | flops | bytes accessed | tf_op | source)
XLA Modules:
  0.0 74.1 jit_solution(15197804976552868625)
XLA Ops:
  0.0 0.8 %fusion.15.refs_1_.refs_2_ = bf16[6,4,384]{2,1,0:T(4,128)(2,1)S(1)} fusion(f32[4,6,4,384]{3,2,1,0:T(4,128)} %param.5), kind=kLoop, calls=%fused_computation.36 | loop fusion | bytes 36864 | tf_op jit(solution)/shard_map/convert_element_type | solution.py:312
  0.8 4.1 %collective-permute-start = (bf16[6,4,384]{2,1,0:T(4,128)(2,1)S(1)}, bf16[6,4,384]{2,1,0:T(4,128)(2,1)S(1)}, u32[]{:S(2)}, u32[]{:S(2)}) collective-permute-start(bf16[6,4,384]{2,1,0:T(4,128)(2,1)S(1)} %fusion.15.refs_1_.refs_2_), channel_id=1, source_target_pairs={{0,3},{1,2},{2,1},{3,0},{4,7},{5,6},{6,5},{7,4},{8,11},{9,10},{10,... | collective-permute-start | bytes 55304 | tf_op jit(solution)/shard_map/ppermute | solution.py:39
  4.9 0.0 collective-permute-start.1
  4.9 0.9 %collective-permute-start.2 = (bf16[6,4,384]{2,1,0:T(4,128)(2,1)S(1)}, bf16[6,4,384]{2,1,0:T(4,128)(2,1)S(1)}, u32[]{:S(2)}, u32[]{:S(2)}) collective-permute-start(bf16[6,4,384]{2,1,0:T(4,128)(2,1)S(1)} %fusion.15.refs_1_.refs_2_), channel_id=1, source_target_pairs={{0,1},{1,0},{2,3},{3,2},{4,5},{5,4},{6,7},{7,6},{8,9},{9,8},{10,11... | collective-permute-start | bytes 55304 | tf_op jit(solution)/shard_map/ppermute | solution.py:39
  5.8 3.1 %shard_map.55 = (s32[2,3,16]{2,1,0:T(4,128)S(1)}, bf16[1,6,384,384]{3,2,1,0:T(8,128)(2,1)S(1)}, bf16[1,16,384,384]{3,2,1,0:T(8,128)(2,1)S(1)}) custom-call(s32[1]{0:T(128)} %bitcast.2.refs_0_, bf16[6,4,384]{2,1,0:T(4,128)(2,1)S(1)} %fusion.15.refs_1_.refs_2_, s32[3,16]{1,0:T(4,128)} %refs_2_.4, s32[3,16]{1,0:T(4,128)} %refs_3_.1, ...), custom_call_target="tpu_custom_call" | custom-call | tf_op jit(solution)/shard_map/pallas_call | solution.py:263
  9.0 0.0 collective-permute-done.refs_3_
  9.0 1.2 %collective-permute-done.1.refs_4_ = bf16[6,4,384]{2,1,0:T(4,128)(2,1)S(1)} collective-permute-done((bf16[6,4,384]{2,1,0:T(4,128)(2,1)S(1)}, bf16[6,4,384]{2,1,0:T(4,128)(2,1)S(1)}, u32[]{:S(2)}, u32[]{:S(2)}) %collective-permute-start.1) | collective-permute-done | bytes 18464 | tf_op jit(solution)/shard_map/ppermute | solution.py:39
  10.2 0.0 collective-permute-done.2.refs_5_
  10.2 1.3 %shard_map.56 = (f32[6,4,384]{2,1,0:T(4,128)S(1)}, bf16[6,16,384]{2,1,0:T(8,128)(2,1)S(1)}, bf16[6,16,384]{2,1,0:T(8,128)(2,1)S(1)}) custom-call(s32[1]{0:T(128)} %bitcast.refs_0_, s32[2,3,16]{2,1,0:T(4,128)S(1)} %get-tuple-element.35.refs_1_.refs_0_, bf16[6,4,384]{2,1,0:T(4,128)(2,1)S(1)} %fusion.15.refs_1_.refs_2_, ...), custom_call_target="tpu_custom_call" | custom-call | tf_op jit(solution)/shard_map/pallas_call | solution.py:183
  11.4 0.1 collective-permute-start.3
  11.5 0.0 slice-start.3
  11.5 1.4 %shard_map.57 = (bf16[6,16,384]{2,1,0:T(8,128)(2,1)S(1)}, bf16[6,16,384]{2,1,0:T(8,128)(2,1)S(1)}, bf16[6,16,384]{2,1,0:T(8,128)(2,1)S(1)}, bf16[2,6,16,384]{3,2,1,0:T(8,128)(2,1)S(1)}) custom-call(s32[2,3,16]{2,1,0:T(4,128)S(1)} %get-tuple-element.35.refs_1_.refs_0_, bf16[1,16,384,384]{3,2,1,0:T(8,128)(2,1)S(1)} %get-tuple-element.37.refs_7_.refs_1_, ...), custom_call_target="tpu_custom_call" | custom-call | tf_op jit(solution)/shard_map/pallas_call | solution.py:197
  12.9 0.0 collective-permute-done.3
  12.9 0.1 add_convert_fusion.2.refs_0_
  13.1 5.4 %collective-permute-start.4 = (bf16[2,6,16,384]{3,2,1,0:T(8,128)(2,1)S(1)}, bf16[2,6,16,384]{3,2,1,0:T(8,128)(2,1)S(1)}, u32[]{:S(2)}, u32[]{:S(2)}) collective-permute-start(bf16[2,6,16,384]{3,2,1,0:T(8,128)(2,1)S(1)} %add_convert_fusion.2.refs_0_), channel_id=1, source_target_pairs={{0,124},{4,8},{8,4},{12,16},{16,12},{20,24},{24,20},{28,32},{32,28... | collective-permute-start | bytes 442376 | tf_op jit(solution)/shard_map/ppermute | solution.py:22
  18.5 0.7 collective-permute-start.5
  19.2 1.5 %shard_map.58 = (bf16[6,16,384]{2,1,0:T(8,128)(2,1)S(1)}, bf16[1,6,384,384]{3,2,1,0:T(8,128)(2,1)S(1)}) custom-call(bf16[2,6,16,384]{3,2,1,0:T(8,128)(2,1)S(1)} %add_convert_fusion.2.refs_0_, bf16[6,16,384]{2,1,0:T(8,128)(2,1)S(1)} %get-tuple-element.43.refs_1_, bf16[4,6,384,384]{3,2,1,0:T(8,128)(2,1)} %refs_2_.7), custom_call_target="tpu_custom_call" | custom-call | tf_op jit(solution)/shard_map/pallas_call | solution.py:293
  20.7 0.7 collective-permute-done.4
  21.3 0.1 collective-permute-start.6
  21.4 0.1 maximum_select_fusion
  21.6 2.8 %collective-permute-done.5 = bf16[6,16,384]{2,1,0:T(8,128)(2,1)S(1)} collective-permute-done((bf16[6,16,384]{2,1,0:T(8,128)(2,1)S(1)}, bf16[6,16,384]{2,1,0:T(8,128)(2,1)S(1)}, u32[]{:S(2)}, u32[]{:S(2)}) %collective-permute-start.5) | collective-permute-done | bytes 73760 | tf_op jit(solution)/shard_map/ppermute | solution.py:22
  24.4 0.0 collective-permute-done.6
  24.4 0.1 fusion.3.refs_2_
  24.4 2.1 %collective-permute-start.7 = (bf16[6,16,384]{2,1,0:T(8,128)(2,1)S(1)}, bf16[6,16,384]{2,1,0:T(8,128)(2,1)S(1)}, u32[]{:S(2)}, u32[]{:S(2)}) collective-permute-start(bf16[6,16,384]{2,1,0:T(8,128)(2,1)S(1)} %fusion.3.refs_2_), channel_id=1, source_target_pairs={{0,2},{1,3},{2,0},{3,1},{4,6},{5,7},{6,4},{7,5},{8,10},{9,11},{10,... | collective-permute-start | bytes 221192 | tf_op jit(solution)/shard_map/ppermute | solution.py:39
  26.6 0.6 collective-permute-start.8
  27.1 0.9 %collective-permute-start.9 = (bf16[6,16,384]{2,1,0:T(8,128)(2,1)S(1)}, bf16[6,16,384]{2,1,0:T(8,128)(2,1)S(1)}, u32[]{:S(2)}, u32[]{:S(2)}) collective-permute-start(bf16[6,16,384]{2,1,0:T(8,128)(2,1)S(1)} %fusion.3.refs_2_), channel_id=1, source_target_pairs={{0,1},{1,0},{2,3},{3,2},{4,5},{5,4},{6,7},{7,6},{8,9},{9,8},{10,11... | collective-permute-start | bytes 221192 | tf_op jit(solution)/shard_map/ppermute | solution.py:39
  28.0 3.0 %collective-permute-done.7.refs_3_ = bf16[6,16,384]{2,1,0:T(8,128)(2,1)S(1)} collective-permute-done((bf16[6,16,384]{2,1,0:T(8,128)(2,1)S(1)}, bf16[6,16,384]{2,1,0:T(8,128)(2,1)S(1)}, u32[]{:S(2)}, u32[]{:S(2)}) %collective-permute-start.7) | collective-permute-done | bytes 73760 | tf_op jit(solution)/shard_map/ppermute | solution.py:39
  31.1 1.1 %collective-permute-done.8.refs_4_ = bf16[6,16,384]{2,1,0:T(8,128)(2,1)S(1)} collective-permute-done((bf16[6,16,384]{2,1,0:T(8,128)(2,1)S(1)}, bf16[6,16,384]{2,1,0:T(8,128)(2,1)S(1)}, u32[]{:S(2)}, u32[]{:S(2)}) %collective-permute-start.8) | collective-permute-done | bytes 73760 | tf_op jit(solution)/shard_map/ppermute | solution.py:39
  32.2 1.2 %shard_map.59 = (f32[6,4,384]{2,1,0:T(4,128)S(1)}, bf16[6,16,384]{2,1,0:T(8,128)(2,1)S(1)}, bf16[6,16,384]{2,1,0:T(8,128)(2,1)S(1)}) custom-call(s32[1]{0:T(128)} %bitcast.refs_0_, s32[2,3,16]{2,1,0:T(4,128)S(1)} %get-tuple-element.35.refs_1_.refs_0_, bf16[6,16,384]{2,1,0:T(8,128)(2,1)S(1)} %fusion.3.refs_2_, ...), custom_call_target="tpu_custom_call" | custom-call | tf_op jit(solution)/shard_map/pallas_call | solution.py:183
  33.4 0.1 collective-permute-start.10
  33.5 1.4 %shard_map.60 = (bf16[6,16,384]{2,1,0:T(8,128)(2,1)S(1)}, bf16[6,16,384]{2,1,0:T(8,128)(2,1)S(1)}, bf16[6,16,384]{2,1,0:T(8,128)(2,1)S(1)}, bf16[2,6,16,384]{3,2,1,0:T(8,128)(2,1)S(1)}) custom-call(s32[2,3,16]{2,1,0:T(4,128)S(1)} %get-tuple-element.35.refs_1_.refs_0_, bf16[3,16,384,384]{3,2,1,0:T(8,128)(2,1)S(1)} %bitcast.53, ...), custom_call_target="tpu_custom_call" | custom-call | tf_op jit(solution)/shard_map/pallas_call | solution.py:197
  34.9 0.0 collective-permute-done.10
  34.9 0.1 add_convert_fusion.1.refs_0_
  35.0 4.3 %collective-permute-start.11 = (bf16[2,6,16,384]{3,2,1,0:T(8,128)(2,1)S(1)}, bf16[2,6,16,384]{3,2,1,0:T(8,128)(2,1)S(1)}, u32[]{:S(2)}, u32[]{:S(2)}) collective-permute-start(bf16[2,6,16,384]{3,2,1,0:T(8,128)(2,1)S(1)} %add_convert_fusion.1.refs_0_), channel_id=1, source_target_pairs={{0,124},{4,8},{8,4},{12,16},{16,12},{20,24},{24,20},{28,32},{32,28... | collective-permute-start | bytes 442376 | tf_op jit(solution)/shard_map/ppermute | solution.py:22
  39.3 0.0 collective-permute-start.12
  39.3 1.5 %shard_map.61 = (bf16[6,16,384]{2,1,0:T(8,128)(2,1)S(1)}, bf16[1,6,384,384]{3,2,1,0:T(8,128)(2,1)S(1)}) custom-call(bf16[2,6,16,384]{3,2,1,0:T(8,128)(2,1)S(1)} %add_convert_fusion.1.refs_0_, bf16[6,16,384]{2,1,0:T(8,128)(2,1)S(1)} %get-tuple-element.51.refs_1_, bf16[4,6,384,384]{3,2,1,0:T(8,128)(2,1)} %refs_2_.7), custom_call_target="tpu_custom_call" | custom-call | tf_op jit(solution)/shard_map/pallas_call | solution.py:293
  40.8 2.3 %collective-permute-done.11 = bf16[2,6,16,384]{3,2,1,0:T(8,128)(2,1)S(1)} collective-permute-done((bf16[2,6,16,384]{3,2,1,0:T(8,128)(2,1)S(1)}, bf16[2,6,16,384]{3,2,1,0:T(8,128)(2,1)S(1)}, u32[]{:S(2)}, u32[]{:S(2)}) %collective-permute-start.11) | collective-permute-done | bytes 147488 | tf_op jit(solution)/shard_map/ppermute | solution.py:22
  43.1 0.1 collective-permute-start.13
  43.2 2.0 %collective-permute-done.12 = bf16[6,16,384]{2,1,0:T(8,128)(2,1)S(1)} collective-permute-done((bf16[6,16,384]{2,1,0:T(8,128)(2,1)S(1)}, bf16[6,16,384]{2,1,0:T(8,128)(2,1)S(1)}, u32[]{:S(2)}, u32[]{:S(2)}) %collective-permute-start.12) | collective-permute-done | bytes 73760 | tf_op jit(solution)/shard_map/ppermute | solution.py:22
  45.2 0.1 fusion.1.refs_2_
  45.3 1.8 %collective-permute-start.14 = (bf16[6,16,384]{2,1,0:T(8,128)(2,1)S(1)}, bf16[6,16,384]{2,1,0:T(8,128)(2,1)S(1)}, u32[]{:S(2)}, u32[]{:S(2)}) collective-permute-start(bf16[6,16,384]{2,1,0:T(8,128)(2,1)S(1)} %fusion.1.refs_2_), channel_id=1, source_target_pairs={{0,2},{1,3},{2,0},{3,1},{4,6},{5,7},{6,4},{7,5},{8,10},{9,11},{10,... | collective-permute-start | bytes 221192 | tf_op jit(solution)/shard_map/ppermute | solution.py:39
  47.1 1.5 %collective-permute-start.15 = (bf16[6,16,384]{2,1,0:T(8,128)(2,1)S(1)}, bf16[6,16,384]{2,1,0:T(8,128)(2,1)S(1)}, u32[]{:S(2)}, u32[]{:S(2)}) collective-permute-start(bf16[6,16,384]{2,1,0:T(8,128)(2,1)S(1)} %fusion.1.refs_2_), channel_id=1, source_target_pairs={{0,3},{1,2},{2,1},{3,0},{4,7},{5,6},{6,5},{7,4},{8,11},{9,10},{10,... | collective-permute-start | bytes 221192 | tf_op jit(solution)/shard_map/ppermute | solution.py:39
  48.6 0.3 collective-permute-start.16
  48.8 2.5 %collective-permute-done.14.refs_3_ = bf16[6,16,384]{2,1,0:T(8,128)(2,1)S(1)} collective-permute-done((bf16[6,16,384]{2,1,0:T(8,128)(2,1)S(1)}, bf16[6,16,384]{2,1,0:T(8,128)(2,1)S(1)}, u32[]{:S(2)}, u32[]{:S(2)}) %collective-permute-start.14) | collective-permute-done | bytes 73760 | tf_op jit(solution)/shard_map/ppermute | solution.py:39
  51.3 1.3 %collective-permute-done.15.refs_4_ = bf16[6,16,384]{2,1,0:T(8,128)(2,1)S(1)} collective-permute-done((bf16[6,16,384]{2,1,0:T(8,128)(2,1)S(1)}, bf16[6,16,384]{2,1,0:T(8,128)(2,1)S(1)}, u32[]{:S(2)}, u32[]{:S(2)}) %collective-permute-start.15) | collective-permute-done | bytes 73760 | tf_op jit(solution)/shard_map/ppermute | solution.py:39
  52.6 0.3 collective-permute-done.16.refs_5_
  52.9 1.2 %shard_map.62 = (f32[6,4,384]{2,1,0:T(4,128)S(1)}, bf16[6,16,384]{2,1,0:T(8,128)(2,1)S(1)}, bf16[6,16,384]{2,1,0:T(8,128)(2,1)S(1)}) custom-call(s32[1]{0:T(128)} %bitcast.refs_0_, s32[2,3,16]{2,1,0:T(4,128)S(1)} %get-tuple-element.35.refs_1_.refs_0_, bf16[6,16,384]{2,1,0:T(8,128)(2,1)S(1)} %fusion.1.refs_2_, ...), custom_call_target="tpu_custom_call" | custom-call | tf_op jit(solution)/shard_map/pallas_call | solution.py:183
  54.2 0.1 collective-permute-start.17
  54.3 1.4 %shard_map.63 = (bf16[6,16,384]{2,1,0:T(8,128)(2,1)S(1)}, bf16[6,16,384]{2,1,0:T(8,128)(2,1)S(1)}, bf16[6,16,384]{2,1,0:T(8,128)(2,1)S(1)}, bf16[2,6,16,384]{3,2,1,0:T(8,128)(2,1)S(1)}) custom-call(s32[2,3,16]{2,1,0:T(4,128)S(1)} %get-tuple-element.35.refs_1_.refs_0_, bf16[3,16,384,384]{3,2,1,0:T(8,128)(2,1)S(1)} %bitcast.53, ...), custom_call_target="tpu_custom_call" | custom-call | tf_op jit(solution)/shard_map/pallas_call | solution.py:197
  55.7 0.0 collective-permute-done.17
  55.7 0.1 add_convert_fusion.refs_0_
  55.8 3.6 %collective-permute-start.18 = (bf16[2,6,16,384]{3,2,1,0:T(8,128)(2,1)S(1)}, bf16[2,6,16,384]{3,2,1,0:T(8,128)(2,1)S(1)}, u32[]{:S(2)}, u32[]{:S(2)}) collective-permute-start(bf16[2,6,16,384]{3,2,1,0:T(8,128)(2,1)S(1)} %add_convert_fusion.refs_0_), channel_id=1, source_target_pairs={{0,124},{4,8},{8,4},{12,16},{16,12},{20,24},{24,20},{28,32},{32,28... | collective-permute-start | bytes 442376 | tf_op jit(solution)/shard_map/ppermute | solution.py:22
  59.5 1.5 %shard_map.64 = (bf16[6,16,384]{2,1,0:T(8,128)(2,1)S(1)}, bf16[1,6,384,384]{3,2,1,0:T(8,128)(2,1)S(1)}) custom-call(bf16[2,6,16,384]{3,2,1,0:T(8,128)(2,1)S(1)} %add_convert_fusion.refs_0_, bf16[6,16,384]{2,1,0:T(8,128)(2,1)S(1)} %get-tuple-element.59.refs_1_, bf16[4,6,384,384]{3,2,1,0:T(8,128)(2,1)} %refs_2_.7), custom_call_target="tpu_custom_call" | custom-call | tf_op jit(solution)/shard_map/pallas_call | solution.py:293
  60.9 2.9 %collective-permute-done.18 = bf16[2,6,16,384]{3,2,1,0:T(8,128)(2,1)S(1)} collective-permute-done((bf16[2,6,16,384]{3,2,1,0:T(8,128)(2,1)S(1)}, bf16[2,6,16,384]{3,2,1,0:T(8,128)(2,1)S(1)}, u32[]{:S(2)}, u32[]{:S(2)}) %collective-permute-start.18) | collective-permute-done | bytes 147488 | tf_op jit(solution)/shard_map/ppermute | solution.py:22
  63.8 0.1 collective-permute-start.20
  63.9 1.4 %collective-permute-done.19 = bf16[6,16,384]{2,1,0:T(8,128)(2,1)S(1)} collective-permute-done((bf16[6,16,384]{2,1,0:T(8,128)(2,1)S(1)}, bf16[6,16,384]{2,1,0:T(8,128)(2,1)S(1)}, u32[]{:S(2)}, u32[]{:S(2)}) %collective-permute-start.19) | collective-permute-done | bytes 73760 | tf_op jit(solution)/shard_map/ppermute | solution.py:22
  65.3 0.1 fusion.5.refs_1_
  65.4 1.8 %collective-permute-start.21 = (bf16[6,16,384]{2,1,0:T(8,128)(2,1)S(1)}, bf16[6,16,384]{2,1,0:T(8,128)(2,1)S(1)}, u32[]{:S(2)}, u32[]{:S(2)}) collective-permute-start(bf16[6,16,384]{2,1,0:T(8,128)(2,1)S(1)} %fusion.5.refs_1_), channel_id=1, source_target_pairs={{0,2},{1,3},{2,0},{3,1},{4,6},{5,7},{6,4},{7,5},{8,10},{9,11},{10,... | collective-permute-start | bytes 221192 | tf_op jit(solution)/shard_map/ppermute | solution.py:39
  67.2 1.5 %collective-permute-start.22 = (bf16[6,16,384]{2,1,0:T(8,128)(2,1)S(1)}, bf16[6,16,384]{2,1,0:T(8,128)(2,1)S(1)}, u32[]{:S(2)}, u32[]{:S(2)}) collective-permute-start(bf16[6,16,384]{2,1,0:T(8,128)(2,1)S(1)} %fusion.5.refs_1_), channel_id=1, source_target_pairs={{0,3},{1,2},{2,1},{3,0},{4,7},{5,6},{6,5},{7,4},{8,11},{9,10},{10,... | collective-permute-start | bytes 221192 | tf_op jit(solution)/shard_map/ppermute | solution.py:39
  68.7 0.3 collective-permute-start.23
  68.9 2.4 %collective-permute-done.21.refs_2_ = bf16[6,16,384]{2,1,0:T(8,128)(2,1)S(1)} collective-permute-done((bf16[6,16,384]{2,1,0:T(8,128)(2,1)S(1)}, bf16[6,16,384]{2,1,0:T(8,128)(2,1)S(1)}, u32[]{:S(2)}, u32[]{:S(2)}) %collective-permute-start.21) | collective-permute-done | bytes 73760 | tf_op jit(solution)/shard_map/ppermute | solution.py:39
  71.4 1.5 %collective-permute-done.22.refs_3_ = bf16[6,16,384]{2,1,0:T(8,128)(2,1)S(1)} collective-permute-done((bf16[6,16,384]{2,1,0:T(8,128)(2,1)S(1)}, bf16[6,16,384]{2,1,0:T(8,128)(2,1)S(1)}, u32[]{:S(2)}, u32[]{:S(2)}) %collective-permute-start.22) | collective-permute-done | bytes 73760 | tf_op jit(solution)/shard_map/ppermute | solution.py:39
  72.9 0.1 collective-permute-done.23.refs_4_
  73.0 1.0 %shard_map.65 = f32[4,6,4,384]{3,2,1,0:T(4,128)} custom-call(s32[1]{0:T(128)} %bitcast.refs_0_, bf16[6,16,384]{2,1,0:T(8,128)(2,1)S(1)} %fusion.5.refs_1_, bf16[6,16,384]{2,1,0:T(8,128)(2,1)S(1)} %collective-permute-done.21.refs_2_, bf16[6,16,384]{2,1,0:T(8,128)(2,1)S(1)} %collective-permute-done.22.refs_3_, ...), custom_call_target="tpu_custom_call" | custom-call | tf_op jit(solution)/shard_map/pallas_call | solution.py:183
  (20 shorter events, 0.1 us)
Async XLA Ops:
  0.8 8.2 %collective-permute-start = (bf16[6,4,384]{2,1,0:T(4,128)(2,1)S(1)}, bf16[6,4,384]{2,1,0:T(4,128)(2,1)S(1)}, u32[]{:S(2)}, u32[]{:S(2)}) collective-permute-start(bf16[6,4,384]{2,1,0:T(4,128)(2,1)S(1)} %fusion.15.refs_1_.refs_2_), channel_id=1, source_target_pairs={{0,3},{1,2},{2,1},{3,0},{4,7},{5,6},{6,5},{7,4},{8,11},{9,10},{10,... | collective-permute-start | bytes 55304 | tf_op jit(solution)/shard_map/ppermute | solution.py:39
  4.9 5.3 %collective-permute-start.1 = (bf16[6,4,384]{2,1,0:T(4,128)(2,1)S(1)}, bf16[6,4,384]{2,1,0:T(4,128)(2,1)S(1)}, u32[]{:S(2)}, u32[]{:S(2)}) collective-permute-start(bf16[6,4,384]{2,1,0:T(4,128)(2,1)S(1)} %fusion.15.refs_1_.refs_2_), channel_id=1, source_target_pairs={{0,2},{1,3},{2,0},{3,1},{4,6},{5,7},{6,4},{7,5},{8,10},{9,11},{10,... | collective-permute-start | bytes 55304 | tf_op jit(solution)/shard_map/ppermute | solution.py:39
  4.9 5.3 %collective-permute-start.2 = (bf16[6,4,384]{2,1,0:T(4,128)(2,1)S(1)}, bf16[6,4,384]{2,1,0:T(4,128)(2,1)S(1)}, u32[]{:S(2)}, u32[]{:S(2)}) collective-permute-start(bf16[6,4,384]{2,1,0:T(4,128)(2,1)S(1)} %fusion.15.refs_1_.refs_2_), channel_id=1, source_target_pairs={{0,1},{1,0},{2,3},{3,2},{4,5},{5,4},{6,7},{7,6},{8,9},{9,8},{10,11... | collective-permute-start | bytes 55304 | tf_op jit(solution)/shard_map/ppermute | solution.py:39
  5.8 26.3 %slice-start = ((s8[14155776]{0:T(1024)(128)(4,1)}), s8[4194304]{0:T(1024)(128)(4,1)S(1)}, s32[]{:S(2)}) async-start(s8[14155776]{0:T(1024)(128)(4,1)} %bitcast.52), calls=%async_computation | async-start | bytes 8388608
  5.8 26.3 %slice-start.1 = ((s8[14155776]{0:T(1024)(128)(4,1)}), s8[4194304]{0:T(1024)(128)(4,1)S(1)}, s32[]{:S(2)}) async-start(s8[14155776]{0:T(1024)(128)(4,1)} %bitcast.52), calls=%async_computation.1 | async-start | bytes 8388608
  5.8 26.3 %slice-start.2 = ((s8[14155776]{0:T(1024)(128)(4,1)}), s8[4194304]{0:T(1024)(128)(4,1)S(1)}, s32[]{:S(2)}) async-start(s8[14155776]{0:T(1024)(128)(4,1)} %bitcast.52), calls=%async_computation.2 | async-start | bytes 8388608
  11.4 1.5 %collective-permute-start.3 = (bf16[6,16,384]{2,1,0:T(8,128)(2,1)S(1)}, bf16[6,16,384]{2,1,0:T(8,128)(2,1)S(1)}, u32[]{:S(2)}, u32[]{:S(2)}) collective-permute-start(bf16[6,16,384]{2,1,0:T(8,128)(2,1)S(1)} %get-tuple-element.41), channel_id=1, source_target_pairs={{0,4},{4,0},{8,12},{12,8},{16,20},{20,16},{24,28},{28,24},{32,36},... | collective-permute-start | bytes 221192 | tf_op jit(solution)/shard_map/ppermute | solution.py:22
  11.5 20.6 %slice-start.3 = ((s8[14155776]{0:T(1024)(128)(4,1)}), s8[1572864]{0:T(1024)(128)(4,1)S(1)}, s32[]{:S(2)}) async-start(s8[14155776]{0:T(1024)(128)(4,1)} %bitcast.52), calls=%async_computation.3 | async-start | bytes 3145728
  13.1 8.2 %collective-permute-start.4 = (bf16[2,6,16,384]{3,2,1,0:T(8,128)(2,1)S(1)}, bf16[2,6,16,384]{3,2,1,0:T(8,128)(2,1)S(1)}, u32[]{:S(2)}, u32[]{:S(2)}) collective-permute-start(bf16[2,6,16,384]{3,2,1,0:T(8,128)(2,1)S(1)} %add_convert_fusion.2.refs_0_), channel_id=1, source_target_pairs={{0,124},{4,8},{8,4},{12,16},{16,12},{20,24},{24,20},{28,32},{32,28... | collective-permute-start | bytes 442376 | tf_op jit(solution)/shard_map/ppermute | solution.py:22
  18.5 5.9 %collective-permute-start.5 = (bf16[6,16,384]{2,1,0:T(8,128)(2,1)S(1)}, bf16[6,16,384]{2,1,0:T(8,128)(2,1)S(1)}, u32[]{:S(2)}, u32[]{:S(2)}) collective-permute-start(bf16[6,16,384]{2,1,0:T(8,128)(2,1)S(1)} %get-tuple-element.42), channel_id=1, source_target_pairs={{0,64},{4,68},{8,72},{12,76},{16,80},{20,84},{24,88},{28,92},{32,9... | collective-permute-start | bytes 221192 | tf_op jit(solution)/shard_map/ppermute | solution.py:22
  19.2 2.3 %copy-start = (f32[4,6,4,384]{3,2,1,0:T(4,128)S(1)}, f32[4,6,4,384]{3,2,1,0:T(4,128)}, u32[]{:S(2)}) copy-start(f32[4,6,4,384]{3,2,1,0:T(4,128)} %param.5) | copy-start | bytes 442372
  21.3 3.1 %collective-permute-start.6 = (bf16[6,16,384]{2,1,0:T(8,128)(2,1)S(1)}, bf16[6,16,384]{2,1,0:T(8,128)(2,1)S(1)}, u32[]{:S(2)}, u32[]{:S(2)}) collective-permute-start(bf16[6,16,384]{2,1,0:T(8,128)(2,1)S(1)} %fusion.12), channel_id=1, source_target_pairs={{0,4},{4,0},{8,12},{12,8},{16,20},{20,16},{24,28},{28,24},{32,36},... | collective-permute-start | bytes 221192 | tf_op jit(solution)/shard_map/ppermute | solution.py:22
  24.4 6.6 %collective-permute-start.7 = (bf16[6,16,384]{2,1,0:T(8,128)(2,1)S(1)}, bf16[6,16,384]{2,1,0:T(8,128)(2,1)S(1)}, u32[]{:S(2)}, u32[]{:S(2)}) collective-permute-start(bf16[6,16,384]{2,1,0:T(8,128)(2,1)S(1)} %fusion.3.refs_2_), channel_id=1, source_target_pairs={{0,2},{1,3},{2,0},{3,1},{4,6},{5,7},{6,4},{7,5},{8,10},{9,11},{10,... | collective-permute-start | bytes 221192 | tf_op jit(solution)/shard_map/ppermute | solution.py:39
  26.6 5.6 %collective-permute-start.8 = (bf16[6,16,384]{2,1,0:T(8,128)(2,1)S(1)}, bf16[6,16,384]{2,1,0:T(8,128)(2,1)S(1)}, u32[]{:S(2)}, u32[]{:S(2)}) collective-permute-start(bf16[6,16,384]{2,1,0:T(8,128)(2,1)S(1)} %fusion.3.refs_2_), channel_id=1, source_target_pairs={{0,3},{1,2},{2,1},{3,0},{4,7},{5,6},{6,5},{7,4},{8,11},{9,10},{10,... | collective-permute-start | bytes 221192 | tf_op jit(solution)/shard_map/ppermute | solution.py:39
  27.1 5.0 %collective-permute-start.9 = (bf16[6,16,384]{2,1,0:T(8,128)(2,1)S(1)}, bf16[6,16,384]{2,1,0:T(8,128)(2,1)S(1)}, u32[]{:S(2)}, u32[]{:S(2)}) collective-permute-start(bf16[6,16,384]{2,1,0:T(8,128)(2,1)S(1)} %fusion.3.refs_2_), channel_id=1, source_target_pairs={{0,1},{1,0},{2,3},{3,2},{4,5},{5,4},{6,7},{7,6},{8,9},{9,8},{10,11... | collective-permute-start | bytes 221192 | tf_op jit(solution)/shard_map/ppermute | solution.py:39
  33.4 1.5 %collective-permute-start.10 = (bf16[6,16,384]{2,1,0:T(8,128)(2,1)S(1)}, bf16[6,16,384]{2,1,0:T(8,128)(2,1)S(1)}, u32[]{:S(2)}, u32[]{:S(2)}) collective-permute-start(bf16[6,16,384]{2,1,0:T(8,128)(2,1)S(1)} %get-tuple-element.49), channel_id=1, source_target_pairs={{0,4},{4,0},{8,12},{12,8},{16,20},{20,16},{24,28},{28,24},{32,36},... | collective-permute-start | bytes 221192 | tf_op jit(solution)/shard_map/ppermute | solution.py:22
  35.0 8.1 %collective-permute-start.11 = (bf16[2,6,16,384]{3,2,1,0:T(8,128)(2,1)S(1)}, bf16[2,6,16,384]{3,2,1,0:T(8,128)(2,1)S(1)}, u32[]{:S(2)}, u32[]{:S(2)}) collective-permute-start(bf16[2,6,16,384]{3,2,1,0:T(8,128)(2,1)S(1)} %add_convert_fusion.1.refs_0_), channel_id=1, source_target_pairs={{0,124},{4,8},{8,4},{12,16},{16,12},{20,24},{24,20},{28,32},{32,28... | collective-permute-start | bytes 442376 | tf_op jit(solution)/shard_map/ppermute | solution.py:22
  39.3 5.9 %collective-permute-start.12 = (bf16[6,16,384]{2,1,0:T(8,128)(2,1)S(1)}, bf16[6,16,384]{2,1,0:T(8,128)(2,1)S(1)}, u32[]{:S(2)}, u32[]{:S(2)}) collective-permute-start(bf16[6,16,384]{2,1,0:T(8,128)(2,1)S(1)} %get-tuple-element.50), channel_id=1, source_target_pairs={{0,64},{4,68},{8,72},{12,76},{16,80},{20,84},{24,88},{28,92},{32,9... | collective-permute-start | bytes 221192 | tf_op jit(solution)/shard_map/ppermute | solution.py:22
  43.1 2.1 %collective-permute-start.13 = (bf16[6,16,384]{2,1,0:T(8,128)(2,1)S(1)}, bf16[6,16,384]{2,1,0:T(8,128)(2,1)S(1)}, u32[]{:S(2)}, u32[]{:S(2)}) collective-permute-start(bf16[6,16,384]{2,1,0:T(8,128)(2,1)S(1)} %fusion.9), channel_id=1, source_target_pairs={{0,4},{4,0},{8,12},{12,8},{16,20},{20,16},{24,28},{28,24},{32,36},... | collective-permute-start | bytes 221192 | tf_op jit(solution)/shard_map/ppermute | solution.py:22
  45.3 6.0 %collective-permute-start.14 = (bf16[6,16,384]{2,1,0:T(8,128)(2,1)S(1)}, bf16[6,16,384]{2,1,0:T(8,128)(2,1)S(1)}, u32[]{:S(2)}, u32[]{:S(2)}) collective-permute-start(bf16[6,16,384]{2,1,0:T(8,128)(2,1)S(1)} %fusion.1.refs_2_), channel_id=1, source_target_pairs={{0,2},{1,3},{2,0},{3,1},{4,6},{5,7},{6,4},{7,5},{8,10},{9,11},{10,... | collective-permute-start | bytes 221192 | tf_op jit(solution)/shard_map/ppermute | solution.py:39
  47.1 5.6 %collective-permute-start.15 = (bf16[6,16,384]{2,1,0:T(8,128)(2,1)S(1)}, bf16[6,16,384]{2,1,0:T(8,128)(2,1)S(1)}, u32[]{:S(2)}, u32[]{:S(2)}) collective-permute-start(bf16[6,16,384]{2,1,0:T(8,128)(2,1)S(1)} %fusion.1.refs_2_), channel_id=1, source_target_pairs={{0,3},{1,2},{2,1},{3,0},{4,7},{5,6},{6,5},{7,4},{8,11},{9,10},{10,... | collective-permute-start | bytes 221192 | tf_op jit(solution)/shard_map/ppermute | solution.py:39
  48.6 4.4 %collective-permute-start.16 = (bf16[6,16,384]{2,1,0:T(8,128)(2,1)S(1)}, bf16[6,16,384]{2,1,0:T(8,128)(2,1)S(1)}, u32[]{:S(2)}, u32[]{:S(2)}) collective-permute-start(bf16[6,16,384]{2,1,0:T(8,128)(2,1)S(1)} %fusion.1.refs_2_), channel_id=1, source_target_pairs={{0,1},{1,0},{2,3},{3,2},{4,5},{5,4},{6,7},{7,6},{8,9},{9,8},{10,11... | collective-permute-start | bytes 221192 | tf_op jit(solution)/shard_map/ppermute | solution.py:39
  54.2 1.5 %collective-permute-start.17 = (bf16[6,16,384]{2,1,0:T(8,128)(2,1)S(1)}, bf16[6,16,384]{2,1,0:T(8,128)(2,1)S(1)}, u32[]{:S(2)}, u32[]{:S(2)}) collective-permute-start(bf16[6,16,384]{2,1,0:T(8,128)(2,1)S(1)} %get-tuple-element.57), channel_id=1, source_target_pairs={{0,4},{4,0},{8,12},{12,8},{16,20},{20,16},{24,28},{28,24},{32,36},... | collective-permute-start | bytes 221192 | tf_op jit(solution)/shard_map/ppermute | solution.py:22
  55.8 8.0 %collective-permute-start.18 = (bf16[2,6,16,384]{3,2,1,0:T(8,128)(2,1)S(1)}, bf16[2,6,16,384]{3,2,1,0:T(8,128)(2,1)S(1)}, u32[]{:S(2)}, u32[]{:S(2)}) collective-permute-start(bf16[2,6,16,384]{3,2,1,0:T(8,128)(2,1)S(1)} %add_convert_fusion.refs_0_), channel_id=1, source_target_pairs={{0,124},{4,8},{8,4},{12,16},{16,12},{20,24},{24,20},{28,32},{32,28... | collective-permute-start | bytes 442376 | tf_op jit(solution)/shard_map/ppermute | solution.py:22
  59.4 5.9 %collective-permute-start.19 = (bf16[6,16,384]{2,1,0:T(8,128)(2,1)S(1)}, bf16[6,16,384]{2,1,0:T(8,128)(2,1)S(1)}, u32[]{:S(2)}, u32[]{:S(2)}) collective-permute-start(bf16[6,16,384]{2,1,0:T(8,128)(2,1)S(1)} %get-tuple-element.58), channel_id=1, source_target_pairs={{0,64},{4,68},{8,72},{12,76},{16,80},{20,84},{24,88},{28,92},{32,9... | collective-permute-start | bytes 221192 | tf_op jit(solution)/shard_map/ppermute | solution.py:22
  63.8 1.5 %collective-permute-start.20 = (bf16[6,16,384]{2,1,0:T(8,128)(2,1)S(1)}, bf16[6,16,384]{2,1,0:T(8,128)(2,1)S(1)}, u32[]{:S(2)}, u32[]{:S(2)}) collective-permute-start(bf16[6,16,384]{2,1,0:T(8,128)(2,1)S(1)} %fusion.6), channel_id=1, source_target_pairs={{0,4},{4,0},{8,12},{12,8},{16,20},{20,16},{24,28},{28,24},{32,36},... | collective-permute-start | bytes 221192 | tf_op jit(solution)/shard_map/ppermute | solution.py:22
  65.4 6.0 %collective-permute-start.21 = (bf16[6,16,384]{2,1,0:T(8,128)(2,1)S(1)}, bf16[6,16,384]{2,1,0:T(8,128)(2,1)S(1)}, u32[]{:S(2)}, u32[]{:S(2)}) collective-permute-start(bf16[6,16,384]{2,1,0:T(8,128)(2,1)S(1)} %fusion.5.refs_1_), channel_id=1, source_target_pairs={{0,2},{1,3},{2,0},{3,1},{4,6},{5,7},{6,4},{7,5},{8,10},{9,11},{10,... | collective-permute-start | bytes 221192 | tf_op jit(solution)/shard_map/ppermute | solution.py:39
  67.2 5.7 %collective-permute-start.22 = (bf16[6,16,384]{2,1,0:T(8,128)(2,1)S(1)}, bf16[6,16,384]{2,1,0:T(8,128)(2,1)S(1)}, u32[]{:S(2)}, u32[]{:S(2)}) collective-permute-start(bf16[6,16,384]{2,1,0:T(8,128)(2,1)S(1)} %fusion.5.refs_1_), channel_id=1, source_target_pairs={{0,3},{1,2},{2,1},{3,0},{4,7},{5,6},{6,5},{7,4},{8,11},{9,10},{10,... | collective-permute-start | bytes 221192 | tf_op jit(solution)/shard_map/ppermute | solution.py:39
  68.7 4.4 %collective-permute-start.23 = (bf16[6,16,384]{2,1,0:T(8,128)(2,1)S(1)}, bf16[6,16,384]{2,1,0:T(8,128)(2,1)S(1)}, u32[]{:S(2)}, u32[]{:S(2)}) collective-permute-start(bf16[6,16,384]{2,1,0:T(8,128)(2,1)S(1)} %fusion.5.refs_1_), channel_id=1, source_target_pairs={{0,1},{1,0},{2,3},{3,2},{4,5},{5,4},{6,7},{7,6},{8,9},{9,8},{10,11... | collective-permute-start | bytes 221192 | tf_op jit(solution)/shard_map/ppermute | solution.py:39

commit v8 on v7

--- a/solution.py
+++ b/solution.py
@@ -115,7 +115,7 @@
         chosen_ref[r] = 0
     count = jnp.int32(0)
     for p in range(mats_ref.shape[1]):
-        row = ids_ref[1, level, p] - HANDED * tiles
+        row = ids_ref[1, p] - HANDED * tiles
         live = jnp.logical_and(row >= 0, row < tiles)
         chosen_ref[jnp.minimum(count, SLOTS)] = jnp.int32(p)
         count = count + live.astype(jnp.int32)
@@ -123,9 +123,9 @@
     for r in range(SLOTS):
         p = chosen_ref[r]
         update = jnp.dot(
-            store_scr[ids_ref[0, level, p]], mats_ref[level, p], preferred_element_type=jnp.float32
-        )
-        row = jnp.where(r < count, ids_ref[1, level, p] - HANDED * tiles, tiles)
+            store_scr[ids_ref[0, p]], mats_ref[level, p], preferred_element_type=jnp.float32
+        )
+        row = jnp.where(r < count, ids_ref[1, p] - HANDED * tiles, tiles)
         acc_scr[row] = acc_scr[row] + update
     handed_ref[...] = acc_scr[:tiles].astype(jnp.bfloat16)
 
@@ -142,14 +142,14 @@
             store_scr[earlier * tiles + t] = stores[earlier][t]
     for p in range(0, mats_ref.shape[1], 2):
         updates_scr[p], updates_scr[p + 1] = two_products(
-            store_scr[ids_ref[0, level, p]],
-            store_scr[ids_ref[0, level, p + 1]],
+            store_scr[ids_ref[0, p]],
+            store_scr[ids_ref[0, p + 1]],
             mats_ref[level, p],
             mats_ref[level, p + 1],
         )
     acc_scr[...] = jnp.zeros_like(acc_scr)
     for p in range(mats_ref.shape[1]):
-        slot = ids_ref[1, level, p]
+        slot = ids_ref[1, p]
         acc_scr[slot] = acc_scr[slot] + updates_scr[p]
 
     def sums(index):
@@ -160,6 +160,28 @@
     far_ref[...] = sums(FAR)
     chip_ref[0] = sums(PASSED)
     chip_ref[1] = sums(DIRECT)
+
+
+def last_body(*refs):
+    *refs, out_ref = refs
+    parts, diag_ref, earlier = refs[:4], refs[4], refs[5:]
+    for level, ref in enumerate(earlier):
+        out_ref[level] = ref[...]
+    for t in range(diag_ref.shape[1]):
+        residual = sum(part[t].astype(jnp.float32) for part in parts).astype(jnp.bfloat16)
+        out_ref[len(earlier), t] = jnp.dot(residual, diag_ref[0, t], preferred_element_type=jnp.float32)
+
+
+def run_last(parts, diag, results, shape):
+    vmem = pl.BlockSpec(memory_space=pltpu.VMEM)
+    args = [*parts, diag, *results]
+    return pl.pallas_call(
+        last_body,
+        out_shape=jax.ShapeDtypeStruct(shape, jnp.float32),
+        in_specs=[vmem] * len(args),
+        out_specs=vmem,
+        compiler_params=pltpu.CompilerParams(vmem_limit_bytes=6 << 20),
+    )(*args)
 
 
 def run_solve(level, last, rep, ids, parts, weights, prev, shape):
@@ -233,9 +255,9 @@
 
 
 def fetch_body(dom_size, *refs):
-    owner_ref, _, src_hbm, dst_hbm, diag_hbm, mats_hbm, ids_ref, diag_ref, mats_ref, dst_ref, sems = refs
+    owner_ref, _, src_hbm, dst_hbm, diag_hbm, mats_hbm, *ids_refs, diag_ref, mats_ref, src_ref, dst_ref, sems = refs
     lists = [
-        pltpu.make_async_copy(src_hbm, ids_ref.at[0], sems.at[1 + CHUNKS]),
+        pltpu.make_async_copy(src_hbm, src_ref, sems.at[1 + CHUNKS]),
         pltpu.make_async_copy(dst_hbm, dst_ref, sems.at[2 + CHUNKS]),
     ]
     for copy in lists:
@@ -251,7 +273,10 @@
         copy.start()
     for copy in lists:
         copy.wait()
-    ids_ref[1] = slots_of(dst_ref[...], owner_ref[0], dom_size, diag_ref.shape[1])
+    slots = slots_of(dst_ref[...], owner_ref[0], dom_size, diag_ref.shape[1])
+    for level, ids_ref in enumerate(ids_refs):
+        ids_ref[0:1] = src_ref[level : level + 1]
+        ids_ref[1:2] = slots[level : level + 1]
     for copy in copies:
         copy.wait()
 
@@ -263,13 +288,13 @@
     return pl.pallas_call(
         functools.partial(fetch_body, lax.axis_size("dom")),
         out_shape=[
-            jax.ShapeDtypeStruct((2, *src.shape), jnp.int32),
+            *[jax.ShapeDtypeStruct((2, src.shape[1]), jnp.int32) for _ in range(src.shape[0])],
             pltpu.VMEM((1, *diag.shape[1:]), diag.dtype),
             pltpu.VMEM((1, *mats.shape[1:]), mats.dtype),
         ],
         in_specs=[pl.BlockSpec(memory_space=pltpu.SMEM), vmem, hbm, hbm, hbm, hbm],
-        out_specs=[vmem, vmem, vmem],
-        scratch_shapes=[pltpu.VMEM(dst.shape, dst.dtype), pltpu.SemaphoreType.DMA((3 + CHUNKS,))],
+        out_specs=[vmem] * (2 + src.shape[0]),
+        scratch_shapes=[pltpu.VMEM(src.shape, src.dtype), pltpu.VMEM(dst.shape, dst.dtype), pltpu.SemaphoreType.DMA((3 + CHUNKS,))],
         compiler_params=pltpu.CompilerParams(vmem_limit_bytes=1 << 20),
     )(owner[None], after, src, dst, diag, mats)
 
@@ -316,26 +341,32 @@
         pltpu.with_memory_space_constraint(x, pltpu.HBM)
         for x in (panel_src, panel_dst, diag_inverse, panel_mats)
     )
-    ids, diag, early_mats = fetch(partial, src, dst, diag_hbm, mats_hbm)
+    *ids, diag, early_mats = fetch(partial, src, dst, diag_hbm, mats_hbm)
     late_mats = pltpu.with_memory_space_constraint(panel_mats, pltpu.VMEM)
     store = []
     results = []
     for level in range(levels):
         last = level + 1 == levels
+        if last:
+            pieces = [
+                sum(
+                    jnp.where(rep ^ apart == index, full[:, index * group : (index + 1) * group], 0.0)
+                    for index in range(rep_size)
+                ).astype(jnp.bfloat16)
+                for apart in (0, *APART)
+            ]
+            parts = pieces[:1] + [along_rep(piece, apart) for piece, apart in zip(pieces[1:], APART)]
+            return run_last(parts, diag, results, right_sides.shape)
         parts = [partial] + [
             along_rep(partial, apart) for apart in (APART if level else APART_FIRST)
         ]
         weights = [diag, late_mats if level else early_mats]
-        if last:
-            return run_solve(
-                level, last, rep[None], None, parts, weights[:1], results, right_sides.shape
-            )
         solved, stored, handed = run_solve(
-            level, last, rep[None], ids, parts, weights, store, right_sides.shape
+            level, last, rep[None], ids[level], parts, weights, store, right_sides.shape
         )
         results.append(solved)
         store.append(stored)
-        own, sibling, far, chip = run_panels(level, ids, weights[1], store)
+        own, sibling, far, chip = run_panels(level, ids[level], weights[1], store)
         handed = jnp.where(top, to_sibling(handed), jnp.zeros_like(handed))
         chip = (chip.astype(jnp.float32) + handed.astype(jnp.float32)).astype(jnp.bfloat16)
         from_chip = to_next_chip(chip)
@@ -345,7 +376,8 @@
             (from_chip[1].astype(jnp.float32) + sibling.astype(jnp.float32)).astype(jnp.bfloat16)
         )
         incoming = sum(piece.astype(jnp.float32) for piece in (own, from_chip[0], from_far, across))
-        partial = (own_rhs[level + 1] - incoming).astype(jnp.bfloat16)
+        full = own_rhs[level + 1] - incoming
+        partial = full.astype(jnp.bfloat16)
 
 
 def solution(mesh):

time: 74.5 us -> 73.6 us (0.988)
    pallas_call x4 -> x3, Pallas kernels: 4.76 us -> 3.56 us  [run_solve(): pl.pallas_call(functools.partial(solve_body, level, last), out_shape=outs...]
    pallas_call x0 -> x1, Pallas kernels: none -> 1.04 us  [run_last(): pl.pallas_call(last_body, out_shape=jax.ShapeDtypeStruct(shape, jnp.float...]
where the time goes in v8:
time: 73.6 us; the launch traced here: 73.4 us
  starting transfers between devices  30.4 us (41%)
  waiting for transfers between devices  24.8 us (34%)
  Pallas kernels  16.1 us (22%)
  other arithmetic  0.9 us (1%)
  local copies, waits for them, and re-layouts  0.8 us (1%)
    ppermute x12, starting transfers between devices, along_rep(): lax.ppermute(value, 'rep', [(i, i ^ apart) for i in range(lax.axis_size('...  15.9 us
    ppermute x12, starting transfers between devices, dom_permute(): lax.ppermute(value, 'dom', [(i, target(i) % size) for i in range(size)])  14.6 us
    ppermute x12, waiting for transfers between devices, along_rep(): lax.ppermute(value, 'rep', [(i, i ^ apart) for i in range(lax.axis_size('...  12.9 us
    ppermute x12, waiting for transfers between devices, dom_permute(): lax.ppermute(value, 'dom', [(i, target(i) % size) for i in range(size)])  12 us
    pallas_call x3, Pallas kernels, next_diag(): pl.pallas_call(functools.partial(next_diag_body, level), out_shape=[jax.S...  4.39 us
    pallas_call x3, Pallas kernels, run_panels(): pl.pallas_call(functools.partial(panels_body, level), out_shape=[jax.Shap...  4 us
    pallas_call x3, Pallas kernels, run_solve(): pl.pallas_call(functools.partial(solve_body, level, last), out_shape=outs...  3.56 us
    pallas_call x1, Pallas kernels, fetch(): pl.pallas_call(functools.partial(fetch_body, lax.axis_size('dom')), out_s...  3.1 us
  transfers between devices with their start and end apart: 24, of which 15 were waited for; matrix products, arithmetic and copies ran while one was open for 0% of the time, Pallas kernels for 16%

profile of v8, /device:TPU:0, one launch (start us, length us, event | category | flops | bytes accessed | tf_op | source)
XLA Modules:
  0.0 73.4 jit_solution(8400907713410289906)
XLA Ops:
  0.0 0.8 %fusion.14.refs_1_.refs_2_ = bf16[6,4,384]{2,1,0:T(4,128)(2,1)S(1)} fusion(f32[4,6,4,384]{3,2,1,0:T(4,128)} %param.5), kind=kLoop, calls=%fused_computation.39 | loop fusion | bytes 36864 | tf_op jit(solution)/shard_map/convert_element_type | solution.py:337
  0.8 4.1 %collective-permute-start = (bf16[6,4,384]{2,1,0:T(4,128)(2,1)S(1)}, bf16[6,4,384]{2,1,0:T(4,128)(2,1)S(1)}, u32[]{:S(2)}, u32[]{:S(2)}) collective-permute-start(bf16[6,4,384]{2,1,0:T(4,128)(2,1)S(1)} %fusion.14.refs_1_.refs_2_), channel_id=1, source_target_pairs={{0,3},{1,2},{2,1},{3,0},{4,7},{5,6},{6,5},{7,4},{8,11},{9,10},{10,... | collective-permute-start | bytes 55304 | tf_op jit(solution)/shard_map/ppermute | solution.py:39
  4.9 0.0 collective-permute-start.1
  4.9 0.9 %collective-permute-start.2 = (bf16[6,4,384]{2,1,0:T(4,128)(2,1)S(1)}, bf16[6,4,384]{2,1,0:T(4,128)(2,1)S(1)}, u32[]{:S(2)}, u32[]{:S(2)}) collective-permute-start(bf16[6,4,384]{2,1,0:T(4,128)(2,1)S(1)} %fusion.14.refs_1_.refs_2_), channel_id=1, source_target_pairs={{0,1},{1,0},{2,3},{3,2},{4,5},{5,4},{6,7},{7,6},{8,9},{9,8},{10,11... | collective-permute-start | bytes 55304 | tf_op jit(solution)/shard_map/ppermute | solution.py:39
  5.8 3.1 %shard_map.55 = (s32[2,16]{1,0:T(2,128)S(1)}, s32[2,16]{1,0:T(2,128)S(1)}, s32[2,16]{1,0:T(2,128)S(1)}, bf16[1,6,384,384]{3,2,1,0:T(8,128)(2,1)S(1)}, bf16[1,16,384,384]{3,2,1,0:T(8,128)(2,1)S(1)}) custom-call(s32[1]{0:T(128)} %bitcast.1.refs_0_, bf16[6,4,384]{2,1,0:T(4,128)(2,1)S(1)} %fusion.14.refs_1_.refs_2_, s32[3,16]{1,0:T(4,128)} %refs_2_.4, ...), custom_call_target="tpu_custom_call" | custom-call | tf_op jit(solution)/shard_map/pallas_call | solution.py:288
  9.0 0.0 collective-permute-done.refs_3_
  9.0 1.2 %collective-permute-done.1.refs_4_ = bf16[6,4,384]{2,1,0:T(4,128)(2,1)S(1)} collective-permute-done((bf16[6,4,384]{2,1,0:T(4,128)(2,1)S(1)}, bf16[6,4,384]{2,1,0:T(4,128)(2,1)S(1)}, u32[]{:S(2)}, u32[]{:S(2)}) %collective-permute-start.1) | collective-permute-done | bytes 18464 | tf_op jit(solution)/shard_map/ppermute | solution.py:39
  10.2 0.0 collective-permute-done.2.refs_5_
  10.2 1.2 %shard_map.56 = (f32[6,4,384]{2,1,0:T(4,128)S(1)}, bf16[6,16,384]{2,1,0:T(8,128)(2,1)S(1)}, bf16[6,16,384]{2,1,0:T(8,128)(2,1)S(1)}) custom-call(s32[1]{0:T(128)} %bitcast.3.refs_0_, s32[2,16]{1,0:T(2,128)S(1)} %get-tuple-element.38.refs_1_.refs_0_, bf16[6,4,384]{2,1,0:T(4,128)(2,1)S(1)} %fusion.14.refs_1_.refs_2_, ...), custom_call_target="tpu_custom_call" | custom-call | tf_op jit(solution)/shard_map/pallas_call | solution.py:205
  11.4 0.1 collective-permute-start.3
  11.5 0.0 slice-start.3
  11.5 1.3 %shard_map.57 = (bf16[6,16,384]{2,1,0:T(8,128)(2,1)S(1)}, bf16[6,16,384]{2,1,0:T(8,128)(2,1)S(1)}, bf16[6,16,384]{2,1,0:T(8,128)(2,1)S(1)}, bf16[2,6,16,384]{3,2,1,0:T(8,128)(2,1)S(1)}) custom-call(s32[2,16]{1,0:T(2,128)S(1)} %get-tuple-element.38.refs_1_.refs_0_, bf16[1,16,384,384]{3,2,1,0:T(8,128)(2,1)S(1)} %get-tuple-element.40.refs_7_.refs_1_, ...), custom_call_target="tpu_custom_call" | custom-call | tf_op jit(solution)/shard_map/pallas_call | solution.py:219
  12.8 0.1 add_convert_fusion.2.refs_0_
  13.0 5.4 %collective-permute-start.4 = (bf16[2,6,16,384]{3,2,1,0:T(8,128)(2,1)S(1)}, bf16[2,6,16,384]{3,2,1,0:T(8,128)(2,1)S(1)}, u32[]{:S(2)}, u32[]{:S(2)}) collective-permute-start(bf16[2,6,16,384]{3,2,1,0:T(8,128)(2,1)S(1)} %add_convert_fusion.2.refs_0_), channel_id=1, source_target_pairs={{0,124},{4,8},{8,4},{12,16},{16,12},{20,24},{24,20},{28,32},{32,28... | collective-permute-start | bytes 442376 | tf_op jit(solution)/shard_map/ppermute | solution.py:22
  18.4 0.7 collective-permute-start.5
  19.1 1.5 %shard_map.58 = (bf16[6,16,384]{2,1,0:T(8,128)(2,1)S(1)}, bf16[1,6,384,384]{3,2,1,0:T(8,128)(2,1)S(1)}) custom-call(bf16[2,6,16,384]{3,2,1,0:T(8,128)(2,1)S(1)} %add_convert_fusion.2.refs_0_, bf16[6,16,384]{2,1,0:T(8,128)(2,1)S(1)} %get-tuple-element.47.refs_1_, bf16[4,6,384,384]{3,2,1,0:T(8,128)(2,1)} %refs_2_.7), custom_call_target="tpu_custom_call" | custom-call | tf_op jit(solution)/shard_map/pallas_call | solution.py:318
  20.6 0.7 collective-permute-done.4
  21.2 0.1 collective-permute-start.6
  21.3 0.1 maximum_select_fusion
  21.5 2.8 %collective-permute-done.5 = bf16[6,16,384]{2,1,0:T(8,128)(2,1)S(1)} collective-permute-done((bf16[6,16,384]{2,1,0:T(8,128)(2,1)S(1)}, bf16[6,16,384]{2,1,0:T(8,128)(2,1)S(1)}, u32[]{:S(2)}, u32[]{:S(2)}) %collective-permute-start.5) | collective-permute-done | bytes 73760 | tf_op jit(solution)/shard_map/ppermute | solution.py:22
  24.3 0.0 collective-permute-done.6
  24.3 0.1 fusion.3.refs_2_
  24.4 2.1 %collective-permute-start.7 = (bf16[6,16,384]{2,1,0:T(8,128)(2,1)S(1)}, bf16[6,16,384]{2,1,0:T(8,128)(2,1)S(1)}, u32[]{:S(2)}, u32[]{:S(2)}) collective-permute-start(bf16[6,16,384]{2,1,0:T(8,128)(2,1)S(1)} %fusion.3.refs_2_), channel_id=1, source_target_pairs={{0,2},{1,3},{2,0},{3,1},{4,6},{5,7},{6,4},{7,5},{8,10},{9,11},{10,... | collective-permute-start | bytes 221192 | tf_op jit(solution)/shard_map/ppermute | solution.py:39
  26.5 0.6 collective-permute-start.8
  27.0 0.9 %collective-permute-start.9 = (bf16[6,16,384]{2,1,0:T(8,128)(2,1)S(1)}, bf16[6,16,384]{2,1,0:T(8,128)(2,1)S(1)}, u32[]{:S(2)}, u32[]{:S(2)}) collective-permute-start(bf16[6,16,384]{2,1,0:T(8,128)(2,1)S(1)} %fusion.3.refs_2_), channel_id=1, source_target_pairs={{0,1},{1,0},{2,3},{3,2},{4,5},{5,4},{6,7},{7,6},{8,9},{9,8},{10,11... | collective-permute-start | bytes 221192 | tf_op jit(solution)/shard_map/ppermute | solution.py:39
  27.9 3.0 %collective-permute-done.7.refs_3_ = bf16[6,16,384]{2,1,0:T(8,128)(2,1)S(1)} collective-permute-done((bf16[6,16,384]{2,1,0:T(8,128)(2,1)S(1)}, bf16[6,16,384]{2,1,0:T(8,128)(2,1)S(1)}, u32[]{:S(2)}, u32[]{:S(2)}) %collective-permute-start.7) | collective-permute-done | bytes 73760 | tf_op jit(solution)/shard_map/ppermute | solution.py:39
  31.0 1.1 %collective-permute-done.8.refs_4_ = bf16[6,16,384]{2,1,0:T(8,128)(2,1)S(1)} collective-permute-done((bf16[6,16,384]{2,1,0:T(8,128)(2,1)S(1)}, bf16[6,16,384]{2,1,0:T(8,128)(2,1)S(1)}, u32[]{:S(2)}, u32[]{:S(2)}) %collective-permute-start.8) | collective-permute-done | bytes 73760 | tf_op jit(solution)/shard_map/ppermute | solution.py:39
  32.0 0.0 collective-permute-done.9.refs_5_
  32.1 1.2 %shard_map.59 = (f32[6,4,384]{2,1,0:T(4,128)S(1)}, bf16[6,16,384]{2,1,0:T(8,128)(2,1)S(1)}, bf16[6,16,384]{2,1,0:T(8,128)(2,1)S(1)}) custom-call(s32[1]{0:T(128)} %bitcast.3.refs_0_, s32[2,16]{1,0:T(2,128)S(1)} %get-tuple-element.42.refs_1_.refs_0_, bf16[6,16,384]{2,1,0:T(8,128)(2,1)S(1)} %fusion.3.refs_2_, ...), custom_call_target="tpu_custom_call" | custom-call | tf_op jit(solution)/shard_map/pallas_call | solution.py:205
  33.3 0.1 collective-permute-start.10
  33.3 1.3 %shard_map.60 = (bf16[6,16,384]{2,1,0:T(8,128)(2,1)S(1)}, bf16[6,16,384]{2,1,0:T(8,128)(2,1)S(1)}, bf16[6,16,384]{2,1,0:T(8,128)(2,1)S(1)}, bf16[2,6,16,384]{3,2,1,0:T(8,128)(2,1)S(1)}) custom-call(s32[2,16]{1,0:T(2,128)S(1)} %get-tuple-element.42.refs_1_.refs_0_, bf16[3,16,384,384]{3,2,1,0:T(8,128)(2,1)S(1)} %bitcast.51, ...), custom_call_target="tpu_custom_call" | custom-call | tf_op jit(solution)/shard_map/pallas_call | solution.py:219
  34.7 0.0 collective-permute-done.10
  34.7 0.1 add_convert_fusion.1.refs_0_
  34.8 4.3 %collective-permute-start.11 = (bf16[2,6,16,384]{3,2,1,0:T(8,128)(2,1)S(1)}, bf16[2,6,16,384]{3,2,1,0:T(8,128)(2,1)S(1)}, u32[]{:S(2)}, u32[]{:S(2)}) collective-permute-start(bf16[2,6,16,384]{3,2,1,0:T(8,128)(2,1)S(1)} %add_convert_fusion.1.refs_0_), channel_id=1, source_target_pairs={{0,124},{4,8},{8,4},{12,16},{16,12},{20,24},{24,20},{28,32},{32,28... | collective-permute-start | bytes 442376 | tf_op jit(solution)/shard_map/ppermute | solution.py:22
  39.1 0.0 collective-permute-start.12
  39.1 1.5 %shard_map.61 = (bf16[6,16,384]{2,1,0:T(8,128)(2,1)S(1)}, bf16[1,6,384,384]{3,2,1,0:T(8,128)(2,1)S(1)}) custom-call(bf16[2,6,16,384]{3,2,1,0:T(8,128)(2,1)S(1)} %add_convert_fusion.1.refs_0_, bf16[6,16,384]{2,1,0:T(8,128)(2,1)S(1)} %get-tuple-element.55.refs_1_, bf16[4,6,384,384]{3,2,1,0:T(8,128)(2,1)} %refs_2_.7), custom_call_target="tpu_custom_call" | custom-call | tf_op jit(solution)/shard_map/pallas_call | solution.py:318
  40.6 2.3 %collective-permute-done.11 = bf16[2,6,16,384]{3,2,1,0:T(8,128)(2,1)S(1)} collective-permute-done((bf16[2,6,16,384]{3,2,1,0:T(8,128)(2,1)S(1)}, bf16[2,6,16,384]{3,2,1,0:T(8,128)(2,1)S(1)}, u32[]{:S(2)}, u32[]{:S(2)}) %collective-permute-start.11) | collective-permute-done | bytes 147488 | tf_op jit(solution)/shard_map/ppermute | solution.py:22
  42.9 0.1 collective-permute-start.13
  43.0 2.0 %collective-permute-done.12 = bf16[6,16,384]{2,1,0:T(8,128)(2,1)S(1)} collective-permute-done((bf16[6,16,384]{2,1,0:T(8,128)(2,1)S(1)}, bf16[6,16,384]{2,1,0:T(8,128)(2,1)S(1)}, u32[]{:S(2)}, u32[]{:S(2)}) %collective-permute-start.12) | collective-permute-done | bytes 73760 | tf_op jit(solution)/shard_map/ppermute | solution.py:22
  45.0 0.1 fusion.1.refs_2_
  45.1 1.8 %collective-permute-start.14 = (bf16[6,16,384]{2,1,0:T(8,128)(2,1)S(1)}, bf16[6,16,384]{2,1,0:T(8,128)(2,1)S(1)}, u32[]{:S(2)}, u32[]{:S(2)}) collective-permute-start(bf16[6,16,384]{2,1,0:T(8,128)(2,1)S(1)} %fusion.1.refs_2_), channel_id=1, source_target_pairs={{0,2},{1,3},{2,0},{3,1},{4,6},{5,7},{6,4},{7,5},{8,10},{9,11},{10,... | collective-permute-start | bytes 221192 | tf_op jit(solution)/shard_map/ppermute | solution.py:39
  46.9 1.5 %collective-permute-start.15 = (bf16[6,16,384]{2,1,0:T(8,128)(2,1)S(1)}, bf16[6,16,384]{2,1,0:T(8,128)(2,1)S(1)}, u32[]{:S(2)}, u32[]{:S(2)}) collective-permute-start(bf16[6,16,384]{2,1,0:T(8,128)(2,1)S(1)} %fusion.1.refs_2_), channel_id=1, source_target_pairs={{0,3},{1,2},{2,1},{3,0},{4,7},{5,6},{6,5},{7,4},{8,11},{9,10},{10,... | collective-permute-start | bytes 221192 | tf_op jit(solution)/shard_map/ppermute | solution.py:39
  48.4 0.3 collective-permute-start.16
  48.6 2.5 %collective-permute-done.14.refs_3_ = bf16[6,16,384]{2,1,0:T(8,128)(2,1)S(1)} collective-permute-done((bf16[6,16,384]{2,1,0:T(8,128)(2,1)S(1)}, bf16[6,16,384]{2,1,0:T(8,128)(2,1)S(1)}, u32[]{:S(2)}, u32[]{:S(2)}) %collective-permute-start.14) | collective-permute-done | bytes 73760 | tf_op jit(solution)/shard_map/ppermute | solution.py:39
  51.1 1.3 %collective-permute-done.15.refs_4_ = bf16[6,16,384]{2,1,0:T(8,128)(2,1)S(1)} collective-permute-done((bf16[6,16,384]{2,1,0:T(8,128)(2,1)S(1)}, bf16[6,16,384]{2,1,0:T(8,128)(2,1)S(1)}, u32[]{:S(2)}, u32[]{:S(2)}) %collective-permute-start.15) | collective-permute-done | bytes 73760 | tf_op jit(solution)/shard_map/ppermute | solution.py:39
  52.5 0.3 collective-permute-done.16.refs_5_
  52.7 1.2 %shard_map.62 = (f32[6,4,384]{2,1,0:T(4,128)S(1)}, bf16[6,16,384]{2,1,0:T(8,128)(2,1)S(1)}, bf16[6,16,384]{2,1,0:T(8,128)(2,1)S(1)}) custom-call(s32[1]{0:T(128)} %bitcast.3.refs_0_, s32[2,16]{1,0:T(2,128)S(1)} %get-tuple-element.37.refs_1_.refs_0_, bf16[6,16,384]{2,1,0:T(8,128)(2,1)S(1)} %fusion.1.refs_2_, ...), custom_call_target="tpu_custom_call" | custom-call | tf_op jit(solution)/shard_map/pallas_call | solution.py:205
  53.9 0.1 collective-permute-start.17
  54.0 1.3 %shard_map.63 = (bf16[6,16,384]{2,1,0:T(8,128)(2,1)S(1)}, bf16[6,16,384]{2,1,0:T(8,128)(2,1)S(1)}, bf16[6,16,384]{2,1,0:T(8,128)(2,1)S(1)}, bf16[2,6,16,384]{3,2,1,0:T(8,128)(2,1)S(1)}) custom-call(s32[2,16]{1,0:T(2,128)S(1)} %get-tuple-element.37.refs_1_.refs_0_, bf16[3,16,384,384]{3,2,1,0:T(8,128)(2,1)S(1)} %bitcast.51, ...), custom_call_target="tpu_custom_call" | custom-call | tf_op jit(solution)/shard_map/pallas_call | solution.py:219
  55.4 0.1 add_convert_fusion.refs_0_
  55.5 3.7 %collective-permute-start.18 = (bf16[2,6,16,384]{3,2,1,0:T(8,128)(2,1)S(1)}, bf16[2,6,16,384]{3,2,1,0:T(8,128)(2,1)S(1)}, u32[]{:S(2)}, u32[]{:S(2)}) collective-permute-start(bf16[2,6,16,384]{3,2,1,0:T(8,128)(2,1)S(1)} %add_convert_fusion.refs_0_), channel_id=1, source_target_pairs={{0,124},{4,8},{8,4},{12,16},{16,12},{20,24},{24,20},{28,32},{32,28... | collective-permute-start | bytes 442376 | tf_op jit(solution)/shard_map/ppermute | solution.py:22
  59.1 1.5 %shard_map.64 = (bf16[6,16,384]{2,1,0:T(8,128)(2,1)S(1)}, bf16[1,6,384,384]{3,2,1,0:T(8,128)(2,1)S(1)}) custom-call(bf16[2,6,16,384]{3,2,1,0:T(8,128)(2,1)S(1)} %add_convert_fusion.refs_0_, bf16[6,16,384]{2,1,0:T(8,128)(2,1)S(1)} %get-tuple-element.63.refs_1_, bf16[4,6,384,384]{3,2,1,0:T(8,128)(2,1)} %refs_2_.7), custom_call_target="tpu_custom_call" | custom-call | tf_op jit(solution)/shard_map/pallas_call | solution.py:318
  60.6 2.9 %collective-permute-done.18 = bf16[2,6,16,384]{3,2,1,0:T(8,128)(2,1)S(1)} collective-permute-done((bf16[2,6,16,384]{3,2,1,0:T(8,128)(2,1)S(1)}, bf16[2,6,16,384]{3,2,1,0:T(8,128)(2,1)S(1)}, u32[]{:S(2)}, u32[]{:S(2)}) %collective-permute-start.18) | collective-permute-done | bytes 147488 | tf_op jit(solution)/shard_map/ppermute | solution.py:22
  63.5 0.1 collective-permute-start.20
  63.6 1.4 %collective-permute-done.19 = bf16[6,16,384]{2,1,0:T(8,128)(2,1)S(1)} collective-permute-done((bf16[6,16,384]{2,1,0:T(8,128)(2,1)S(1)}, bf16[6,16,384]{2,1,0:T(8,128)(2,1)S(1)}, u32[]{:S(2)}, u32[]{:S(2)}) %collective-permute-start.19) | collective-permute-done | bytes 73760 | tf_op jit(solution)/shard_map/ppermute | solution.py:22
  65.1 0.1 add_convert_fusion.4
  65.1 1.8 %collective-permute-start.21 = (bf16[6,4,384]{2,1,0:T(4,128)(2,1)S(1)}, bf16[6,4,384]{2,1,0:T(4,128)(2,1)S(1)}, u32[]{:S(2)}, u32[]{:S(2)}) collective-permute-start(bf16[6,4,384]{2,1,0:T(4,128)(2,1)S(1)} %get-tuple-element.72), channel_id=1, source_target_pairs={{0,2},{1,3},{2,0},{3,1},{4,6},{5,7},{6,4},{7,5},{8,10},{9,11},{10,... | collective-permute-start | bytes 55304 | tf_op jit(solution)/shard_map/ppermute | solution.py:39
  67.0 1.5 %collective-permute-start.22 = (bf16[6,4,384]{2,1,0:T(4,128)(2,1)S(1)}, bf16[6,4,384]{2,1,0:T(4,128)(2,1)S(1)}, u32[]{:S(2)}, u32[]{:S(2)}) collective-permute-start(bf16[6,4,384]{2,1,0:T(4,128)(2,1)S(1)} %get-tuple-element.71), channel_id=1, source_target_pairs={{0,3},{1,2},{2,1},{3,0},{4,7},{5,6},{6,5},{7,4},{8,11},{9,10},{10,... | collective-permute-start | bytes 55304 | tf_op jit(solution)/shard_map/ppermute | solution.py:39
  68.4 0.1 add_convert_fusion.3
  68.5 0.3 collective-permute-start.23
  68.8 1.6 %collective-permute-done.21.refs_1_ = bf16[6,4,384]{2,1,0:T(4,128)(2,1)S(1)} collective-permute-done((bf16[6,4,384]{2,1,0:T(4,128)(2,1)S(1)}, bf16[6,4,384]{2,1,0:T(4,128)(2,1)S(1)}, u32[]{:S(2)}, u32[]{:S(2)}) %collective-permute-start.21) | collective-permute-done | bytes 18464 | tf_op jit(solution)/shard_map/ppermute | solution.py:39
  70.5 1.4 %collective-permute-done.22.refs_2_ = bf16[6,4,384]{2,1,0:T(4,128)(2,1)S(1)} collective-permute-done((bf16[6,4,384]{2,1,0:T(4,128)(2,1)S(1)}, bf16[6,4,384]{2,1,0:T(4,128)(2,1)S(1)}, u32[]{:S(2)}, u32[]{:S(2)}) %collective-permute-start.22) | collective-permute-done | bytes 18464 | tf_op jit(solution)/shard_map/ppermute | solution.py:39
  71.9 0.4 collective-permute-done.23.refs_3_
  72.3 1.0 %shard_map.65 = f32[4,6,4,384]{3,2,1,0:T(4,128)} custom-call(bf16[6,4,384]{2,1,0:T(4,128)(2,1)S(1)} %get-tuple-element.70.refs_0_, bf16[6,4,384]{2,1,0:T(4,128)(2,1)S(1)} %collective-permute-done.21.refs_1_, bf16[6,4,384]{2,1,0:T(4,128)(2,1)S(1)} %collective-permute-done.22.refs_2_, bf16[6,4,384]{2,1,0:T(4,128)(2,1)S(1)} %collective-permute-done.23.refs_3_, ...), custom_call_target="tpu_custom_call" | custom-call | tf_op jit(solution)/shard_map/pallas_call | solution.py:178
  (22 shorter events, 0.2 us)
Async XLA Ops:
  0.8 8.2 %collective-permute-start = (bf16[6,4,384]{2,1,0:T(4,128)(2,1)S(1)}, bf16[6,4,384]{2,1,0:T(4,128)(2,1)S(1)}, u32[]{:S(2)}, u32[]{:S(2)}) collective-permute-start(bf16[6,4,384]{2,1,0:T(4,128)(2,1)S(1)} %fusion.14.refs_1_.refs_2_), channel_id=1, source_target_pairs={{0,3},{1,2},{2,1},{3,0},{4,7},{5,6},{6,5},{7,4},{8,11},{9,10},{10,... | collective-permute-start | bytes 55304 | tf_op jit(solution)/shard_map/ppermute | solution.py:39
  4.9 5.3 %collective-permute-start.1 = (bf16[6,4,384]{2,1,0:T(4,128)(2,1)S(1)}, bf16[6,4,384]{2,1,0:T(4,128)(2,1)S(1)}, u32[]{:S(2)}, u32[]{:S(2)}) collective-permute-start(bf16[6,4,384]{2,1,0:T(4,128)(2,1)S(1)} %fusion.14.refs_1_.refs_2_), channel_id=1, source_target_pairs={{0,2},{1,3},{2,0},{3,1},{4,6},{5,7},{6,4},{7,5},{8,10},{9,11},{10,... | collective-permute-start | bytes 55304 | tf_op jit(solution)/shard_map/ppermute | solution.py:39
  4.9 5.3 %collective-permute-start.2 = (bf16[6,4,384]{2,1,0:T(4,128)(2,1)S(1)}, bf16[6,4,384]{2,1,0:T(4,128)(2,1)S(1)}, u32[]{:S(2)}, u32[]{:S(2)}) collective-permute-start(bf16[6,4,384]{2,1,0:T(4,128)(2,1)S(1)} %fusion.14.refs_1_.refs_2_), channel_id=1, source_target_pairs={{0,1},{1,0},{2,3},{3,2},{4,5},{5,4},{6,7},{7,6},{8,9},{9,8},{10,11... | collective-permute-start | bytes 55304 | tf_op jit(solution)/shard_map/ppermute | solution.py:39
  5.8 26.2 %slice-start = ((s8[14155776]{0:T(1024)(128)(4,1)}), s8[4194304]{0:T(1024)(128)(4,1)S(1)}, s32[]{:S(2)}) async-start(s8[14155776]{0:T(1024)(128)(4,1)} %bitcast.50), calls=%async_computation | async-start | bytes 8388608
  5.8 26.2 %slice-start.1 = ((s8[14155776]{0:T(1024)(128)(4,1)}), s8[4194304]{0:T(1024)(128)(4,1)S(1)}, s32[]{:S(2)}) async-start(s8[14155776]{0:T(1024)(128)(4,1)} %bitcast.50), calls=%async_computation.1 | async-start | bytes 8388608
  5.8 26.2 %slice-start.2 = ((s8[14155776]{0:T(1024)(128)(4,1)}), s8[4194304]{0:T(1024)(128)(4,1)S(1)}, s32[]{:S(2)}) async-start(s8[14155776]{0:T(1024)(128)(4,1)} %bitcast.50), calls=%async_computation.2 | async-start | bytes 8388608
  11.4 1.5 %collective-permute-start.3 = (bf16[6,16,384]{2,1,0:T(8,128)(2,1)S(1)}, bf16[6,16,384]{2,1,0:T(8,128)(2,1)S(1)}, u32[]{:S(2)}, u32[]{:S(2)}) collective-permute-start(bf16[6,16,384]{2,1,0:T(8,128)(2,1)S(1)} %get-tuple-element.45), channel_id=1, source_target_pairs={{0,4},{4,0},{8,12},{12,8},{16,20},{20,16},{24,28},{28,24},{32,36},... | collective-permute-start | bytes 221192 | tf_op jit(solution)/shard_map/ppermute | solution.py:22
  11.5 20.6 %slice-start.3 = ((s8[14155776]{0:T(1024)(128)(4,1)}), s8[1572864]{0:T(1024)(128)(4,1)S(1)}, s32[]{:S(2)}) async-start(s8[14155776]{0:T(1024)(128)(4,1)} %bitcast.50), calls=%async_computation.3 | async-start | bytes 3145728
  13.0 8.2 %collective-permute-start.4 = (bf16[2,6,16,384]{3,2,1,0:T(8,128)(2,1)S(1)}, bf16[2,6,16,384]{3,2,1,0:T(8,128)(2,1)S(1)}, u32[]{:S(2)}, u32[]{:S(2)}) collective-permute-start(bf16[2,6,16,384]{3,2,1,0:T(8,128)(2,1)S(1)} %add_convert_fusion.2.refs_0_), channel_id=1, source_target_pairs={{0,124},{4,8},{8,4},{12,16},{16,12},{20,24},{24,20},{28,32},{32,28... | collective-permute-start | bytes 442376 | tf_op jit(solution)/shard_map/ppermute | solution.py:22
  18.4 5.9 %collective-permute-start.5 = (bf16[6,16,384]{2,1,0:T(8,128)(2,1)S(1)}, bf16[6,16,384]{2,1,0:T(8,128)(2,1)S(1)}, u32[]{:S(2)}, u32[]{:S(2)}) collective-permute-start(bf16[6,16,384]{2,1,0:T(8,128)(2,1)S(1)} %get-tuple-element.46), channel_id=1, source_target_pairs={{0,64},{4,68},{8,72},{12,76},{16,80},{20,84},{24,88},{28,92},{32,9... | collective-permute-start | bytes 221192 | tf_op jit(solution)/shard_map/ppermute | solution.py:22
  19.1 2.3 %copy-start = (f32[4,6,4,384]{3,2,1,0:T(4,128)S(1)}, f32[4,6,4,384]{3,2,1,0:T(4,128)}, u32[]{:S(2)}) copy-start(f32[4,6,4,384]{3,2,1,0:T(4,128)} %param.5) | copy-start | bytes 442372
  21.2 3.0 %collective-permute-start.6 = (bf16[6,16,384]{2,1,0:T(8,128)(2,1)S(1)}, bf16[6,16,384]{2,1,0:T(8,128)(2,1)S(1)}, u32[]{:S(2)}, u32[]{:S(2)}) collective-permute-start(bf16[6,16,384]{2,1,0:T(8,128)(2,1)S(1)} %fusion.11), channel_id=1, source_target_pairs={{0,4},{4,0},{8,12},{12,8},{16,20},{20,16},{24,28},{28,24},{32,36},... | collective-permute-start | bytes 221192 | tf_op jit(solution)/shard_map/ppermute | solution.py:22
  24.4 6.6 %collective-permute-start.7 = (bf16[6,16,384]{2,1,0:T(8,128)(2,1)S(1)}, bf16[6,16,384]{2,1,0:T(8,128)(2,1)S(1)}, u32[]{:S(2)}, u32[]{:S(2)}) collective-permute-start(bf16[6,16,384]{2,1,0:T(8,128)(2,1)S(1)} %fusion.3.refs_2_), channel_id=1, source_target_pairs={{0,2},{1,3},{2,0},{3,1},{4,6},{5,7},{6,4},{7,5},{8,10},{9,11},{10,... | collective-permute-start | bytes 221192 | tf_op jit(solution)/shard_map/ppermute | solution.py:39
  26.5 5.6 %collective-permute-start.8 = (bf16[6,16,384]{2,1,0:T(8,128)(2,1)S(1)}, bf16[6,16,384]{2,1,0:T(8,128)(2,1)S(1)}, u32[]{:S(2)}, u32[]{:S(2)}) collective-permute-start(bf16[6,16,384]{2,1,0:T(8,128)(2,1)S(1)} %fusion.3.refs_2_), channel_id=1, source_target_pairs={{0,3},{1,2},{2,1},{3,0},{4,7},{5,6},{6,5},{7,4},{8,11},{9,10},{10,... | collective-permute-start | bytes 221192 | tf_op jit(solution)/shard_map/ppermute | solution.py:39
  27.0 5.0 %collective-permute-start.9 = (bf16[6,16,384]{2,1,0:T(8,128)(2,1)S(1)}, bf16[6,16,384]{2,1,0:T(8,128)(2,1)S(1)}, u32[]{:S(2)}, u32[]{:S(2)}) collective-permute-start(bf16[6,16,384]{2,1,0:T(8,128)(2,1)S(1)} %fusion.3.refs_2_), channel_id=1, source_target_pairs={{0,1},{1,0},{2,3},{3,2},{4,5},{5,4},{6,7},{7,6},{8,9},{9,8},{10,11... | collective-permute-start | bytes 221192 | tf_op jit(solution)/shard_map/ppermute | solution.py:39
  33.3 1.4 %collective-permute-start.10 = (bf16[6,16,384]{2,1,0:T(8,128)(2,1)S(1)}, bf16[6,16,384]{2,1,0:T(8,128)(2,1)S(1)}, u32[]{:S(2)}, u32[]{:S(2)}) collective-permute-start(bf16[6,16,384]{2,1,0:T(8,128)(2,1)S(1)} %get-tuple-element.53), channel_id=1, source_target_pairs={{0,4},{4,0},{8,12},{12,8},{16,20},{20,16},{24,28},{28,24},{32,36},... | collective-permute-start | bytes 221192 | tf_op jit(solution)/shard_map/ppermute | solution.py:22
  34.8 8.1 %collective-permute-start.11 = (bf16[2,6,16,384]{3,2,1,0:T(8,128)(2,1)S(1)}, bf16[2,6,16,384]{3,2,1,0:T(8,128)(2,1)S(1)}, u32[]{:S(2)}, u32[]{:S(2)}) collective-permute-start(bf16[2,6,16,384]{3,2,1,0:T(8,128)(2,1)S(1)} %add_convert_fusion.1.refs_0_), channel_id=1, source_target_pairs={{0,124},{4,8},{8,4},{12,16},{16,12},{20,24},{24,20},{28,32},{32,28... | collective-permute-start | bytes 442376 | tf_op jit(solution)/shard_map/ppermute | solution.py:22
  39.1 5.9 %collective-permute-start.12 = (bf16[6,16,384]{2,1,0:T(8,128)(2,1)S(1)}, bf16[6,16,384]{2,1,0:T(8,128)(2,1)S(1)}, u32[]{:S(2)}, u32[]{:S(2)}) collective-permute-start(bf16[6,16,384]{2,1,0:T(8,128)(2,1)S(1)} %get-tuple-element.54), channel_id=1, source_target_pairs={{0,64},{4,68},{8,72},{12,76},{16,80},{20,84},{24,88},{28,92},{32,9... | collective-permute-start | bytes 221192 | tf_op jit(solution)/shard_map/ppermute | solution.py:22
  42.9 2.1 %collective-permute-start.13 = (bf16[6,16,384]{2,1,0:T(8,128)(2,1)S(1)}, bf16[6,16,384]{2,1,0:T(8,128)(2,1)S(1)}, u32[]{:S(2)}, u32[]{:S(2)}) collective-permute-start(bf16[6,16,384]{2,1,0:T(8,128)(2,1)S(1)} %fusion.8), channel_id=1, source_target_pairs={{0,4},{4,0},{8,12},{12,8},{16,20},{20,16},{24,28},{28,24},{32,36},... | collective-permute-start | bytes 221192 | tf_op jit(solution)/shard_map/ppermute | solution.py:22
  45.1 6.0 %collective-permute-start.14 = (bf16[6,16,384]{2,1,0:T(8,128)(2,1)S(1)}, bf16[6,16,384]{2,1,0:T(8,128)(2,1)S(1)}, u32[]{:S(2)}, u32[]{:S(2)}) collective-permute-start(bf16[6,16,384]{2,1,0:T(8,128)(2,1)S(1)} %fusion.1.refs_2_), channel_id=1, source_target_pairs={{0,2},{1,3},{2,0},{3,1},{4,6},{5,7},{6,4},{7,5},{8,10},{9,11},{10,... | collective-permute-start | bytes 221192 | tf_op jit(solution)/shard_map/ppermute | solution.py:39
  46.9 5.6 %collective-permute-start.15 = (bf16[6,16,384]{2,1,0:T(8,128)(2,1)S(1)}, bf16[6,16,384]{2,1,0:T(8,128)(2,1)S(1)}, u32[]{:S(2)}, u32[]{:S(2)}) collective-permute-start(bf16[6,16,384]{2,1,0:T(8,128)(2,1)S(1)} %fusion.1.refs_2_), channel_id=1, source_target_pairs={{0,3},{1,2},{2,1},{3,0},{4,7},{5,6},{6,5},{7,4},{8,11},{9,10},{10,... | collective-permute-start | bytes 221192 | tf_op jit(solution)/shard_map/ppermute | solution.py:39
  48.4 4.4 %collective-permute-start.16 = (bf16[6,16,384]{2,1,0:T(8,128)(2,1)S(1)}, bf16[6,16,384]{2,1,0:T(8,128)(2,1)S(1)}, u32[]{:S(2)}, u32[]{:S(2)}) collective-permute-start(bf16[6,16,384]{2,1,0:T(8,128)(2,1)S(1)} %fusion.1.refs_2_), channel_id=1, source_target_pairs={{0,1},{1,0},{2,3},{3,2},{4,5},{5,4},{6,7},{7,6},{8,9},{9,8},{10,11... | collective-permute-start | bytes 221192 | tf_op jit(solution)/shard_map/ppermute | solution.py:39
  53.9 1.4 %collective-permute-start.17 = (bf16[6,16,384]{2,1,0:T(8,128)(2,1)S(1)}, bf16[6,16,384]{2,1,0:T(8,128)(2,1)S(1)}, u32[]{:S(2)}, u32[]{:S(2)}) collective-permute-start(bf16[6,16,384]{2,1,0:T(8,128)(2,1)S(1)} %get-tuple-element.61), channel_id=1, source_target_pairs={{0,4},{4,0},{8,12},{12,8},{16,20},{20,16},{24,28},{28,24},{32,36},... | collective-permute-start | bytes 221192 | tf_op jit(solution)/shard_map/ppermute | solution.py:22
  55.5 8.0 %collective-permute-start.18 = (bf16[2,6,16,384]{3,2,1,0:T(8,128)(2,1)S(1)}, bf16[2,6,16,384]{3,2,1,0:T(8,128)(2,1)S(1)}, u32[]{:S(2)}, u32[]{:S(2)}) collective-permute-start(bf16[2,6,16,384]{3,2,1,0:T(8,128)(2,1)S(1)} %add_convert_fusion.refs_0_), channel_id=1, source_target_pairs={{0,124},{4,8},{8,4},{12,16},{16,12},{20,24},{24,20},{28,32},{32,28... | collective-permute-start | bytes 442376 | tf_op jit(solution)/shard_map/ppermute | solution.py:22
  59.1 5.9 %collective-permute-start.19 = (bf16[6,16,384]{2,1,0:T(8,128)(2,1)S(1)}, bf16[6,16,384]{2,1,0:T(8,128)(2,1)S(1)}, u32[]{:S(2)}, u32[]{:S(2)}) collective-permute-start(bf16[6,16,384]{2,1,0:T(8,128)(2,1)S(1)} %get-tuple-element.62), channel_id=1, source_target_pairs={{0,64},{4,68},{8,72},{12,76},{16,80},{20,84},{24,88},{28,92},{32,9... | collective-permute-start | bytes 221192 | tf_op jit(solution)/shard_map/ppermute | solution.py:22
  63.5 1.5 %collective-permute-start.20 = (bf16[6,16,384]{2,1,0:T(8,128)(2,1)S(1)}, bf16[6,16,384]{2,1,0:T(8,128)(2,1)S(1)}, u32[]{:S(2)}, u32[]{:S(2)}) collective-permute-start(bf16[6,16,384]{2,1,0:T(8,128)(2,1)S(1)} %fusion.5), channel_id=1, source_target_pairs={{0,4},{4,0},{8,12},{12,8},{16,20},{20,16},{24,28},{28,24},{32,36},... | collective-permute-start | bytes 221192 | tf_op jit(solution)/shard_map/ppermute | solution.py:22
  65.1 5.4 %collective-permute-start.21 = (bf16[6,4,384]{2,1,0:T(4,128)(2,1)S(1)}, bf16[6,4,384]{2,1,0:T(4,128)(2,1)S(1)}, u32[]{:S(2)}, u32[]{:S(2)}) collective-permute-start(bf16[6,4,384]{2,1,0:T(4,128)(2,1)S(1)} %get-tuple-element.72), channel_id=1, source_target_pairs={{0,2},{1,3},{2,0},{3,1},{4,6},{5,7},{6,4},{7,5},{8,10},{9,11},{10,... | collective-permute-start | bytes 55304 | tf_op jit(solution)/shard_map/ppermute | solution.py:39
  67.0 5.0 %collective-permute-start.22 = (bf16[6,4,384]{2,1,0:T(4,128)(2,1)S(1)}, bf16[6,4,384]{2,1,0:T(4,128)(2,1)S(1)}, u32[]{:S(2)}, u32[]{:S(2)}) collective-permute-start(bf16[6,4,384]{2,1,0:T(4,128)(2,1)S(1)} %get-tuple-element.71), channel_id=1, source_target_pairs={{0,3},{1,2},{2,1},{3,0},{4,7},{5,6},{6,5},{7,4},{8,11},{9,10},{10,... | collective-permute-start | bytes 55304 | tf_op jit(solution)/shard_map/ppermute | solution.py:39
  68.5 3.8 %collective-permute-start.23 = (bf16[6,4,384]{2,1,0:T(4,128)(2,1)S(1)}, bf16[6,4,384]{2,1,0:T(4,128)(2,1)S(1)}, u32[]{:S(2)}, u32[]{:S(2)}) collective-permute-start(bf16[6,4,384]{2,1,0:T(4,128)(2,1)S(1)} %get-tuple-element.69), channel_id=1, source_target_pairs={{0,1},{1,0},{2,3},{3,2},{4,5},{5,4},{6,7},{7,6},{8,9},{9,8},{10,11... | collective-permute-start | bytes 55304 | tf_op jit(solution)/shard_map/ppermute | solution.py:39

commit v9 on v8

--- a/solution.py
+++ b/solution.py
@@ -353,9 +353,9 @@
                     jnp.where(rep ^ apart == index, full[:, index * group : (index + 1) * group], 0.0)
                     for index in range(rep_size)
                 ).astype(jnp.bfloat16)
-                for apart in (0, *APART)
+                for apart in (0, *APART_FIRST)
             ]
-            parts = pieces[:1] + [along_rep(piece, apart) for piece, apart in zip(pieces[1:], APART)]
+            parts = pieces[:1] + [along_rep(piece, apart) for piece, apart in zip(pieces[1:], APART_FIRST)]
             return run_last(parts, diag, results, right_sides.shape)
         parts = [partial] + [
             along_rep(partial, apart) for apart in (APART if level else APART_FIRST)

time: 73.6 us -> 73.8 us (level)
  transfers between devices with their start and end apart: 24 -> 24, of which waited for: 15 -> 14; matrix products, arithmetic and copies ran while one was open for 0% -> 0% of each run, Pallas kernels for 16% -> 16%
where the time goes in v9:
time: 73.8 us; the launch traced here: 73.5 us
  starting transfers between devices  31 us (42%)
  waiting for transfers between devices  24.4 us (33%)
  Pallas kernels  16.1 us (22%)
  other arithmetic  0.9 us (1%)
  local copies, waits for them, and re-layouts  0.8 us (1%)
    ppermute x12, starting transfers between devices, along_rep(): lax.ppermute(value, 'rep', [(i, i ^ apart) for i in range(lax.axis_size('...  16.5 us
    ppermute x12, starting transfers between devices, dom_permute(): lax.ppermute(value, 'dom', [(i, target(i) % size) for i in range(size)])  14.6 us
    ppermute x12, waiting for transfers between devices, along_rep(): lax.ppermute(value, 'rep', [(i, i ^ apart) for i in range(lax.axis_size('...  12.4 us
    ppermute x12, waiting for transfers between devices, dom_permute(): lax.ppermute(value, 'dom', [(i, target(i) % size) for i in range(size)])  12 us
    pallas_call x3, Pallas kernels, next_diag(): pl.pallas_call(functools.partial(next_diag_body, level), out_shape=[jax.S...  4.39 us
    pallas_call x3, Pallas kernels, run_panels(): pl.pallas_call(functools.partial(panels_body, level), out_shape=[jax.Shap...  4 us
    pallas_call x3, Pallas kernels, run_solve(): pl.pallas_call(functools.partial(solve_body, level, last), out_shape=outs...  3.57 us
    pallas_call x1, Pallas kernels, fetch(): pl.pallas_call(functools.partial(fetch_body, lax.axis_size('dom')), out_s...  3.1 us
  transfers between devices with their start and end apart: 24, of which 14 were waited for; matrix products, arithmetic and copies ran while one was open for 0% of the time, Pallas kernels for 16%

profile of v9, /device:TPU:0, one launch (start us, length us, event | category | flops | bytes accessed | tf_op | source)
XLA Modules:
  0.0 73.5 jit_solution(4213136755660980346)
XLA Ops:
  0.0 0.8 %fusion.14.refs_1_.refs_2_ = bf16[6,4,384]{2,1,0:T(4,128)(2,1)S(1)} fusion(f32[4,6,4,384]{3,2,1,0:T(4,128)} %param.5), kind=kLoop, calls=%fused_computation.39 | loop fusion | bytes 36864 | tf_op jit(solution)/shard_map/convert_element_type | solution.py:337
  0.8 4.1 %collective-permute-start = (bf16[6,4,384]{2,1,0:T(4,128)(2,1)S(1)}, bf16[6,4,384]{2,1,0:T(4,128)(2,1)S(1)}, u32[]{:S(2)}, u32[]{:S(2)}) collective-permute-start(bf16[6,4,384]{2,1,0:T(4,128)(2,1)S(1)} %fusion.14.refs_1_.refs_2_), channel_id=1, source_target_pairs={{0,3},{1,2},{2,1},{3,0},{4,7},{5,6},{6,5},{7,4},{8,11},{9,10},{10,... | collective-permute-start | bytes 55304 | tf_op jit(solution)/shard_map/ppermute | solution.py:39
  4.9 0.9 %collective-permute-start.2 = (bf16[6,4,384]{2,1,0:T(4,128)(2,1)S(1)}, bf16[6,4,384]{2,1,0:T(4,128)(2,1)S(1)}, u32[]{:S(2)}, u32[]{:S(2)}) collective-permute-start(bf16[6,4,384]{2,1,0:T(4,128)(2,1)S(1)} %fusion.14.refs_1_.refs_2_), channel_id=1, source_target_pairs={{0,1},{1,0},{2,3},{3,2},{4,5},{5,4},{6,7},{7,6},{8,9},{9,8},{10,11... | collective-permute-start | bytes 55304 | tf_op jit(solution)/shard_map/ppermute | solution.py:39
  5.8 3.1 %shard_map.55 = (s32[2,16]{1,0:T(2,128)S(1)}, s32[2,16]{1,0:T(2,128)S(1)}, s32[2,16]{1,0:T(2,128)S(1)}, bf16[1,6,384,384]{3,2,1,0:T(8,128)(2,1)S(1)}, bf16[1,16,384,384]{3,2,1,0:T(8,128)(2,1)S(1)}) custom-call(s32[1]{0:T(128)} %bitcast.1.refs_0_, bf16[6,4,384]{2,1,0:T(4,128)(2,1)S(1)} %fusion.14.refs_1_.refs_2_, s32[3,16]{1,0:T(4,128)} %refs_2_.4, ...), custom_call_target="tpu_custom_call" | custom-call | tf_op jit(solution)/shard_map/pallas_call | solution.py:288
  9.0 0.0 collective-permute-done.refs_3_
  9.0 1.2 %collective-permute-done.1.refs_4_ = bf16[6,4,384]{2,1,0:T(4,128)(2,1)S(1)} collective-permute-done((bf16[6,4,384]{2,1,0:T(4,128)(2,1)S(1)}, bf16[6,4,384]{2,1,0:T(4,128)(2,1)S(1)}, u32[]{:S(2)}, u32[]{:S(2)}) %collective-permute-start.1) | collective-permute-done | bytes 18464 | tf_op jit(solution)/shard_map/ppermute | solution.py:39
  10.2 0.0 collective-permute-done.2.refs_5_
  10.2 1.2 %shard_map.56 = (f32[6,4,384]{2,1,0:T(4,128)S(1)}, bf16[6,16,384]{2,1,0:T(8,128)(2,1)S(1)}, bf16[6,16,384]{2,1,0:T(8,128)(2,1)S(1)}) custom-call(s32[1]{0:T(128)} %bitcast.3.refs_0_, s32[2,16]{1,0:T(2,128)S(1)} %get-tuple-element.38.refs_1_.refs_0_, bf16[6,4,384]{2,1,0:T(4,128)(2,1)S(1)} %fusion.14.refs_1_.refs_2_, ...), custom_call_target="tpu_custom_call" | custom-call | tf_op jit(solution)/shard_map/pallas_call | solution.py:205
  11.4 0.1 collective-permute-start.3
  11.5 0.0 slice-start.3
  11.5 1.3 %shard_map.57 = (bf16[6,16,384]{2,1,0:T(8,128)(2,1)S(1)}, bf16[6,16,384]{2,1,0:T(8,128)(2,1)S(1)}, bf16[6,16,384]{2,1,0:T(8,128)(2,1)S(1)}, bf16[2,6,16,384]{3,2,1,0:T(8,128)(2,1)S(1)}) custom-call(s32[2,16]{1,0:T(2,128)S(1)} %get-tuple-element.38.refs_1_.refs_0_, bf16[1,16,384,384]{3,2,1,0:T(8,128)(2,1)S(1)} %get-tuple-element.40.refs_7_.refs_1_, ...), custom_call_target="tpu_custom_call" | custom-call | tf_op jit(solution)/shard_map/pallas_call | solution.py:219
  12.8 0.0 collective-permute-done.3
  12.8 0.1 add_convert_fusion.2.refs_0_
  13.0 5.4 %collective-permute-start.4 = (bf16[2,6,16,384]{3,2,1,0:T(8,128)(2,1)S(1)}, bf16[2,6,16,384]{3,2,1,0:T(8,128)(2,1)S(1)}, u32[]{:S(2)}, u32[]{:S(2)}) collective-permute-start(bf16[2,6,16,384]{3,2,1,0:T(8,128)(2,1)S(1)} %add_convert_fusion.2.refs_0_), channel_id=1, source_target_pairs={{0,124},{4,8},{8,4},{12,16},{16,12},{20,24},{24,20},{28,32},{32,28... | collective-permute-start | bytes 442376 | tf_op jit(solution)/shard_map/ppermute | solution.py:22
  18.4 0.7 collective-permute-start.5
  19.1 1.5 %shard_map.58 = (bf16[6,16,384]{2,1,0:T(8,128)(2,1)S(1)}, bf16[1,6,384,384]{3,2,1,0:T(8,128)(2,1)S(1)}) custom-call(bf16[2,6,16,384]{3,2,1,0:T(8,128)(2,1)S(1)} %add_convert_fusion.2.refs_0_, bf16[6,16,384]{2,1,0:T(8,128)(2,1)S(1)} %get-tuple-element.47.refs_1_, bf16[4,6,384,384]{3,2,1,0:T(8,128)(2,1)} %refs_2_.7), custom_call_target="tpu_custom_call" | custom-call | tf_op jit(solution)/shard_map/pallas_call | solution.py:318
  20.6 0.7 collective-permute-done.4
  21.2 0.1 collective-permute-start.6
  21.3 0.1 maximum_select_fusion
  21.5 2.8 %collective-permute-done.5 = bf16[6,16,384]{2,1,0:T(8,128)(2,1)S(1)} collective-permute-done((bf16[6,16,384]{2,1,0:T(8,128)(2,1)S(1)}, bf16[6,16,384]{2,1,0:T(8,128)(2,1)S(1)}, u32[]{:S(2)}, u32[]{:S(2)}) %collective-permute-start.5) | collective-permute-done | bytes 73760 | tf_op jit(solution)/shard_map/ppermute | solution.py:22
  24.3 0.0 collective-permute-done.6
  24.3 0.1 fusion.3.refs_2_
  24.4 2.1 %collective-permute-start.7 = (bf16[6,16,384]{2,1,0:T(8,128)(2,1)S(1)}, bf16[6,16,384]{2,1,0:T(8,128)(2,1)S(1)}, u32[]{:S(2)}, u32[]{:S(2)}) collective-permute-start(bf16[6,16,384]{2,1,0:T(8,128)(2,1)S(1)} %fusion.3.refs_2_), channel_id=1, source_target_pairs={{0,2},{1,3},{2,0},{3,1},{4,6},{5,7},{6,4},{7,5},{8,10},{9,11},{10,... | collective-permute-start | bytes 221192 | tf_op jit(solution)/shard_map/ppermute | solution.py:39
  26.5 0.6 collective-permute-start.8
  27.0 0.9 %collective-permute-start.9 = (bf16[6,16,384]{2,1,0:T(8,128)(2,1)S(1)}, bf16[6,16,384]{2,1,0:T(8,128)(2,1)S(1)}, u32[]{:S(2)}, u32[]{:S(2)}) collective-permute-start(bf16[6,16,384]{2,1,0:T(8,128)(2,1)S(1)} %fusion.3.refs_2_), channel_id=1, source_target_pairs={{0,1},{1,0},{2,3},{3,2},{4,5},{5,4},{6,7},{7,6},{8,9},{9,8},{10,11... | collective-permute-start | bytes 221192 | tf_op jit(solution)/shard_map/ppermute | solution.py:39
  27.9 3.0 %collective-permute-done.7.refs_3_ = bf16[6,16,384]{2,1,0:T(8,128)(2,1)S(1)} collective-permute-done((bf16[6,16,384]{2,1,0:T(8,128)(2,1)S(1)}, bf16[6,16,384]{2,1,0:T(8,128)(2,1)S(1)}, u32[]{:S(2)}, u32[]{:S(2)}) %collective-permute-start.7) | collective-permute-done | bytes 73760 | tf_op jit(solution)/shard_map/ppermute | solution.py:39
  31.0 1.1 %collective-permute-done.8.refs_4_ = bf16[6,16,384]{2,1,0:T(8,128)(2,1)S(1)} collective-permute-done((bf16[6,16,384]{2,1,0:T(8,128)(2,1)S(1)}, bf16[6,16,384]{2,1,0:T(8,128)(2,1)S(1)}, u32[]{:S(2)}, u32[]{:S(2)}) %collective-permute-start.8) | collective-permute-done | bytes 73760 | tf_op jit(solution)/shard_map/ppermute | solution.py:39
  32.0 0.0 collective-permute-done.9.refs_5_
  32.1 1.2 %shard_map.59 = (f32[6,4,384]{2,1,0:T(4,128)S(1)}, bf16[6,16,384]{2,1,0:T(8,128)(2,1)S(1)}, bf16[6,16,384]{2,1,0:T(8,128)(2,1)S(1)}) custom-call(s32[1]{0:T(128)} %bitcast.3.refs_0_, s32[2,16]{1,0:T(2,128)S(1)} %get-tuple-element.42.refs_1_.refs_0_, bf16[6,16,384]{2,1,0:T(8,128)(2,1)S(1)} %fusion.3.refs_2_, ...), custom_call_target="tpu_custom_call" | custom-call | tf_op jit(solution)/shard_map/pallas_call | solution.py:205
  33.2 0.1 collective-permute-start.10
  33.3 1.3 %shard_map.60 = (bf16[6,16,384]{2,1,0:T(8,128)(2,1)S(1)}, bf16[6,16,384]{2,1,0:T(8,128)(2,1)S(1)}, bf16[6,16,384]{2,1,0:T(8,128)(2,1)S(1)}, bf16[2,6,16,384]{3,2,1,0:T(8,128)(2,1)S(1)}) custom-call(s32[2,16]{1,0:T(2,128)S(1)} %get-tuple-element.42.refs_1_.refs_0_, bf16[3,16,384,384]{3,2,1,0:T(8,128)(2,1)S(1)} %bitcast.51, ...), custom_call_target="tpu_custom_call" | custom-call | tf_op jit(solution)/shard_map/pallas_call | solution.py:219
  34.7 0.1 add_convert_fusion.1.refs_0_
  34.8 4.3 %collective-permute-start.11 = (bf16[2,6,16,384]{3,2,1,0:T(8,128)(2,1)S(1)}, bf16[2,6,16,384]{3,2,1,0:T(8,128)(2,1)S(1)}, u32[]{:S(2)}, u32[]{:S(2)}) collective-permute-start(bf16[2,6,16,384]{3,2,1,0:T(8,128)(2,1)S(1)} %add_convert_fusion.1.refs_0_), channel_id=1, source_target_pairs={{0,124},{4,8},{8,4},{12,16},{16,12},{20,24},{24,20},{28,32},{32,28... | collective-permute-start | bytes 442376 | tf_op jit(solution)/shard_map/ppermute | solution.py:22
  39.1 1.5 %shard_map.61 = (bf16[6,16,384]{2,1,0:T(8,128)(2,1)S(1)}, bf16[1,6,384,384]{3,2,1,0:T(8,128)(2,1)S(1)}) custom-call(bf16[2,6,16,384]{3,2,1,0:T(8,128)(2,1)S(1)} %add_convert_fusion.1.refs_0_, bf16[6,16,384]{2,1,0:T(8,128)(2,1)S(1)} %get-tuple-element.55.refs_1_, bf16[4,6,384,384]{3,2,1,0:T(8,128)(2,1)} %refs_2_.7), custom_call_target="tpu_custom_call" | custom-call | tf_op jit(solution)/shard_map/pallas_call | solution.py:318
  40.6 2.3 %collective-permute-done.11 = bf16[2,6,16,384]{3,2,1,0:T(8,128)(2,1)S(1)} collective-permute-done((bf16[2,6,16,384]{3,2,1,0:T(8,128)(2,1)S(1)}, bf16[2,6,16,384]{3,2,1,0:T(8,128)(2,1)S(1)}, u32[]{:S(2)}, u32[]{:S(2)}) %collective-permute-start.11) | collective-permute-done | bytes 147488 | tf_op jit(solution)/shard_map/ppermute | solution.py:22
  42.9 0.1 collective-permute-start.13
  43.0 2.0 %collective-permute-done.12 = bf16[6,16,384]{2,1,0:T(8,128)(2,1)S(1)} collective-permute-done((bf16[6,16,384]{2,1,0:T(8,128)(2,1)S(1)}, bf16[6,16,384]{2,1,0:T(8,128)(2,1)S(1)}, u32[]{:S(2)}, u32[]{:S(2)}) %collective-permute-start.12) | collective-permute-done | bytes 73760 | tf_op jit(solution)/shard_map/ppermute | solution.py:22
  45.0 0.0 collective-permute-done.13
  45.0 0.1 fusion.1.refs_2_
  45.1 1.8 %collective-permute-start.14 = (bf16[6,16,384]{2,1,0:T(8,128)(2,1)S(1)}, bf16[6,16,384]{2,1,0:T(8,128)(2,1)S(1)}, u32[]{:S(2)}, u32[]{:S(2)}) collective-permute-start(bf16[6,16,384]{2,1,0:T(8,128)(2,1)S(1)} %fusion.1.refs_2_), channel_id=1, source_target_pairs={{0,2},{1,3},{2,0},{3,1},{4,6},{5,7},{6,4},{7,5},{8,10},{9,11},{10,... | collective-permute-start | bytes 221192 | tf_op jit(solution)/shard_map/ppermute | solution.py:39
  46.9 1.5 %collective-permute-start.15 = (bf16[6,16,384]{2,1,0:T(8,128)(2,1)S(1)}, bf16[6,16,384]{2,1,0:T(8,128)(2,1)S(1)}, u32[]{:S(2)}, u32[]{:S(2)}) collective-permute-start(bf16[6,16,384]{2,1,0:T(8,128)(2,1)S(1)} %fusion.1.refs_2_), channel_id=1, source_target_pairs={{0,3},{1,2},{2,1},{3,0},{4,7},{5,6},{6,5},{7,4},{8,11},{9,10},{10,... | collective-permute-start | bytes 221192 | tf_op jit(solution)/shard_map/ppermute | solution.py:39
  48.4 0.3 collective-permute-start.16
  48.6 2.5 %collective-permute-done.14.refs_3_ = bf16[6,16,384]{2,1,0:T(8,128)(2,1)S(1)} collective-permute-done((bf16[6,16,384]{2,1,0:T(8,128)(2,1)S(1)}, bf16[6,16,384]{2,1,0:T(8,128)(2,1)S(1)}, u32[]{:S(2)}, u32[]{:S(2)}) %collective-permute-start.14) | collective-permute-done | bytes 73760 | tf_op jit(solution)/shard_map/ppermute | solution.py:39
  51.1 1.3 %collective-permute-done.15.refs_4_ = bf16[6,16,384]{2,1,0:T(8,128)(2,1)S(1)} collective-permute-done((bf16[6,16,384]{2,1,0:T(8,128)(2,1)S(1)}, bf16[6,16,384]{2,1,0:T(8,128)(2,1)S(1)}, u32[]{:S(2)}, u32[]{:S(2)}) %collective-permute-start.15) | collective-permute-done | bytes 73760 | tf_op jit(solution)/shard_map/ppermute | solution.py:39
  52.4 0.3 collective-permute-done.16.refs_5_
  52.7 1.2 %shard_map.62 = (f32[6,4,384]{2,1,0:T(4,128)S(1)}, bf16[6,16,384]{2,1,0:T(8,128)(2,1)S(1)}, bf16[6,16,384]{2,1,0:T(8,128)(2,1)S(1)}) custom-call(s32[1]{0:T(128)} %bitcast.3.refs_0_, s32[2,16]{1,0:T(2,128)S(1)} %get-tuple-element.37.refs_1_.refs_0_, bf16[6,16,384]{2,1,0:T(8,128)(2,1)S(1)} %fusion.1.refs_2_, ...), custom_call_target="tpu_custom_call" | custom-call | tf_op jit(solution)/shard_map/pallas_call | solution.py:205
  53.9 0.1 collective-permute-start.17
  54.0 1.3 %shard_map.63 = (bf16[6,16,384]{2,1,0:T(8,128)(2,1)S(1)}, bf16[6,16,384]{2,1,0:T(8,128)(2,1)S(1)}, bf16[6,16,384]{2,1,0:T(8,128)(2,1)S(1)}, bf16[2,6,16,384]{3,2,1,0:T(8,128)(2,1)S(1)}) custom-call(s32[2,16]{1,0:T(2,128)S(1)} %get-tuple-element.37.refs_1_.refs_0_, bf16[3,16,384,384]{3,2,1,0:T(8,128)(2,1)S(1)} %bitcast.51, ...), custom_call_target="tpu_custom_call" | custom-call | tf_op jit(solution)/shard_map/pallas_call | solution.py:219
  55.4 0.0 collective-permute-done.17
  55.4 0.1 add_convert_fusion.refs_0_
  55.5 3.6 %collective-permute-start.18 = (bf16[2,6,16,384]{3,2,1,0:T(8,128)(2,1)S(1)}, bf16[2,6,16,384]{3,2,1,0:T(8,128)(2,1)S(1)}, u32[]{:S(2)}, u32[]{:S(2)}) collective-permute-start(bf16[2,6,16,384]{3,2,1,0:T(8,128)(2,1)S(1)} %add_convert_fusion.refs_0_), channel_id=1, source_target_pairs={{0,124},{4,8},{8,4},{12,16},{16,12},{20,24},{24,20},{28,32},{32,28... | collective-permute-start | bytes 442376 | tf_op jit(solution)/shard_map/ppermute | solution.py:22
  59.2 0.0 collective-permute-start.19
  59.2 1.5 %shard_map.64 = (bf16[6,16,384]{2,1,0:T(8,128)(2,1)S(1)}, bf16[1,6,384,384]{3,2,1,0:T(8,128)(2,1)S(1)}) custom-call(bf16[2,6,16,384]{3,2,1,0:T(8,128)(2,1)S(1)} %add_convert_fusion.refs_0_, bf16[6,16,384]{2,1,0:T(8,128)(2,1)S(1)} %get-tuple-element.63.refs_1_, bf16[4,6,384,384]{3,2,1,0:T(8,128)(2,1)} %refs_2_.7), custom_call_target="tpu_custom_call" | custom-call | tf_op jit(solution)/shard_map/pallas_call | solution.py:318
  60.6 2.9 %collective-permute-done.18 = bf16[2,6,16,384]{3,2,1,0:T(8,128)(2,1)S(1)} collective-permute-done((bf16[2,6,16,384]{3,2,1,0:T(8,128)(2,1)S(1)}, bf16[2,6,16,384]{3,2,1,0:T(8,128)(2,1)S(1)}, u32[]{:S(2)}, u32[]{:S(2)}) %collective-permute-start.18) | collective-permute-done | bytes 147488 | tf_op jit(solution)/shard_map/ppermute | solution.py:22
  63.5 0.1 collective-permute-start.20
  63.6 1.4 %collective-permute-done.19 = bf16[6,16,384]{2,1,0:T(8,128)(2,1)S(1)} collective-permute-done((bf16[6,16,384]{2,1,0:T(8,128)(2,1)S(1)}, bf16[6,16,384]{2,1,0:T(8,128)(2,1)S(1)}, u32[]{:S(2)}, u32[]{:S(2)}) %collective-permute-start.19) | collective-permute-done | bytes 73760 | tf_op jit(solution)/shard_map/ppermute | solution.py:22
  65.1 0.1 add_convert_fusion.4
  65.1 2.1 %collective-permute-start.21 = (bf16[6,4,384]{2,1,0:T(4,128)(2,1)S(1)}, bf16[6,4,384]{2,1,0:T(4,128)(2,1)S(1)}, u32[]{:S(2)}, u32[]{:S(2)}) collective-permute-start(bf16[6,4,384]{2,1,0:T(4,128)(2,1)S(1)} %get-tuple-element.72), channel_id=1, source_target_pairs={{0,3},{1,2},{2,1},{3,0},{4,7},{5,6},{6,5},{7,4},{8,11},{9,10},{10,... | collective-permute-start | bytes 55304 | tf_op jit(solution)/shard_map/ppermute | solution.py:39
  67.2 0.6 collective-permute-start.22
  67.8 0.1 add_convert_fusion.3
  67.9 1.5 %collective-permute-start.23 = (bf16[6,4,384]{2,1,0:T(4,128)(2,1)S(1)}, bf16[6,4,384]{2,1,0:T(4,128)(2,1)S(1)}, u32[]{:S(2)}, u32[]{:S(2)}) collective-permute-start(bf16[6,4,384]{2,1,0:T(4,128)(2,1)S(1)} %get-tuple-element.69), channel_id=1, source_target_pairs={{0,1},{1,0},{2,3},{3,2},{4,5},{5,4},{6,7},{7,6},{8,9},{9,8},{10,11... | collective-permute-start | bytes 55304 | tf_op jit(solution)/shard_map/ppermute | solution.py:39
  69.4 0.7 %collective-permute-done.21.refs_1_ = bf16[6,4,384]{2,1,0:T(4,128)(2,1)S(1)} collective-permute-done((bf16[6,4,384]{2,1,0:T(4,128)(2,1)S(1)}, bf16[6,4,384]{2,1,0:T(4,128)(2,1)S(1)}, u32[]{:S(2)}, u32[]{:S(2)}) %collective-permute-start.21) | collective-permute-done | bytes 18464 | tf_op jit(solution)/shard_map/ppermute | solution.py:39
  70.2 2.3 %collective-permute-done.22.refs_2_ = bf16[6,4,384]{2,1,0:T(4,128)(2,1)S(1)} collective-permute-done((bf16[6,4,384]{2,1,0:T(4,128)(2,1)S(1)}, bf16[6,4,384]{2,1,0:T(4,128)(2,1)S(1)}, u32[]{:S(2)}, u32[]{:S(2)}) %collective-permute-start.22) | collective-permute-done | bytes 18464 | tf_op jit(solution)/shard_map/ppermute | solution.py:39
  72.5 1.0 %shard_map.65 = f32[4,6,4,384]{3,2,1,0:T(4,128)} custom-call(bf16[6,4,384]{2,1,0:T(4,128)(2,1)S(1)} %get-tuple-element.70.refs_0_, bf16[6,4,384]{2,1,0:T(4,128)(2,1)S(1)} %collective-permute-done.21.refs_1_, bf16[6,4,384]{2,1,0:T(4,128)(2,1)S(1)} %collective-permute-done.22.refs_2_, bf16[6,4,384]{2,1,0:T(4,128)(2,1)S(1)} %collective-permute-done.23.refs_3_, ...), custom_call_target="tpu_custom_call" | custom-call | tf_op jit(solution)/shard_map/pallas_call | solution.py:178
  (22 shorter events, 0.2 us)
Async XLA Ops:
  0.8 8.2 %collective-permute-start = (bf16[6,4,384]{2,1,0:T(4,128)(2,1)S(1)}, bf16[6,4,384]{2,1,0:T(4,128)(2,1)S(1)}, u32[]{:S(2)}, u32[]{:S(2)}) collective-permute-start(bf16[6,4,384]{2,1,0:T(4,128)(2,1)S(1)} %fusion.14.refs_1_.refs_2_), channel_id=1, source_target_pairs={{0,3},{1,2},{2,1},{3,0},{4,7},{5,6},{6,5},{7,4},{8,11},{9,10},{10,... | collective-permute-start | bytes 55304 | tf_op jit(solution)/shard_map/ppermute | solution.py:39
  4.9 5.3 %collective-permute-start.1 = (bf16[6,4,384]{2,1,0:T(4,128)(2,1)S(1)}, bf16[6,4,384]{2,1,0:T(4,128)(2,1)S(1)}, u32[]{:S(2)}, u32[]{:S(2)}) collective-permute-start(bf16[6,4,384]{2,1,0:T(4,128)(2,1)S(1)} %fusion.14.refs_1_.refs_2_), channel_id=1, source_target_pairs={{0,2},{1,3},{2,0},{3,1},{4,6},{5,7},{6,4},{7,5},{8,10},{9,11},{10,... | collective-permute-start | bytes 55304 | tf_op jit(solution)/shard_map/ppermute | solution.py:39
  4.9 5.3 %collective-permute-start.2 = (bf16[6,4,384]{2,1,0:T(4,128)(2,1)S(1)}, bf16[6,4,384]{2,1,0:T(4,128)(2,1)S(1)}, u32[]{:S(2)}, u32[]{:S(2)}) collective-permute-start(bf16[6,4,384]{2,1,0:T(4,128)(2,1)S(1)} %fusion.14.refs_1_.refs_2_), channel_id=1, source_target_pairs={{0,1},{1,0},{2,3},{3,2},{4,5},{5,4},{6,7},{7,6},{8,9},{9,8},{10,11... | collective-permute-start | bytes 55304 | tf_op jit(solution)/shard_map/ppermute | solution.py:39
  5.8 26.2 %slice-start = ((s8[14155776]{0:T(1024)(128)(4,1)}), s8[4194304]{0:T(1024)(128)(4,1)S(1)}, s32[]{:S(2)}) async-start(s8[14155776]{0:T(1024)(128)(4,1)} %bitcast.50), calls=%async_computation | async-start | bytes 8388608
  5.8 26.2 %slice-start.1 = ((s8[14155776]{0:T(1024)(128)(4,1)}), s8[4194304]{0:T(1024)(128)(4,1)S(1)}, s32[]{:S(2)}) async-start(s8[14155776]{0:T(1024)(128)(4,1)} %bitcast.50), calls=%async_computation.1 | async-start | bytes 8388608
  5.8 26.2 %slice-start.2 = ((s8[14155776]{0:T(1024)(128)(4,1)}), s8[4194304]{0:T(1024)(128)(4,1)S(1)}, s32[]{:S(2)}) async-start(s8[14155776]{0:T(1024)(128)(4,1)} %bitcast.50), calls=%async_computation.2 | async-start | bytes 8388608
  11.4 1.5 %collective-permute-start.3 = (bf16[6,16,384]{2,1,0:T(8,128)(2,1)S(1)}, bf16[6,16,384]{2,1,0:T(8,128)(2,1)S(1)}, u32[]{:S(2)}, u32[]{:S(2)}) collective-permute-start(bf16[6,16,384]{2,1,0:T(8,128)(2,1)S(1)} %get-tuple-element.45), channel_id=1, source_target_pairs={{0,4},{4,0},{8,12},{12,8},{16,20},{20,16},{24,28},{28,24},{32,36},... | collective-permute-start | bytes 221192 | tf_op jit(solution)/shard_map/ppermute | solution.py:22
  11.5 20.6 %slice-start.3 = ((s8[14155776]{0:T(1024)(128)(4,1)}), s8[1572864]{0:T(1024)(128)(4,1)S(1)}, s32[]{:S(2)}) async-start(s8[14155776]{0:T(1024)(128)(4,1)} %bitcast.50), calls=%async_computation.3 | async-start | bytes 3145728
  13.0 8.2 %collective-permute-start.4 = (bf16[2,6,16,384]{3,2,1,0:T(8,128)(2,1)S(1)}, bf16[2,6,16,384]{3,2,1,0:T(8,128)(2,1)S(1)}, u32[]{:S(2)}, u32[]{:S(2)}) collective-permute-start(bf16[2,6,16,384]{3,2,1,0:T(8,128)(2,1)S(1)} %add_convert_fusion.2.refs_0_), channel_id=1, source_target_pairs={{0,124},{4,8},{8,4},{12,16},{16,12},{20,24},{24,20},{28,32},{32,28... | collective-permute-start | bytes 442376 | tf_op jit(solution)/shard_map/ppermute | solution.py:22
  18.4 5.9 %collective-permute-start.5 = (bf16[6,16,384]{2,1,0:T(8,128)(2,1)S(1)}, bf16[6,16,384]{2,1,0:T(8,128)(2,1)S(1)}, u32[]{:S(2)}, u32[]{:S(2)}) collective-permute-start(bf16[6,16,384]{2,1,0:T(8,128)(2,1)S(1)} %get-tuple-element.46), channel_id=1, source_target_pairs={{0,64},{4,68},{8,72},{12,76},{16,80},{20,84},{24,88},{28,92},{32,9... | collective-permute-start | bytes 221192 | tf_op jit(solution)/shard_map/ppermute | solution.py:22
  19.1 2.3 %copy-start = (f32[4,6,4,384]{3,2,1,0:T(4,128)S(1)}, f32[4,6,4,384]{3,2,1,0:T(4,128)}, u32[]{:S(2)}) copy-start(f32[4,6,4,384]{3,2,1,0:T(4,128)} %param.5) | copy-start | bytes 442372
  21.2 3.1 %collective-permute-start.6 = (bf16[6,16,384]{2,1,0:T(8,128)(2,1)S(1)}, bf16[6,16,384]{2,1,0:T(8,128)(2,1)S(1)}, u32[]{:S(2)}, u32[]{:S(2)}) collective-permute-start(bf16[6,16,384]{2,1,0:T(8,128)(2,1)S(1)} %fusion.11), channel_id=1, source_target_pairs={{0,4},{4,0},{8,12},{12,8},{16,20},{20,16},{24,28},{28,24},{32,36},... | collective-permute-start | bytes 221192 | tf_op jit(solution)/shard_map/ppermute | solution.py:22
  24.4 6.6 %collective-permute-start.7 = (bf16[6,16,384]{2,1,0:T(8,128)(2,1)S(1)}, bf16[6,16,384]{2,1,0:T(8,128)(2,1)S(1)}, u32[]{:S(2)}, u32[]{:S(2)}) collective-permute-start(bf16[6,16,384]{2,1,0:T(8,128)(2,1)S(1)} %fusion.3.refs_2_), channel_id=1, source_target_pairs={{0,2},{1,3},{2,0},{3,1},{4,6},{5,7},{6,4},{7,5},{8,10},{9,11},{10,... | collective-permute-start | bytes 221192 | tf_op jit(solution)/shard_map/ppermute | solution.py:39
  26.5 5.6 %collective-permute-start.8 = (bf16[6,16,384]{2,1,0:T(8,128)(2,1)S(1)}, bf16[6,16,384]{2,1,0:T(8,128)(2,1)S(1)}, u32[]{:S(2)}, u32[]{:S(2)}) collective-permute-start(bf16[6,16,384]{2,1,0:T(8,128)(2,1)S(1)} %fusion.3.refs_2_), channel_id=1, source_target_pairs={{0,3},{1,2},{2,1},{3,0},{4,7},{5,6},{6,5},{7,4},{8,11},{9,10},{10,... | collective-permute-start | bytes 221192 | tf_op jit(solution)/shard_map/ppermute | solution.py:39
  27.0 5.0 %collective-permute-start.9 = (bf16[6,16,384]{2,1,0:T(8,128)(2,1)S(1)}, bf16[6,16,384]{2,1,0:T(8,128)(2,1)S(1)}, u32[]{:S(2)}, u32[]{:S(2)}) collective-permute-start(bf16[6,16,384]{2,1,0:T(8,128)(2,1)S(1)} %fusion.3.refs_2_), channel_id=1, source_target_pairs={{0,1},{1,0},{2,3},{3,2},{4,5},{5,4},{6,7},{7,6},{8,9},{9,8},{10,11... | collective-permute-start | bytes 221192 | tf_op jit(solution)/shard_map/ppermute | solution.py:39
  33.2 1.4 %collective-permute-start.10 = (bf16[6,16,384]{2,1,0:T(8,128)(2,1)S(1)}, bf16[6,16,384]{2,1,0:T(8,128)(2,1)S(1)}, u32[]{:S(2)}, u32[]{:S(2)}) collective-permute-start(bf16[6,16,384]{2,1,0:T(8,128)(2,1)S(1)} %get-tuple-element.53), channel_id=1, source_target_pairs={{0,4},{4,0},{8,12},{12,8},{16,20},{20,16},{24,28},{28,24},{32,36},... | collective-permute-start | bytes 221192 | tf_op jit(solution)/shard_map/ppermute | solution.py:22
  34.8 8.1 %collective-permute-start.11 = (bf16[2,6,16,384]{3,2,1,0:T(8,128)(2,1)S(1)}, bf16[2,6,16,384]{3,2,1,0:T(8,128)(2,1)S(1)}, u32[]{:S(2)}, u32[]{:S(2)}) collective-permute-start(bf16[2,6,16,384]{3,2,1,0:T(8,128)(2,1)S(1)} %add_convert_fusion.1.refs_0_), channel_id=1, source_target_pairs={{0,124},{4,8},{8,4},{12,16},{16,12},{20,24},{24,20},{28,32},{32,28... | collective-permute-start | bytes 442376 | tf_op jit(solution)/shard_map/ppermute | solution.py:22
  39.1 5.9 %collective-permute-start.12 = (bf16[6,16,384]{2,1,0:T(8,128)(2,1)S(1)}, bf16[6,16,384]{2,1,0:T(8,128)(2,1)S(1)}, u32[]{:S(2)}, u32[]{:S(2)}) collective-permute-start(bf16[6,16,384]{2,1,0:T(8,128)(2,1)S(1)} %get-tuple-element.54), channel_id=1, source_target_pairs={{0,64},{4,68},{8,72},{12,76},{16,80},{20,84},{24,88},{28,92},{32,9... | collective-permute-start | bytes 221192 | tf_op jit(solution)/shard_map/ppermute | solution.py:22
  42.9 2.1 %collective-permute-start.13 = (bf16[6,16,384]{2,1,0:T(8,128)(2,1)S(1)}, bf16[6,16,384]{2,1,0:T(8,128)(2,1)S(1)}, u32[]{:S(2)}, u32[]{:S(2)}) collective-permute-start(bf16[6,16,384]{2,1,0:T(8,128)(2,1)S(1)} %fusion.8), channel_id=1, source_target_pairs={{0,4},{4,0},{8,12},{12,8},{16,20},{20,16},{24,28},{28,24},{32,36},... | collective-permute-start | bytes 221192 | tf_op jit(solution)/shard_map/ppermute | solution.py:22
  45.1 6.1 %collective-permute-start.14 = (bf16[6,16,384]{2,1,0:T(8,128)(2,1)S(1)}, bf16[6,16,384]{2,1,0:T(8,128)(2,1)S(1)}, u32[]{:S(2)}, u32[]{:S(2)}) collective-permute-start(bf16[6,16,384]{2,1,0:T(8,128)(2,1)S(1)} %fusion.1.refs_2_), channel_id=1, source_target_pairs={{0,2},{1,3},{2,0},{3,1},{4,6},{5,7},{6,4},{7,5},{8,10},{9,11},{10,... | collective-permute-start | bytes 221192 | tf_op jit(solution)/shard_map/ppermute | solution.py:39
  46.9 5.6 %collective-permute-start.15 = (bf16[6,16,384]{2,1,0:T(8,128)(2,1)S(1)}, bf16[6,16,384]{2,1,0:T(8,128)(2,1)S(1)}, u32[]{:S(2)}, u32[]{:S(2)}) collective-permute-start(bf16[6,16,384]{2,1,0:T(8,128)(2,1)S(1)} %fusion.1.refs_2_), channel_id=1, source_target_pairs={{0,3},{1,2},{2,1},{3,0},{4,7},{5,6},{6,5},{7,4},{8,11},{9,10},{10,... | collective-permute-start | bytes 221192 | tf_op jit(solution)/shard_map/ppermute | solution.py:39
  48.4 4.4 %collective-permute-start.16 = (bf16[6,16,384]{2,1,0:T(8,128)(2,1)S(1)}, bf16[6,16,384]{2,1,0:T(8,128)(2,1)S(1)}, u32[]{:S(2)}, u32[]{:S(2)}) collective-permute-start(bf16[6,16,384]{2,1,0:T(8,128)(2,1)S(1)} %fusion.1.refs_2_), channel_id=1, source_target_pairs={{0,1},{1,0},{2,3},{3,2},{4,5},{5,4},{6,7},{7,6},{8,9},{9,8},{10,11... | collective-permute-start | bytes 221192 | tf_op jit(solution)/shard_map/ppermute | solution.py:39
  53.9 1.4 %collective-permute-start.17 = (bf16[6,16,384]{2,1,0:T(8,128)(2,1)S(1)}, bf16[6,16,384]{2,1,0:T(8,128)(2,1)S(1)}, u32[]{:S(2)}, u32[]{:S(2)}) collective-permute-start(bf16[6,16,384]{2,1,0:T(8,128)(2,1)S(1)} %get-tuple-element.61), channel_id=1, source_target_pairs={{0,4},{4,0},{8,12},{12,8},{16,20},{20,16},{24,28},{28,24},{32,36},... | collective-permute-start | bytes 221192 | tf_op jit(solution)/shard_map/ppermute | solution.py:22
  55.5 8.0 %collective-permute-start.18 = (bf16[2,6,16,384]{3,2,1,0:T(8,128)(2,1)S(1)}, bf16[2,6,16,384]{3,2,1,0:T(8,128)(2,1)S(1)}, u32[]{:S(2)}, u32[]{:S(2)}) collective-permute-start(bf16[2,6,16,384]{3,2,1,0:T(8,128)(2,1)S(1)} %add_convert_fusion.refs_0_), channel_id=1, source_target_pairs={{0,124},{4,8},{8,4},{12,16},{16,12},{20,24},{24,20},{28,32},{32,28... | collective-permute-start | bytes 442376 | tf_op jit(solution)/shard_map/ppermute | solution.py:22
  59.2 5.9 %collective-permute-start.19 = (bf16[6,16,384]{2,1,0:T(8,128)(2,1)S(1)}, bf16[6,16,384]{2,1,0:T(8,128)(2,1)S(1)}, u32[]{:S(2)}, u32[]{:S(2)}) collective-permute-start(bf16[6,16,384]{2,1,0:T(8,128)(2,1)S(1)} %get-tuple-element.62), channel_id=1, source_target_pairs={{0,64},{4,68},{8,72},{12,76},{16,80},{20,84},{24,88},{28,92},{32,9... | collective-permute-start | bytes 221192 | tf_op jit(solution)/shard_map/ppermute | solution.py:22
  63.5 1.5 %collective-permute-start.20 = (bf16[6,16,384]{2,1,0:T(8,128)(2,1)S(1)}, bf16[6,16,384]{2,1,0:T(8,128)(2,1)S(1)}, u32[]{:S(2)}, u32[]{:S(2)}) collective-permute-start(bf16[6,16,384]{2,1,0:T(8,128)(2,1)S(1)} %fusion.5), channel_id=1, source_target_pairs={{0,4},{4,0},{8,12},{12,8},{16,20},{20,16},{24,28},{28,24},{32,36},... | collective-permute-start | bytes 221192 | tf_op jit(solution)/shard_map/ppermute | solution.py:22
  65.1 5.1 %collective-permute-start.21 = (bf16[6,4,384]{2,1,0:T(4,128)(2,1)S(1)}, bf16[6,4,384]{2,1,0:T(4,128)(2,1)S(1)}, u32[]{:S(2)}, u32[]{:S(2)}) collective-permute-start(bf16[6,4,384]{2,1,0:T(4,128)(2,1)S(1)} %get-tuple-element.72), channel_id=1, source_target_pairs={{0,3},{1,2},{2,1},{3,0},{4,7},{5,6},{6,5},{7,4},{8,11},{9,10},{10,... | collective-permute-start | bytes 55304 | tf_op jit(solution)/shard_map/ppermute | solution.py:39
  67.2 5.3 %collective-permute-start.22 = (bf16[6,4,384]{2,1,0:T(4,128)(2,1)S(1)}, bf16[6,4,384]{2,1,0:T(4,128)(2,1)S(1)}, u32[]{:S(2)}, u32[]{:S(2)}) collective-permute-start(bf16[6,4,384]{2,1,0:T(4,128)(2,1)S(1)} %get-tuple-element.71), channel_id=1, source_target_pairs={{0,2},{1,3},{2,0},{3,1},{4,6},{5,7},{6,4},{7,5},{8,10},{9,11},{10,... | collective-permute-start | bytes 55304 | tf_op jit(solution)/shard_map/ppermute | solution.py:39
  67.9 4.6 %collective-permute-start.23 = (bf16[6,4,384]{2,1,0:T(4,128)(2,1)S(1)}, bf16[6,4,384]{2,1,0:T(4,128)(2,1)S(1)}, u32[]{:S(2)}, u32[]{:S(2)}) collective-permute-start(bf16[6,4,384]{2,1,0:T(4,128)(2,1)S(1)} %get-tuple-element.69), channel_id=1, source_target_pairs={{0,1},{1,0},{2,3},{3,2},{4,5},{5,4},{6,7},{7,6},{8,9},{9,8},{10,11... | collective-permute-start | bytes 55304 | tf_op jit(solution)/shard_map/ppermute | solution.py:39
